TPU v7x, 256 devices: a whole 4x4x8 slice. The times are simulated.
256 devices in a mesh: dp: 32 (over y_lo, z, core), seq: 8 (over y_hi, x).
Axes of the slice: x: 4, y: 4 (y_hi: 2, y_lo: 2; y = y_hi * 2 + y_lo), z: 8, core: 2. Of those that a mesh axis runs over, the one named last changes fastest.
Arguments:
- inputs: bfloat16 [32, 2048, 1024], P('dp', 'seq'), may hold values from -6 to 6
- d_output: bfloat16 [32, 2048, 1024], P('dp', 'seq'), may hold values from -0.046875 to 0.046875
- loss_mask: int32 [32, 2048], P('dp', 'seq'), may hold values 0 or 1
- queries: bfloat16 [32, 2048, 8, 128], P('dp', None, 'seq'), may hold values from -10 to 10
- keys: bfloat16 [32, 2048, 8, 128], P('dp', None, 'seq'), may hold values from -10 to 10
- values: bfloat16 [32, 2048, 8, 128], P('dp', None, 'seq'), may hold values from -6 to 6
- out_weight: bfloat16 [1024, 1024], P('dp'), may hold values from -0.1875 to 0.1875
- block_mask: int32 [32, 8, 16, 16], P('dp', 'seq'), may hold values from 0 to 1, as said below
Outputs:
- grad_query: float32 [128, 8, 1024], P('dp', 'seq')
- grad_key: float32 [128, 8, 1024], P('dp', 'seq')
- grad_value: float32 [128, 8, 1024], P('dp', 'seq')
- grad_out: float32 [128, 8, 1024], P('dp', 'seq')
Inputs may be any that keep to these rules, and one draw needn't show every extreme that they name: `block_mask`: every block on the diagonal is 1.
All inputs are finite; a program needn't handle non-finite values. No bound on the sum of `loss_mask` on one device may be relied on, other than what follows from the above.
Results may differ from a plain program's by a relative error of at most 0.025.
Values may be sent and summed in bfloat16 or wider, within the bound.
A program may use at most 128 MiB of HBM per device.

v0:
```python
import jax
import jax.numpy as jnp
from jax import lax
from jax.sharding import PartitionSpec as P

HW = 8
HD = 128


masked_score = -1e30


def expand_blocks(blocks, block_size):
    block_rows = blocks.shape[0]
    block_cols = blocks.shape[1]
    live_blocks = blocks[:, None, :, None] > 0
    return jnp.broadcast_to(live_blocks, (block_rows, block_size, block_cols, block_size)).reshape(
        block_rows * block_size, block_cols * block_size
    )


def head_backward(query_rows, key_rows, value_rows, grad_rows, blocks):
    length = query_rows.shape[0]
    head_width = query_rows.shape[1]
    block_size = length // blocks.shape[0]
    tile_rows = 4 * block_size
    tile_count = length // tile_rows
    softmax_scale = head_width ** (-0.5)
    tile_live = jnp.max(blocks.reshape(tile_count, 4, tile_count, 4), axis=(1, 3)) > 0
    key_tiles = key_rows.reshape(tile_count, tile_rows, head_width)
    value_tiles = value_rows.reshape(tile_count, tile_rows, head_width)

    def query_tile(carry, tile_index):
        key_sum, value_sum = carry
        first_row = tile_index * tile_rows
        query_part = lax.dynamic_slice_in_dim(query_rows, first_row, tile_rows, 0)
        grad_part = lax.dynamic_slice_in_dim(grad_rows, first_row, tile_rows, 0)
        block_band = lax.dynamic_slice_in_dim(blocks, tile_index * 4, 4, 0)
        live_flags = tile_live[tile_index]

        def score_tile(inner_index):
            sub_blocks = lax.dynamic_slice_in_dim(block_band, inner_index * 4, 4, 1)

            def compute_scores(unused_index):
                raw_scores = (
                    jnp.dot(
                        query_part, key_tiles[inner_index].T, preferred_element_type=jnp.float32
                    )
                    * softmax_scale
                )
                return jnp.where(expand_blocks(sub_blocks, block_size), raw_scores, masked_score)

            def empty_scores(unused_index):
                return jnp.full((tile_rows, tile_rows), masked_score, jnp.float32)

            return lax.cond(live_flags[inner_index], compute_scores, empty_scores, inner_index)

        scores = lax.map(score_tile, jnp.arange(tile_count))
        row_max = jnp.max(scores, axis=(0, 2))
        weights = jnp.exp(scores - row_max[None, :, None])
        row_total = jnp.sum(weights, axis=(0, 2))
        prob_full = weights / row_total[None, :, None]
        prob_low = prob_full.astype(jnp.bfloat16)

        def attend_tile(running, inner_index):

            def add_tile(partial_sum):
                return partial_sum + jnp.dot(
                    prob_low[inner_index],
                    value_tiles[inner_index],
                    preferred_element_type=jnp.float32,
                )

            def keep_tile(partial_sum):
                return partial_sum

            return (lax.cond(live_flags[inner_index], add_tile, keep_tile, running), None)

        output_sum, unused = lax.scan(
            attend_tile, jnp.zeros((tile_rows, head_width), jnp.float32), jnp.arange(tile_count)
        )
        attended = output_sum.astype(jnp.bfloat16)
        row_delta = jnp.sum(
            grad_part.astype(jnp.float32) * attended.astype(jnp.float32), axis=1, keepdims=True
        )

        def grad_tile(query_acc, inner_index):

            def compute_grads(running):
                d_prob = jnp.dot(
                    grad_part, value_tiles[inner_index].T, preferred_element_type=jnp.float32
                )
                d_score = (prob_full[inner_index] * (d_prob - row_delta)).astype(jnp.bfloat16)
                query_next = running + jnp.dot(
                    d_score, key_tiles[inner_index], preferred_element_type=jnp.float32
                )
                key_part = jnp.dot(d_score.T, query_part, preferred_element_type=jnp.float32)
                value_part = jnp.dot(
                    prob_low[inner_index].T, grad_part, preferred_element_type=jnp.float32
                )
                return (query_next, key_part, value_part)

            def skip_grads(running):
                blank_part = jnp.zeros((tile_rows, head_width), jnp.float32)
                return (running, blank_part, blank_part)

            query_next, key_part, value_part = lax.cond(
                live_flags[inner_index], compute_grads, skip_grads, query_acc
            )
            return (query_next, (key_part, value_part))

        query_acc, tile_parts = lax.scan(
            grad_tile, jnp.zeros((tile_rows, head_width), jnp.float32), jnp.arange(tile_count)
        )
        key_sum = key_sum + tile_parts[0].reshape(length, head_width)
        value_sum = value_sum + tile_parts[1].reshape(length, head_width)
        d_query = (query_acc * softmax_scale).astype(jnp.bfloat16)
        return ((key_sum, value_sum), (d_query, attended))

    initial = (
        jnp.zeros((length, head_width), jnp.float32),
        jnp.zeros((length, head_width), jnp.float32),
    )
    sums_final, per_tile = lax.scan(query_tile, initial, jnp.arange(tile_count))
    d_key = (sums_final[0] * softmax_scale).astype(jnp.bfloat16)
    d_value = sums_final[1].astype(jnp.bfloat16)
    d_query = per_tile[0].reshape(length, head_width)
    attended = per_tile[1].reshape(length, head_width)
    return (d_query, d_key, d_value, attended)


def weight_terms(grad_list, source_list, pattern):
    return jnp.stack(
        [
            jnp.einsum(pattern, grad_part, source_part, preferred_element_type=jnp.float32)
            for grad_part, source_part in zip(grad_list, source_list)
        ],
        axis=1,
    )


def local(inputs, d_output, loss_mask, queries, keys, values, out_weight, block_mask):
    layer_in = inputs[0]
    masked = d_output[0] * loss_mask[0][:, None].astype(jnp.bfloat16)
    token_count = layer_in.shape[0]
    local_queries = queries[0]
    local_keys = keys[0]
    local_values = values[0]
    local_blocks = block_mask[0]
    local_heads = local_queries.shape[1]
    d_attn = jnp.dot(
        masked,
        lax.all_gather(out_weight, "dp", axis=0, tiled=True).T,
        preferred_element_type=jnp.float32,
    )
    d_heads = lax.all_to_all(
        d_attn.astype(jnp.bfloat16).reshape(token_count, HW, HD),
        "seq",
        split_axis=1,
        concat_axis=0,
        tiled=True,
    )

    def one_head(head_index):
        return head_backward(
            local_queries[:, head_index],
            local_keys[:, head_index],
            local_values[:, head_index],
            d_heads[:, head_index],
            local_blocks[head_index],
        )

    d_query, d_key, d_value, attended = lax.map(one_head, jnp.arange(local_heads))
    returned = (
        lax.all_to_all(d_query, "seq", split_axis=1, concat_axis=0, tiled=True),
        lax.all_to_all(d_key, "seq", split_axis=1, concat_axis=0, tiled=True),
        lax.all_to_all(d_value, "seq", split_axis=1, concat_axis=0, tiled=True),
        lax.all_to_all(attended, "seq", split_axis=1, concat_axis=0, tiled=True),
    )
    sources = (layer_in, layer_in, layer_in, masked)
    picked = [grad_array for grad_array in returned]
    shared = lax.psum_scatter(
        weight_terms(picked, sources, "htd,tf->dhf"), "dp", scatter_dimension=0, tiled=True
    )
    owned = lax.psum_scatter(shared, "seq", scatter_dimension=2, tiled=True)
    return (owned[:, 0], owned[:, 1], owned[:, 2], owned[:, 3])


def solution(mesh):
    in_specs = (
        P("dp", "seq", None),
        P("dp", "seq", None),
        P("dp", "seq"),
        P("dp", None, "seq", None),
        P("dp", None, "seq", None),
        P("dp", None, "seq", None),
        P("dp", None),
        P("dp", "seq", None, None),
    )
    out_specs = (
        P("dp", "seq", None),
        P("dp", "seq", None),
        P("dp", "seq", None),
        P("dp", "seq", None),
    )
    return jax.shard_map(local, mesh=mesh, in_specs=in_specs, out_specs=out_specs, check_vma=False)
```

profile of v0, /device:TPU:2, one launch (start us, length us, event | category | flops | bytes accessed | tf_op | source)
XLA Modules:
  0.0 1034.3 jit_solution(2678883377690505003)
XLA Ops:
  8.6 68.9 %all-gather.2.cloned.1.call-done = bf16[1024,1024]{1,0:T(8,128)(2,1)} async-done(((bf16[32,1024]{1,0:T(8,128)(2,1)}), bf16[1024,1024]{1,0:T(8,128)(2,1)}) %all-gather.2.cloned.1.call-update) | async-done | bytes 2097168 | tf_op jit(solution)/shard_map/all_gather | solution.py:153
  81.0 7.0 all-to-all-start
  88.3 10.5 %all-to-all-done = bf16[256,8,128]{2,0,1:T(8,128)(2,1)S(1)} async-done(((bf16[256,8,128]{2,0,1:T(8,128)(2,1)}), bf16[256,8,128]{2,0,1:T(8,128)(2,1)S(1)}, u32[]{:S(2)}, u32[]{:S(2)}) %all-to-all-start) | async-done | bytes 524320 | tf_op jit(solution)/shard_map/all_to_all | solution.py:156
  98.8 521.2 %while.76 = (s32[]{:T(128)}, f32[2048,128]{1,0:T(8,128)}, f32[2048,128]{1,0:T(8,128)}, bf16[4,512,128]{2,1,0:T(8,128)(2,1)}, bf16[4,512,128]{2,1,0:T(8,128)(2,1)...) while((s32[]{:T(128)}, f32[2048,128]{1,0:T(8,128)}, ...), condition=%wide.region_17.18_spmd.clone, body=%wide.region_1.17_spmd.clone.sunk | while | flops 410909248 | bytes 63983828 | solution.py:124
  103.8 31.8 %while.77 = (s32[]{:T(128)}, f32[4,512,512]{1,2,0:T(8,128)}, s32[4]{0:T(128)S(1)}, pred[4]{0:T(512)(128)(4,1)S(1)}, s32[4,16]{0,1:T(8,128)S(1)}, /*index=5*/bf16...) while((s32[]{:T(128)}, f32[4,512,512]{1,2,0:T(8,128)}, ...), condition=%wide.region_5.5_spmd, body=%wide.region_2.4_spmd.sunk | while | flops 67633184 | bytes 3933054 | solution.py:58
  130.4 4.1 conditional.6
  147.4 24.7 %while.78 = (s32[]{:T(128)}, f32[512,128]{1,0:T(8,128)S(1)}, s32[4]{0:T(128)S(1)}, pred[4]{0:T(512)(128)(4,1)S(1)}, bf16[4,512,512]{2,1,0:T(8,128)(2,1)S(1)}, /*...) while((s32[]{:T(128)}, f32[512,128]{1,0:T(8,128)S(1)}, s32[4]{0:T(128)S(1)}, ...), condition=%wide.region_11.11_spmd, body=%wide.region_8.10_spmd.sunk | while | flops 67174408 | bytes 1180896 | solution.py:79
  174.1 42.7 %while.79 = (s32[]{:T(128)}, f32[512,128]{1,0:T(8,128)}, f32[4,512,128]{2,1,0:T(8,128)}, f32[4,512,128]{2,1,0:T(8,128)}, s32[4]{0:T(128)}, /*index=5*/pred[4]{0:...) while((s32[]{:T(128)}, f32[512,128]{1,0:T(8,128)}, ...), condition=%wide.region_16.16_spmd, body=%wide.region_13.15_spmd.sunk | while | flops 269287424 | bytes 5902168 | solution.py:112
  178.7 6.9 conditional.8
  191.1 6.9 conditional.8
  209.1 6.9 conditional.8
  226.7 35.7 %while.77 = (s32[]{:T(128)}, f32[4,512,512]{1,2,0:T(8,128)}, s32[4]{0:T(128)S(1)}, pred[4]{0:T(512)(128)(4,1)S(1)}, s32[4,16]{0,1:T(8,128)S(1)}, /*index=5*/bf16...) while((s32[]{:T(128)}, f32[4,512,512]{1,2,0:T(8,128)}, ...), condition=%wide.region_5.5_spmd, body=%wide.region_2.4_spmd.sunk | while | flops 67633184 | bytes 3933054 | solution.py:58
  274.3 27.9 %while.78 = (s32[]{:T(128)}, f32[512,128]{1,0:T(8,128)S(1)}, s32[4]{0:T(128)S(1)}, pred[4]{0:T(512)(128)(4,1)S(1)}, bf16[4,512,512]{2,1,0:T(8,128)(2,1)S(1)}, /*...) while((s32[]{:T(128)}, f32[512,128]{1,0:T(8,128)S(1)}, s32[4]{0:T(128)S(1)}, ...), condition=%wide.region_11.11_spmd, body=%wide.region_8.10_spmd.sunk | while | flops 67174408 | bytes 1180896 | solution.py:79
  304.1 49.5 %while.79 = (s32[]{:T(128)}, f32[512,128]{1,0:T(8,128)}, f32[4,512,128]{2,1,0:T(8,128)}, f32[4,512,128]{2,1,0:T(8,128)}, s32[4]{0:T(128)}, /*index=5*/pred[4]{0:...) while((s32[]{:T(128)}, f32[512,128]{1,0:T(8,128)}, ...), condition=%wide.region_16.16_spmd, body=%wide.region_13.15_spmd.sunk | while | flops 269287424 | bytes 5902168 | solution.py:112
  308.7 6.9 conditional.8
  321.1 6.9 conditional.8
  333.5 6.9 conditional.8
  345.9 6.9 conditional.8
  364.1 31.8 %while.77 = (s32[]{:T(128)}, f32[4,512,512]{1,2,0:T(8,128)}, s32[4]{0:T(128)S(1)}, pred[4]{0:T(512)(128)(4,1)S(1)}, s32[4,16]{0,1:T(8,128)S(1)}, /*index=5*/bf16...) while((s32[]{:T(128)}, f32[4,512,512]{1,2,0:T(8,128)}, ...), condition=%wide.region_5.5_spmd, body=%wide.region_2.4_spmd.sunk | while | flops 67633184 | bytes 3933054 | solution.py:58
  390.7 4.1 conditional.6
  407.8 24.7 %while.78 = (s32[]{:T(128)}, f32[512,128]{1,0:T(8,128)S(1)}, s32[4]{0:T(128)S(1)}, pred[4]{0:T(512)(128)(4,1)S(1)}, bf16[4,512,512]{2,1,0:T(8,128)(2,1)S(1)}, /*...) while((s32[]{:T(128)}, f32[512,128]{1,0:T(8,128)S(1)}, s32[4]{0:T(128)S(1)}, ...), condition=%wide.region_11.11_spmd, body=%wide.region_8.10_spmd.sunk | while | flops 67174408 | bytes 1180896 | solution.py:79
  434.4 42.7 %while.79 = (s32[]{:T(128)}, f32[512,128]{1,0:T(8,128)}, f32[4,512,128]{2,1,0:T(8,128)}, f32[4,512,128]{2,1,0:T(8,128)}, s32[4]{0:T(128)}, /*index=5*/pred[4]{0:...) while((s32[]{:T(128)}, f32[512,128]{1,0:T(8,128)}, ...), condition=%wide.region_16.16_spmd, body=%wide.region_13.15_spmd.sunk | while | flops 269287424 | bytes 5902168 | solution.py:112
  444.6 6.9 conditional.8
  457.0 6.9 conditional.8
  469.4 6.9 conditional.8
  487.6 35.7 %while.77 = (s32[]{:T(128)}, f32[4,512,512]{1,2,0:T(8,128)}, s32[4]{0:T(128)S(1)}, pred[4]{0:T(512)(128)(4,1)S(1)}, s32[4,16]{0,1:T(8,128)S(1)}, /*index=5*/bf16...) while((s32[]{:T(128)}, f32[4,512,512]{1,2,0:T(8,128)}, ...), condition=%wide.region_5.5_spmd, body=%wide.region_2.4_spmd.sunk | while | flops 67633184 | bytes 3933054 | solution.py:58
  500.3 4.1 conditional.6
  535.2 27.9 %while.78 = (s32[]{:T(128)}, f32[512,128]{1,0:T(8,128)S(1)}, s32[4]{0:T(128)S(1)}, pred[4]{0:T(512)(128)(4,1)S(1)}, bf16[4,512,512]{2,1,0:T(8,128)(2,1)S(1)}, /*...) while((s32[]{:T(128)}, f32[512,128]{1,0:T(8,128)S(1)}, s32[4]{0:T(128)S(1)}, ...), condition=%wide.region_11.11_spmd, body=%wide.region_8.10_spmd.sunk | while | flops 67174408 | bytes 1180896 | solution.py:79
  565.0 49.5 %while.79 = (s32[]{:T(128)}, f32[512,128]{1,0:T(8,128)}, f32[4,512,128]{2,1,0:T(8,128)}, f32[4,512,128]{2,1,0:T(8,128)}, s32[4]{0:T(128)}, /*index=5*/pred[4]{0:...) while((s32[]{:T(128)}, f32[512,128]{1,0:T(8,128)}, ...), condition=%wide.region_16.16_spmd, body=%wide.region_13.15_spmd.sunk | while | flops 269287424 | bytes 5902168 | solution.py:112
  569.7 6.9 conditional.8
  582.1 6.9 conditional.8
  594.5 6.9 conditional.8
  606.8 6.9 conditional.8
  621.8 8.1 copy.87
  630.4 11.8 %reduce.3 = bf16[2048,128]{1,0:T(8,128)(2,1)S(1)} reduce(bf16[2048,1,128]{2,1,0:T(2,128)(2,1)S(1)} %bitcast.192, bf16[]{:T(256)} %broadcast.81), dimensions={1}, to_apply=%bitcast.160.reduce_sub_computation | reduce | bytes 1048578
  643.1 32.4 %all-to-all-start.3 = ((bf16[8,2,16384]{2,1,0:T(2,128)(2,1)}), bf16[8,2,16384]{2,1,0:T(2,128)(2,1)S(1)}, u32[]{:S(2)}, u32[]{:S(2)}) async-start(bf16[8,2,16384]{2,1,0:T(2,128)(2,1)} %reshape.86), calls=%async_computation.3 | async-start | bytes 1048576 | tf_op jit(solution)/shard_map/all_to_all | solution.py:177
  675.5 8.1 copy.88
  683.6 11.5 %reduce.4 = bf16[2048,128]{1,0:T(8,128)(2,1)S(1)} reduce(bf16[2048,1,128]{2,1,0:T(2,128)(2,1)S(1)} %bitcast.194, bf16[]{:T(256)} %broadcast.81), dimensions={1}, to_apply=%bitcast.161.reduce_sub_computation | reduce | bytes 1048578
  696.1 7.5 all-to-all-start.2
  703.6 8.1 copy.86
  711.7 11.5 %reduce.2 = bf16[2048,128]{1,0:T(8,128)(2,1)S(1)} reduce(bf16[2048,1,128]{2,1,0:T(2,128)(2,1)S(1)} %bitcast.195, bf16[]{:T(256)} %broadcast.81), dimensions={1}, to_apply=%bitcast.159.reduce_sub_computation | reduce | bytes 1048578
  724.2 7.6 all-to-all-start.4
  733.6 12.3 %reduce.5 = bf16[2048,128]{1,0:T(8,128)(2,1)} reduce(bf16[2048,1,128]{2,1,0:T(2,128)(2,1)S(1)} %bitcast.193, bf16[]{:T(256)} %broadcast.81), dimensions={1}, to_apply=%bitcast.162.reduce_sub_computation | reduce | bytes 1048578
  748.6 7.2 all-to-all-start.1
  769.9 4.8 pad_maximum_fusion
  774.7 19.5 %copy.59 = f32[128,4,8,1024]{3,2,1,0:T(8,128)} copy(f32[128,4,8,1024]{3,0,2,1:T(8,128)S(1)} %pad_maximum_fusion) | data formatting | bytes 33554432 | tf_op jit(solution)/shard_map/stack | solution.py:133
  794.2 144.0 %reduce-scatter.3.cloned.1.call-done = f32[4,4,8,1024]{3,2,1,0:T(8,128)} async-done(((f32[128,4,8,1024]{3,2,1,0:T(8,128)}), f32[4,4,8,1024]{3,2,1,0:T(8,128)}) %reduce-scatter.3.cloned.1.call-update) | async-done | bytes 524304 | tf_op jit(solution)/shard_map/reduce_scatter | solution.py:182
  941.0 82.6 %all-reduce.3.cloned.1.call-done = f32[4,4,8,1024]{3,0,2,1:T(4,128)} async-done(((f32[4,4,8,1024]{3,0,2,1:T(4,128)}), f32[4,4,8,1024]{3,0,2,1:T(4,128)}) %all-reduce.3.cloned.1.call-update) | async-done | bytes 524304
  (485 shorter events, 426.2 us)
Async XLA Ops:
  7.2 748.7 %copy-start = (bf16[1,256,1024]{2,1,0:T(8,128)(2,1)S(1)}, bf16[1,256,1024]{2,1,0:T(8,128)(2,1)}, u32[]{:S(2)}) copy-start(bf16[1,256,1024]{2,1,0:T(8,128)(2,1)} %param.22) | copy-start | bytes 1572868
  7.2 80.8 %copy-start.8 = (s32[1,1,16,16]{3,2,1,0:T(8,128)S(1)}, s32[1,1,16,16]{3,2,1,0:T(8,128)}, u32[]{:S(2)}) copy-start(s32[1,1,16,16]{3,2,1,0:T(8,128)} %param.29) | copy-start | bytes 3076
  7.2 70.4 %all-gather.2.cloned.1.call-start = ((), (), s32[]{:S(2)}) async-start(), calls=%async_computation.6 | async-start | bytes 2162688 | tf_op jit(solution)/shard_map/all_gather | solution.py:153
  81.0 17.8 %all-to-all-start = ((bf16[256,8,128]{2,0,1:T(8,128)(2,1)}), bf16[256,8,128]{2,0,1:T(8,128)(2,1)S(1)}, u32[]{:S(2)}, u32[]{:S(2)}) async-start(bf16[256,8,128]{2,0,1:T(8,128)(2,1)} %bitcast.158), calls=%async_computation | async-start | bytes 1048576 | tf_op jit(solution)/shard_map/all_to_all | solution.py:156
  98.8 5.0 copy-start.9
  98.8 5.0 copy-start.12
  98.8 73.9 %copy-start.4 = (bf16[2048,128]{1,0:T(8,128)(2,1)}, bf16[2048,128]{1,0:T(8,128)(2,1)S(1)}, u32[]{:S(2)}) copy-start(bf16[2048,128]{1,0:T(8,128)(2,1)S(1)} %get-tuple-element.992) | copy-start | bytes 1572868 | tf_op jit(solution)/shard_map/while/body/eval_jaxpr/while
  135.5 5.5 copy-start.2
  138.1 3.4 copy-start.1
  172.2 0.5 copy-start.14
  216.8 4.8 copy-start.5
  216.8 4.9 copy-start.10
  216.8 4.9 copy-start.13
  221.7 5.0 copy-start.9
  221.7 5.0 copy-start.12
  221.7 81.0 %copy-start.4 = (bf16[2048,128]{1,0:T(8,128)(2,1)}, bf16[2048,128]{1,0:T(8,128)(2,1)S(1)}, u32[]{:S(2)}) copy-start(bf16[2048,128]{1,0:T(8,128)(2,1)S(1)} %get-tuple-element.992) | copy-start | bytes 1572868 | tf_op jit(solution)/shard_map/while/body/eval_jaxpr/while
  262.4 5.5 copy-start.2
  265.0 3.4 copy-start.1
  302.2 0.5 copy-start.14
  353.6 5.4 copy-start.5
  353.6 5.4 copy-start.10
  353.6 5.4 copy-start.13
  359.1 5.0 copy-start.9
  359.1 5.0 copy-start.12
  359.1 73.9 %copy-start.4 = (bf16[2048,128]{1,0:T(8,128)(2,1)}, bf16[2048,128]{1,0:T(8,128)(2,1)S(1)}, u32[]{:S(2)}) copy-start(bf16[2048,128]{1,0:T(8,128)(2,1)S(1)} %get-tuple-element.992) | copy-start | bytes 1572868 | tf_op jit(solution)/shard_map/while/body/eval_jaxpr/while
  395.9 5.5 copy-start.2
  398.4 3.4 copy-start.1
  477.1 5.5 copy-start.5
  477.1 5.5 copy-start.10
  477.1 5.5 copy-start.13
  482.6 5.0 copy-start.9
  482.6 5.0 copy-start.12
  482.6 81.0 %copy-start.4 = (bf16[2048,128]{1,0:T(8,128)(2,1)}, bf16[2048,128]{1,0:T(8,128)(2,1)S(1)}, u32[]{:S(2)}) copy-start(bf16[2048,128]{1,0:T(8,128)(2,1)S(1)} %get-tuple-element.992) | copy-start | bytes 1572868 | tf_op jit(solution)/shard_map/while/body/eval_jaxpr/while
  523.3 5.5 copy-start.2
  525.9 3.4 copy-start.1
  614.6 5.5 copy-start.5
  614.6 5.5 copy-start.10
  614.6 5.5 copy-start.13
  630.4 73.2 %copy-start.7 = (bf16[4,512,128]{2,1,0:T(8,128)(2,1)S(1)}, bf16[4,512,128]{2,1,0:T(8,128)(2,1)}, u32[]{:S(2)}) copy-start(bf16[4,512,128]{2,1,0:T(8,128)(2,1)} %get-tuple-element.348) | copy-start | bytes 1572868
  643.1 53.0 %all-to-all-start.3 = ((bf16[8,2,16384]{2,1,0:T(2,128)(2,1)}), bf16[8,2,16384]{2,1,0:T(2,128)(2,1)S(1)}, u32[]{:S(2)}, u32[]{:S(2)}) async-start(bf16[8,2,16384]{2,1,0:T(2,128)(2,1)} %reshape.86), calls=%async_computation.3 | async-start | bytes 1048576 | tf_op jit(solution)/shard_map/all_to_all | solution.py:177
  696.1 28.1 %all-to-all-start.2 = ((bf16[8,2,16384]{2,1,0:T(2,128)(2,1)}), bf16[8,2,16384]{2,1,0:T(2,128)(2,1)S(1)}, u32[]{:S(2)}, u32[]{:S(2)}) async-start(bf16[8,2,16384]{2,1,0:T(2,128)(2,1)} %reshape.88), calls=%async_computation.2 | async-start | bytes 1048576 | tf_op jit(solution)/shard_map/all_to_all | solution.py:176
  724.2 24.4 %all-to-all-start.4 = ((bf16[8,2,16384]{2,1,0:T(2,128)(2,1)}), bf16[8,2,16384]{2,1,0:T(2,128)(2,1)S(1)}, u32[]{:S(2)}, u32[]{:S(2)}) async-start(bf16[8,2,16384]{2,1,0:T(2,128)(2,1)} %reshape.84), calls=%async_computation.4 | async-start | bytes 1048576 | tf_op jit(solution)/shard_map/all_to_all | solution.py:178
  748.6 16.9 %all-to-all-start.1 = ((bf16[8,2,16384]{2,1,0:T(2,128)(2,1)}), bf16[8,2,16384]{2,1,0:T(2,128)(2,1)}, u32[]{:S(2)}, u32[]{:S(2)}) async-start(bf16[8,2,16384]{2,1,0:T(2,128)(2,1)} %reshape.90), calls=%async_computation.1 | async-start | bytes 1048576 | tf_op jit(solution)/shard_map/all_to_all | solution.py:175
  755.8 182.4 %reduce-scatter.3.cloned.1.call-start = ((), (), s32[]{:S(2)}) async-start(), calls=%async_computation.7 | async-start | bytes 17301504 | tf_op jit(solution)/shard_map/reduce_scatter | solution.py:182
  759.3 3.4 copy-start.6
  767.7 2.2 copy-start.3
  794.2 146.3 %copy-start.11 = (u32[256]{0:T(256)S(1)}, u32[256]{0:T(256)}, u32[]{:S(2)}) copy-start(u32[256]{0:T(256)} %constant.130) | copy-start | bytes 3076
  794.2 229.5 %all-reduce.3.cloned.1.call-start = ((), (), s32[]{:S(2)}) async-start(), calls=%async_computation.8 | async-start | bytes 1048576
  (2 other events, 1.0 us)
Sparse Core Ops, SparseCore 0:
  9.9 67.6 all-gather.1
  794.3 143.8 reduce-scatter.2
  940.9 82.7 all-reduce.2
where the time goes:
time: 1050 us; the launch traced here: 1030 us
  waiting for transfers between devices  307 us (29%)
  loops' own time  220 us (21%)
  local copies, waits for them, and re-layouts  204 us (19%)
  matrix products  119 us (11%)
  other arithmetic  109 us (10%)
  starting transfers between devices  61.8 us (6%)
  between operations  14.2 us (1%)
    reduce_scatter x1, waiting for transfers between devices, local(): lax.psum_scatter(weight_terms(picked, sources, 'htd,tf->dhf'), 'dp', scat...  144 us
    unnamed x4, waiting for transfers between devices  83.3 us
    all_gather x1, waiting for transfers between devices, local(): lax.all_gather(out_weight, 'dp', axis=0, tiled=True)  68.9 us
    unnamed x6, other arithmetic  47.2 us
    another operation x4, loops' own time, query_tile(): lax.scan(attend_tile, jnp.zeros((tile_rows, head_width), jnp.float32), jn...  41.9 us
    another operation x4, loops' own time, query_tile(): scores = lax.map(score_tile, jnp.arange(tile_count))  41.7 us
    dynamic_slice x52, local copies, waits for them, and re-layouts, head_backward(): sums_final, per_tile = lax.scan(query_tile, initial, jnp.arange(tile_count))  40.7 us
    another operation x16, loops' own time, score_tile(): lax.cond(live_flags[inner_index], compute_scores, empty_scores, inner_index)  36.8 us
  transfers between devices with their start and end apart: 8, of which 4 were waited for; matrix products, arithmetic and copies ran while one was open for 7% of the time, Pallas kernels for 0%

commit v1 on v0

v1 whole, which is shorter than its diff:
```python
import functools

import jax
import jax.numpy as jnp
from jax import lax
from jax.experimental import pallas as pl
from jax.experimental.pallas import tpu as pltpu
from jax.sharding import PartitionSpec as P

HD = 128
BLOCK = 128
ROWS = 256

masked_score = -1e30


def attention_kernel(q_ref, k_ref, v_ref, g_ref, m_ref, dq_ref, att_ref, dk_ref, dv_ref, dk_acc, dv_acc):
    step = pl.program_id(0)
    steps = pl.num_programs(0)
    scale = HD ** (-0.5)
    groups = ROWS // BLOCK

    @pl.when(step == 0)
    def _():
        dk_acc[...] = jnp.zeros_like(dk_acc)
        dv_acc[...] = jnp.zeros_like(dv_acc)

    q = q_ref[...]
    k = k_ref[...]
    v = v_ref[...]
    g = g_ref[...]
    length = k.shape[0]
    nt = (((1,), (1,)), ((), ()))
    tn = (((0,), (0,)), ((), ()))
    scores = lax.dot_general(q, k, nt, preferred_element_type=jnp.float32) * scale
    live = m_ref[...]
    scores = scores.reshape(groups, BLOCK, length)
    scores = jnp.where(live > 0, scores, masked_score).reshape(ROWS, length)
    row_max = jnp.max(scores, axis=1, keepdims=True)
    weights = jnp.exp(scores - row_max)
    row_total = jnp.sum(weights, axis=1, keepdims=True)
    prob = weights / row_total
    prob_low = prob.astype(jnp.bfloat16)
    attended = jnp.dot(prob_low, v, preferred_element_type=jnp.float32).astype(jnp.bfloat16)
    row_delta = jnp.sum(g.astype(jnp.float32) * attended.astype(jnp.float32), axis=1, keepdims=True)
    d_prob = lax.dot_general(g, v, nt, preferred_element_type=jnp.float32)
    d_score = (prob * (d_prob - row_delta)).astype(jnp.bfloat16)
    dq_ref[...] = (jnp.dot(d_score, k, preferred_element_type=jnp.float32) * scale).astype(jnp.bfloat16)
    att_ref[...] = attended
    dk_acc[...] += lax.dot_general(d_score, q, tn, preferred_element_type=jnp.float32)
    dv_acc[...] += lax.dot_general(prob_low, g, tn, preferred_element_type=jnp.float32)

    @pl.when(step == steps - 1)
    def _():
        dk_ref[...] = (dk_acc[...] * scale).astype(jnp.bfloat16)
        dv_ref[...] = dv_acc[...].astype(jnp.bfloat16)


def attention_backward(q, k, v, g, live_cols):
    length = q.shape[0]
    row_spec = pl.BlockSpec((ROWS, HD), lambda i: (i, 0))
    full_spec = pl.BlockSpec((length, HD), lambda i: (0, 0))
    mask_spec = pl.BlockSpec((ROWS // BLOCK, 1, length), lambda i: (i, 0, 0))
    out = jax.ShapeDtypeStruct((length, HD), jnp.bfloat16)
    flops = 12 * length * length * HD
    return pl.pallas_call(
        attention_kernel,
        grid=(length // ROWS,),
        in_specs=[row_spec, full_spec, full_spec, row_spec, mask_spec],
        out_specs=[row_spec, row_spec, full_spec, full_spec],
        out_shape=[out, out, out, out],
        scratch_shapes=[pltpu.VMEM((length, HD), jnp.float32), pltpu.VMEM((length, HD), jnp.float32)],
        compiler_params=pltpu.CompilerParams(vmem_limit_bytes=48 * 1024 * 1024),
        cost_estimate=pl.CostEstimate(
            flops=flops, transcendentals=length * length, bytes_accessed=8 * length * HD * 2
        ),
    )(q, k, v, g, live_cols)


def local(inputs, d_output, loss_mask, queries, keys, values, out_weight, block_mask):
    head = lax.axis_index("seq")
    row_owner = lax.axis_index("dp")
    masked = d_output[0] * loss_mask[0][:, None].astype(jnp.bfloat16)
    own_rows = out_weight.shape[0]
    per_head = HD // own_rows
    placed = jnp.zeros((per_head, own_rows, out_weight.shape[1]), out_weight.dtype)
    placed = lax.dynamic_update_index_in_dim(placed, out_weight, row_owner % per_head, 0)
    placed = jnp.where(row_owner // per_head == head, placed, jnp.zeros_like(placed))
    head_weight = lax.psum(placed.reshape(HD, out_weight.shape[1]), "dp")
    masked_all = lax.all_gather(masked, "seq", axis=0, tiled=True)
    inputs_all = lax.all_gather(inputs[0], "seq", axis=0, tiled=True)
    d_attn = lax.dot_general(
        masked_all, head_weight, (((1,), (1,)), ((), ())), preferred_element_type=jnp.float32
    ).astype(jnp.bfloat16)
    blocks = block_mask[0, 0]
    live_cols = jnp.repeat(blocks, BLOCK, axis=1)[:, None, :]
    d_query, attended, d_key, d_value = attention_backward(
        queries[0, :, 0], keys[0, :, 0], values[0, :, 0], d_attn, live_cols
    )
    tn = (((0,), (0,)), ((), ()))
    terms = jnp.stack(
        [
            lax.dot_general(d_query, inputs_all, tn, preferred_element_type=jnp.float32),
            lax.dot_general(d_key, inputs_all, tn, preferred_element_type=jnp.float32),
            lax.dot_general(d_value, inputs_all, tn, preferred_element_type=jnp.float32),
            lax.dot_general(attended, masked_all, tn, preferred_element_type=jnp.float32),
        ],
        axis=1,
    )
    owned = lax.psum_scatter(terms, "dp", scatter_dimension=0, tiled=True)
    return tuple(owned[:, part][:, None, :] for part in range(4))


def solution(mesh):
    in_specs = (
        P("dp", "seq", None),
        P("dp", "seq", None),
        P("dp", "seq"),
        P("dp", None, "seq", None),
        P("dp", None, "seq", None),
        P("dp", None, "seq", None),
        P("dp", None),
        P("dp", "seq", None, None),
    )
    out_specs = (
        P("dp", "seq", None),
        P("dp", "seq", None),
        P("dp", "seq", None),
        P("dp", "seq", None),
    )
    return jax.shard_map(local, mesh=mesh, in_specs=in_specs, out_specs=out_specs, check_vma=False)
```

time: 1050 us -> 505 us (0.48); the launches traced: 1030 us -> 504 us
  loops' own time: 220 us -> 0 us
  local copies, waits for them, and re-layouts: 204 us -> 5.11 us
  waiting for transfers between devices: 307 us -> 450 us
  matrix products: 119 us -> 8.77 us
  other arithmetic: 109 us -> 4.3 us
  starting transfers between devices: 61.8 us -> 0.17 us
  Pallas kernels: 0 us -> 19.4 us
    psum x0 -> x1, waiting for transfers between devices: none -> 224 us  [local(): head_weight = lax.psum(placed.reshape(HD, out_weight.shape[1]), 'dp')]
    another operation x61 -> x0, loops' own time: 220 us -> none  [the longest x4 41.9 us: query_tile(): lax.scan(attend_tile, jnp.zeros((tile_rows, head_width), jnp.float32), jn...]
    reduce_scatter x1 -> x0, waiting for transfers between devices: 144 us -> none  [local(): lax.psum_scatter(weight_terms(picked, sources, 'htd,tf->dhf'), 'dp', scat...]
    unnamed x4 -> x5, waiting for transfers between devices: 83.3 us -> 226 us
    dot_general x89 -> x5, matrix products: 119 us -> 8.77 us  [the longest x1 3.47 us: local(): lax.dot_general(masked_all, head_weight, (((1,), (1,)), ((), ())), prefer...]
    dynamic_slice x108 -> x0, local copies, waits for them, and re-layouts: 83.3 us -> none  [the longest x52 40.7 us: head_backward(): sums_final, per_tile = lax.scan(query_tile, initial, jnp.arange(tile_count))]
    all_gather x1 -> x2, waiting for transfers between devices: 68.9 us -> 0.03 us  [the longest x1 0.03 us: local(): inputs_all = lax.all_gather(inputs[0], 'seq', axis=0, tiled=True)]
    all_to_all x5 -> x0, starting transfers between devices: 61.7 us -> none  [the longest x1 32.4 us: local(): lax.all_to_all(d_value, 'seq', split_axis=1, concat_axis=0, tiled=True)]
  transfers between devices with their start and end apart: 8 -> 4, of which waited for: 4 -> 2; matrix products, arithmetic and copies ran while one was open for 7% -> 2% of each run, Pallas kernels for 0% -> 4%
where the time goes in v1:
time: 505 us; the launch traced here: 504 us
  waiting for transfers between devices  450 us (89%)
  Pallas kernels  19.4 us (4%)
  between operations  16.4 us (3%)
  matrix products  8.77 us (2%)
  local copies, waits for them, and re-layouts  5.11 us (1%)
    unnamed x5, waiting for transfers between devices  226 us
    psum x1, waiting for transfers between devices, local(): head_weight = lax.psum(placed.reshape(HD, out_weight.shape[1]), 'dp')  224 us
    pallas_call x1, Pallas kernels, attention_backward(): pl.pallas_call(attention_kernel, grid=(length // ROWS,), in_specs=[row_sp...  19.4 us
  transfers between devices with their start and end apart: 4, of which 2 were waited for; matrix products, arithmetic and copies ran while one was open for 2% of the time, Pallas kernels for 4%

profile of v1, /device:TPU:2, one launch (start us, length us, event | category | flops | bytes accessed | tf_op | source)
XLA Modules:
  0.0 503.6 jit_solution(4639977884861109158)
XLA Ops:
  8.0 0.0 all-reduce.4.cloned.1.call-start
  8.1 0.0 copy-start.5
  8.1 0.7 copy-done.5
  8.9 0.0 all-reduce.4.cloned.1.call-update
  8.9 0.0 copy-start.6
  8.9 0.0 all-gather.4.cloned.1.call-start
  8.9 0.7 convert_reduce_fusion
  9.6 0.0 copy-start
  9.6 0.0 copy-start.1
  9.7 0.0 copy-start.2
  9.7 2.1 bitcast_multiply_fusion
  11.8 0.0 all-gather.4.cloned.1.call-update
  11.8 0.0 all-gather.6.cloned.1.call-start
  11.8 0.5 all-gather.6.cloned.1.call-update
  12.4 0.0 all-reduce.6.cloned.1.call-start
  12.4 223.8 %all-reduce.4.cloned.1.call-done = bf16[128,1024]{1,0:T(8,128)(2,1)} async-done(((bf16[128,1024]{1,0:T(8,128)(2,1)}), bf16[128,1024]{1,0:T(8,128)(2,1)}) %all-reduce.4.cloned.1.call-update) | async-done | bytes 262160 | tf_op jit(solution)/shard_map/psum | solution.py:89
  236.2 0.0 all-gather.4.cloned.1.call-done
  236.2 3.5 convolution_convert_fusion.g_ref
  239.7 0.0 copy-done.6
  239.7 0.1 broadcast_in_dim.5
  239.8 0.0 copy-done
  239.8 0.0 copy-done.1
  239.8 0.0 copy-done.2
  239.8 0.0 copy-start.4
  239.8 19.4 %shard_map.111 = (bf16[2048,128]{1,0:T(8,128)(2,1)S(1)}, bf16[2048,128]{1,0:T(8,128)(2,1)S(1)}, bf16[2048,128]{1,0:T(8,128)(2,1)S(1)}, bf16[2048,128]{1,0:T(8,128)(2,1)S(1)}) custom-call(bf16[2048,128]{1,0:T(8,128)(2,1)S(1)} %bitcast.40, bf16[2048,128]{1,0:T(8,128)(2,1)S(1)} %bitcast.41, bf16[2048,128]{1,0:T(8,128)(2,1)S(1)} %bitcast.42, ...), custom_call_target="tpu_custom_call" | custom-call | flops 6442450944 | bytes 4194304 | tf_op jit(solution)/shard_map/pallas_call | solution.py:66
  259.3 0.0 copy-done.4
  259.3 0.7 convolution_bitcast_fusion
  260.0 0.0 all-gather.6.cloned.1.call-done
  260.1 0.0 copy-start.3
  260.1 3.1 fusion.12
  263.1 0.4 copy-done.3
  263.5 0.7 fusion.9
  264.3 0.8 fusion.6
  265.0 0.0 copy-start.7
  265.0 1.5 pad_maximum_fusion
  266.5 0.0 all-reduce.6.cloned.1.call-update
  266.5 0.0 copy-done.7
  266.6 0.6 dynamic-slice.2
  267.8 225.1 %all-reduce.6.cloned.1.call-done = f32[128,4,1024]{2,0,1:T(8,128)} async-done(((f32[128,4,1024]{2,0,1:T(8,128)}), f32[128,4,1024]{2,0,1:T(8,128)}) %all-reduce.6.cloned.1.call-update) | async-done | bytes 2097168
  492.9 0.8 constant_dynamic-slice_fusion.3
  493.7 0.6 copy.16
  494.4 0.6 copy.17
  495.0 0.6 copy.18
  495.6 0.6 copy.19
  (2 shorter events, 0.0 us)
Async XLA Ops:
  8.0 228.2 %all-reduce.4.cloned.1.call-start = ((), (), s32[]{:S(2)}) async-start(), calls=%async_computation.1 | async-start | bytes 524288 | tf_op jit(solution)/shard_map/psum | solution.py:89
  8.1 0.7 copy-start.5
  8.9 230.8 %copy-start.6 = (s32[1,1,16,16]{3,2,1,0:T(8,128)S(1)}, s32[1,1,16,16]{3,2,1,0:T(8,128)}, u32[]{:S(2)}) copy-start(s32[1,1,16,16]{3,2,1,0:T(8,128)} %param.15) | copy-start | bytes 3076
  8.9 227.3 %all-gather.4.cloned.1.call-start = ((), (), s32[]{:S(2)}) async-start(), calls=%async_computation | async-start | bytes 4718592 | tf_op jit(solution)/shard_map/all_gather | solution.py:90
  9.6 230.2 %copy-start = (bf16[1,2048,1,128]{3,1,2,0:T(8,128)(2,1)S(1)}, bf16[1,2048,1,128]{3,1,2,0:T(8,128)(2,1)}, u32[]{:S(2)}) copy-start(bf16[1,2048,1,128]{3,1,2,0:T(8,128)(2,1)} %param.11) | copy-start | bytes 1572868
  9.6 230.2 %copy-start.1 = (bf16[1,2048,1,128]{3,1,2,0:T(8,128)(2,1)S(1)}, bf16[1,2048,1,128]{3,1,2,0:T(8,128)(2,1)}, u32[]{:S(2)}) copy-start(bf16[1,2048,1,128]{3,1,2,0:T(8,128)(2,1)} %param.12) | copy-start | bytes 1572868
  9.7 230.2 %copy-start.2 = (bf16[1,2048,1,128]{3,1,2,0:T(8,128)(2,1)S(1)}, bf16[1,2048,1,128]{3,1,2,0:T(8,128)(2,1)}, u32[]{:S(2)}) copy-start(bf16[1,2048,1,128]{3,1,2,0:T(8,128)(2,1)} %param.13) | copy-start | bytes 1572868
  11.8 248.3 %all-gather.6.cloned.1.call-start = ((), (), s32[]{:S(2)}) async-start(), calls=%async_computation.2 | async-start | bytes 4718592 | tf_op jit(solution)/shard_map/all_gather | solution.py:91
  12.4 480.5 %all-reduce.6.cloned.1.call-start = ((), (), s32[]{:S(2)}) async-start(), calls=%async_computation.3 | async-start | bytes 4194304
  239.8 19.4 %copy-start.4 = (bf16[2048,1024]{1,0:T(8,128)(2,1)S(1)}, bf16[2048,1024]{1,0:T(8,128)(2,1)}, u32[]{:S(2)}) copy-start(bf16[2048,1024]{1,0:T(8,128)(2,1)} %all-gather.4.cloned.1.call-done) | copy-start | bytes 12582916
  260.1 3.5 copy-start.3
  265.0 1.5 copy-start.7
Sparse Core Ops, SparseCore 0:
  11.4 224.7 all-reduce.3
  266.7 226.2 all-reduce.5
Sparse Core Ops, SparseCore 1:
  12.3 79.5 all-gather.3
  94.8 74.6 all-gather.5

commit v2 on v1

--- a/solution.py
+++ b/solution.py
@@ -77,18 +77,24 @@
     )(q, k, v, g, live_cols)
 
 
+DP = ("dpy", "dpz", "dpc")
+SQ = ("sqy", "sqx")
+
+
 def local(inputs, d_output, loss_mask, queries, keys, values, out_weight, block_mask):
-    head = lax.axis_index("seq")
-    row_owner = lax.axis_index("dp")
+    sizes = {name: lax.axis_size(name) for name in DP + SQ}
+    head = lax.axis_index("sqy") * sizes["sqx"] + lax.axis_index("sqx")
     masked = d_output[0] * loss_mask[0][:, None].astype(jnp.bfloat16)
-    own_rows = out_weight.shape[0]
-    per_head = HD // own_rows
-    placed = jnp.zeros((per_head, own_rows, out_weight.shape[1]), out_weight.dtype)
-    placed = lax.dynamic_update_index_in_dim(placed, out_weight, row_owner % per_head, 0)
-    placed = jnp.where(row_owner // per_head == head, placed, jnp.zeros_like(placed))
-    head_weight = lax.psum(placed.reshape(HD, out_weight.shape[1]), "dp")
-    masked_all = lax.all_gather(masked, "seq", axis=0, tiled=True)
-    inputs_all = lax.all_gather(inputs[0], "seq", axis=0, tiled=True)
+    own_rows, width = out_weight.shape
+    gathered = lax.all_gather(out_weight, "dpc", axis=0)
+    gathered = lax.all_gather(gathered, "dpy", axis=0)
+    gathered = lax.all_gather(gathered, "dpz", axis=0)
+    gathered = jnp.transpose(gathered, (1, 0, 2, 3, 4)).reshape(-1, width)
+    head_weight = lax.dynamic_slice_in_dim(gathered, head * HD, HD, 0)
+    masked_all = lax.all_gather(lax.all_gather(masked, "sqy", axis=0), "sqx", axis=0)
+    inputs_all = lax.all_gather(lax.all_gather(inputs[0], "sqy", axis=0), "sqx", axis=0)
+    masked_all = jnp.transpose(masked_all, (1, 0, 2, 3)).reshape(-1, width)
+    inputs_all = jnp.transpose(inputs_all, (1, 0, 2, 3)).reshape(-1, width)
     d_attn = lax.dot_general(
         masked_all, head_weight, (((1,), (1,)), ((), ())), preferred_element_type=jnp.float32
     ).astype(jnp.bfloat16)
@@ -107,25 +113,34 @@
         ],
         axis=1,
     )
-    owned = lax.psum_scatter(terms, "dp", scatter_dimension=0, tiled=True)
+    chunk = terms.shape[0] // (sizes["dpy"] * sizes["dpz"] * sizes["dpc"])
+    terms = terms.reshape(sizes["dpy"], sizes["dpz"], sizes["dpc"], chunk, 4, width)
+    terms = jnp.transpose(terms, (2, 0, 1, 3, 4, 5)).reshape(-1, 4 * width // 128, 128)
+    owned = lax.psum_scatter(terms, "dpc", scatter_dimension=0, tiled=True)
+    owned = lax.psum_scatter(owned, "dpy", scatter_dimension=0, tiled=True)
+    owned = lax.psum_scatter(owned, "dpz", scatter_dimension=0, tiled=True)
+    owned = owned.reshape(chunk, 4, width)
     return tuple(owned[:, part][:, None, :] for part in range(4))
 
 
 def solution(mesh):
+    dp, seq = mesh.devices.shape
+    devices = mesh.devices.reshape(2, dp // 4, 2, 2, seq // 2)
+    fine = jax.sharding.Mesh(devices, DP + SQ)
     in_specs = (
-        P("dp", "seq", None),
-        P("dp", "seq", None),
-        P("dp", "seq"),
-        P("dp", None, "seq", None),
-        P("dp", None, "seq", None),
-        P("dp", None, "seq", None),
-        P("dp", None),
-        P("dp", "seq", None, None),
+        P(DP, SQ, None),
+        P(DP, SQ, None),
+        P(DP, SQ),
+        P(DP, None, SQ, None),
+        P(DP, None, SQ, None),
+        P(DP, None, SQ, None),
+        P(DP, None),
+        P(DP, SQ, None, None),
     )
     out_specs = (
-        P("dp", "seq", None),
-        P("dp", "seq", None),
-        P("dp", "seq", None),
-        P("dp", "seq", None),
+        P(DP, SQ, None),
+        P(DP, SQ, None),
+        P(DP, SQ, None),
+        P(DP, SQ, None),
     )
-    return jax.shard_map(local, mesh=mesh, in_specs=in_specs, out_specs=out_specs, check_vma=False)
+    return jax.shard_map(local, mesh=fine, in_specs=in_specs, out_specs=out_specs, check_vma=False)

time: 505 us -> 329 us (0.65)
  waiting for transfers between devices: 450 us -> 256 us
  local copies, waits for them, and re-layouts: 5.11 us -> 17 us
  blocking collectives: 0 us -> 8.44 us
    unnamed x5 -> x8, waiting for transfers between devices: 226 us -> 0.81 us
    psum x1 -> x0, waiting for transfers between devices: 224 us -> none  [local(): head_weight = lax.psum(placed.reshape(HD, out_weight.shape[1]), 'dp')]
    all_gather x2 -> x5, waiting for transfers between devices: 0.03 us -> 170 us  [the longest x1 48.6 us: local(): lax.all_gather(lax.all_gather(masked, 'sqy', axis=0), 'sqx', axis=0)]
    reduce_scatter x0 -> x3, waiting for transfers between devices: none -> 86.1 us  [the longest x1 40.8 us: local(): owned = lax.psum_scatter(owned, 'dpz', scatter_dimension=0, tiled=True)]
    all_gather x0 -> x2, blocking collectives: none -> 8.44 us  [the longest x1 6.33 us: local(): gathered = lax.all_gather(gathered, 'dpy', axis=0)]
    all_gather x0 -> x2, local copies, waits for them, and re-layouts: none -> 7.22 us  [the longest x1 4.59 us: local(): lax.all_gather(lax.all_gather(inputs[0], 'sqy', axis=0), 'sqx', axis=0)]
  transfers between devices with their start and end apart: 4 -> 8, of which waited for: 2 -> 8; matrix products, arithmetic and copies ran while one was open for 2% -> 2% of each run, Pallas kernels for 4% -> 6%
where the time goes in v2:
time: 329 us; the launch traced here: 328 us
  waiting for transfers between devices  256 us (78%)
  Pallas kernels  19.4 us (6%)
  local copies, waits for them, and re-layouts  17 us (5%)
  between operations  14.3 us (4%)
  matrix products  9.75 us (3%)
  blocking collectives  8.44 us (3%)
    all_gather x1, waiting for transfers between devices, local(): lax.all_gather(lax.all_gather(masked, 'sqy', axis=0), 'sqx', axis=0)  48.6 us
    all_gather x1, waiting for transfers between devices, local(): gathered = lax.all_gather(gathered, 'dpz', axis=0)  42.3 us
    reduce_scatter x1, waiting for transfers between devices, local(): owned = lax.psum_scatter(owned, 'dpz', scatter_dimension=0, tiled=True)  40.8 us
    reduce_scatter x1, waiting for transfers between devices, local(): owned = lax.psum_scatter(owned, 'dpy', scatter_dimension=0, tiled=True)  29.3 us
    all_gather x1, waiting for transfers between devices, local(): lax.all_gather(inputs[0], 'sqy', axis=0)  29.1 us
    all_gather x1, waiting for transfers between devices, local(): lax.all_gather(lax.all_gather(inputs[0], 'sqy', axis=0), 'sqx', axis=0)  27.8 us
    all_gather x1, waiting for transfers between devices, local(): lax.all_gather(masked, 'sqy', axis=0)  21.7 us
    pallas_call x1, Pallas kernels, attention_backward(): pl.pallas_call(attention_kernel, grid=(length // ROWS,), in_specs=[row_sp...  19.4 us
  transfers between devices with their start and end apart: 8, of which 8 were waited for; matrix products, arithmetic and copies ran while one was open for 2% of the time, Pallas kernels for 6%

profile of v2, /device:TPU:2, one launch (start us, length us, event | category | flops | bytes accessed | tf_op | source)
XLA Modules:
  0.0 328.5 jit_solution(9808868460992037015)
XLA Ops:
  7.2 0.0 all-gather.11.cloned.1.call-start
  7.2 0.7 convert_reduce_fusion
  7.9 1.9 broadcast_multiply_fusion
  9.9 0.0 all-gather.13.cloned.1.call-start
  9.9 0.7 all-gather.13.cloned.1.call-update
  10.6 0.0 all-gather.17.cloned.1.call-start
  10.7 2.1 all-gather.1
  12.8 6.3 %all-gather.2 = bf16[4,32,1024]{2,1,0:T(8,128)(2,1)} all-gather(bf16[2,32,1024]{2,1,0:T(8,128)(2,1)S(1)} %bitcast.64), channel_id=4, replica_groups=mesh['dpy'=2,'dpz'=8,'dpc'=2,'sqy'=2,'sqx'=4] {'dpy'}, dimensions={0}, use_global_device_ids=true | all-gather | bytes 393216 | tf_op jit(solution)/shard_map/all_gather | solution.py:90
  19.2 0.0 all-gather.15.cloned.1.call-start
  19.2 21.7 %all-gather.11.cloned.1.call-done = bf16[2,256,1024]{2,1,0:T(8,128)(2,1)} async-done(((bf16[1,256,1024]{2,1,0:T(8,128)(2,1)}), bf16[2,256,1024]{2,1,0:T(8,128)(2,1)}) %all-gather.11.cloned.1.call-update) | async-done | bytes 1048592 | tf_op jit(solution)/shard_map/all_gather | solution.py:94
  40.9 0.0 all-gather.19.cloned.1.call-start
  41.0 29.1 %all-gather.13.cloned.1.call-done = bf16[2,256,1024]{2,1,0:T(8,128)(2,1)} async-done(((bf16[1,256,1024]{2,1,0:T(8,128)(2,1)}), bf16[2,256,1024]{2,1,0:T(8,128)(2,1)}) %all-gather.13.cloned.1.call-update) | async-done | bytes 1048592 | tf_op jit(solution)/shard_map/all_gather | solution.py:95
  70.1 0.0 reduce-scatter.4.cloned.1.call-start
  70.2 42.3 %all-gather.17.cloned.1.call-done = bf16[16,2,32,1024]{3,2,1,0:T(8,128)(2,1)} async-done(((bf16[2,2,32,1024]{3,2,1,0:T(8,128)(2,1)}), bf16[16,2,32,1024]{3,2,1,0:T(8,128)(2,1)}) %all-gather.17.cloned.1.call-update) | async-done | bytes 2097168 | tf_op jit(solution)/shard_map/all_gather | solution.py:91
  112.5 1.8 copy.42
  114.3 48.6 %all-gather.15.cloned.1.call-done = bf16[8,256,1024]{2,1,0:T(8,128)(2,1)} async-done(((bf16[2,256,1024]{2,1,0:T(8,128)(2,1)}), bf16[8,256,1024]{2,1,0:T(8,128)(2,1)}) %all-gather.15.cloned.1.call-update) | async-done | bytes 4194320 | tf_op jit(solution)/shard_map/all_gather | solution.py:94
  162.9 2.6 copy.41
  165.6 1.3 convolution_convert_fusion.g_ref
  166.9 0.1 broadcast_in_dim.3
  167.0 0.5 copy-done.4
  167.5 0.6 copy-done.2
  168.1 19.4 %shard_map.111 = (bf16[2048,128]{1,0:T(8,128)(2,1)S(1)}, bf16[2048,128]{1,0:T(8,128)(2,1)S(1)}, bf16[2048,128]{1,0:T(8,128)(2,1)S(1)}, bf16[2048,128]{1,0:T(8,128)(2,1)S(1)}) custom-call(bf16[2048,128]{1,0:T(8,128)(2,1)S(1)} %bitcast.51, bf16[2048,128]{1,0:T(8,128)(2,1)S(1)} %bitcast.52, bf16[2048,128]{1,0:T(8,128)(2,1)S(1)} %bitcast.53, ...), custom_call_target="tpu_custom_call" | custom-call | flops 6442450944 | bytes 4194304 | tf_op jit(solution)/shard_map/pallas_call | solution.py:66
  187.5 0.2 copy.50
  187.7 0.2 dot_general.53
  187.9 27.8 %all-gather.19.cloned.1.call-done = bf16[8,256,1024]{2,1,0:T(8,128)(2,1)} async-done(((bf16[2,256,1024]{2,1,0:T(8,128)(2,1)}), bf16[8,256,1024]{2,1,0:T(8,128)(2,1)}) %all-gather.19.cloned.1.call-update) | async-done | bytes 4194320 | tf_op jit(solution)/shard_map/all_gather | solution.py:95
  215.7 4.6 %copy.44 = bf16[4,2,256,1024]{3,2,0,1:T(8,128)(2,1)} copy(bf16[4,2,256,1024]{3,2,1,0:T(8,128)(2,1)} %bitcast.59) | data formatting | bytes 8388608 | tf_op jit(solution)/shard_map/all_gather | solution.py:95
  220.3 0.2 copy.48
  220.5 0.2 dot_general.49
  220.7 0.2 copy.46
  221.0 0.2 dot_general.45
  221.2 3.3 convolution_bitcast_fusion.1
  224.4 0.2 copy-done.3
  224.6 1.0 convolution_bitcast_fusion.2
  225.6 0.2 copy.43
  225.8 0.2 dot_general.41
  226.0 3.3 convolution_bitcast_fusion.3
  229.3 0.2 copy-done.5
  229.5 1.0 convolution_bitcast_fusion
  230.4 0.2 maximum_bitcast_fusion
  230.6 1.4 copy.52
  232.0 1.8 reshape.70
  233.9 0.0 reduce-scatter.6.cloned.1.call-start
  233.9 16.1 %reduce-scatter.4.cloned.1.call-done = f32[64,32,128]{2,1,0:T(8,128)} async-done(((f32[128,32,128]{2,1,0:T(8,128)}), f32[64,32,128]{2,1,0:T(8,128)}) %reduce-scatter.4.cloned.1.call-update) | async-done | bytes 1048592 | tf_op jit(solution)/shard_map/reduce_scatter | solution.py:119
  250.0 0.0 reduce-scatter.8.cloned.1.call-start
  250.0 29.3 %reduce-scatter.6.cloned.1.call-done = f32[32,32,128]{2,1,0:T(8,128)} async-done(((f32[64,32,128]{2,1,0:T(8,128)}), f32[32,32,128]{2,1,0:T(8,128)}) %reduce-scatter.6.cloned.1.call-update) | async-done | bytes 524304 | tf_op jit(solution)/shard_map/reduce_scatter | solution.py:120
  279.3 40.8 %reduce-scatter.8.cloned.1.call-done = f32[4,32,128]{2,1,0:T(8,128)} async-done(((f32[32,32,128]{2,1,0:T(8,128)}), f32[4,32,128]{2,1,0:T(8,128)}) %reduce-scatter.8.cloned.1.call-update) | async-done | bytes 65552 | tf_op jit(solution)/shard_map/reduce_scatter | solution.py:121
  320.1 0.9 reshape.71
  321.0 0.7 fusion.6
  (17 shorter events, 0.2 us)
Async XLA Ops:
  7.2 33.7 %all-gather.11.cloned.1.call-start = ((), (), s32[]{:S(2)}) async-start(), calls=%async_computation.3 | async-start | bytes 1572864 | tf_op jit(solution)/shard_map/all_gather | solution.py:94
  9.9 60.2 %all-gather.13.cloned.1.call-start = ((), (), s32[]{:S(2)}) async-start(), calls=%async_computation.4 | async-start | bytes 1572864 | tf_op jit(solution)/shard_map/all_gather | solution.py:95
  10.6 101.8 %all-gather.17.cloned.1.call-start = ((), (), s32[]{:S(2)}) async-start(), calls=%async_computation.9 | async-start | bytes 2359296 | tf_op jit(solution)/shard_map/all_gather | solution.py:91
  19.2 143.7 %all-gather.15.cloned.1.call-start = ((), (), s32[]{:S(2)}) async-start(), calls=%async_computation.8 | async-start | bytes 5242880 | tf_op jit(solution)/shard_map/all_gather | solution.py:94
  40.9 174.8 %all-gather.19.cloned.1.call-start = ((), (), s32[]{:S(2)}) async-start(), calls=%async_computation.10 | async-start | bytes 5242880 | tf_op jit(solution)/shard_map/all_gather | solution.py:95
  70.1 179.9 %reduce-scatter.4.cloned.1.call-start = ((), (), s32[]{:S(2)}) async-start(), calls=%async_computation.5 | async-start | bytes 3145728 | tf_op jit(solution)/shard_map/reduce_scatter | solution.py:119
  165.5 2.0 copy-start.4
  165.5 1.4 copy-start.6
  165.5 2.0 copy-start
  165.5 2.0 copy-start.1
  165.5 2.5 copy-start.2
  221.2 3.5 %copy-start.3 = (bf16[4,2,256,1024]{3,2,0,1:T(8,128)(2,1)S(1)}, bf16[4,2,256,1024]{3,2,0,1:T(8,128)(2,1)}, u32[]{:S(2)}) copy-start(bf16[4,2,256,1024]{3,2,0,1:T(8,128)(2,1)} %copy.44) | copy-start | bytes 12582916
  226.0 3.5 %copy-start.5 = (bf16[4,2,256,1024]{3,2,0,1:T(8,128)(2,1)S(1)}, bf16[4,2,256,1024]{3,2,0,1:T(8,128)(2,1)}, u32[]{:S(2)}) copy-start(bf16[4,2,256,1024]{3,2,0,1:T(8,128)(2,1)} %copy-done.4) | copy-start | bytes 12582916
  233.9 45.5 %reduce-scatter.6.cloned.1.call-start = ((), (), s32[]{:S(2)}) async-start(), calls=%async_computation.6 | async-start | bytes 1572864 | tf_op jit(solution)/shard_map/reduce_scatter | solution.py:120
  250.0 70.1 %reduce-scatter.8.cloned.1.call-start = ((), (), s32[]{:S(2)}) async-start(), calls=%async_computation.7 | async-start | bytes 589824 | tf_op jit(solution)/shard_map/reduce_scatter | solution.py:121
Sparse Core Ops, SparseCore 0:
  10.0 30.8 all-gather.10
  42.7 27.3 all-gather.12
  71.9 40.5 all-gather.16
  114.1 48.6 all-gather.14
  164.5 51.1 all-gather.18
  234.0 15.9 reduce-scatter.3
  252.6 26.6 reduce-scatter.5
  281.8 38.2 reduce-scatter.7

commit v3 on v2

--- a/solution.py
+++ b/solution.py
@@ -77,6 +77,52 @@
     )(q, k, v, g, live_cols)
 
 
+def gather_kernel(nseq, sx, a_ref, b_ref, a_out, b_out, send_sem, recv_sem, copy_sem):
+    me = lax.axis_index("sqy") * sx + lax.axis_index("sqx")
+    mesh_id = pl.DeviceIdType.MESH
+    barrier = pltpu.get_barrier_semaphore()
+    for off in range(1, nseq):
+        peer = (me + off) % nseq
+        pl.semaphore_signal(barrier, 1, device_id={"sqy": peer // sx, "sqx": peer % sx}, device_id_type=mesh_id)
+    pl.semaphore_wait(barrier, nseq - 1)
+    copies = []
+    for t, (src, dst) in enumerate(((a_ref, a_out), (b_ref, b_out))):
+        local = pltpu.make_async_copy(src, dst.at[me], copy_sem.at[t])
+        local.start()
+        copies.append(local)
+        for off in range(1, nseq):
+            peer = (me + off) % nseq
+            remote = pltpu.make_async_remote_copy(
+                src_ref=src,
+                dst_ref=dst.at[me],
+                send_sem=send_sem.at[t, off - 1],
+                recv_sem=recv_sem.at[t, off - 1],
+                device_id={"sqy": peer // sx, "sqx": peer % sx},
+                device_id_type=mesh_id,
+            )
+            remote.start()
+            copies.append(remote)
+    for copy in copies:
+        copy.wait()
+
+
+def seq_gather(a, b, nseq, sx):
+    any_spec = pl.BlockSpec(memory_space=pl.ANY)
+    out = jax.ShapeDtypeStruct((nseq,) + a.shape, a.dtype)
+    return pl.pallas_call(
+        functools.partial(gather_kernel, nseq, sx),
+        in_specs=[any_spec, any_spec],
+        out_specs=[any_spec, any_spec],
+        out_shape=[out, out],
+        scratch_shapes=[
+            pltpu.SemaphoreType.DMA((2, nseq - 1)),
+            pltpu.SemaphoreType.DMA((2, nseq - 1)),
+            pltpu.SemaphoreType.DMA((2,)),
+        ],
+        compiler_params=pltpu.CompilerParams(collective_id=0, has_side_effects=True),
+    )(a, b)
+
+
 DP = ("dpy", "dpz", "dpc")
 SQ = ("sqy", "sqx")
 
@@ -91,10 +137,10 @@
     gathered = lax.all_gather(gathered, "dpz", axis=0)
     gathered = jnp.transpose(gathered, (1, 0, 2, 3, 4)).reshape(-1, width)
     head_weight = lax.dynamic_slice_in_dim(gathered, head * HD, HD, 0)
-    masked_all = lax.all_gather(lax.all_gather(masked, "sqy", axis=0), "sqx", axis=0)
-    inputs_all = lax.all_gather(lax.all_gather(inputs[0], "sqy", axis=0), "sqx", axis=0)
-    masked_all = jnp.transpose(masked_all, (1, 0, 2, 3)).reshape(-1, width)
-    inputs_all = jnp.transpose(inputs_all, (1, 0, 2, 3)).reshape(-1, width)
+    nseq = sizes["sqy"] * sizes["sqx"]
+    masked_all, inputs_all = seq_gather(masked, inputs[0], nseq, sizes["sqx"])
+    masked_all = masked_all.reshape(-1, width)
+    inputs_all = inputs_all.reshape(-1, width)
     d_attn = lax.dot_general(
         masked_all, head_weight, (((1,), (1,)), ((), ())), preferred_element_type=jnp.float32
     ).astype(jnp.bfloat16)

time: 329 us -> 280 us (0.85)
  waiting for transfers between devices: 256 us -> 89.7 us
  Pallas kernels: 19.4 us -> 144 us
  local copies, waits for them, and re-layouts: 17 us -> 9.45 us
    all_gather x4 -> x0, waiting for transfers between devices: 127 us -> none  [the longest x1 48.6 us: local(): lax.all_gather(lax.all_gather(masked, 'sqy', axis=0), 'sqx', axis=0)]
    pallas_call x0 -> x1, Pallas kernels: none -> 124 us  [seq_gather(): pl.pallas_call(functools.partial(gather_kernel, nseq, sx), in_specs=[any_...]
    all_gather x1, waiting for transfers between devices: 42.3 us -> 0.02 us  [local(): gathered = lax.all_gather(gathered, 'dpz', axis=0)]
    all_gather x2 -> x0, local copies, waits for them, and re-layouts: 7.22 us -> none  [the longest x1 4.59 us: local(): lax.all_gather(lax.all_gather(inputs[0], 'sqy', axis=0), 'sqx', axis=0)]
    reduce_scatter x1, waiting for transfers between devices: 16.1 us -> 19.7 us  [local(): owned = lax.psum_scatter(terms, 'dpc', scatter_dimension=0, tiled=True)]
  transfers between devices with their start and end apart: 8 -> 4, of which waited for: 8 -> 3; matrix products, arithmetic and copies ran while one was open for 2% -> 1% of each run, Pallas kernels for 6% -> 44%
where the time goes in v3:
time: 280 us
  Pallas kernels  144 us (51%)
  waiting for transfers between devices  89.7 us (32%)
  between operations  14 us (5%)
  matrix products  11.7 us (4%)
  local copies, waits for them, and re-layouts  9.45 us (3%)
  blocking collectives  8.44 us (3%)
  other arithmetic  2.83 us (1%)
    pallas_call x1, Pallas kernels, seq_gather(): pl.pallas_call(functools.partial(gather_kernel, nseq, sx), in_specs=[any_...  124 us
    reduce_scatter x1, waiting for transfers between devices, local(): owned = lax.psum_scatter(owned, 'dpz', scatter_dimension=0, tiled=True)  40.6 us
    reduce_scatter x1, waiting for transfers between devices, local(): owned = lax.psum_scatter(owned, 'dpy', scatter_dimension=0, tiled=True)  29.3 us
    reduce_scatter x1, waiting for transfers between devices, local(): owned = lax.psum_scatter(terms, 'dpc', scatter_dimension=0, tiled=True)  19.7 us
    pallas_call x1, Pallas kernels, attention_backward(): pl.pallas_call(attention_kernel, grid=(length // ROWS,), in_specs=[row_sp...  19.4 us
    all_gather x1, blocking collectives, local(): gathered = lax.all_gather(gathered, 'dpy', axis=0)  6.33 us
  transfers between devices with their start and end apart: 4, of which 3 were waited for; matrix products, arithmetic and copies ran while one was open for 1% of the time, Pallas kernels for 44%

profile of v3, /device:TPU:2, one launch (start us, length us, event | category | flops | bytes accessed | tf_op | source)
XLA Modules:
  0.0 280.0 jit_solution(2309004293578748699)
XLA Ops:
  7.2 0.0 all-gather.5.cloned.1.call-start
  7.2 2.1 all-gather
  9.3 6.3 %all-gather.1 = bf16[4,32,1024]{2,1,0:T(8,128)(2,1)} all-gather(bf16[2,32,1024]{2,1,0:T(8,128)(2,1)S(1)} %bitcast.59), channel_id=3, replica_groups=mesh['dpy'=2,'dpz'=8,'dpc'=2,'sqy'=2,'sqx'=4] {'dpy'}, dimensions={0}, use_global_device_ids=true | all-gather | bytes 393216 | tf_op jit(solution)/shard_map/all_gather | solution.py:136
  15.7 0.0 all-gather.5.cloned.1.call-update
  15.7 0.0 reduce-scatter.4.cloned.1.call-start
  15.7 0.7 convert_reduce_fusion
  16.4 2.0 bitcast_multiply_fusion.a_ref
  18.4 124.3 %shard_map.111 = (bf16[8,256,1024]{2,1,0:T(8,128)(2,1)}, bf16[8,256,1024]{2,1,0:T(8,128)(2,1)}) custom-call(bf16[256,1024]{1,0:T(8,128)(2,1)} %bitcast_multiply_fusion.a_ref, bf16[256,1024]{1,0:T(8,128)(2,1)} %bitcast.60), custom_call_target="tpu_custom_call" | custom-call | tf_op jit(solution)/shard_map/pallas_call | solution.py:112
  142.7 0.0 all-gather.5.cloned.1.call-done
  142.7 0.0 copy-start.4
  142.7 0.0 copy-start.5
  142.7 1.9 copy.35
  144.7 0.0 copy-start
  144.7 0.0 copy-start.1
  144.7 0.0 copy-start.2
  144.7 0.8 copy-done.4
  145.5 1.3 convolution_convert_fusion.g_ref
  146.8 0.1 broadcast_in_dim.3
  146.9 0.0 copy-done
  146.9 0.0 copy-done.1
  147.0 0.0 copy-done.2
  147.0 19.4 %shard_map.112 = (bf16[2048,128]{1,0:T(8,128)(2,1)S(1)}, bf16[2048,128]{1,0:T(8,128)(2,1)S(1)}, bf16[2048,128]{1,0:T(8,128)(2,1)S(1)}, bf16[2048,128]{1,0:T(8,128)(2,1)S(1)}) custom-call(bf16[2048,128]{1,0:T(8,128)(2,1)S(1)} %bitcast.48, bf16[2048,128]{1,0:T(8,128)(2,1)S(1)} %bitcast.49, bf16[2048,128]{1,0:T(8,128)(2,1)S(1)} %bitcast.50, ...), custom_call_target="tpu_custom_call" | custom-call | flops 6442450944 | bytes 4194304 | tf_op jit(solution)/shard_map/pallas_call | solution.py:66
  166.4 0.2 copy.36
  166.6 0.2 dot_general.41
  166.8 0.2 copy.38
  167.0 0.2 dot_general.45
  167.2 3.3 %convolution_bitcast_fusion.3 = f32[2,8,2,4,1,1024]{5,1,3,2,0,4:T(8,128)S(1)} fusion(bf16[2048,1024,1,1,1]{1,0,4,3,2:T(8,128)(2,1)} %bitcast.51, bf16[2,8,2,4,2048]{4,3,2,1,0:T(4,128)(2,1)S(1)} %dot_general.41), kind=kOutput, calls=%fused_computation.5 | convolution fusion | flops 536870912 | bytes 5242880 | tf_op jit(solution)/shard_map/dot_general | solution.py:155
  170.5 0.2 copy-done.3
  170.7 1.0 convolution_bitcast_fusion.2
  171.6 0.2 copy.40
  171.9 0.2 dot_general.49
  172.1 3.1 %convolution_bitcast_fusion.1 = f32[2,8,2,4,1,1024]{5,1,3,2,0,4:T(8,128)S(1)} fusion(bf16[2048,1024,1,1,1]{1,0,4,3,2:T(8,128)(2,1)} %bitcast.52, bf16[2,8,2,4,2048]{4,3,2,1,0:T(4,128)(2,1)S(1)} %dot_general.49), kind=kOutput, calls=%fused_computation.3 | convolution fusion | flops 536870912 | bytes 5242880 | tf_op jit(solution)/shard_map/dot_general | solution.py:157
  175.2 0.2 copy.42
  175.4 0.2 dot_general.53
  175.6 3.1 %convolution_bitcast_fusion = f32[2,8,2,4,1,1024]{5,1,3,2,0,4:T(8,128)S(1)} fusion(bf16[2048,1024,1,1,1]{1,0,4,3,2:T(8,128)(2,1)} %bitcast.54, bf16[2,8,2,4,2048]{4,3,2,1,0:T(4,128)(2,1)S(1)} %dot_general.53), kind=kOutput, calls=%fused_computation.2 | convolution fusion | flops 536870912 | bytes 5242880 | tf_op jit(solution)/shard_map/dot_general | solution.py:158
  178.7 0.2 maximum_bitcast_fusion
  178.9 1.4 copy.44
  180.2 1.9 reshape.63
  182.1 0.0 reduce-scatter.4.cloned.1.call-update
  182.2 0.0 reduce-scatter.6.cloned.1.call-start
  182.2 19.7 %reduce-scatter.4.cloned.1.call-done = f32[64,32,128]{2,1,0:T(8,128)} async-done(((f32[128,32,128]{2,1,0:T(8,128)}), f32[64,32,128]{2,1,0:T(8,128)}) %reduce-scatter.4.cloned.1.call-update) | async-done | bytes 1048592 | tf_op jit(solution)/shard_map/reduce_scatter | solution.py:165
  202.0 0.0 reduce-scatter.6.cloned.1.call-update
  202.0 0.0 reduce-scatter.8.cloned.1.call-start
  202.0 29.3 %reduce-scatter.6.cloned.1.call-done = f32[32,32,128]{2,1,0:T(8,128)} async-done(((f32[64,32,128]{2,1,0:T(8,128)}), f32[32,32,128]{2,1,0:T(8,128)}) %reduce-scatter.6.cloned.1.call-update) | async-done | bytes 524304 | tf_op jit(solution)/shard_map/reduce_scatter | solution.py:166
  231.3 0.0 reduce-scatter.8.cloned.1.call-update
  231.3 40.6 %reduce-scatter.8.cloned.1.call-done = f32[4,32,128]{2,1,0:T(8,128)} async-done(((f32[32,32,128]{2,1,0:T(8,128)}), f32[4,32,128]{2,1,0:T(8,128)}) %reduce-scatter.8.cloned.1.call-update) | async-done | bytes 65552 | tf_op jit(solution)/shard_map/reduce_scatter | solution.py:167
  272.0 0.9 reshape.64
  272.8 0.7 fusion.6
  (2 shorter events, 0.0 us)
Async XLA Ops:
  7.2 135.5 %all-gather.5.cloned.1.call-start = ((), (), s32[]{:S(2)}) async-start(), calls=%async_computation.6 | async-start | bytes 2359296 | tf_op jit(solution)/shard_map/all_gather | solution.py:137
  15.7 186.3 %reduce-scatter.4.cloned.1.call-start = ((), (), s32[]{:S(2)}) async-start(), calls=%async_computation.3 | async-start | bytes 3145728 | tf_op jit(solution)/shard_map/reduce_scatter | solution.py:165
  142.7 2.8 %copy-start.4 = (bf16[8,256,1024]{2,1,0:T(8,128)(2,1)S(1)}, bf16[8,256,1024]{2,1,0:T(8,128)(2,1)}, u32[]{:S(2)}) copy-start(bf16[8,256,1024]{2,1,0:T(8,128)(2,1)} %get-tuple-element.10) | copy-start | bytes 12582916
  142.7 4.1 %copy-start.5 = (s32[1,1,16,16]{3,2,1,0:T(8,128)S(1)}, s32[1,1,16,16]{3,2,1,0:T(8,128)}, u32[]{:S(2)}) copy-start(s32[1,1,16,16]{3,2,1,0:T(8,128)} %param.15) | copy-start | bytes 3076
  144.7 2.3 copy-start
  144.7 2.3 copy-start.1
  144.7 2.3 copy-start.2
  167.2 3.5 %copy-start.3 = (bf16[8,256,1024]{2,1,0:T(8,128)(2,1)S(1)}, bf16[8,256,1024]{2,1,0:T(8,128)(2,1)}, u32[]{:S(2)}) copy-start(bf16[8,256,1024]{2,1,0:T(8,128)(2,1)} %get-tuple-element.12) | copy-start | bytes 12582916
  182.2 49.2 %reduce-scatter.6.cloned.1.call-start = ((), (), s32[]{:S(2)}) async-start(), calls=%async_computation.4 | async-start | bytes 1572864 | tf_op jit(solution)/shard_map/reduce_scatter | solution.py:166
  202.0 70.0 %reduce-scatter.8.cloned.1.call-start = ((), (), s32[]{:S(2)}) async-start(), calls=%async_computation.5 | async-start | bytes 589824 | tf_op jit(solution)/shard_map/reduce_scatter | solution.py:167
Sparse Core Ops, SparseCore 0:
  15.8 48.3 all-gather.4
  182.3 19.6 reduce-scatter.3
  204.6 26.6 reduce-scatter.5
  233.7 38.2 reduce-scatter.7

commit v4 on v3

--- a/solution.py
+++ b/solution.py
@@ -77,13 +77,13 @@
     )(q, k, v, g, live_cols)
 
 
-def gather_kernel(nseq, sx, a_ref, b_ref, a_out, b_out, send_sem, recv_sem, copy_sem):
-    me = lax.axis_index("sqy") * sx + lax.axis_index("sqx")
+def gather_kernel(nseq, a_ref, b_ref, a_out, b_out, send_sem, recv_sem, copy_sem):
+    me = lax.axis_index("sqx")
     mesh_id = pl.DeviceIdType.MESH
     barrier = pltpu.get_barrier_semaphore()
     for off in range(1, nseq):
         peer = (me + off) % nseq
-        pl.semaphore_signal(barrier, 1, device_id={"sqy": peer // sx, "sqx": peer % sx}, device_id_type=mesh_id)
+        pl.semaphore_signal(barrier, 1, device_id={"sqx": peer}, device_id_type=mesh_id)
     pl.semaphore_wait(barrier, nseq - 1)
     copies = []
     for t, (src, dst) in enumerate(((a_ref, a_out), (b_ref, b_out))):
@@ -97,7 +97,7 @@
                 dst_ref=dst.at[me],
                 send_sem=send_sem.at[t, off - 1],
                 recv_sem=recv_sem.at[t, off - 1],
-                device_id={"sqy": peer // sx, "sqx": peer % sx},
+                device_id={"sqx": peer},
                 device_id_type=mesh_id,
             )
             remote.start()
@@ -106,11 +106,11 @@
         copy.wait()
 
 
-def seq_gather(a, b, nseq, sx):
+def seq_gather(a, b, nseq):
     any_spec = pl.BlockSpec(memory_space=pl.ANY)
     out = jax.ShapeDtypeStruct((nseq,) + a.shape, a.dtype)
     return pl.pallas_call(
-        functools.partial(gather_kernel, nseq, sx),
+        functools.partial(gather_kernel, nseq),
         in_specs=[any_spec, any_spec],
         out_specs=[any_spec, any_spec],
         out_shape=[out, out],
@@ -129,7 +129,12 @@
 
 def local(inputs, d_output, loss_mask, queries, keys, values, out_weight, block_mask):
     sizes = {name: lax.axis_size(name) for name in DP + SQ}
-    head = lax.axis_index("sqy") * sizes["sqx"] + lax.axis_index("sqx")
+    half = lax.axis_index("sqy")
+    other = 1 - half
+    col = lax.axis_index("sqx")
+    head = half * sizes["sqx"] + col
+    partner_head = other * sizes["sqx"] + col
+    swap = [(0, 1), (1, 0)]
     masked = d_output[0] * loss_mask[0][:, None].astype(jnp.bfloat16)
     own_rows, width = out_weight.shape
     gathered = lax.all_gather(out_weight, "dpc", axis=0)
@@ -137,35 +142,53 @@
     gathered = lax.all_gather(gathered, "dpz", axis=0)
     gathered = jnp.transpose(gathered, (1, 0, 2, 3, 4)).reshape(-1, width)
     head_weight = lax.dynamic_slice_in_dim(gathered, head * HD, HD, 0)
-    nseq = sizes["sqy"] * sizes["sqx"]
-    masked_all, inputs_all = seq_gather(masked, inputs[0], nseq, sizes["sqx"])
-    masked_all = masked_all.reshape(-1, width)
-    inputs_all = inputs_all.reshape(-1, width)
-    d_attn = lax.dot_general(
-        masked_all, head_weight, (((1,), (1,)), ((), ())), preferred_element_type=jnp.float32
-    ).astype(jnp.bfloat16)
+    partner_weight = lax.dynamic_slice_in_dim(gathered, partner_head * HD, HD, 0)
+    masked_half, inputs_half = seq_gather(masked, inputs[0], sizes["sqx"])
+    masked_half = masked_half.reshape(-1, width)
+    inputs_half = inputs_half.reshape(-1, width)
+    half_len = masked_half.shape[0]
+    nt = (((1,), (1,)), ((), ()))
+    d_own = lax.dot_general(masked_half, head_weight, nt, preferred_element_type=jnp.float32).astype(jnp.bfloat16)
+    d_give = lax.dot_general(masked_half, partner_weight, nt, preferred_element_type=jnp.float32).astype(jnp.bfloat16)
+    d_got = lax.ppermute(d_give, "sqy", swap)
+    d_attn = jnp.zeros((2 * half_len, HD), jnp.bfloat16)
+    d_attn = lax.dynamic_update_slice_in_dim(d_attn, d_own, half * half_len, 0)
+    d_attn = lax.dynamic_update_slice_in_dim(d_attn, d_got, other * half_len, 0)
     blocks = block_mask[0, 0]
     live_cols = jnp.repeat(blocks, BLOCK, axis=1)[:, None, :]
     d_query, attended, d_key, d_value = attention_backward(
         queries[0, :, 0], keys[0, :, 0], values[0, :, 0], d_attn, live_cols
     )
+    grads = jnp.stack([d_query, d_key, d_value, attended])
+    grads_own = lax.dynamic_slice_in_dim(grads, half * half_len, half_len, 1)
+    grads_give = lax.dynamic_slice_in_dim(grads, other * half_len, half_len, 1)
+    grads_got = lax.ppermute(grads_give, "sqy", swap)
     tn = (((0,), (0,)), ((), ()))
-    terms = jnp.stack(
-        [
-            lax.dot_general(d_query, inputs_all, tn, preferred_element_type=jnp.float32),
-            lax.dot_general(d_key, inputs_all, tn, preferred_element_type=jnp.float32),
-            lax.dot_general(d_value, inputs_all, tn, preferred_element_type=jnp.float32),
-            lax.dot_general(attended, masked_all, tn, preferred_element_type=jnp.float32),
-        ],
-        axis=1,
-    )
+
+    def terms_of(parts):
+        return jnp.stack(
+            [
+                lax.dot_general(parts[0], inputs_half, tn, preferred_element_type=jnp.float32),
+                lax.dot_general(parts[1], inputs_half, tn, preferred_element_type=jnp.float32),
+                lax.dot_general(parts[2], inputs_half, tn, preferred_element_type=jnp.float32),
+                lax.dot_general(parts[3], masked_half, tn, preferred_element_type=jnp.float32),
+            ],
+            axis=1,
+        )
+
+    own_terms = terms_of(grads_own)
+    got_terms = terms_of(grads_got)
+    terms = jnp.where(half == 0, jnp.stack([own_terms, got_terms], 1), jnp.stack([got_terms, own_terms], 1))
     chunk = terms.shape[0] // (sizes["dpy"] * sizes["dpz"] * sizes["dpc"])
-    terms = terms.reshape(sizes["dpy"], sizes["dpz"], sizes["dpc"], chunk, 4, width)
-    terms = jnp.transpose(terms, (2, 0, 1, 3, 4, 5)).reshape(-1, 4 * width // 128, 128)
+    terms = terms.reshape(sizes["dpy"], sizes["dpz"], sizes["dpc"], chunk, 2 * 4 * width)
+    terms = jnp.transpose(terms, (2, 0, 1, 3, 4)).reshape(-1, 2 * 4 * width // 128, 128)
     owned = lax.psum_scatter(terms, "dpc", scatter_dimension=0, tiled=True)
     owned = lax.psum_scatter(owned, "dpy", scatter_dimension=0, tiled=True)
     owned = lax.psum_scatter(owned, "dpz", scatter_dimension=0, tiled=True)
-    owned = owned.reshape(chunk, 4, width)
+    owned = owned.reshape(chunk, 2, 4 * width)
+    kept = lax.dynamic_index_in_dim(owned, half, 1, keepdims=False)
+    sent = lax.dynamic_index_in_dim(owned, other, 1, keepdims=False)
+    owned = (kept + lax.ppermute(sent, "sqy", swap)).reshape(chunk, 4, width)
     return tuple(owned[:, part][:, None, :] for part in range(4))
 
 

time: 280 us -> 274 us (0.979)
  Pallas kernels: 144 us -> 68.5 us
  waiting for transfers between devices: 89.7 us -> 130 us
  local copies, waits for them, and re-layouts: 9.45 us -> 27.7 us
  starting transfers between devices: 0.16 us -> 7.62 us
    pallas_call x1, Pallas kernels: 124 us -> 49.1 us  [seq_gather(): pl.pallas_call(functools.partial(gather_kernel, nseq), in_specs=[any_spec...]
    ppermute x0 -> x3, waiting for transfers between devices: none -> 25.9 us  [the longest x1 17 us: local(): grads_got = lax.ppermute(grads_give, 'sqy', swap)]
    reduce_scatter x1, waiting for transfers between devices: 29.3 us -> 40.8 us  [local(): owned = lax.psum_scatter(owned, 'dpy', scatter_dimension=0, tiled=True)]
    select_n x0 -> x2, local copies, waits for them, and re-layouts: none -> 11.3 us  [local(): jnp.where(half == 0, jnp.stack([own_terms, got_terms], 1), jnp.stack([got...]
    ppermute x0 -> x3, starting transfers between devices: none -> 7.46 us  [the longest x1 3.03 us: local(): owned = (kept + lax.ppermute(sent, 'sqy', swap)).reshape(chunk, 4, width)]
    reshape x2 -> x3, local copies, waits for them, and re-layouts: 2.76 us -> 7.11 us  [the longest x1 6.07 us: local(): jnp.transpose(terms, (2, 0, 1, 3, 4)).reshape(-1, 2 * 4 * width // 128, 128)]
    transpose x1, local copies, waits for them, and re-layouts: 1.35 us -> 4.6 us  [local(): jnp.transpose(terms, (2, 0, 1, 3, 4)).reshape(-1, 2 * 4 * width // 128, 128)]
    dot_general x5 -> x10, matrix products: 11.7 us -> 13.1 us  [the longest x2 2.98 us: terms_of(): lax.dot_general(parts[1], inputs_half, tn, preferred_element_type=jnp.flo...]
  transfers between devices with their start and end apart: 4 -> 7, of which waited for: 3 -> 6; matrix products, arithmetic and copies ran while one was open for 1% -> 3% of each run, Pallas kernels for 44% -> 18%
where the time goes in v4:
time: 274 us
  waiting for transfers between devices  130 us (47%)
  Pallas kernels  68.5 us (25%)
  local copies, waits for them, and re-layouts  27.7 us (10%)
  between operations  14 us (5%)
  matrix products  13.1 us (5%)
  blocking collectives  8.44 us (3%)
  starting transfers between devices  7.62 us (3%)
  other arithmetic  4.07 us (1%)
    pallas_call x1, Pallas kernels, seq_gather(): pl.pallas_call(functools.partial(gather_kernel, nseq), in_specs=[any_spec...  49.1 us
    reduce_scatter x1, waiting for transfers between devices, local(): owned = lax.psum_scatter(owned, 'dpz', scatter_dimension=0, tiled=True)  42 us
    reduce_scatter x1, waiting for transfers between devices, local(): owned = lax.psum_scatter(owned, 'dpy', scatter_dimension=0, tiled=True)  40.8 us
    reduce_scatter x1, waiting for transfers between devices, local(): owned = lax.psum_scatter(terms, 'dpc', scatter_dimension=0, tiled=True)  21.5 us
    pallas_call x1, Pallas kernels, attention_backward(): pl.pallas_call(attention_kernel, grid=(length // ROWS,), in_specs=[row_sp...  19.4 us
    ppermute x1, waiting for transfers between devices, local(): grads_got = lax.ppermute(grads_give, 'sqy', swap)  17 us
    select_n x2, local copies, waits for them, and re-layouts, local(): jnp.where(half == 0, jnp.stack([own_terms, got_terms], 1), jnp.stack([got...  11.3 us
    all_gather x1, blocking collectives, local(): gathered = lax.all_gather(gathered, 'dpy', axis=0)  6.33 us
  transfers between devices with their start and end apart: 7, of which 6 were waited for; matrix products, arithmetic and copies ran while one was open for 3% of the time, Pallas kernels for 18%

profile of v4, /device:TPU:2, one launch (start us, length us, event | category | flops | bytes accessed | tf_op | source)
XLA Modules:
  0.0 273.8 jit_solution(18139306545011101107)
XLA Ops:
  7.2 0.0 all-gather.5.cloned.1.call-start
  7.2 2.1 all-gather
  9.3 6.3 %all-gather.1 = bf16[4,32,1024]{2,1,0:T(8,128)(2,1)} all-gather(bf16[2,32,1024]{2,1,0:T(8,128)(2,1)S(1)} %bitcast.103), channel_id=3, replica_groups=mesh['dpy'=2,'dpz'=8,'dpc'=2,'sqy'=2,'sqx'=4] {'dpy'}, dimensions={0}, use_global_device_ids=true | all-gather | bytes 393216 | tf_op jit(solution)/shard_map/all_gather | solution.py:141
  15.7 0.0 reduce-scatter.4.cloned.1.call-start
  15.7 0.7 convert_reduce_fusion
  16.4 1.9 bitcast_multiply_fusion.a_ref
  18.4 49.1 %shard_map.111 = (bf16[4,256,1024]{2,1,0:T(8,128)(2,1)}, bf16[4,256,1024]{2,1,0:T(8,128)(2,1)}) custom-call(bf16[256,1024]{1,0:T(8,128)(2,1)} %bitcast_multiply_fusion.a_ref, bf16[256,1024]{1,0:T(8,128)(2,1)} %bitcast.104), custom_call_target="tpu_custom_call" | custom-call | tf_op jit(solution)/shard_map/pallas_call | solution.py:112
  67.5 1.9 copy.17
  69.4 0.3 copy-done.4
  69.7 0.7 convolution_convert_fusion
  70.5 2.2 collective-permute-start
  72.7 0.1 broadcast_in_dim.6
  72.8 0.8 fusion
  73.6 6.0 %collective-permute-done = bf16[1024,128]{1,0:T(8,128)(2,1)S(1)} collective-permute-done((bf16[1024,128]{1,0:T(8,128)(2,1)S(1)}, bf16[1024,128]{1,0:T(8,128)(2,1)S(1)}, u32[]{:S(2)}, u32[]{:S(2)}) %collective-permute-start) | collective-permute-done | bytes 262176 | tf_op jit(solution)/shard_map/ppermute | solution.py:153
  79.7 0.1 broadcast_in_dim.7
  79.8 19.4 %shard_map.112 = (bf16[2048,128]{1,0:T(8,128)(2,1)S(1)}, bf16[2048,128]{1,0:T(8,128)(2,1)S(1)}, bf16[2048,128]{1,0:T(8,128)(2,1)S(1)}, bf16[2048,128]{1,0:T(8,128)(2,1)S(1)}) custom-call(bf16[2048,128]{1,0:T(8,128)(2,1)S(1)} %bitcast.85, bf16[2048,128]{1,0:T(8,128)(2,1)S(1)} %bitcast.86, bf16[2048,128]{1,0:T(8,128)(2,1)S(1)} %bitcast.87, ...), custom_call_target="tpu_custom_call" | custom-call | flops 6442450944 | bytes 4194304 | tf_op jit(solution)/shard_map/pallas_call | solution.py:66
  99.3 0.3 pad_maximum_fusion
  99.5 1.3 copy-done.6
  100.9 0.1 constant_dynamic-slice_fusion.2
  101.0 2.2 collective-permute-start.1
  103.1 1.4 convolution_bitcast_fusion.7
  104.6 1.4 convolution_bitcast_fusion.5
  106.0 1.6 convolution_bitcast_fusion.6
  107.6 0.1 copy-done.5
  107.7 1.4 convolution_bitcast_fusion.4
  109.1 0.1 maximum_bitcast_fusion
  109.3 17.0 %collective-permute-done.1 = bf16[4,1024,128]{2,1,0:T(8,128)(2,1)} collective-permute-done((bf16[4,1024,128]{2,1,0:T(8,128)(2,1)S(1)}, bf16[4,1024,128]{2,1,0:T(8,128)(2,1)}, u32[]{:S(2)}, u32[]{:S(2)}) %collective-permute-start.1) | collective-permute-done | bytes 1048608 | tf_op jit(solution)/shard_map/ppermute | solution.py:165
  126.3 1.4 convolution_bitcast_fusion
  127.7 1.4 convolution_bitcast_fusion.1
  129.2 1.4 convolution_bitcast_fusion.2
  130.6 1.4 convolution_bitcast_fusion.3
  132.0 0.1 maximum_bitcast_fusion.1
  132.1 0.8 maximum_select_fusion
  133.0 4.7 %copy.18 = f32[128,2,4,1024]{3,2,1,0:T(4,128)} copy(f32[128,2,4,1024]{3,0,2,1:T(8,128)S(1)} %maximum_select_fusion) | data formatting | bytes 8388608 | tf_op jit(solution)/shard_map/jit(_where)/select_n | solution.py:181
  137.7 6.6 %select_n.39 = f32[2,8,2,4,8192]{4,3,2,1,0:T(4,128)} reshape(f32[128,2,4,1024]{3,2,1,0:T(4,128)} %copy.18) | data formatting | bytes 8388608 | tf_op jit(solution)/shard_map/jit(_where)/select_n | solution.py:181
  144.3 4.6 %copy.19 = f32[2,2,8,4,8192]{4,3,2,1,0:T(4,128)} copy(f32[2,2,8,4,8192]{4,3,0,2,1:T(4,128)} %bitcast.98) | data formatting | bytes 8388608 | tf_op jit(solution)/shard_map/transpose | solution.py:184
  148.9 6.1 %reshape.42 = f32[128,64,128]{2,1,0:T(8,128)} reshape(f32[2,2,8,4,8192]{4,3,2,1,0:T(4,128)} %copy.19) | data formatting | bytes 8388608 | tf_op jit(solution)/shard_map/reshape | solution.py:184
  155.0 0.0 reduce-scatter.6.cloned.1.call-start
  155.0 21.5 %reduce-scatter.4.cloned.1.call-done = f32[64,64,128]{2,1,0:T(8,128)} async-done(((f32[128,64,128]{2,1,0:T(8,128)}), f32[64,64,128]{2,1,0:T(8,128)}) %reduce-scatter.4.cloned.1.call-update) | async-done | bytes 2097168 | tf_op jit(solution)/shard_map/reduce_scatter | solution.py:185
  176.6 40.8 %reduce-scatter.6.cloned.1.call-done = f32[32,64,128]{2,1,0:T(8,128)} async-done(((f32[64,64,128]{2,1,0:T(8,128)}), f32[32,64,128]{2,1,0:T(8,128)}) %reduce-scatter.6.cloned.1.call-update) | async-done | bytes 1048592 | tf_op jit(solution)/shard_map/reduce_scatter | solution.py:186
  217.4 42.0 %reduce-scatter.8.cloned.1.call-done = f32[4,64,128]{2,1,0:T(8,128)} async-done(((f32[32,64,128]{2,1,0:T(8,128)}), f32[4,64,128]{2,1,0:T(8,128)}) %reduce-scatter.8.cloned.1.call-update) | async-done | bytes 131088 | tf_op jit(solution)/shard_map/reduce_scatter | solution.py:187
  259.4 1.0 reshape.43
  260.4 0.1 constant_dynamic-slice_fusion.1
  260.6 3.0 %collective-permute-start.2 = (f32[4,4096]{1,0:T(4,128)S(1)}, f32[4,4096]{1,0:T(4,128)S(1)}, u32[]{:S(2)}, u32[]{:S(2)}) collective-permute-start(f32[4,4096]{1,0:T(4,128)S(1)} %bitcast.105), channel_id=1, source_target_pairs={{0,4},{4,0},{1,5},{5,1},{2,6},{6,2},{3,7},{7,3},{8,12},{12,8},{9,1... | collective-permute-start | bytes 196616 | tf_op jit(solution)/shard_map/ppermute | solution.py:191
  263.6 2.8 %collective-permute-done.2 = f32[4,4096]{1,0:T(4,128)S(1)} collective-permute-done((f32[4,4096]{1,0:T(4,128)S(1)}, f32[4,4096]{1,0:T(4,128)S(1)}, u32[]{:S(2)}, u32[]{:S(2)}) %collective-permute-start.2) | collective-permute-done | bytes 65568 | tf_op jit(solution)/shard_map/ppermute | solution.py:191
  266.5 0.1 bitcast_add_fusion
  266.5 0.1 reshape.44
  266.6 0.7 fusion.9
  (21 shorter events, 0.2 us)
Async XLA Ops:
  7.2 60.3 %all-gather.5.cloned.1.call-start = ((), (), s32[]{:S(2)}) async-start(), calls=%async_computation.6 | async-start | bytes 2359296 | tf_op jit(solution)/shard_map/all_gather | solution.py:142
  15.7 160.8 %reduce-scatter.4.cloned.1.call-start = ((), (), s32[]{:S(2)}) async-start(), calls=%async_computation.3 | async-start | bytes 6291456 | tf_op jit(solution)/shard_map/reduce_scatter | solution.py:185
  67.5 2.2 copy-start.4
  70.4 9.3 %copy-start.7 = (s32[1,1,16,16]{3,2,1,0:T(8,128)S(1)}, s32[1,1,16,16]{3,2,1,0:T(8,128)}, u32[]{:S(2)}) copy-start(s32[1,1,16,16]{3,2,1,0:T(8,128)} %param.15) | copy-start | bytes 3076
  70.5 9.4 %copy-start = (bf16[1,2048,1,128]{3,1,2,0:T(8,128)(2,1)S(1)}, bf16[1,2048,1,128]{3,1,2,0:T(8,128)(2,1)}, u32[]{:S(2)}) copy-start(bf16[1,2048,1,128]{3,1,2,0:T(8,128)(2,1)} %param.11) | copy-start | bytes 1572868
  70.5 9.4 %copy-start.1 = (bf16[1,2048,1,128]{3,1,2,0:T(8,128)(2,1)S(1)}, bf16[1,2048,1,128]{3,1,2,0:T(8,128)(2,1)}, u32[]{:S(2)}) copy-start(bf16[1,2048,1,128]{3,1,2,0:T(8,128)(2,1)} %param.12) | copy-start | bytes 1572868
  70.5 9.4 %copy-start.2 = (bf16[1,2048,1,128]{3,1,2,0:T(8,128)(2,1)S(1)}, bf16[1,2048,1,128]{3,1,2,0:T(8,128)(2,1)}, u32[]{:S(2)}) copy-start(bf16[1,2048,1,128]{3,1,2,0:T(8,128)(2,1)} %param.13) | copy-start | bytes 1572868
  70.5 9.2 %collective-permute-start = (bf16[1024,128]{1,0:T(8,128)(2,1)S(1)}, bf16[1024,128]{1,0:T(8,128)(2,1)S(1)}, u32[]{:S(2)}, u32[]{:S(2)}) collective-permute-start(bf16[1024,128]{1,0:T(8,128)(2,1)S(1)} %convolution_convert_fusion), channel_id=1, source_target_pairs={{0,4},{4,0},{1,5},{5,1},{2,6},{6,2},{3,7},{7,3},{8,12},{12,8},{9,1... | collective-permute-start | bytes 786440 | tf_op jit(solution)/shard_map/ppermute | solution.py:153
  99.5 1.3 copy-start.6
  100.9 2.3 copy-start.3
  101.0 25.3 %collective-permute-start.1 = (bf16[4,1024,128]{2,1,0:T(8,128)(2,1)S(1)}, bf16[4,1024,128]{2,1,0:T(8,128)(2,1)}, u32[]{:S(2)}, u32[]{:S(2)}) collective-permute-start(bf16[4,1024,128]{2,1,0:T(8,128)(2,1)S(1)} %constant_dynamic-slice_fusion.2), channel_id=1, source_target_pairs={{0,4},{4,0},{1,5},{5,1},{2,6},{6,2},{3,7},{7,3},{8,12},{12,8},{9,1... | collective-permute-start | bytes 3145736 | tf_op jit(solution)/shard_map/ppermute | solution.py:165
  106.0 1.7 copy-start.5
  155.0 62.4 %reduce-scatter.6.cloned.1.call-start = ((), (), s32[]{:S(2)}) async-start(), calls=%async_computation.4 | async-start | bytes 3145728 | tf_op jit(solution)/shard_map/reduce_scatter | solution.py:186
  176.5 82.9 %reduce-scatter.8.cloned.1.call-start = ((), (), s32[]{:S(2)}) async-start(), calls=%async_computation.5 | async-start | bytes 1179648 | tf_op jit(solution)/shard_map/reduce_scatter | solution.py:187
  260.6 5.9 %collective-permute-start.2 = (f32[4,4096]{1,0:T(4,128)S(1)}, f32[4,4096]{1,0:T(4,128)S(1)}, u32[]{:S(2)}, u32[]{:S(2)}) collective-permute-start(f32[4,4096]{1,0:T(4,128)S(1)} %bitcast.105), channel_id=1, source_target_pairs={{0,4},{4,0},{1,5},{5,1},{2,6},{6,2},{3,7},{7,3},{8,12},{12,8},{9,1... | collective-permute-start | bytes 196616 | tf_op jit(solution)/shard_map/ppermute | solution.py:191
Sparse Core Ops, SparseCore 0:
  15.8 45.9 all-gather.4
  155.1 21.3 reduce-scatter.3
  179.1 38.1 reduce-scatter.5
  219.8 39.6 reduce-scatter.7

commit v5 on v4

--- a/solution.py
+++ b/solution.py
@@ -173,22 +173,26 @@
                 lax.dot_general(parts[2], inputs_half, tn, preferred_element_type=jnp.float32),
                 lax.dot_general(parts[3], masked_half, tn, preferred_element_type=jnp.float32),
             ],
-            axis=1,
+            axis=0,
         )
 
-    own_terms = terms_of(grads_own)
-    got_terms = terms_of(grads_got)
-    terms = jnp.where(half == 0, jnp.stack([own_terms, got_terms], 1), jnp.stack([got_terms, own_terms], 1))
-    chunk = terms.shape[0] // (sizes["dpy"] * sizes["dpz"] * sizes["dpc"])
-    terms = terms.reshape(sizes["dpy"], sizes["dpz"], sizes["dpc"], chunk, 2 * 4 * width)
-    terms = jnp.transpose(terms, (2, 0, 1, 3, 4)).reshape(-1, 2 * 4 * width // 128, 128)
-    owned = lax.psum_scatter(terms, "dpc", scatter_dimension=0, tiled=True)
-    owned = lax.psum_scatter(owned, "dpy", scatter_dimension=0, tiled=True)
-    owned = lax.psum_scatter(owned, "dpz", scatter_dimension=0, tiled=True)
-    owned = owned.reshape(chunk, 2, 4 * width)
-    kept = lax.dynamic_index_in_dim(owned, half, 1, keepdims=False)
-    sent = lax.dynamic_index_in_dim(owned, other, 1, keepdims=False)
-    owned = (kept + lax.ppermute(sent, "sqy", swap)).reshape(chunk, 4, width)
+    terms = jnp.stack([terms_of(grads_own), terms_of(grads_got)])
+    ny, nz, nc = sizes["dpy"], sizes["dpz"], sizes["dpc"]
+    chunk = terms.shape[2] // (ny * nz * nc)
+    terms = terms.reshape(2, 4, ny, nz, nc, chunk, width)
+    core = lax.axis_index("dpc")
+    kept = lax.dynamic_index_in_dim(terms, core, 4, keepdims=False)
+    sent = lax.dynamic_index_in_dim(terms, 1 - core, 4, keepdims=False)
+    terms = kept + lax.ppermute(sent, "dpc", swap)
+    row = lax.axis_index("dpy")
+    kept = lax.dynamic_index_in_dim(terms, row, 2, keepdims=False)
+    sent = lax.dynamic_index_in_dim(terms, 1 - row, 2, keepdims=False)
+    terms = kept + lax.ppermute(sent, "dpy", swap)
+    terms = jnp.transpose(terms.reshape(2, 4, nz, chunk * width), (2, 0, 1, 3))
+    terms = lax.psum_scatter(terms.reshape(nz, -1, 128), "dpz", scatter_dimension=0, tiled=True)
+    terms = terms.reshape(2, 4, chunk, width)
+    owned = terms[0] + lax.ppermute(terms[1], "sqy", swap)
+    owned = jnp.transpose(owned, (1, 0, 2))
     return tuple(owned[:, part][:, None, :] for part in range(4))
 
 

time: 274 us -> 235 us (0.86)
  waiting for transfers between devices: 130 us -> 83.5 us
  matrix products: 13.1 us -> 17.5 us
  other arithmetic: 4.07 us -> 7.45 us
    reduce_scatter x3 -> x1, waiting for transfers between devices: 104 us -> 42.6 us  [local(): lax.psum_scatter(terms.reshape(nz, -1, 128), 'dpz', scatter_dimension=0,...]
    ppermute x1 -> x3, waiting for transfers between devices: 2.82 us -> 32.2 us  [the longest x1 25.1 us: local(): terms = kept + lax.ppermute(sent, 'dpy', swap)]
    ppermute x1, waiting for transfers between devices: 17 us -> 2.59 us  [local(): grads_got = lax.ppermute(grads_give, 'sqy', swap)]
    select_n x2 -> x0, local copies, waits for them, and re-layouts: 11.3 us -> none  [local(): jnp.where(half == 0, jnp.stack([own_terms, got_terms], 1), jnp.stack([got...]
    dot_general x0 -> x10, local copies, waits for them, and re-layouts: none -> 8.97 us  [the longest x4 4.11 us: terms_of(): lax.dot_general(parts[0], inputs_half, tn, preferred_element_type=jnp.flo...]
    another operation x0 -> x8, local copies, waits for them, and re-layouts: none -> 7.45 us
    reshape x3 -> x1, local copies, waits for them, and re-layouts: 7.11 us -> 1.72 us  [local(): terms.reshape(nz, -1, 128)]
    transpose x1, local copies, waits for them, and re-layouts: 4.6 us -> 0.68 us  [local(): terms = jnp.transpose(terms.reshape(2, 4, nz, chunk * width), (2, 0, 1, 3))]
  transfers between devices with their start and end apart: 7 -> 7, of which waited for: 6 -> 6; matrix products, arithmetic and copies ran while one was open for 3% -> 10% of each run, Pallas kernels for 18% -> 21%
where the time goes in v5:
time: 235 us; the launch traced here: 234 us
  waiting for transfers between devices  83.5 us (36%)
  Pallas kernels  68.5 us (29%)
  local copies, waits for them, and re-layouts  26.8 us (11%)
  matrix products  17.5 us (7%)
  between operations  14.5 us (6%)
  blocking collectives  8.44 us (4%)
  starting transfers between devices  7.8 us (3%)
  other arithmetic  7.45 us (3%)
    pallas_call x1, Pallas kernels, seq_gather(): pl.pallas_call(functools.partial(gather_kernel, nseq), in_specs=[any_spec...  49.1 us
    reduce_scatter x1, waiting for transfers between devices, local(): lax.psum_scatter(terms.reshape(nz, -1, 128), 'dpz', scatter_dimension=0,...  42.6 us
    ppermute x1, waiting for transfers between devices, local(): terms = kept + lax.ppermute(sent, 'dpy', swap)  25.1 us
    pallas_call x1, Pallas kernels, attention_backward(): pl.pallas_call(attention_kernel, grid=(length // ROWS,), in_specs=[row_sp...  19.4 us
    another operation x8, local copies, waits for them, and re-layouts  7.45 us
    all_gather x1, blocking collectives, local(): gathered = lax.all_gather(gathered, 'dpy', axis=0)  6.33 us
    dot_general x2, matrix products, terms_of(): lax.dot_general(parts[0], inputs_half, tn, preferred_element_type=jnp.flo...  6.07 us
    ppermute x1, waiting for transfers between devices, local(): d_got = lax.ppermute(d_give, 'sqy', swap)  6.05 us
  transfers between devices with their start and end apart: 7, of which 6 were waited for; matrix products, arithmetic and copies ran while one was open for 10% of the time, Pallas kernels for 21%

profile of v5, /device:TPU:2, one launch (start us, length us, event | category | flops | bytes accessed | tf_op | source)
XLA Modules:
  0.0 234.4 jit_solution(10150243154262023704)
XLA Ops:
  7.2 2.1 all-gather
  9.3 6.3 %all-gather.1 = bf16[4,32,1024]{2,1,0:T(8,128)(2,1)} all-gather(bf16[2,32,1024]{2,1,0:T(8,128)(2,1)S(1)} %bitcast.116), channel_id=3, replica_groups=mesh['dpy'=2,'dpz'=8,'dpc'=2,'sqy'=2,'sqx'=4] {'dpy'}, dimensions={0}, use_global_device_ids=true | all-gather | bytes 393216 | tf_op jit(solution)/shard_map/all_gather | solution.py:141
  15.7 0.7 convert_reduce_fusion
  16.4 1.9 bitcast_multiply_fusion.a_ref
  18.4 49.1 %shard_map.111 = (bf16[4,256,1024]{2,1,0:T(8,128)(2,1)}, bf16[4,256,1024]{2,1,0:T(8,128)(2,1)}) custom-call(bf16[256,1024]{1,0:T(8,128)(2,1)} %bitcast_multiply_fusion.a_ref, bf16[256,1024]{1,0:T(8,128)(2,1)} %bitcast.117), custom_call_target="tpu_custom_call" | custom-call | tf_op jit(solution)/shard_map/pallas_call | solution.py:112
  67.5 2.0 copy.83
  69.7 0.7 convolution_convert_fusion
  70.5 2.2 collective-permute-start
  72.8 0.8 fusion
  73.6 6.0 %collective-permute-done = bf16[1024,128]{1,0:T(8,128)(2,1)S(1)} collective-permute-done((bf16[1024,128]{1,0:T(8,128)(2,1)S(1)}, bf16[1024,128]{1,0:T(8,128)(2,1)S(1)}, u32[]{:S(2)}, u32[]{:S(2)}) %collective-permute-start) | collective-permute-done | bytes 262176 | tf_op jit(solution)/shard_map/ppermute | solution.py:153
  79.9 19.4 %shard_map.112 = (bf16[2048,128]{1,0:T(8,128)(2,1)S(1)}, bf16[2048,128]{1,0:T(8,128)(2,1)S(1)}, bf16[2048,128]{1,0:T(8,128)(2,1)S(1)}, bf16[2048,128]{1,0:T(8,128)(2,1)S(1)}) custom-call(bf16[2048,128]{1,0:T(8,128)(2,1)S(1)} %bitcast.104, bf16[2048,128]{1,0:T(8,128)(2,1)S(1)} %bitcast.105, bf16[2048,128]{1,0:T(8,128)(2,1)S(1)} %bitcast.106, ...), custom_call_target="tpu_custom_call" | custom-call | flops 6442450944 | bytes 4194304 | tf_op jit(solution)/shard_map/pallas_call | solution.py:66
  99.6 2.2 collective-permute-start.1
  101.8 0.9 dynamic-slice_bitcast_fusion.5
  102.7 1.8 copy.84
  104.5 1.7 reshape.107
  106.3 1.8 copy.88
  108.1 1.7 reshape.110
  109.8 1.8 copy.86
  111.6 1.8 reshape.109
  113.4 0.8 copy.90
  114.2 1.1 reshape.111
  115.3 3.1 %convolution_bitcast_fusion.7 = f32[1,1,2,8,2,4,1024]{6,3,5,4,2,1,0:T(8,128)} fusion(bf16[1024,1024,1,1,1]{1,0,4,3,2:T(8,128)(2,1)} %bitcast.119, bf16[2,8,2,4,1024]{4,3,2,1,0:T(4,128)(2,1)} %reshape.107), kind=kOutput, calls=%fused_computation.11 | convolution fusion | flops 268435456 | bytes 2883584 | tf_op jit(solution)/shard_map/dot_general | solution.py:171
  118.4 1.3 convolution_bitcast_fusion.5
  119.8 1.3 convolution_bitcast_fusion.6
  121.1 1.3 convolution_bitcast_fusion.4
  122.4 2.6 %collective-permute-done.1 = bf16[4,1024,128]{2,1,0:T(8,128)(2,1)} collective-permute-done((bf16[4,1024,128]{2,1,0:T(8,128)(2,1)S(1)}, bf16[4,1024,128]{2,1,0:T(8,128)(2,1)}, u32[]{:S(2)}, u32[]{:S(2)}) %collective-permute-start.1) | collective-permute-done | bytes 1048608 | tf_op jit(solution)/shard_map/ppermute | solution.py:165
  125.0 1.3 slice_bitcast_fusion.3
  126.6 2.9 %convolution_bitcast_fusion.3 = f32[1,1,2,8,2,4,1024]{6,3,5,4,2,1,0:T(8,128)} fusion(bf16[1024,1024,1,1,1]{1,0,4,3,2:T(8,128)(2,1)} %bitcast.120, bf16[2,8,2,4,1024]{4,3,2,1,0:T(4,128)(2,1)S(1)} %reshape.112), kind=kOutput, calls=%fused_computation.7 | convolution fusion | flops 268435456 | bytes 2883584 | tf_op jit(solution)/shard_map/dot_general | solution.py:171
  129.6 0.8 reshape.115
  130.5 1.5 convolution_bitcast_fusion
  132.2 2.1 convolution_bitcast_fusion.1
  134.6 2.3 convolution_bitcast_fusion.2
  137.0 0.5 maximum_maximum_fusion
  137.8 1.7 copy-done.3
  139.5 4.3 %collective-permute-done.2 = f32[2,4,2,8,4,1024]{5,3,4,2,1,0:T(8,128)} collective-permute-done((f32[2,4,2,8,4,1024]{5,3,4,2,1,0:T(8,128)S(1)}, f32[2,4,2,8,4,1024]{5,3,4,2,1,0:T(8,128)}, u32[]{:S(2)}, u32[]{:S(2)}) %collective-permute-start.2) | collective-permute-done | bytes 2097184 | tf_op jit(solution)/shard_map/ppermute | solution.py:186
  143.8 2.6 %bitcast_add_fusion = f32[2,4,2,8,4,1024]{5,3,4,2,1,0:T(8,128)S(1)} fusion(f32[2,4,2,8,4,1024]{5,3,4,2,1,0:T(8,128)} %collective-permute-done.2, f32[2,4,2,8,2,4,1024]{6,3,5,4,2,1,0:T(8,128)} %copy-done.3, s32[]{:T(128)S(6)} %select_n.32), kind=kLoop, calls=%fused_computation.2 | loop fusion | flops 524288 | bytes 6291460 | tf_op jit(solution)/shard_map/add | solution.py:186
  146.8 25.1 %collective-permute-done.3 = f32[2,4,8,4,1024]{4,2,3,1,0:T(8,128)} collective-permute-done((f32[2,4,8,4,1024]{4,2,3,1,0:T(8,128)S(1)}, f32[2,4,8,4,1024]{4,2,3,1,0:T(8,128)}, u32[]{:S(2)}, u32[]{:S(2)}) %collective-permute-start.3) | collective-permute-done | bytes 1048608 | tf_op jit(solution)/shard_map/ppermute | solution.py:190
  171.9 1.4 bitcast_add_fusion.1
  173.3 0.7 copy.100
  173.9 1.7 reshape.117
  175.7 42.6 %reduce-scatter.2.cloned.1.call-done = f32[1,256,128]{2,1,0:T(8,128)} async-done(((f32[8,256,128]{2,1,0:T(8,128)}), f32[1,256,128]{2,1,0:T(8,128)}) %reduce-scatter.2.cloned.1.call-update) | async-done | bytes 131088 | tf_op jit(solution)/shard_map/reduce_scatter | solution.py:192
  218.3 0.9 fusion.13
  219.2 3.0 %collective-permute-start.4 = (f32[4,4,1024]{2,1,0:T(4,128)S(1)}, f32[4,4,1024]{2,1,0:T(4,128)S(1)}, u32[]{:S(2)}, u32[]{:S(2)}) collective-permute-start(f32[4,4,1024]{2,1,0:T(4,128)S(1)} %squeeze.81), channel_id=1, source_target_pairs={{0,4},{4,0},{1,5},{5,1},{2,6},{6,2},{3,7},{7,3},{8,12},{12,8},{9,1... | collective-permute-start | bytes 196616 | tf_op jit(solution)/shard_map/ppermute | solution.py:194
  222.3 2.8 %collective-permute-done.4 = f32[4,4,1024]{2,1,0:T(4,128)S(1)} collective-permute-done((f32[4,4,1024]{2,1,0:T(4,128)S(1)}, f32[4,4,1024]{2,1,0:T(4,128)S(1)}, u32[]{:S(2)}, u32[]{:S(2)}) %collective-permute-start.4) | collective-permute-done | bytes 65568 | tf_op jit(solution)/shard_map/ppermute | solution.py:194
  225.1 0.6 copy.104
  225.7 0.6 copy.103
  226.3 0.6 copy.102
  227.0 0.6 copy.101
  (52 shorter events, 2.5 us)
Async XLA Ops:
  7.2 60.3 %all-gather.5.cloned.1.call-start = ((), (), s32[]{:S(2)}) async-start(), calls=%async_computation.2 | async-start | bytes 2359296 | tf_op jit(solution)/shard_map/all_gather | solution.py:142
  15.7 202.6 %reduce-scatter.2.cloned.1.call-start = ((), (), s32[]{:S(2)}) async-start(), calls=%async_computation.1 | async-start | bytes 1179648 | tf_op jit(solution)/shard_map/reduce_scatter | solution.py:192
  67.5 2.2 copy-start.4
  70.4 9.3 %copy-start.12 = (s32[1,1,16,16]{3,2,1,0:T(8,128)S(1)}, s32[1,1,16,16]{3,2,1,0:T(8,128)}, u32[]{:S(2)}) copy-start(s32[1,1,16,16]{3,2,1,0:T(8,128)} %param.15) | copy-start | bytes 3076
  70.5 9.4 %copy-start = (bf16[1,2048,1,128]{3,1,2,0:T(8,128)(2,1)S(1)}, bf16[1,2048,1,128]{3,1,2,0:T(8,128)(2,1)}, u32[]{:S(2)}) copy-start(bf16[1,2048,1,128]{3,1,2,0:T(8,128)(2,1)} %param.11) | copy-start | bytes 1572868
  70.5 9.4 %copy-start.1 = (bf16[1,2048,1,128]{3,1,2,0:T(8,128)(2,1)S(1)}, bf16[1,2048,1,128]{3,1,2,0:T(8,128)(2,1)}, u32[]{:S(2)}) copy-start(bf16[1,2048,1,128]{3,1,2,0:T(8,128)(2,1)} %param.12) | copy-start | bytes 1572868
  70.5 9.4 %copy-start.2 = (bf16[1,2048,1,128]{3,1,2,0:T(8,128)(2,1)S(1)}, bf16[1,2048,1,128]{3,1,2,0:T(8,128)(2,1)}, u32[]{:S(2)}) copy-start(bf16[1,2048,1,128]{3,1,2,0:T(8,128)(2,1)} %param.13) | copy-start | bytes 1572868
  70.5 9.2 %collective-permute-start = (bf16[1024,128]{1,0:T(8,128)(2,1)S(1)}, bf16[1024,128]{1,0:T(8,128)(2,1)S(1)}, u32[]{:S(2)}, u32[]{:S(2)}) collective-permute-start(bf16[1024,128]{1,0:T(8,128)(2,1)S(1)} %convolution_convert_fusion), channel_id=1, source_target_pairs={{0,4},{4,0},{1,5},{5,1},{2,6},{6,2},{3,7},{7,3},{8,12},{12,8},{9,1... | collective-permute-start | bytes 786440 | tf_op jit(solution)/shard_map/ppermute | solution.py:153
  99.6 25.4 %collective-permute-start.1 = (bf16[4,1024,128]{2,1,0:T(8,128)(2,1)S(1)}, bf16[4,1024,128]{2,1,0:T(8,128)(2,1)}, u32[]{:S(2)}, u32[]{:S(2)}) collective-permute-start(bf16[4,1024,128]{2,1,0:T(8,128)(2,1)S(1)} %constant_dynamic-slice_fusion), channel_id=1, source_target_pairs={{0,4},{4,0},{1,5},{5,1},{2,6},{6,2},{3,7},{7,3},{8,12},{12,8},{9,1... | collective-permute-start | bytes 3145736 | tf_op jit(solution)/shard_map/ppermute | solution.py:165
  115.3 3.2 %copy-start.10 = (bf16[2,8,2,4,1024]{4,3,2,1,0:T(4,128)(2,1)S(1)}, bf16[2,8,2,4,1024]{4,3,2,1,0:T(4,128)(2,1)}, u32[]{:S(2)}) copy-start(bf16[2,8,2,4,1024]{4,3,2,1,0:T(4,128)(2,1)} %reshape.110) | copy-start | bytes 786436
  115.3 3.2 %copy-start.13 = (bf16[4,256,1024]{2,1,0:T(8,128)(2,1)S(1)}, bf16[4,256,1024]{2,1,0:T(8,128)(2,1)}, u32[]{:S(2)}) copy-start(bf16[4,256,1024]{2,1,0:T(8,128)(2,1)} %get-tuple-element.15) | copy-start | bytes 6291460
  118.4 1.3 copy-start.11
  134.6 2.3 copy-start.5
  134.6 2.3 copy-start.6
  134.6 2.3 copy-start.7
  134.6 2.3 copy-start.8
  134.6 2.3 copy-start.9
  137.5 1.9 copy-start.3
  139.5 4.3 %collective-permute-start.2 = (f32[2,4,2,8,4,1024]{5,3,4,2,1,0:T(8,128)S(1)}, f32[2,4,2,8,4,1024]{5,3,4,2,1,0:T(8,128)}, u32[]{:S(2)}, u32[]{:S(2)}) collective-permute-start(f32[2,4,2,8,4,1024]{5,3,4,2,1,0:T(8,128)S(1)} %dynamic-slice_bitcast_fusion), channel_id=1, source_target_pairs={{0,8},{8,0},{1,9},{9,1},{2,10},{10,2},{3,11},{11,3},{4,12},{12,4},... | collective-permute-start | bytes 6291464 | tf_op jit(solution)/shard_map/ppermute | solution.py:186
  146.5 25.4 %collective-permute-start.3 = (f32[2,4,8,4,1024]{4,2,3,1,0:T(8,128)S(1)}, f32[2,4,8,4,1024]{4,2,3,1,0:T(8,128)}, u32[]{:S(2)}, u32[]{:S(2)}) collective-permute-start(f32[2,4,8,4,1024]{4,2,3,1,0:T(8,128)S(1)} %dynamic-slice_bitcast_fusion.1), channel_id=1, source_target_pairs={{0,128},{128,0},{1,129},{129,1},{2,130},{130,2},{3,131},{131,3},{4... | collective-permute-start | bytes 3145736 | tf_op jit(solution)/shard_map/ppermute | solution.py:190
  219.2 5.9 %collective-permute-start.4 = (f32[4,4,1024]{2,1,0:T(4,128)S(1)}, f32[4,4,1024]{2,1,0:T(4,128)S(1)}, u32[]{:S(2)}, u32[]{:S(2)}) collective-permute-start(f32[4,4,1024]{2,1,0:T(4,128)S(1)} %squeeze.81), channel_id=1, source_target_pairs={{0,4},{4,0},{1,5},{5,1},{2,6},{6,2},{3,7},{7,3},{8,12},{12,8},{9,1... | collective-permute-start | bytes 196616 | tf_op jit(solution)/shard_map/ppermute | solution.py:194
Sparse Core Ops, SparseCore 0:
  15.8 45.9 all-gather.4
  175.8 42.4 reduce-scatter.1

commit v6 on v5

--- a/solution.py
+++ b/solution.py
@@ -14,14 +14,21 @@
 masked_score = -1e30
 
 
-def attention_kernel(q_ref, k_ref, v_ref, g_ref, m_ref, dq_ref, att_ref, dk_ref, dv_ref, dk_acc, dv_acc):
+def attention_kernel(
+    nseq, q_ref, k_ref, v_ref, g_ref, m_ref, x_ref, dq_ref, att_ref, dk_ref, dv_ref, x_out,
+    dk_acc, dv_acc, send_sem, recv_sem, copy_sem,
+):
     step = pl.program_id(0)
     steps = pl.num_programs(0)
     scale = HD ** (-0.5)
     groups = ROWS // BLOCK
+    copies = start_gather(nseq, x_ref, x_out, send_sem, recv_sem, copy_sem)
 
     @pl.when(step == 0)
     def _():
+        enter_barrier(nseq)
+        for copy in copies:
+            copy.start()
         dk_acc[...] = jnp.zeros_like(dk_acc)
         dv_acc[...] = jnp.zeros_like(dv_acc)
 
@@ -54,73 +61,90 @@
     def _():
         dk_ref[...] = (dk_acc[...] * scale).astype(jnp.bfloat16)
         dv_ref[...] = dv_acc[...].astype(jnp.bfloat16)
-
-
-def attention_backward(q, k, v, g, live_cols):
+        for copy in copies:
+            copy.wait()
+
+
+def attention_backward(q, k, v, g, live_cols, x, nseq):
     length = q.shape[0]
     row_spec = pl.BlockSpec((ROWS, HD), lambda i: (i, 0))
     full_spec = pl.BlockSpec((length, HD), lambda i: (0, 0))
     mask_spec = pl.BlockSpec((ROWS // BLOCK, 1, length), lambda i: (i, 0, 0))
     out = jax.ShapeDtypeStruct((length, HD), jnp.bfloat16)
     flops = 12 * length * length * HD
+    any_spec = pl.BlockSpec(memory_space=pl.ANY)
     return pl.pallas_call(
-        attention_kernel,
+        functools.partial(attention_kernel, nseq),
         grid=(length // ROWS,),
-        in_specs=[row_spec, full_spec, full_spec, row_spec, mask_spec],
-        out_specs=[row_spec, row_spec, full_spec, full_spec],
-        out_shape=[out, out, out, out],
-        scratch_shapes=[pltpu.VMEM((length, HD), jnp.float32), pltpu.VMEM((length, HD), jnp.float32)],
-        compiler_params=pltpu.CompilerParams(vmem_limit_bytes=48 * 1024 * 1024),
+        in_specs=[row_spec, full_spec, full_spec, row_spec, mask_spec, any_spec],
+        out_specs=[row_spec, row_spec, full_spec, full_spec, any_spec],
+        out_shape=[out, out, out, out, jax.ShapeDtypeStruct((nseq,) + x.shape, x.dtype)],
+        scratch_shapes=[
+            pltpu.VMEM((length, HD), jnp.float32),
+            pltpu.VMEM((length, HD), jnp.float32),
+            pltpu.SemaphoreType.DMA((nseq - 1,)),
+            pltpu.SemaphoreType.DMA((nseq - 1,)),
+            pltpu.SemaphoreType.DMA(()),
+        ],
+        compiler_params=pltpu.CompilerParams(
+            vmem_limit_bytes=48 * 1024 * 1024, collective_id=1, has_side_effects=True
+        ),
         cost_estimate=pl.CostEstimate(
             flops=flops, transcendentals=length * length, bytes_accessed=8 * length * HD * 2
         ),
-    )(q, k, v, g, live_cols)
-
-
-def gather_kernel(nseq, a_ref, b_ref, a_out, b_out, send_sem, recv_sem, copy_sem):
+    )(q, k, v, g, live_cols, x)
+
+
+def start_gather(nseq, src, dst, send_sem, recv_sem, copy_sem):
     me = lax.axis_index("sqx")
-    mesh_id = pl.DeviceIdType.MESH
+    copies = [pltpu.make_async_copy(src, dst.at[me], copy_sem)]
+    for off in range(1, nseq):
+        peer = (me + off) % nseq
+        copies.append(
+            pltpu.make_async_remote_copy(
+                src_ref=src,
+                dst_ref=dst.at[me],
+                send_sem=send_sem.at[off - 1],
+                recv_sem=recv_sem.at[off - 1],
+                device_id={"sqx": peer},
+                device_id_type=pl.DeviceIdType.MESH,
+            )
+        )
+    return copies
+
+
+def enter_barrier(nseq):
+    me = lax.axis_index("sqx")
     barrier = pltpu.get_barrier_semaphore()
     for off in range(1, nseq):
         peer = (me + off) % nseq
-        pl.semaphore_signal(barrier, 1, device_id={"sqx": peer}, device_id_type=mesh_id)
+        pl.semaphore_signal(barrier, 1, device_id={"sqx": peer}, device_id_type=pl.DeviceIdType.MESH)
     pl.semaphore_wait(barrier, nseq - 1)
-    copies = []
-    for t, (src, dst) in enumerate(((a_ref, a_out), (b_ref, b_out))):
-        local = pltpu.make_async_copy(src, dst.at[me], copy_sem.at[t])
-        local.start()
-        copies.append(local)
-        for off in range(1, nseq):
-            peer = (me + off) % nseq
-            remote = pltpu.make_async_remote_copy(
-                src_ref=src,
-                dst_ref=dst.at[me],
-                send_sem=send_sem.at[t, off - 1],
-                recv_sem=recv_sem.at[t, off - 1],
-                device_id={"sqx": peer},
-                device_id_type=mesh_id,
-            )
-            remote.start()
-            copies.append(remote)
+
+
+def gather_kernel(nseq, a_ref, a_out, send_sem, recv_sem, copy_sem):
+    enter_barrier(nseq)
+    copies = start_gather(nseq, a_ref, a_out, send_sem, recv_sem, copy_sem)
+    for copy in copies:
+        copy.start()
     for copy in copies:
         copy.wait()
 
 
-def seq_gather(a, b, nseq):
+def seq_gather(a, nseq):
     any_spec = pl.BlockSpec(memory_space=pl.ANY)
-    out = jax.ShapeDtypeStruct((nseq,) + a.shape, a.dtype)
     return pl.pallas_call(
         functools.partial(gather_kernel, nseq),
-        in_specs=[any_spec, any_spec],
-        out_specs=[any_spec, any_spec],
-        out_shape=[out, out],
+        in_specs=[any_spec],
+        out_specs=any_spec,
+        out_shape=jax.ShapeDtypeStruct((nseq,) + a.shape, a.dtype),
         scratch_shapes=[
-            pltpu.SemaphoreType.DMA((2, nseq - 1)),
-            pltpu.SemaphoreType.DMA((2, nseq - 1)),
-            pltpu.SemaphoreType.DMA((2,)),
+            pltpu.SemaphoreType.DMA((nseq - 1,)),
+            pltpu.SemaphoreType.DMA((nseq - 1,)),
+            pltpu.SemaphoreType.DMA(()),
         ],
         compiler_params=pltpu.CompilerParams(collective_id=0, has_side_effects=True),
-    )(a, b)
+    )(a)
 
 
 DP = ("dpy", "dpz", "dpc")
@@ -143,9 +167,7 @@
     gathered = jnp.transpose(gathered, (1, 0, 2, 3, 4)).reshape(-1, width)
     head_weight = lax.dynamic_slice_in_dim(gathered, head * HD, HD, 0)
     partner_weight = lax.dynamic_slice_in_dim(gathered, partner_head * HD, HD, 0)
-    masked_half, inputs_half = seq_gather(masked, inputs[0], sizes["sqx"])
-    masked_half = masked_half.reshape(-1, width)
-    inputs_half = inputs_half.reshape(-1, width)
+    masked_half = seq_gather(masked, sizes["sqx"]).reshape(-1, width)
     half_len = masked_half.shape[0]
     nt = (((1,), (1,)), ((), ()))
     d_own = lax.dot_general(masked_half, head_weight, nt, preferred_element_type=jnp.float32).astype(jnp.bfloat16)
@@ -156,9 +178,10 @@
     d_attn = lax.dynamic_update_slice_in_dim(d_attn, d_got, other * half_len, 0)
     blocks = block_mask[0, 0]
     live_cols = jnp.repeat(blocks, BLOCK, axis=1)[:, None, :]
-    d_query, attended, d_key, d_value = attention_backward(
-        queries[0, :, 0], keys[0, :, 0], values[0, :, 0], d_attn, live_cols
+    d_query, attended, d_key, d_value, inputs_half = attention_backward(
+        queries[0, :, 0], keys[0, :, 0], values[0, :, 0], d_attn, live_cols, inputs[0], sizes["sqx"]
     )
+    inputs_half = inputs_half.reshape(-1, width)
     grads = jnp.stack([d_query, d_key, d_value, attended])
     grads_own = lax.dynamic_slice_in_dim(grads, half * half_len, half_len, 1)
     grads_give = lax.dynamic_slice_in_dim(grads, other * half_len, half_len, 1)

time: 235 us -> 224 us (0.953)
  Pallas kernels: 68.5 us -> 48.4 us
  waiting for transfers between devices: 83.5 us -> 89.6 us
  starting transfers between devices: 7.8 us -> 11 us
    pallas_call x1, Pallas kernels: 49.1 us -> 26.5 us  [seq_gather(): pl.pallas_call(functools.partial(gather_kernel, nseq), in_specs=[any_spec...]
    all_gather x1, waiting for transfers between devices: 0.02 us -> 15.1 us  [local(): gathered = lax.all_gather(gathered, 'dpz', axis=0)]
    reduce_scatter x1, waiting for transfers between devices: 42.6 us -> 38.4 us  [local(): lax.psum_scatter(terms.reshape(nz, -1, 128), 'dpz', scatter_dimension=0,...]
    pallas_call x1, Pallas kernels: 19.4 us -> 21.9 us  [attention_backward(): pl.pallas_call(functools.partial(attention_kernel, nseq), grid=(length //...]
  transfers between devices with their start and end apart: 7 -> 7, of which waited for: 6 -> 7; matrix products, arithmetic and copies ran while one was open for 10% -> 11% of each run, Pallas kernels for 21% -> 12%
where the time goes in v6:
time: 224 us
  waiting for transfers between devices  89.6 us (40%)
  Pallas kernels  48.4 us (22%)
  local copies, waits for them, and re-layouts  26.8 us (12%)
  matrix products  17.5 us (8%)
  between operations  14.5 us (6%)
  starting transfers between devices  11 us (5%)
  blocking collectives  8.44 us (4%)
  other arithmetic  7.45 us (3%)
    reduce_scatter x1, waiting for transfers between devices, local(): lax.psum_scatter(terms.reshape(nz, -1, 128), 'dpz', scatter_dimension=0,...  38.4 us
    pallas_call x1, Pallas kernels, seq_gather(): pl.pallas_call(functools.partial(gather_kernel, nseq), in_specs=[any_spec...  26.5 us
    ppermute x1, waiting for transfers between devices, local(): terms = kept + lax.ppermute(sent, 'dpy', swap)  23.8 us
    pallas_call x1, Pallas kernels, attention_backward(): pl.pallas_call(functools.partial(attention_kernel, nseq), grid=(length //...  21.9 us
    all_gather x1, waiting for transfers between devices, local(): gathered = lax.all_gather(gathered, 'dpz', axis=0)  15.1 us
    another operation x8, local copies, waits for them, and re-layouts  7.45 us
    all_gather x1, blocking collectives, local(): gathered = lax.all_gather(gathered, 'dpy', axis=0)  6.33 us
    dot_general x2, matrix products, terms_of(): lax.dot_general(parts[0], inputs_half, tn, preferred_element_type=jnp.flo...  6.07 us
  transfers between devices with their start and end apart: 7, of which 7 were waited for; matrix products, arithmetic and copies ran while one was open for 11% of the time, Pallas kernels for 12%

profile of v6, /device:TPU:2, one launch (start us, length us, event | category | flops | bytes accessed | tf_op | source)
XLA Modules:
  0.0 223.7 jit_solution(15113012638909869863)
XLA Ops:
  7.2 2.1 all-gather
  9.3 6.3 %all-gather.1 = bf16[4,32,1024]{2,1,0:T(8,128)(2,1)} all-gather(bf16[2,32,1024]{2,1,0:T(8,128)(2,1)S(1)} %bitcast.117), channel_id=3, replica_groups=mesh['dpy'=2,'dpz'=8,'dpc'=2,'sqy'=2,'sqx'=4] {'dpy'}, dimensions={0}, use_global_device_ids=true | all-gather | bytes 393216 | tf_op jit(solution)/shard_map/all_gather | solution.py:165
  15.7 0.7 convert_reduce_fusion
  16.4 1.9 bitcast_multiply_fusion.a_ref
  18.4 26.5 %shard_map.111 = bf16[4,256,1024]{2,1,0:T(8,128)(2,1)} custom-call(bf16[256,1024]{1,0:T(8,128)(2,1)} %bitcast_multiply_fusion.a_ref), custom_call_target="tpu_custom_call" | custom-call | tf_op jit(solution)/shard_map/pallas_call | solution.py:136
  44.9 15.1 %all-gather.5.cloned.1.call-done = bf16[16,2,32,1024]{3,2,1,0:T(8,128)(2,1)} async-done(((bf16[2,2,32,1024]{3,2,1,0:T(8,128)(2,1)}), bf16[16,2,32,1024]{3,2,1,0:T(8,128)(2,1)}) %all-gather.5.cloned.1.call-update) | async-done | bytes 2097168 | tf_op jit(solution)/shard_map/all_gather | solution.py:166
  60.1 2.0 copy.83
  62.3 0.7 convolution_convert_fusion
  63.1 3.1 %collective-permute-start = (bf16[1024,128]{1,0:T(8,128)(2,1)S(1)}, bf16[1024,128]{1,0:T(8,128)(2,1)S(1)}, u32[]{:S(2)}, u32[]{:S(2)}) collective-permute-start(bf16[1024,128]{1,0:T(8,128)(2,1)S(1)} %convolution_convert_fusion), channel_id=1, source_target_pairs={{0,4},{4,0},{1,5},{5,1},{2,6},{6,2},{3,7},{7,3},{8,12},{12,8},{9,1... | collective-permute-start | bytes 786440 | tf_op jit(solution)/shard_map/ppermute | solution.py:175
  66.3 0.8 fusion
  67.1 4.0 %collective-permute-done = bf16[1024,128]{1,0:T(8,128)(2,1)S(1)} collective-permute-done((bf16[1024,128]{1,0:T(8,128)(2,1)S(1)}, bf16[1024,128]{1,0:T(8,128)(2,1)S(1)}, u32[]{:S(2)}, u32[]{:S(2)}) %collective-permute-start) | collective-permute-done | bytes 262176 | tf_op jit(solution)/shard_map/ppermute | solution.py:175
  71.2 21.9 %shard_map.112 = (bf16[2048,128]{1,0:T(8,128)(2,1)S(1)}, bf16[2048,128]{1,0:T(8,128)(2,1)S(1)}, bf16[2048,128]{1,0:T(8,128)(2,1)S(1)}, bf16[2048,128]{1,0:T(8,128)(2,1)S(1)}, bf16[4,256,1024]{2,1,0:T(8,128)(2,1)}) custom-call(bf16[2048,128]{1,0:T(8,128)(2,1)S(1)} %bitcast.104, bf16[2048,128]{1,0:T(8,128)(2,1)S(1)} %bitcast.105, ...), custom_call_target="tpu_custom_call" | custom-call | flops 6442450944 | bytes 4194304 | tf_op jit(solution)/shard_map/pallas_call | solution.py:76
  93.5 3.2 %collective-permute-start.1 = (bf16[4,1024,128]{2,1,0:T(8,128)(2,1)S(1)}, bf16[4,1024,128]{2,1,0:T(8,128)(2,1)}, u32[]{:S(2)}, u32[]{:S(2)}) collective-permute-start(bf16[4,1024,128]{2,1,0:T(8,128)(2,1)S(1)} %constant_dynamic-slice_fusion), channel_id=1, source_target_pairs={{0,4},{4,0},{1,5},{5,1},{2,6},{6,2},{3,7},{7,3},{8,12},{12,8},{9,1... | collective-permute-start | bytes 3145736 | tf_op jit(solution)/shard_map/ppermute | solution.py:188
  96.7 0.9 dynamic-slice_bitcast_fusion.5
  97.6 1.8 copy.84
  99.4 1.7 reshape.107
  101.2 1.8 copy.88
  103.0 1.7 reshape.110
  104.7 1.8 copy.86
  106.5 1.8 reshape.109
  108.3 0.8 copy.90
  109.1 1.1 reshape.111
  110.2 3.1 %convolution_bitcast_fusion.7 = f32[1,1,2,8,2,4,1024]{6,3,5,4,2,1,0:T(8,128)} fusion(bf16[1024,1024,1,1,1]{1,0,4,3,2:T(8,128)(2,1)} %bitcast.119, bf16[2,8,2,4,1024]{4,3,2,1,0:T(4,128)(2,1)} %reshape.107), kind=kOutput, calls=%fused_computation.11 | convolution fusion | flops 268435456 | bytes 2883584 | tf_op jit(solution)/shard_map/dot_general | solution.py:194
  113.3 1.3 convolution_bitcast_fusion.5
  114.7 1.3 convolution_bitcast_fusion.6
  116.0 1.3 convolution_bitcast_fusion.4
  117.3 1.1 collective-permute-done.1
  118.5 1.3 slice_bitcast_fusion.3
  120.0 2.9 %convolution_bitcast_fusion.3 = f32[1,1,2,8,2,4,1024]{6,3,5,4,2,1,0:T(8,128)} fusion(bf16[1024,1024,1,1,1]{1,0,4,3,2:T(8,128)(2,1)} %bitcast.120, bf16[2,8,2,4,1024]{4,3,2,1,0:T(4,128)(2,1)S(1)} %reshape.112), kind=kOutput, calls=%fused_computation.7 | convolution fusion | flops 268435456 | bytes 2883584 | tf_op jit(solution)/shard_map/dot_general | solution.py:194
  123.1 0.8 reshape.115
  123.9 1.5 convolution_bitcast_fusion
  125.6 2.1 convolution_bitcast_fusion.1
  128.1 2.3 %convolution_bitcast_fusion.2 = f32[1,1,2,8,2,4,1024]{6,3,5,4,2,1,0:T(8,128)S(1)} fusion(bf16[1024,1024,1,1,1]{1,0,4,3,2:T(8,128)(2,1)} %bitcast.122, bf16[2,8,2,4,1024]{4,3,2,1,0:T(4,128)(2,1)S(1)} %reshape.113), kind=kOutput, calls=%fused_computation.6 | convolution fusion | flops 268435456 | bytes 2883584 | tf_op jit(solution)/shard_map/dot_general | solution.py:195
  131.2 1.7 copy-done.4
  132.9 4.3 %collective-permute-done.2 = f32[2,4,2,8,4,1024]{5,3,4,2,1,0:T(8,128)} collective-permute-done((f32[2,4,2,8,4,1024]{5,3,4,2,1,0:T(8,128)S(1)}, f32[2,4,2,8,4,1024]{5,3,4,2,1,0:T(8,128)}, u32[]{:S(2)}, u32[]{:S(2)}) %collective-permute-start.2) | collective-permute-done | bytes 2097184 | tf_op jit(solution)/shard_map/ppermute | solution.py:209
  137.2 2.6 %bitcast_add_fusion = f32[2,4,2,8,4,1024]{5,3,4,2,1,0:T(8,128)S(1)} fusion(f32[2,4,2,8,4,1024]{5,3,4,2,1,0:T(8,128)} %collective-permute-done.2, f32[2,4,2,8,2,4,1024]{6,3,5,4,2,1,0:T(8,128)} %copy-done.4, s32[]{:T(128)S(6)} %select_n.32), kind=kLoop, calls=%fused_computation.2 | loop fusion | flops 524288 | bytes 6291460 | tf_op jit(solution)/shard_map/add | solution.py:209
  139.9 1.6 collective-permute-start.3
  141.5 23.8 %collective-permute-done.3 = f32[2,4,8,4,1024]{4,2,3,1,0:T(8,128)} collective-permute-done((f32[2,4,8,4,1024]{4,2,3,1,0:T(8,128)S(1)}, f32[2,4,8,4,1024]{4,2,3,1,0:T(8,128)}, u32[]{:S(2)}, u32[]{:S(2)}) %collective-permute-start.3) | collective-permute-done | bytes 1048608 | tf_op jit(solution)/shard_map/ppermute | solution.py:213
  165.3 1.4 bitcast_add_fusion.1
  166.7 0.7 copy.100
  167.4 1.7 reshape.117
  169.1 38.4 %reduce-scatter.2.cloned.1.call-done = f32[1,256,128]{2,1,0:T(8,128)} async-done(((f32[8,256,128]{2,1,0:T(8,128)}), f32[1,256,128]{2,1,0:T(8,128)}) %reduce-scatter.2.cloned.1.call-update) | async-done | bytes 131088 | tf_op jit(solution)/shard_map/reduce_scatter | solution.py:215
  207.5 0.9 fusion.13
  208.5 3.0 %collective-permute-start.4 = (f32[4,4,1024]{2,1,0:T(4,128)S(1)}, f32[4,4,1024]{2,1,0:T(4,128)S(1)}, u32[]{:S(2)}, u32[]{:S(2)}) collective-permute-start(f32[4,4,1024]{2,1,0:T(4,128)S(1)} %squeeze.81), channel_id=1, source_target_pairs={{0,4},{4,0},{1,5},{5,1},{2,6},{6,2},{3,7},{7,3},{8,12},{12,8},{9,1... | collective-permute-start | bytes 196616 | tf_op jit(solution)/shard_map/ppermute | solution.py:217
  211.5 2.8 %collective-permute-done.4 = f32[4,4,1024]{2,1,0:T(4,128)S(1)} collective-permute-done((f32[4,4,1024]{2,1,0:T(4,128)S(1)}, f32[4,4,1024]{2,1,0:T(4,128)S(1)}, u32[]{:S(2)}, u32[]{:S(2)}) %collective-permute-start.4) | collective-permute-done | bytes 65568 | tf_op jit(solution)/shard_map/ppermute | solution.py:217
  214.4 0.6 copy.104
  215.0 0.6 copy.103
  215.6 0.6 copy.102
  (54 shorter events, 3.4 us)
Async XLA Ops:
  7.2 52.9 %all-gather.5.cloned.1.call-start = ((), (), s32[]{:S(2)}) async-start(), calls=%async_computation.2 | async-start | bytes 2359296 | tf_op jit(solution)/shard_map/all_gather | solution.py:166
  15.7 191.9 %reduce-scatter.2.cloned.1.call-start = ((), (), s32[]{:S(2)}) async-start(), calls=%async_computation.1 | async-start | bytes 1179648 | tf_op jit(solution)/shard_map/reduce_scatter | solution.py:215
  60.1 2.2 copy-start.5
  63.0 8.1 %copy-start.13 = (s32[1,1,16,16]{3,2,1,0:T(8,128)S(1)}, s32[1,1,16,16]{3,2,1,0:T(8,128)}, u32[]{:S(2)}) copy-start(s32[1,1,16,16]{3,2,1,0:T(8,128)} %param.15) | copy-start | bytes 3076
  63.0 8.2 %copy-start = (bf16[1,2048,1,128]{3,1,2,0:T(8,128)(2,1)S(1)}, bf16[1,2048,1,128]{3,1,2,0:T(8,128)(2,1)}, u32[]{:S(2)}) copy-start(bf16[1,2048,1,128]{3,1,2,0:T(8,128)(2,1)} %param.11) | copy-start | bytes 1572868
  63.1 8.2 %copy-start.1 = (bf16[1,2048,1,128]{3,1,2,0:T(8,128)(2,1)S(1)}, bf16[1,2048,1,128]{3,1,2,0:T(8,128)(2,1)}, u32[]{:S(2)}) copy-start(bf16[1,2048,1,128]{3,1,2,0:T(8,128)(2,1)} %param.12) | copy-start | bytes 1572868
  63.1 8.2 %copy-start.2 = (bf16[1,2048,1,128]{3,1,2,0:T(8,128)(2,1)S(1)}, bf16[1,2048,1,128]{3,1,2,0:T(8,128)(2,1)}, u32[]{:S(2)}) copy-start(bf16[1,2048,1,128]{3,1,2,0:T(8,128)(2,1)} %param.13) | copy-start | bytes 1572868
  63.1 8.2 %copy-start.3 = (bf16[1,256,1024]{2,1,0:T(8,128)(2,1)S(1)}, bf16[1,256,1024]{2,1,0:T(8,128)(2,1)}, u32[]{:S(2)}) copy-start(bf16[1,256,1024]{2,1,0:T(8,128)(2,1)} %param.8) | copy-start | bytes 1572868
  63.1 8.0 %collective-permute-start = (bf16[1024,128]{1,0:T(8,128)(2,1)S(1)}, bf16[1024,128]{1,0:T(8,128)(2,1)S(1)}, u32[]{:S(2)}, u32[]{:S(2)}) collective-permute-start(bf16[1024,128]{1,0:T(8,128)(2,1)S(1)} %convolution_convert_fusion), channel_id=1, source_target_pairs={{0,4},{4,0},{1,5},{5,1},{2,6},{6,2},{3,7},{7,3},{8,12},{12,8},{9,1... | collective-permute-start | bytes 786440 | tf_op jit(solution)/shard_map/ppermute | solution.py:175
  93.5 25.0 %collective-permute-start.1 = (bf16[4,1024,128]{2,1,0:T(8,128)(2,1)S(1)}, bf16[4,1024,128]{2,1,0:T(8,128)(2,1)}, u32[]{:S(2)}, u32[]{:S(2)}) collective-permute-start(bf16[4,1024,128]{2,1,0:T(8,128)(2,1)S(1)} %constant_dynamic-slice_fusion), channel_id=1, source_target_pairs={{0,4},{4,0},{1,5},{5,1},{2,6},{6,2},{3,7},{7,3},{8,12},{12,8},{9,1... | collective-permute-start | bytes 3145736 | tf_op jit(solution)/shard_map/ppermute | solution.py:188
  110.2 3.2 %copy-start.11 = (bf16[2,8,2,4,1024]{4,3,2,1,0:T(4,128)(2,1)S(1)}, bf16[2,8,2,4,1024]{4,3,2,1,0:T(4,128)(2,1)}, u32[]{:S(2)}) copy-start(bf16[2,8,2,4,1024]{4,3,2,1,0:T(4,128)(2,1)} %reshape.110) | copy-start | bytes 786436
  110.2 3.2 %copy-start.14 = (bf16[4,256,1024]{2,1,0:T(8,128)(2,1)S(1)}, bf16[4,256,1024]{2,1,0:T(8,128)(2,1)}, u32[]{:S(2)}) copy-start(bf16[4,256,1024]{2,1,0:T(8,128)(2,1)} %get-tuple-element.13) | copy-start | bytes 6291460
  113.3 1.3 copy-start.12
  128.0 2.3 %copy-start.6 = (f32[1,1,2,8,2,4,1024]{6,3,5,4,2,1,0:T(8,128)S(1)}, f32[1,1,2,8,2,4,1024]{6,3,5,4,2,1,0:T(8,128)}, u32[]{:S(2)}) copy-start(f32[1,1,2,8,2,4,1024]{6,3,5,4,2,1,0:T(8,128)} %convolution_bitcast_fusion.7) | copy-start | bytes 1572868
  128.0 2.3 %copy-start.7 = (f32[1,1,2,8,2,4,1024]{6,3,5,4,2,1,0:T(8,128)S(1)}, f32[1,1,2,8,2,4,1024]{6,3,5,4,2,1,0:T(8,128)}, u32[]{:S(2)}) copy-start(f32[1,1,2,8,2,4,1024]{6,3,5,4,2,1,0:T(8,128)} %convolution_bitcast_fusion.5) | copy-start | bytes 1572868
  128.0 2.3 %copy-start.8 = (f32[1,1,2,8,2,4,1024]{6,3,5,4,2,1,0:T(8,128)S(1)}, f32[1,1,2,8,2,4,1024]{6,3,5,4,2,1,0:T(8,128)}, u32[]{:S(2)}) copy-start(f32[1,1,2,8,2,4,1024]{6,3,5,4,2,1,0:T(8,128)} %convolution_bitcast_fusion.6) | copy-start | bytes 1572868
  128.0 2.3 %copy-start.9 = (f32[1,1,2,8,2,4,1024]{6,3,5,4,2,1,0:T(8,128)S(1)}, f32[1,1,2,8,2,4,1024]{6,3,5,4,2,1,0:T(8,128)}, u32[]{:S(2)}) copy-start(f32[1,1,2,8,2,4,1024]{6,3,5,4,2,1,0:T(8,128)} %convolution_bitcast_fusion.4) | copy-start | bytes 1572868
  128.1 2.3 %copy-start.10 = (f32[1,1,2,8,2,4,1024]{6,3,5,4,2,1,0:T(8,128)S(1)}, f32[1,1,2,8,2,4,1024]{6,3,5,4,2,1,0:T(8,128)}, u32[]{:S(2)}) copy-start(f32[1,1,2,8,2,4,1024]{6,3,5,4,2,1,0:T(8,128)} %convolution_bitcast_fusion.3) | copy-start | bytes 1572868
  131.0 1.9 copy-start.4
  132.9 4.3 %collective-permute-start.2 = (f32[2,4,2,8,4,1024]{5,3,4,2,1,0:T(8,128)S(1)}, f32[2,4,2,8,4,1024]{5,3,4,2,1,0:T(8,128)}, u32[]{:S(2)}, u32[]{:S(2)}) collective-permute-start(f32[2,4,2,8,4,1024]{5,3,4,2,1,0:T(8,128)S(1)} %dynamic-slice_bitcast_fusion), channel_id=1, source_target_pairs={{0,8},{8,0},{1,9},{9,1},{2,10},{10,2},{3,11},{11,3},{4,12},{12,4},... | collective-permute-start | bytes 6291464 | tf_op jit(solution)/shard_map/ppermute | solution.py:209
  139.9 25.4 %collective-permute-start.3 = (f32[2,4,8,4,1024]{4,2,3,1,0:T(8,128)S(1)}, f32[2,4,8,4,1024]{4,2,3,1,0:T(8,128)}, u32[]{:S(2)}, u32[]{:S(2)}) collective-permute-start(f32[2,4,8,4,1024]{4,2,3,1,0:T(8,128)S(1)} %dynamic-slice_bitcast_fusion.1), channel_id=1, source_target_pairs={{0,128},{128,0},{1,129},{129,1},{2,130},{130,2},{3,131},{131,3},{4... | collective-permute-start | bytes 3145736 | tf_op jit(solution)/shard_map/ppermute | solution.py:213
  208.5 5.9 %collective-permute-start.4 = (f32[4,4,1024]{2,1,0:T(4,128)S(1)}, f32[4,4,1024]{2,1,0:T(4,128)S(1)}, u32[]{:S(2)}, u32[]{:S(2)}) collective-permute-start(f32[4,4,1024]{2,1,0:T(4,128)S(1)} %squeeze.81), channel_id=1, source_target_pairs={{0,4},{4,0},{1,5},{5,1},{2,6},{6,2},{3,7},{7,3},{8,12},{12,8},{9,1... | collective-permute-start | bytes 196616 | tf_op jit(solution)/shard_map/ppermute | solution.py:217
Sparse Core Ops, SparseCore 0:
  15.8 44.2 all-gather.4
  169.2 38.2 reduce-scatter.1

commit v7 on v6

--- a/solution.py
+++ b/solution.py
@@ -113,38 +113,90 @@
     return copies
 
 
-def enter_barrier(nseq):
+def enter_barrier(nseq, nz=1):
     me = lax.axis_index("sqx")
+    zme = lax.axis_index("dpz")
     barrier = pltpu.get_barrier_semaphore()
     for off in range(1, nseq):
         peer = (me + off) % nseq
         pl.semaphore_signal(barrier, 1, device_id={"sqx": peer}, device_id_type=pl.DeviceIdType.MESH)
-    pl.semaphore_wait(barrier, nseq - 1)
-
-
-def gather_kernel(nseq, a_ref, a_out, send_sem, recv_sem, copy_sem):
-    enter_barrier(nseq)
+    for off in range(1, nz):
+        peer = (zme + off) % nz
+        pl.semaphore_signal(barrier, 1, device_id={"dpz": peer}, device_id_type=pl.DeviceIdType.MESH)
+    pl.semaphore_wait(barrier, nseq - 1 + nz - 1)
+
+
+def gather_kernel(nseq, nz, a_ref, w_ref, a_out, w_out, send_sem, recv_sem, copy_sem, w_send, w_recv, w_copy):
+    enter_barrier(nseq, nz)
     copies = start_gather(nseq, a_ref, a_out, send_sem, recv_sem, copy_sem)
     for copy in copies:
         copy.start()
+    zme = lax.axis_index("dpz")
+    col = lax.axis_index("sqx")
+    slot = zme % 2
+    w_local = pltpu.make_async_copy(w_ref, w_out.at[slot], w_copy)
+    w_sends = [
+        pltpu.make_async_remote_copy(
+            src_ref=w_ref,
+            dst_ref=w_out.at[slot],
+            send_sem=w_send.at[off - 1],
+            recv_sem=w_recv.at[slot],
+            device_id={"dpz": (zme + off) % nz},
+            device_id_type=pl.DeviceIdType.MESH,
+        )
+        for off in range(1, nz)
+    ]
+
+    @pl.when(zme // 2 == col)
+    def _():
+        w_local.start()
+        for copy in w_sends:
+            copy.start()
+
     for copy in copies:
         copy.wait()
 
-
-def seq_gather(a, nseq):
+    @pl.when(zme // 2 == col)
+    def _():
+        w_local.wait()
+        for copy in w_sends:
+            copy.wait_send()
+
+    for part in range(2):
+        incoming = pltpu.make_async_remote_copy(
+            src_ref=w_ref,
+            dst_ref=w_out.at[part],
+            send_sem=w_send.at[0],
+            recv_sem=w_recv.at[part],
+            device_id={"dpz": 2 * col + part},
+            device_id_type=pl.DeviceIdType.MESH,
+        )
+
+        @pl.when(2 * col + part != zme)
+        def _():
+            incoming.wait_recv()
+
+
+def seq_gather(a, w, nseq, nz):
     any_spec = pl.BlockSpec(memory_space=pl.ANY)
     return pl.pallas_call(
-        functools.partial(gather_kernel, nseq),
-        in_specs=[any_spec],
-        out_specs=any_spec,
-        out_shape=jax.ShapeDtypeStruct((nseq,) + a.shape, a.dtype),
+        functools.partial(gather_kernel, nseq, nz),
+        in_specs=[any_spec, any_spec],
+        out_specs=[any_spec, any_spec],
+        out_shape=[
+            jax.ShapeDtypeStruct((nseq,) + a.shape, a.dtype),
+            jax.ShapeDtypeStruct((2,) + w.shape, w.dtype),
+        ],
         scratch_shapes=[
             pltpu.SemaphoreType.DMA((nseq - 1,)),
             pltpu.SemaphoreType.DMA((nseq - 1,)),
+            pltpu.SemaphoreType.DMA(()),
+            pltpu.SemaphoreType.DMA((nz - 1,)),
+            pltpu.SemaphoreType.DMA((2,)),
             pltpu.SemaphoreType.DMA(()),
         ],
         compiler_params=pltpu.CompilerParams(collective_id=0, has_side_effects=True),
-    )(a)
+    )(a, w)
 
 
 DP = ("dpy", "dpz", "dpc")
@@ -163,11 +215,10 @@
     own_rows, width = out_weight.shape
     gathered = lax.all_gather(out_weight, "dpc", axis=0)
     gathered = lax.all_gather(gathered, "dpy", axis=0)
-    gathered = lax.all_gather(gathered, "dpz", axis=0)
-    gathered = jnp.transpose(gathered, (1, 0, 2, 3, 4)).reshape(-1, width)
-    head_weight = lax.dynamic_slice_in_dim(gathered, head * HD, HD, 0)
-    partner_weight = lax.dynamic_slice_in_dim(gathered, partner_head * HD, HD, 0)
-    masked_half = seq_gather(masked, sizes["sqx"]).reshape(-1, width)
+    masked_half, pair_weight = seq_gather(masked, gathered, sizes["sqx"], sizes["dpz"])
+    masked_half = masked_half.reshape(-1, width)
+    head_weight = lax.dynamic_index_in_dim(pair_weight, half, 1, keepdims=False).reshape(HD, width)
+    partner_weight = lax.dynamic_index_in_dim(pair_weight, other, 1, keepdims=False).reshape(HD, width)
     half_len = masked_half.shape[0]
     nt = (((1,), (1,)), ((), ()))
     d_own = lax.dot_general(masked_half, head_weight, nt, preferred_element_type=jnp.float32).astype(jnp.bfloat16)

time: 224 us -> 228 us (1.018)
  Pallas kernels: 48.4 us -> 65.6 us
  local copies, waits for them, and re-layouts: 26.8 us -> 13.7 us
  waiting for transfers between devices: 89.6 us -> 87 us
    all_gather x1 -> x0, waiting for transfers between devices: 15.1 us -> none  [local(): gathered = lax.all_gather(gathered, 'dpz', axis=0)]
    ppermute x1, waiting for transfers between devices: 1.11 us -> 13.5 us  [local(): grads_got = lax.ppermute(grads_give, 'sqy', swap)]
    pallas_call x1, Pallas kernels: 26.5 us -> 37.8 us  [seq_gather(): pl.pallas_call(functools.partial(gather_kernel, nseq, nz), in_specs=[any_...]
    another operation x8, local copies, waits for them, and re-layouts: 7.45 us -> 1.55 us
    pallas_call x1, Pallas kernels: 21.9 us -> 27.7 us  [attention_backward(): pl.pallas_call(functools.partial(attention_kernel, nseq), grid=(length //...]
    dot_general x4, local copies, waits for them, and re-layouts: 4.11 us -> 1.62 us  [terms_of(): lax.dot_general(parts[0], inputs_half, tn, preferred_element_type=jnp.flo...]
    unnamed x34 -> x32, local copies, waits for them, and re-layouts: 4.44 us -> 4.64 us
  transfers between devices with their start and end apart: 7 -> 6, of which waited for: 7 -> 6; matrix products, arithmetic and copies ran while one was open for 11% -> 5% of each run, Pallas kernels for 12% -> 0%
where the time goes in v7:
time: 228 us
  waiting for transfers between devices  87 us (38%)
  Pallas kernels  65.6 us (29%)
  matrix products  19.6 us (9%)
  between operations  14.5 us (6%)
  local copies, waits for them, and re-layouts  13.7 us (6%)
  starting transfers between devices  11.6 us (5%)
  blocking collectives  8.43 us (4%)
  other arithmetic  7.44 us (3%)
    reduce_scatter x1, waiting for transfers between devices, local(): lax.psum_scatter(terms.reshape(nz, -1, 128), 'dpz', scatter_dimension=0,...  39.8 us
    pallas_call x1, Pallas kernels, seq_gather(): pl.pallas_call(functools.partial(gather_kernel, nseq, nz), in_specs=[any_...  37.8 us
    pallas_call x1, Pallas kernels, attention_backward(): pl.pallas_call(functools.partial(attention_kernel, nseq), grid=(length //...  27.7 us
    ppermute x1, waiting for transfers between devices, local(): terms = kept + lax.ppermute(sent, 'dpy', swap)  23.7 us
    ppermute x1, waiting for transfers between devices, local(): grads_got = lax.ppermute(grads_give, 'sqy', swap)  13.5 us
    all_gather x1, blocking collectives, local(): gathered = lax.all_gather(gathered, 'dpy', axis=0)  6.33 us
    dot_general x2, matrix products, terms_of(): lax.dot_general(parts[0], inputs_half, tn, preferred_element_type=jnp.flo...  5.99 us
    unnamed x32, local copies, waits for them, and re-layouts  4.64 us
  transfers between devices with their start and end apart: 6, of which 6 were waited for; matrix products, arithmetic and copies ran while one was open for 5% of the time, Pallas kernels for 0%

profile of v7, /device:TPU:2, one launch (start us, length us, event | category | flops | bytes accessed | tf_op | source)
XLA Modules:
  0.0 227.8 jit_solution(17962914991253713581)
XLA Ops:
  7.2 0.7 convert_reduce_fusion
  7.9 2.1 all-gather
  10.0 6.3 %all-gather.1 = bf16[4,32,1024]{2,1,0:T(8,128)(2,1)} all-gather(bf16[2,32,1024]{2,1,0:T(8,128)(2,1)S(1)} %bitcast.115), channel_id=3, replica_groups=mesh['dpy'=2,'dpz'=8,'dpc'=2,'sqy'=2,'sqx'=4] {'dpy'}, dimensions={0}, use_global_device_ids=true | all-gather | bytes 393216 | tf_op jit(solution)/shard_map/all_gather | solution.py:217
  16.3 1.9 bitcast_multiply_fusion.a_ref
  18.3 37.8 %shard_map.111 = (bf16[4,256,1024]{2,1,0:T(8,128)(2,1)}, bf16[2,2,2,32,1024]{4,3,2,1,0:T(8,128)(2,1)}) custom-call(bf16[256,1024]{1,0:T(8,128)(2,1)} %bitcast_multiply_fusion.a_ref, bf16[2,2,32,1024]{3,2,1,0:T(8,128)(2,1)} %bitcast.114), custom_call_target="tpu_custom_call" | custom-call | tf_op jit(solution)/shard_map/pallas_call | solution.py:182
  56.1 1.1 constant_dynamic-slice_fusion.1
  57.2 2.3 %convolution_convert_fusion = bf16[1024,128]{1,0:T(8,128)(2,1)S(1)} fusion(bf16[1024,1024]{1,0:T(8,128)(2,1)} %bitcast.109, bf16[128,1024]{1,0:T(8,128)(2,1)S(1)} %bitcast.113), kind=kOutput, calls=%fused_computation.12 | convolution fusion | flops 268566528 | bytes 2621440 | tf_op jit(solution)/shard_map/dot_general | solution.py:225
  59.6 3.3 %collective-permute-start = (bf16[1024,128]{1,0:T(8,128)(2,1)S(1)}, bf16[1024,128]{1,0:T(8,128)(2,1)S(1)}, u32[]{:S(2)}, u32[]{:S(2)}) collective-permute-start(bf16[1024,128]{1,0:T(8,128)(2,1)S(1)} %convolution_convert_fusion), channel_id=1, source_target_pairs={{0,4},{4,0},{1,5},{5,1},{2,6},{6,2},{3,7},{7,3},{8,12},{12,8},{9,1... | collective-permute-start | bytes 786440 | tf_op jit(solution)/shard_map/ppermute | solution.py:226
  63.0 2.4 %fusion = bf16[2048,128]{1,0:T(8,128)(2,1)S(1)} fusion(bf16[2048,128]{1,0:T(8,128)(2,1)S(1)} %broadcast_in_dim.6, s32[]{:T(128)S(6)} %select_n.30, bf16[1024,1024]{1,0:T(8,128)(2,1)} %bitcast.110, bf16[128,1024]{1,0:T(8,128)(2,1)S(1)} %bitcast.116), kind=kOutput, calls=%fused_computation.14 | convolution fusion | flops 268566528 | bytes 2621444 | tf_op jit(solution)/shard_map/dot_general | solution.py:224
  65.4 3.0 %collective-permute-done = bf16[1024,128]{1,0:T(8,128)(2,1)S(1)} collective-permute-done((bf16[1024,128]{1,0:T(8,128)(2,1)S(1)}, bf16[1024,128]{1,0:T(8,128)(2,1)S(1)}, u32[]{:S(2)}, u32[]{:S(2)}) %collective-permute-start) | collective-permute-done | bytes 262176 | tf_op jit(solution)/shard_map/ppermute | solution.py:226
  68.5 27.7 %shard_map.112 = (bf16[2048,128]{1,0:T(8,128)(2,1)S(1)}, bf16[2048,128]{1,0:T(8,128)(2,1)S(1)}, bf16[2048,128]{1,0:T(8,128)(2,1)S(1)}, bf16[2048,128]{1,0:T(8,128)(2,1)S(1)}, bf16[4,256,1024]{2,1,0:T(8,128)(2,1)}) custom-call(bf16[2048,128]{1,0:T(8,128)(2,1)S(1)} %bitcast.104, bf16[2048,128]{1,0:T(8,128)(2,1)S(1)} %bitcast.105, ...), custom_call_target="tpu_custom_call" | custom-call | flops 6442450944 | bytes 4194304 | tf_op jit(solution)/shard_map/pallas_call | solution.py:76
  96.2 0.3 pad_maximum_fusion
  96.6 3.5 %collective-permute-start.1 = (bf16[4,1024,128]{2,1,0:T(8,128)(2,1)S(1)}, bf16[4,1024,128]{2,1,0:T(8,128)(2,1)}, u32[]{:S(2)}, u32[]{:S(2)}) collective-permute-start(bf16[4,1024,128]{2,1,0:T(8,128)(2,1)S(1)} %constant_dynamic-slice_fusion), channel_id=1, source_target_pairs={{0,4},{4,0},{1,5},{5,1},{2,6},{6,2},{3,7},{7,3},{8,12},{12,8},{9,1... | collective-permute-start | bytes 3145736 | tf_op jit(solution)/shard_map/ppermute | solution.py:239
  100.1 0.1 copy.81
  100.4 0.1 copy.85
  100.7 0.1 copy.83
  100.9 0.1 copy.87
  101.1 0.8 reshape.117
  101.9 3.1 %convolution_bitcast_fusion.7 = f32[1,1,2,8,2,4,1024]{6,3,5,4,2,1,0:T(8,128)} fusion(bf16[1024,1024,1,1,1]{1,0,4,3,2:T(8,128)(2,1)} %bitcast.118, bf16[2,8,2,4,1024]{4,3,2,1,0:T(4,128)(2,1)S(1)} %reshape.113), kind=kOutput, calls=%fused_computation.11 | convolution fusion | flops 268435456 | bytes 2883584 | tf_op jit(solution)/shard_map/dot_general | solution.py:245
  105.0 1.3 convolution_bitcast_fusion.5
  106.3 1.4 convolution_bitcast_fusion.6
  107.7 0.4 copy-done.5
  108.1 1.3 convolution_bitcast_fusion.4
  109.4 13.5 %collective-permute-done.1 = bf16[4,1024,128]{2,1,0:T(8,128)(2,1)} collective-permute-done((bf16[4,1024,128]{2,1,0:T(8,128)(2,1)S(1)}, bf16[4,1024,128]{2,1,0:T(8,128)(2,1)}, u32[]{:S(2)}, u32[]{:S(2)}) %collective-permute-start.1) | collective-permute-done | bytes 1048608 | tf_op jit(solution)/shard_map/ppermute | solution.py:239
  122.9 1.3 slice_bitcast_fusion.3
  124.2 0.1 copy.89
  124.4 2.9 %convolution_bitcast_fusion.3 = f32[1,1,2,8,2,4,1024]{6,3,5,4,2,1,0:T(8,128)} fusion(bf16[1024,1024,1,1,1]{1,0,4,3,2:T(8,128)(2,1)} %bitcast.119, bf16[2,8,2,4,1024]{4,3,2,1,0:T(4,128)(2,1)S(1)} %reshape.118), kind=kOutput, calls=%fused_computation.7 | convolution fusion | flops 268435456 | bytes 2883584 | tf_op jit(solution)/shard_map/dot_general | solution.py:245
  127.6 0.5 convolution_bitcast_fusion
  128.4 2.1 convolution_bitcast_fusion.1
  130.8 2.3 convolution_bitcast_fusion.2
  133.2 0.5 maximum_maximum_fusion
  133.7 0.2 dynamic-slice_bitcast_fusion
  134.0 1.7 copy-done.4
  135.7 4.3 %collective-permute-done.2 = f32[2,4,2,8,4,1024]{5,3,4,2,1,0:T(8,128)} collective-permute-done((f32[2,4,2,8,4,1024]{5,3,4,2,1,0:T(8,128)S(1)}, f32[2,4,2,8,4,1024]{5,3,4,2,1,0:T(8,128)}, u32[]{:S(2)}, u32[]{:S(2)}) %collective-permute-start.2) | collective-permute-done | bytes 2097184 | tf_op jit(solution)/shard_map/ppermute | solution.py:260
  139.9 2.6 %bitcast_add_fusion = f32[2,4,2,8,4,1024]{5,3,4,2,1,0:T(8,128)S(1)} fusion(f32[2,4,2,8,4,1024]{5,3,4,2,1,0:T(8,128)} %collective-permute-done.2, f32[2,4,2,8,2,4,1024]{6,3,5,4,2,1,0:T(8,128)} %copy-done.4, s32[]{:T(128)S(6)} %select_n.33), kind=kLoop, calls=%fused_computation.2 | loop fusion | flops 524288 | bytes 6291460 | tf_op jit(solution)/shard_map/add | solution.py:260
  142.7 1.7 collective-permute-start.3
  144.3 23.7 %collective-permute-done.3 = f32[2,4,8,4,1024]{4,2,3,1,0:T(8,128)} collective-permute-done((f32[2,4,8,4,1024]{4,2,3,1,0:T(8,128)S(1)}, f32[2,4,8,4,1024]{4,2,3,1,0:T(8,128)}, u32[]{:S(2)}, u32[]{:S(2)}) %collective-permute-start.3) | collective-permute-done | bytes 1048608 | tf_op jit(solution)/shard_map/ppermute | solution.py:264
  168.1 1.4 bitcast_add_fusion.1
  169.4 0.7 copy.97
  170.1 1.7 reshape.123
  171.9 39.8 %reduce-scatter.2.cloned.1.call-done = f32[1,256,128]{2,1,0:T(8,128)} async-done(((f32[8,256,128]{2,1,0:T(8,128)}), f32[1,256,128]{2,1,0:T(8,128)}) %reduce-scatter.2.cloned.1.call-update) | async-done | bytes 131088 | tf_op jit(solution)/shard_map/reduce_scatter | solution.py:266
  211.7 0.9 fusion.9
  212.6 3.1 %collective-permute-start.4 = (f32[4,4,1024]{2,1,0:T(4,128)S(1)}, f32[4,4,1024]{2,1,0:T(4,128)S(1)}, u32[]{:S(2)}, u32[]{:S(2)}) collective-permute-start(f32[4,4,1024]{2,1,0:T(4,128)S(1)} %squeeze.84), channel_id=1, source_target_pairs={{0,4},{4,0},{1,5},{5,1},{2,6},{6,2},{3,7},{7,3},{8,12},{12,8},{9,1... | collective-permute-start | bytes 196616 | tf_op jit(solution)/shard_map/ppermute | solution.py:268
  215.7 2.7 %collective-permute-done.4 = f32[4,4,1024]{2,1,0:T(4,128)S(1)} collective-permute-done((f32[4,4,1024]{2,1,0:T(4,128)S(1)}, f32[4,4,1024]{2,1,0:T(4,128)S(1)}, u32[]{:S(2)}, u32[]{:S(2)}) %collective-permute-start.4) | collective-permute-done | bytes 65568 | tf_op jit(solution)/shard_map/ppermute | solution.py:268
  218.5 0.6 copy.101
  219.1 0.6 copy.100
  219.7 0.6 copy.99
  220.4 0.6 copy.98
  (49 shorter events, 1.8 us)
Async XLA Ops:
  7.2 204.5 %reduce-scatter.2.cloned.1.call-start = ((), (), s32[]{:S(2)}) async-start(), calls=%async_computation.1 | async-start | bytes 1179648 | tf_op jit(solution)/shard_map/reduce_scatter | solution.py:266
  59.5 8.8 %copy-start.12 = (s32[1,1,16,16]{3,2,1,0:T(8,128)S(1)}, s32[1,1,16,16]{3,2,1,0:T(8,128)}, u32[]{:S(2)}) copy-start(s32[1,1,16,16]{3,2,1,0:T(8,128)} %param.15) | copy-start | bytes 3076
  59.5 8.9 %copy-start = (bf16[1,2048,1,128]{3,1,2,0:T(8,128)(2,1)S(1)}, bf16[1,2048,1,128]{3,1,2,0:T(8,128)(2,1)}, u32[]{:S(2)}) copy-start(bf16[1,2048,1,128]{3,1,2,0:T(8,128)(2,1)} %param.11) | copy-start | bytes 1572868
  59.6 8.9 %copy-start.1 = (bf16[1,2048,1,128]{3,1,2,0:T(8,128)(2,1)S(1)}, bf16[1,2048,1,128]{3,1,2,0:T(8,128)(2,1)}, u32[]{:S(2)}) copy-start(bf16[1,2048,1,128]{3,1,2,0:T(8,128)(2,1)} %param.12) | copy-start | bytes 1572868
  59.6 8.9 %copy-start.2 = (bf16[1,2048,1,128]{3,1,2,0:T(8,128)(2,1)S(1)}, bf16[1,2048,1,128]{3,1,2,0:T(8,128)(2,1)}, u32[]{:S(2)}) copy-start(bf16[1,2048,1,128]{3,1,2,0:T(8,128)(2,1)} %param.13) | copy-start | bytes 1572868
  59.6 8.9 %copy-start.3 = (bf16[1,256,1024]{2,1,0:T(8,128)(2,1)S(1)}, bf16[1,256,1024]{2,1,0:T(8,128)(2,1)}, u32[]{:S(2)}) copy-start(bf16[1,256,1024]{2,1,0:T(8,128)(2,1)} %param.8) | copy-start | bytes 1572868
  59.6 8.7 %collective-permute-start = (bf16[1024,128]{1,0:T(8,128)(2,1)S(1)}, bf16[1024,128]{1,0:T(8,128)(2,1)S(1)}, u32[]{:S(2)}, u32[]{:S(2)}) collective-permute-start(bf16[1024,128]{1,0:T(8,128)(2,1)S(1)} %convolution_convert_fusion), channel_id=1, source_target_pairs={{0,4},{4,0},{1,5},{5,1},{2,6},{6,2},{3,7},{7,3},{8,12},{12,8},{9,1... | collective-permute-start | bytes 786440 | tf_op jit(solution)/shard_map/ppermute | solution.py:226
  96.6 26.3 %collective-permute-start.1 = (bf16[4,1024,128]{2,1,0:T(8,128)(2,1)S(1)}, bf16[4,1024,128]{2,1,0:T(8,128)(2,1)}, u32[]{:S(2)}, u32[]{:S(2)}) collective-permute-start(bf16[4,1024,128]{2,1,0:T(8,128)(2,1)S(1)} %constant_dynamic-slice_fusion), channel_id=1, source_target_pairs={{0,4},{4,0},{1,5},{5,1},{2,6},{6,2},{3,7},{7,3},{8,12},{12,8},{9,1... | collective-permute-start | bytes 3145736 | tf_op jit(solution)/shard_map/ppermute | solution.py:239
  101.9 3.1 %copy-start.13 = (bf16[4,256,1024]{2,1,0:T(8,128)(2,1)S(1)}, bf16[4,256,1024]{2,1,0:T(8,128)(2,1)}, u32[]{:S(2)}) copy-start(bf16[4,256,1024]{2,1,0:T(8,128)(2,1)} %get-tuple-element.17) | copy-start | bytes 6291460
  106.3 1.8 copy-start.5
  106.3 1.8 copy-start.11
  130.8 2.3 %copy-start.6 = (f32[1,1,2,8,2,4,1024]{6,3,5,4,2,1,0:T(8,128)S(1)}, f32[1,1,2,8,2,4,1024]{6,3,5,4,2,1,0:T(8,128)}, u32[]{:S(2)}) copy-start(f32[1,1,2,8,2,4,1024]{6,3,5,4,2,1,0:T(8,128)} %convolution_bitcast_fusion.7) | copy-start | bytes 1572868
  130.8 2.3 %copy-start.7 = (f32[1,1,2,8,2,4,1024]{6,3,5,4,2,1,0:T(8,128)S(1)}, f32[1,1,2,8,2,4,1024]{6,3,5,4,2,1,0:T(8,128)}, u32[]{:S(2)}) copy-start(f32[1,1,2,8,2,4,1024]{6,3,5,4,2,1,0:T(8,128)} %convolution_bitcast_fusion.5) | copy-start | bytes 1572868
  130.8 2.3 %copy-start.8 = (f32[1,1,2,8,2,4,1024]{6,3,5,4,2,1,0:T(8,128)S(1)}, f32[1,1,2,8,2,4,1024]{6,3,5,4,2,1,0:T(8,128)}, u32[]{:S(2)}) copy-start(f32[1,1,2,8,2,4,1024]{6,3,5,4,2,1,0:T(8,128)} %convolution_bitcast_fusion.6) | copy-start | bytes 1572868
  130.8 2.3 %copy-start.9 = (f32[1,1,2,8,2,4,1024]{6,3,5,4,2,1,0:T(8,128)S(1)}, f32[1,1,2,8,2,4,1024]{6,3,5,4,2,1,0:T(8,128)}, u32[]{:S(2)}) copy-start(f32[1,1,2,8,2,4,1024]{6,3,5,4,2,1,0:T(8,128)} %convolution_bitcast_fusion.4) | copy-start | bytes 1572868
  130.8 2.3 %copy-start.10 = (f32[1,1,2,8,2,4,1024]{6,3,5,4,2,1,0:T(8,128)S(1)}, f32[1,1,2,8,2,4,1024]{6,3,5,4,2,1,0:T(8,128)}, u32[]{:S(2)}) copy-start(f32[1,1,2,8,2,4,1024]{6,3,5,4,2,1,0:T(8,128)} %convolution_bitcast_fusion.3) | copy-start | bytes 1572868
  133.7 1.9 copy-start.4
  135.6 4.3 %collective-permute-start.2 = (f32[2,4,2,8,4,1024]{5,3,4,2,1,0:T(8,128)S(1)}, f32[2,4,2,8,4,1024]{5,3,4,2,1,0:T(8,128)}, u32[]{:S(2)}, u32[]{:S(2)}) collective-permute-start(f32[2,4,2,8,4,1024]{5,3,4,2,1,0:T(8,128)S(1)} %dynamic-slice_bitcast_fusion), channel_id=1, source_target_pairs={{0,8},{8,0},{1,9},{9,1},{2,10},{10,2},{3,11},{11,3},{4,12},{12,4},... | collective-permute-start | bytes 6291464 | tf_op jit(solution)/shard_map/ppermute | solution.py:260
  142.7 25.4 %collective-permute-start.3 = (f32[2,4,8,4,1024]{4,2,3,1,0:T(8,128)S(1)}, f32[2,4,8,4,1024]{4,2,3,1,0:T(8,128)}, u32[]{:S(2)}, u32[]{:S(2)}) collective-permute-start(f32[2,4,8,4,1024]{4,2,3,1,0:T(8,128)S(1)} %dynamic-slice_bitcast_fusion.1), channel_id=1, source_target_pairs={{0,128},{128,0},{1,129},{129,1},{2,130},{130,2},{3,131},{131,3},{4... | collective-permute-start | bytes 3145736 | tf_op jit(solution)/shard_map/ppermute | solution.py:264
  212.6 5.9 %collective-permute-start.4 = (f32[4,4,1024]{2,1,0:T(4,128)S(1)}, f32[4,4,1024]{2,1,0:T(4,128)S(1)}, u32[]{:S(2)}, u32[]{:S(2)}) collective-permute-start(f32[4,4,1024]{2,1,0:T(4,128)S(1)} %squeeze.84), channel_id=1, source_target_pairs={{0,4},{4,0},{1,5},{5,1},{2,6},{6,2},{3,7},{7,3},{8,12},{12,8},{9,1... | collective-permute-start | bytes 196616 | tf_op jit(solution)/shard_map/ppermute | solution.py:268
Sparse Core Ops, SparseCore 0:
  172.0 39.6 reduce-scatter.1

commit v8 on v6

--- a/solution.py
+++ b/solution.py
@@ -161,10 +161,10 @@
     swap = [(0, 1), (1, 0)]
     masked = d_output[0] * loss_mask[0][:, None].astype(jnp.bfloat16)
     own_rows, width = out_weight.shape
-    gathered = lax.all_gather(out_weight, "dpc", axis=0)
+    gathered = lax.all_gather(out_weight, "dpz", axis=0)
+    gathered = lax.all_gather(gathered, "dpc", axis=0)
     gathered = lax.all_gather(gathered, "dpy", axis=0)
-    gathered = lax.all_gather(gathered, "dpz", axis=0)
-    gathered = jnp.transpose(gathered, (1, 0, 2, 3, 4)).reshape(-1, width)
+    gathered = jnp.transpose(gathered, (0, 2, 1, 3, 4)).reshape(-1, width)
     head_weight = lax.dynamic_slice_in_dim(gathered, head * HD, HD, 0)
     partner_weight = lax.dynamic_slice_in_dim(gathered, partner_head * HD, HD, 0)
     masked_half = seq_gather(masked, sizes["sqx"]).reshape(-1, width)

time: 224 us -> 266 us (1.19)
  blocking collectives: 8.44 us -> 31.2 us
  waiting for transfers between devices: 89.6 us -> 109 us
  Pallas kernels: 48.4 us -> 51.5 us
    all_gather x2 -> x1, blocking collectives: 8.44 us -> 31.2 us  [local(): gathered = lax.all_gather(out_weight, 'dpz', axis=0)]
    all_gather x1 -> x2, waiting for transfers between devices: 15.1 us -> 27.9 us  [the longest x1 14 us: local(): gathered = lax.all_gather(gathered, 'dpc', axis=0)]
    pallas_call x1, Pallas kernels: 21.9 us -> 25 us  [attention_backward(): pl.pallas_call(functools.partial(attention_kernel, nseq), grid=(length //...]
    reduce_scatter x1, waiting for transfers between devices: 38.4 us -> 41.3 us  [local(): lax.psum_scatter(terms.reshape(nz, -1, 128), 'dpz', scatter_dimension=0,...]
  transfers between devices with their start and end apart: 7 -> 8, of which waited for: 7 -> 8; matrix products, arithmetic and copies ran while one was open for 11% -> 8% of each run, Pallas kernels for 12% -> 10%
where the time goes in v8:
time: 266 us
  waiting for transfers between devices  109 us (41%)
  Pallas kernels  51.5 us (19%)
  blocking collectives  31.2 us (12%)
  local copies, waits for them, and re-layouts  26.9 us (10%)
  matrix products  17.6 us (7%)
  between operations  14.2 us (5%)
  starting transfers between devices  9.65 us (4%)
  other arithmetic  5.73 us (2%)
    reduce_scatter x1, waiting for transfers between devices, local(): lax.psum_scatter(terms.reshape(nz, -1, 128), 'dpz', scatter_dimension=0,...  41.3 us
    all_gather x1, blocking collectives, local(): gathered = lax.all_gather(out_weight, 'dpz', axis=0)  31.2 us
    pallas_call x1, Pallas kernels, seq_gather(): pl.pallas_call(functools.partial(gather_kernel, nseq), in_specs=[any_spec...  26.4 us
    pallas_call x1, Pallas kernels, attention_backward(): pl.pallas_call(functools.partial(attention_kernel, nseq), grid=(length //...  25 us
    ppermute x1, waiting for transfers between devices, local(): terms = kept + lax.ppermute(sent, 'dpy', swap)  24.8 us
    all_gather x1, waiting for transfers between devices, local(): gathered = lax.all_gather(gathered, 'dpc', axis=0)  14 us
    all_gather x1, waiting for transfers between devices, local(): gathered = lax.all_gather(gathered, 'dpy', axis=0)  13.9 us
    another operation x8, local copies, waits for them, and re-layouts  7.47 us
  transfers between devices with their start and end apart: 8, of which 8 were waited for; matrix products, arithmetic and copies ran while one was open for 8% of the time, Pallas kernels for 10%

profile of v8, /device:TPU:2, one launch (start us, length us, event | category | flops | bytes accessed | tf_op | source)
XLA Modules:
  0.0 265.9 jit_solution(18009713735472909967)
XLA Ops:
  7.2 31.2 %all-gather = bf16[256,1024]{1,0:T(8,128)(2,1)} all-gather(bf16[32,1024]{1,0:T(8,128)(2,1)} %param.14), channel_id=2, replica_groups=mesh['dpy'=2,'dpz'=8,'dpc'=2,'sqy'=2,'sqx'=4] {'dpz'}, dimensions={0}, use_global_device_ids=true | all-gather | bytes 589824 | tf_op jit(solution)/shard_map/all_gather | solution.py:164
  38.5 14.0 %all-gather.6.cloned.1.call-done = bf16[16,32,1024]{2,1,0:T(8,128)(2,1)} async-done(((bf16[8,32,1024]{2,1,0:T(8,128)(2,1)}), bf16[16,32,1024]{2,1,0:T(8,128)(2,1)}) %all-gather.6.cloned.1.call-update) | async-done | bytes 1048592 | tf_op jit(solution)/shard_map/all_gather | solution.py:165
  52.7 0.9 bitcast_multiply_fusion.a_ref
  53.6 26.4 %shard_map.111 = bf16[4,256,1024]{2,1,0:T(8,128)(2,1)} custom-call(bf16[256,1024]{1,0:T(8,128)(2,1)} %bitcast_multiply_fusion.a_ref), custom_call_target="tpu_custom_call" | custom-call | tf_op jit(solution)/shard_map/pallas_call | solution.py:136
  80.0 13.9 %all-gather.8.cloned.1.call-done = bf16[4,8,32,1024]{3,2,1,0:T(8,128)(2,1)} async-done(((bf16[2,8,32,1024]{3,2,1,0:T(8,128)(2,1)}), bf16[4,8,32,1024]{3,2,1,0:T(8,128)(2,1)}) %all-gather.8.cloned.1.call-update) | async-done | bytes 2097168 | tf_op jit(solution)/shard_map/all_gather | solution.py:166
  93.9 2.0 copy.83
  96.1 0.7 convolution_convert_fusion
  96.9 2.8 %collective-permute-start = (bf16[1024,128]{1,0:T(8,128)(2,1)S(1)}, bf16[1024,128]{1,0:T(8,128)(2,1)S(1)}, u32[]{:S(2)}, u32[]{:S(2)}) collective-permute-start(bf16[1024,128]{1,0:T(8,128)(2,1)S(1)} %convolution_convert_fusion), channel_id=1, source_target_pairs={{0,4},{4,0},{1,5},{5,1},{2,6},{6,2},{3,7},{7,3},{8,12},{12,8},{9,1... | collective-permute-start | bytes 786440 | tf_op jit(solution)/shard_map/ppermute | solution.py:175
  99.8 0.8 fusion
  100.6 5.9 %collective-permute-done = bf16[1024,128]{1,0:T(8,128)(2,1)S(1)} collective-permute-done((bf16[1024,128]{1,0:T(8,128)(2,1)S(1)}, bf16[1024,128]{1,0:T(8,128)(2,1)S(1)}, u32[]{:S(2)}, u32[]{:S(2)}) %collective-permute-start) | collective-permute-done | bytes 262176 | tf_op jit(solution)/shard_map/ppermute | solution.py:175
  106.7 25.0 %shard_map.112 = (bf16[2048,128]{1,0:T(8,128)(2,1)S(1)}, bf16[2048,128]{1,0:T(8,128)(2,1)S(1)}, bf16[2048,128]{1,0:T(8,128)(2,1)S(1)}, bf16[2048,128]{1,0:T(8,128)(2,1)S(1)}, bf16[4,256,1024]{2,1,0:T(8,128)(2,1)}) custom-call(bf16[2048,128]{1,0:T(8,128)(2,1)S(1)} %bitcast.104, bf16[2048,128]{1,0:T(8,128)(2,1)S(1)} %bitcast.105, ...), custom_call_target="tpu_custom_call" | custom-call | flops 6442450944 | bytes 4194304 | tf_op jit(solution)/shard_map/pallas_call | solution.py:76
  132.1 3.0 %collective-permute-start.1 = (bf16[4,1024,128]{2,1,0:T(8,128)(2,1)S(1)}, bf16[4,1024,128]{2,1,0:T(8,128)(2,1)}, u32[]{:S(2)}, u32[]{:S(2)}) collective-permute-start(bf16[4,1024,128]{2,1,0:T(8,128)(2,1)S(1)} %constant_dynamic-slice_fusion), channel_id=1, source_target_pairs={{0,4},{4,0},{1,5},{5,1},{2,6},{6,2},{3,7},{7,3},{8,12},{12,8},{9,1... | collective-permute-start | bytes 3145736 | tf_op jit(solution)/shard_map/ppermute | solution.py:188
  135.1 0.9 dynamic-slice_bitcast_fusion.5
  136.0 1.8 copy.84
  137.8 1.7 reshape.107
  139.6 1.8 copy.88
  141.4 1.8 reshape.110
  143.1 1.8 copy.86
  145.0 1.8 reshape.109
  146.7 0.8 copy.90
  147.6 1.1 reshape.111
  148.7 3.2 %convolution_bitcast_fusion.7 = f32[1,1,2,8,2,4,1024]{6,3,5,4,2,1,0:T(8,128)} fusion(bf16[1024,1024,1,1,1]{1,0,4,3,2:T(8,128)(2,1)} %bitcast.119, bf16[2,8,2,4,1024]{4,3,2,1,0:T(4,128)(2,1)} %reshape.107), kind=kOutput, calls=%fused_computation.11 | convolution fusion | flops 268435456 | bytes 2883584 | tf_op jit(solution)/shard_map/dot_general | solution.py:194
  151.8 1.3 convolution_bitcast_fusion.5
  153.2 1.4 convolution_bitcast_fusion.6
  154.5 1.4 convolution_bitcast_fusion.4
  155.9 2.2 collective-permute-done.1
  158.1 1.3 slice_bitcast_fusion.3
  159.6 2.9 %convolution_bitcast_fusion.3 = f32[1,1,2,8,2,4,1024]{6,3,5,4,2,1,0:T(8,128)} fusion(bf16[1024,1024,1,1,1]{1,0,4,3,2:T(8,128)(2,1)} %bitcast.120, bf16[2,8,2,4,1024]{4,3,2,1,0:T(4,128)(2,1)S(1)} %reshape.112), kind=kOutput, calls=%fused_computation.7 | convolution fusion | flops 268435456 | bytes 2883584 | tf_op jit(solution)/shard_map/dot_general | solution.py:194
  162.7 0.8 reshape.115
  163.6 1.5 convolution_bitcast_fusion
  165.3 2.1 convolution_bitcast_fusion.1
  167.8 2.3 convolution_bitcast_fusion.2
  170.9 1.7 copy-done.4
  172.6 4.3 %collective-permute-done.2 = f32[2,4,2,8,4,1024]{5,3,4,2,1,0:T(8,128)} collective-permute-done((f32[2,4,2,8,4,1024]{5,3,4,2,1,0:T(8,128)S(1)}, f32[2,4,2,8,4,1024]{5,3,4,2,1,0:T(8,128)}, u32[]{:S(2)}, u32[]{:S(2)}) %collective-permute-start.2) | collective-permute-done | bytes 2097184 | tf_op jit(solution)/shard_map/ppermute | solution.py:209
  176.9 2.6 bitcast_add_fusion
  179.6 0.6 collective-permute-start.3
  180.2 24.8 %collective-permute-done.3 = f32[2,4,8,4,1024]{4,2,3,1,0:T(8,128)} collective-permute-done((f32[2,4,8,4,1024]{4,2,3,1,0:T(8,128)S(1)}, f32[2,4,8,4,1024]{4,2,3,1,0:T(8,128)}, u32[]{:S(2)}, u32[]{:S(2)}) %collective-permute-start.3) | collective-permute-done | bytes 1048608 | tf_op jit(solution)/shard_map/ppermute | solution.py:213
  205.0 1.4 bitcast_add_fusion.1
  206.4 0.7 copy.100
  207.1 1.7 reshape.117
  208.8 41.3 %reduce-scatter.2.cloned.1.call-done = f32[1,256,128]{2,1,0:T(8,128)} async-done(((f32[8,256,128]{2,1,0:T(8,128)}), f32[1,256,128]{2,1,0:T(8,128)}) %reduce-scatter.2.cloned.1.call-update) | async-done | bytes 131088 | tf_op jit(solution)/shard_map/reduce_scatter | solution.py:215
  250.1 0.9 fusion.13
  251.0 3.1 %collective-permute-start.4 = (f32[4,4,1024]{2,1,0:T(4,128)S(1)}, f32[4,4,1024]{2,1,0:T(4,128)S(1)}, u32[]{:S(2)}, u32[]{:S(2)}) collective-permute-start(f32[4,4,1024]{2,1,0:T(4,128)S(1)} %squeeze.81), channel_id=1, source_target_pairs={{0,4},{4,0},{1,5},{5,1},{2,6},{6,2},{3,7},{7,3},{8,12},{12,8},{9,1... | collective-permute-start | bytes 196616 | tf_op jit(solution)/shard_map/ppermute | solution.py:217
  254.2 2.7 %collective-permute-done.4 = f32[4,4,1024]{2,1,0:T(4,128)S(1)} collective-permute-done((f32[4,4,1024]{2,1,0:T(4,128)S(1)}, f32[4,4,1024]{2,1,0:T(4,128)S(1)}, u32[]{:S(2)}, u32[]{:S(2)}) %collective-permute-start.4) | collective-permute-done | bytes 65568 | tf_op jit(solution)/shard_map/ppermute | solution.py:217
  256.9 0.6 copy.104
  257.5 0.6 copy.103
  258.2 0.6 copy.102
  258.8 0.6 copy.101
  (60 shorter events, 2.9 us)
Async XLA Ops:
  7.2 45.5 %copy-start.15 = (s32[1,256]{1,0:T(1,128)S(1)}, s32[1,256]{1,0:T(1,128)}, u32[]{:S(2)}) copy-start(s32[1,256]{1,0:T(1,128)} %param.10) | copy-start | bytes 3076
  7.2 45.5 %copy-start.11 = (bf16[1,256,1024]{2,1,0:T(8,128)(2,1)S(1)}, bf16[1,256,1024]{2,1,0:T(8,128)(2,1)}, u32[]{:S(2)}) copy-start(bf16[1,256,1024]{2,1,0:T(8,128)(2,1)} %param.9) | copy-start | bytes 1572868
  7.2 45.4 %all-gather.6.cloned.1.call-start = ((), (), s32[]{:S(2)}) async-start(), calls=%async_computation.2 | async-start | bytes 1572864 | tf_op jit(solution)/shard_map/all_gather | solution.py:165
  38.5 55.4 %all-gather.8.cloned.1.call-start = ((), (), s32[]{:S(2)}) async-start(), calls=%async_computation.3 | async-start | bytes 3145728 | tf_op jit(solution)/shard_map/all_gather | solution.py:166
  52.6 197.5 %reduce-scatter.2.cloned.1.call-start = ((), (), s32[]{:S(2)}) async-start(), calls=%async_computation.1 | async-start | bytes 1179648 | tf_op jit(solution)/shard_map/reduce_scatter | solution.py:215
  93.9 2.2 copy-start.5
  96.8 9.7 %copy-start.14 = (s32[1,1,16,16]{3,2,1,0:T(8,128)S(1)}, s32[1,1,16,16]{3,2,1,0:T(8,128)}, u32[]{:S(2)}) copy-start(s32[1,1,16,16]{3,2,1,0:T(8,128)} %param.15) | copy-start | bytes 3076
  96.8 9.8 %copy-start = (bf16[1,2048,1,128]{3,1,2,0:T(8,128)(2,1)S(1)}, bf16[1,2048,1,128]{3,1,2,0:T(8,128)(2,1)}, u32[]{:S(2)}) copy-start(bf16[1,2048,1,128]{3,1,2,0:T(8,128)(2,1)} %param.11) | copy-start | bytes 1572868
  96.9 9.8 %copy-start.1 = (bf16[1,2048,1,128]{3,1,2,0:T(8,128)(2,1)S(1)}, bf16[1,2048,1,128]{3,1,2,0:T(8,128)(2,1)}, u32[]{:S(2)}) copy-start(bf16[1,2048,1,128]{3,1,2,0:T(8,128)(2,1)} %param.12) | copy-start | bytes 1572868
  96.9 9.8 %copy-start.2 = (bf16[1,2048,1,128]{3,1,2,0:T(8,128)(2,1)S(1)}, bf16[1,2048,1,128]{3,1,2,0:T(8,128)(2,1)}, u32[]{:S(2)}) copy-start(bf16[1,2048,1,128]{3,1,2,0:T(8,128)(2,1)} %param.13) | copy-start | bytes 1572868
  96.9 9.8 %copy-start.3 = (bf16[1,256,1024]{2,1,0:T(8,128)(2,1)S(1)}, bf16[1,256,1024]{2,1,0:T(8,128)(2,1)}, u32[]{:S(2)}) copy-start(bf16[1,256,1024]{2,1,0:T(8,128)(2,1)} %param.8) | copy-start | bytes 1572868
  96.9 9.6 %collective-permute-start = (bf16[1024,128]{1,0:T(8,128)(2,1)S(1)}, bf16[1024,128]{1,0:T(8,128)(2,1)S(1)}, u32[]{:S(2)}, u32[]{:S(2)}) collective-permute-start(bf16[1024,128]{1,0:T(8,128)(2,1)S(1)} %convolution_convert_fusion), channel_id=1, source_target_pairs={{0,4},{4,0},{1,5},{5,1},{2,6},{6,2},{3,7},{7,3},{8,12},{12,8},{9,1... | collective-permute-start | bytes 786440 | tf_op jit(solution)/shard_map/ppermute | solution.py:175
  132.1 26.0 %collective-permute-start.1 = (bf16[4,1024,128]{2,1,0:T(8,128)(2,1)S(1)}, bf16[4,1024,128]{2,1,0:T(8,128)(2,1)}, u32[]{:S(2)}, u32[]{:S(2)}) collective-permute-start(bf16[4,1024,128]{2,1,0:T(8,128)(2,1)S(1)} %constant_dynamic-slice_fusion), channel_id=1, source_target_pairs={{0,4},{4,0},{1,5},{5,1},{2,6},{6,2},{3,7},{7,3},{8,12},{12,8},{9,1... | collective-permute-start | bytes 3145736 | tf_op jit(solution)/shard_map/ppermute | solution.py:188
  148.6 3.2 %copy-start.12 = (bf16[2,8,2,4,1024]{4,3,2,1,0:T(4,128)(2,1)S(1)}, bf16[2,8,2,4,1024]{4,3,2,1,0:T(4,128)(2,1)}, u32[]{:S(2)}) copy-start(bf16[2,8,2,4,1024]{4,3,2,1,0:T(4,128)(2,1)} %reshape.110) | copy-start | bytes 786436
  148.6 3.2 %copy-start.16 = (bf16[4,256,1024]{2,1,0:T(8,128)(2,1)S(1)}, bf16[4,256,1024]{2,1,0:T(8,128)(2,1)}, u32[]{:S(2)}) copy-start(bf16[4,256,1024]{2,1,0:T(8,128)(2,1)} %get-tuple-element.13) | copy-start | bytes 6291460
  151.8 1.3 copy-start.13
  167.7 2.3 copy-start.6
  167.7 2.3 copy-start.7
  167.7 2.3 copy-start.8
  167.7 2.3 copy-start.9
  167.7 2.3 copy-start.10
  170.6 2.0 copy-start.4
  172.6 4.3 %collective-permute-start.2 = (f32[2,4,2,8,4,1024]{5,3,4,2,1,0:T(8,128)S(1)}, f32[2,4,2,8,4,1024]{5,3,4,2,1,0:T(8,128)}, u32[]{:S(2)}, u32[]{:S(2)}) collective-permute-start(f32[2,4,2,8,4,1024]{5,3,4,2,1,0:T(8,128)S(1)} %dynamic-slice_bitcast_fusion), channel_id=1, source_target_pairs={{0,8},{8,0},{1,9},{9,1},{2,10},{10,2},{3,11},{11,3},{4,12},{12,4},... | collective-permute-start | bytes 6291464 | tf_op jit(solution)/shard_map/ppermute | solution.py:209
  179.6 25.4 %collective-permute-start.3 = (f32[2,4,8,4,1024]{4,2,3,1,0:T(8,128)S(1)}, f32[2,4,8,4,1024]{4,2,3,1,0:T(8,128)}, u32[]{:S(2)}, u32[]{:S(2)}) collective-permute-start(f32[2,4,8,4,1024]{4,2,3,1,0:T(8,128)S(1)} %dynamic-slice_bitcast_fusion.1), channel_id=1, source_target_pairs={{0,128},{128,0},{1,129},{129,1},{2,130},{130,2},{3,131},{131,3},{4... | collective-permute-start | bytes 3145736 | tf_op jit(solution)/shard_map/ppermute | solution.py:213
  251.0 5.9 %collective-permute-start.4 = (f32[4,4,1024]{2,1,0:T(4,128)S(1)}, f32[4,4,1024]{2,1,0:T(4,128)S(1)}, u32[]{:S(2)}, u32[]{:S(2)}) collective-permute-start(f32[4,4,1024]{2,1,0:T(4,128)S(1)} %squeeze.81), channel_id=1, source_target_pairs={{0,4},{4,0},{1,5},{5,1},{2,6},{6,2},{3,7},{7,3},{8,12},{12,8},{9,1... | collective-permute-start | bytes 196616 | tf_op jit(solution)/shard_map/ppermute | solution.py:217
Sparse Core Ops, SparseCore 0:
  38.6 13.9 all-gather.5
  54.4 39.4 all-gather.7
  208.9 41.1 reduce-scatter.1

commit v9 on v6

--- a/solution.py
+++ b/solution.py
@@ -207,13 +207,13 @@
     kept = lax.dynamic_index_in_dim(terms, core, 4, keepdims=False)
     sent = lax.dynamic_index_in_dim(terms, 1 - core, 4, keepdims=False)
     terms = kept + lax.ppermute(sent, "dpc", swap)
+    terms = jnp.transpose(terms, (3, 0, 1, 2, 4, 5))
+    terms = lax.psum_scatter(terms.reshape(nz, -1, 128), "dpz", scatter_dimension=0, tiled=True)
+    terms = terms.reshape(2, 4, ny, chunk, width)
     row = lax.axis_index("dpy")
     kept = lax.dynamic_index_in_dim(terms, row, 2, keepdims=False)
     sent = lax.dynamic_index_in_dim(terms, 1 - row, 2, keepdims=False)
     terms = kept + lax.ppermute(sent, "dpy", swap)
-    terms = jnp.transpose(terms.reshape(2, 4, nz, chunk * width), (2, 0, 1, 3))
-    terms = lax.psum_scatter(terms.reshape(nz, -1, 128), "dpz", scatter_dimension=0, tiled=True)
-    terms = terms.reshape(2, 4, chunk, width)
     owned = terms[0] + lax.ppermute(terms[1], "sqy", swap)
     owned = jnp.transpose(owned, (1, 0, 2))
     return tuple(owned[:, part][:, None, :] for part in range(4))

time: 224 us -> 208 us (0.929)
  waiting for transfers between devices: 89.6 us -> 74.3 us
    ppermute x1, waiting for transfers between devices: 23.8 us -> 4.27 us  [local(): terms = kept + lax.ppermute(sent, 'dpy', swap)]
    reduce_scatter x1, waiting for transfers between devices: 38.4 us -> 42 us  [local(): lax.psum_scatter(terms.reshape(nz, -1, 128), 'dpz', scatter_dimension=0,...]
    add x1 -> x0, other arithmetic: 2.62 us -> none  [local(): terms = kept + lax.ppermute(sent, 'dpc', swap)]
  transfers between devices with their start and end apart: 7 -> 7, of which waited for: 7 -> 7; matrix products, arithmetic and copies ran while one was open for 11% -> 12% of each run, Pallas kernels for 12% -> 13%
where the time goes in v9:
time: 208 us; the launch traced here: 207 us
  waiting for transfers between devices  74.3 us (36%)
  Pallas kernels  48.4 us (23%)
  local copies, waits for them, and re-layouts  28.4 us (14%)
  matrix products  17.5 us (8%)
  between operations  14.4 us (7%)
  starting transfers between devices  10.3 us (5%)
  blocking collectives  8.44 us (4%)
  other arithmetic  5.49 us (3%)
    reduce_scatter x1, waiting for transfers between devices, local(): lax.psum_scatter(terms.reshape(nz, -1, 128), 'dpz', scatter_dimension=0,...  42 us
    pallas_call x1, Pallas kernels, seq_gather(): pl.pallas_call(functools.partial(gather_kernel, nseq), in_specs=[any_spec...  26.5 us
    pallas_call x1, Pallas kernels, attention_backward(): pl.pallas_call(functools.partial(attention_kernel, nseq), grid=(length //...  21.9 us
    all_gather x1, waiting for transfers between devices, local(): gathered = lax.all_gather(gathered, 'dpz', axis=0)  15.1 us
    another operation x8, local copies, waits for them, and re-layouts  7.47 us
    all_gather x1, blocking collectives, local(): gathered = lax.all_gather(gathered, 'dpy', axis=0)  6.33 us
    dot_general x2, matrix products, terms_of(): lax.dot_general(parts[0], inputs_half, tn, preferred_element_type=jnp.flo...  6.09 us
    ppermute x1, waiting for transfers between devices, local(): terms = kept + lax.ppermute(sent, 'dpc', swap)  4.37 us
  transfers between devices with their start and end apart: 7, of which 7 were waited for; matrix products, arithmetic and copies ran while one was open for 12% of the time, Pallas kernels for 13%

profile of v9, /device:TPU:2, one launch (start us, length us, event | category | flops | bytes accessed | tf_op | source)
XLA Modules:
  0.0 207.3 jit_solution(17050249465614227602)
XLA Ops:
  7.2 2.1 %all-gather = bf16[64,1024]{1,0:T(8,128)(2,1)S(1)} all-gather(bf16[32,1024]{1,0:T(8,128)(2,1)} %param.14), channel_id=2, replica_groups=mesh['dpy'=2,'dpz'=8,'dpc'=2,'sqy'=2,'sqx'=4] {'dpc'}, dimensions={0}, use_global_device_ids=true | all-gather | bytes 196608 | tf_op jit(solution)/shard_map/all_gather | solution.py:164
  9.3 6.3 %all-gather.1 = bf16[4,32,1024]{2,1,0:T(8,128)(2,1)} all-gather(bf16[2,32,1024]{2,1,0:T(8,128)(2,1)S(1)} %bitcast.125), channel_id=3, replica_groups=mesh['dpy'=2,'dpz'=8,'dpc'=2,'sqy'=2,'sqx'=4] {'dpy'}, dimensions={0}, use_global_device_ids=true | all-gather | bytes 393216 | tf_op jit(solution)/shard_map/all_gather | solution.py:165
  15.7 0.7 convert_reduce_fusion
  16.4 1.9 bitcast_multiply_fusion.a_ref
  18.4 26.5 %shard_map.111 = bf16[4,256,1024]{2,1,0:T(8,128)(2,1)} custom-call(bf16[256,1024]{1,0:T(8,128)(2,1)} %bitcast_multiply_fusion.a_ref), custom_call_target="tpu_custom_call" | custom-call | tf_op jit(solution)/shard_map/pallas_call | solution.py:136
  44.9 15.1 %all-gather.5.cloned.1.call-done = bf16[16,2,32,1024]{3,2,1,0:T(8,128)(2,1)} async-done(((bf16[2,2,32,1024]{3,2,1,0:T(8,128)(2,1)}), bf16[16,2,32,1024]{3,2,1,0:T(8,128)(2,1)}) %all-gather.5.cloned.1.call-update) | async-done | bytes 2097168 | tf_op jit(solution)/shard_map/all_gather | solution.py:166
  60.1 2.0 copy.58
  62.3 0.7 convolution_convert_fusion
  63.1 3.1 %collective-permute-start = (bf16[1024,128]{1,0:T(8,128)(2,1)S(1)}, bf16[1024,128]{1,0:T(8,128)(2,1)S(1)}, u32[]{:S(2)}, u32[]{:S(2)}) collective-permute-start(bf16[1024,128]{1,0:T(8,128)(2,1)S(1)} %convolution_convert_fusion), channel_id=1, source_target_pairs={{0,4},{4,0},{1,5},{5,1},{2,6},{6,2},{3,7},{7,3},{8,12},{12,8},{9,1... | collective-permute-start | bytes 786440 | tf_op jit(solution)/shard_map/ppermute | solution.py:175
  66.3 0.8 fusion.1
  67.1 4.0 %collective-permute-done = bf16[1024,128]{1,0:T(8,128)(2,1)S(1)} collective-permute-done((bf16[1024,128]{1,0:T(8,128)(2,1)S(1)}, bf16[1024,128]{1,0:T(8,128)(2,1)S(1)}, u32[]{:S(2)}, u32[]{:S(2)}) %collective-permute-start) | collective-permute-done | bytes 262176 | tf_op jit(solution)/shard_map/ppermute | solution.py:175
  71.2 21.9 %shard_map.112 = (bf16[2048,128]{1,0:T(8,128)(2,1)S(1)}, bf16[2048,128]{1,0:T(8,128)(2,1)S(1)}, bf16[2048,128]{1,0:T(8,128)(2,1)S(1)}, bf16[2048,128]{1,0:T(8,128)(2,1)S(1)}, bf16[4,256,1024]{2,1,0:T(8,128)(2,1)}) custom-call(bf16[2048,128]{1,0:T(8,128)(2,1)S(1)} %bitcast.113, bf16[2048,128]{1,0:T(8,128)(2,1)S(1)} %bitcast.114, ...), custom_call_target="tpu_custom_call" | custom-call | flops 6442450944 | bytes 4194304 | tf_op jit(solution)/shard_map/pallas_call | solution.py:76
  93.5 3.2 %collective-permute-start.1 = (bf16[4,1024,128]{2,1,0:T(8,128)(2,1)S(1)}, bf16[4,1024,128]{2,1,0:T(8,128)(2,1)}, u32[]{:S(2)}, u32[]{:S(2)}) collective-permute-start(bf16[4,1024,128]{2,1,0:T(8,128)(2,1)S(1)} %constant_dynamic-slice_fusion), channel_id=1, source_target_pairs={{0,4},{4,0},{1,5},{5,1},{2,6},{6,2},{3,7},{7,3},{8,12},{12,8},{9,1... | collective-permute-start | bytes 3145736 | tf_op jit(solution)/shard_map/ppermute | solution.py:188
  96.7 0.9 dynamic-slice_bitcast_fusion.4
  97.6 1.8 copy.59
  99.4 1.7 reshape.102
  101.2 1.8 copy.63
  103.0 1.8 reshape.105
  104.7 1.8 copy.61
  106.5 1.8 reshape.104
  108.3 0.9 copy.65
  109.2 1.1 reshape.106
  110.2 3.2 %convolution_bitcast_fusion.7 = f32[1,1,2,8,2,4,1024]{6,3,5,4,2,1,0:T(8,128)} fusion(bf16[1024,1024,1,1,1]{1,0,4,3,2:T(8,128)(2,1)} %bitcast.127, bf16[2,8,2,4,1024]{4,3,2,1,0:T(4,128)(2,1)} %reshape.102), kind=kOutput, calls=%fused_computation.12 | convolution fusion | flops 268435456 | bytes 2883584 | tf_op jit(solution)/shard_map/dot_general | solution.py:194
  113.4 1.3 convolution_bitcast_fusion.5
  114.7 1.3 convolution_bitcast_fusion.6
  116.1 1.3 convolution_bitcast_fusion.4
  117.4 1.0 collective-permute-done.1
  118.5 1.3 slice_bitcast_fusion.3
  120.0 2.9 %convolution_bitcast_fusion.3 = f32[1,1,2,8,2,4,1024]{6,3,5,4,2,1,0:T(8,128)} fusion(bf16[1024,1024,1,1,1]{1,0,4,3,2:T(8,128)(2,1)} %bitcast.128, bf16[2,8,2,4,1024]{4,3,2,1,0:T(4,128)(2,1)S(1)} %reshape.107), kind=kOutput, calls=%fused_computation.8 | convolution fusion | flops 268435456 | bytes 2883584 | tf_op jit(solution)/shard_map/dot_general | solution.py:194
  123.1 0.8 reshape.110
  123.9 1.5 convolution_bitcast_fusion
  125.6 2.1 %convolution_bitcast_fusion.1 = f32[1,1,2,8,2,4,1024]{6,3,5,4,2,1,0:T(8,128)S(1)} fusion(bf16[1024,1024,1,1,1]{1,0,4,3,2:T(8,128)(2,1)} %bitcast.129, bf16[2,8,2,4,1024]{4,3,2,1,0:T(4,128)(2,1)S(1)} %reshape.109), kind=kOutput, calls=%fused_computation.6 | convolution fusion | flops 268435456 | bytes 2883584 | tf_op jit(solution)/shard_map/dot_general | solution.py:196
  128.1 2.3 %convolution_bitcast_fusion.2 = f32[1,1,2,8,2,4,1024]{6,3,5,4,2,1,0:T(8,128)S(1)} fusion(bf16[1024,1024,1,1,1]{1,0,4,3,2:T(8,128)(2,1)} %bitcast.130, bf16[2,8,2,4,1024]{4,3,2,1,0:T(4,128)(2,1)S(1)} %reshape.108), kind=kOutput, calls=%fused_computation.7 | convolution fusion | flops 268435456 | bytes 2883584 | tf_op jit(solution)/shard_map/dot_general | solution.py:195
  131.0 1.6 dynamic-slice_bitcast_fusion
  132.5 1.0 copy-done.4
  133.6 4.4 %collective-permute-done.2 = f32[2,4,2,8,4,1024]{5,3,4,2,1,0:T(8,128)S(1)} collective-permute-done((f32[2,4,2,8,4,1024]{5,3,4,2,1,0:T(8,128)}, f32[2,4,2,8,4,1024]{5,3,4,2,1,0:T(8,128)S(1)}, u32[]{:S(2)}, u32[]{:S(2)}) %collective-permute-start.2) | collective-permute-done | bytes 2097184 | tf_op jit(solution)/shard_map/ppermute | solution.py:209
  137.9 2.0 fusion
  139.9 1.4 copy.75
  141.3 1.8 reshape.111
  143.1 42.0 %reduce-scatter.2.cloned.1.call-done = f32[1,512,128]{2,1,0:T(8,128)} async-done(((f32[8,512,128]{2,1,0:T(8,128)}), f32[1,512,128]{2,1,0:T(8,128)}) %reduce-scatter.2.cloned.1.call-update) | async-done | bytes 262160 | tf_op jit(solution)/shard_map/reduce_scatter | solution.py:211
  185.1 1.0 reshape.112
  186.2 1.5 collective-permute-start.3
  187.7 4.3 %collective-permute-done.3 = f32[2,4,4,1024]{3,2,1,0:T(4,128)S(1)} collective-permute-done((f32[2,4,4,1024]{3,2,1,0:T(4,128)S(1)}, f32[2,4,4,1024]{3,2,1,0:T(4,128)S(1)}, u32[]{:S(2)}, u32[]{:S(2)}) %collective-permute-start.3) | collective-permute-done | bytes 131104 | tf_op jit(solution)/shard_map/ppermute | solution.py:216
  192.0 2.4 %collective-permute-start.4 = (f32[4,4,1024]{2,1,0:T(4,128)S(1)}, f32[4,4,1024]{2,1,0:T(4,128)S(1)}, u32[]{:S(2)}, u32[]{:S(2)}) collective-permute-start(f32[4,4,1024]{2,1,0:T(4,128)S(1)} %slice_bitcast_fusion.4), channel_id=1, source_target_pairs={{0,4},{4,0},{1,5},{5,1},{2,6},{6,2},{3,7},{7,3},{8,12},{12,8},{9,1... | collective-permute-start | bytes 196616 | tf_op jit(solution)/shard_map/ppermute | solution.py:217
  194.4 3.5 %collective-permute-done.4 = f32[4,4,1024]{2,1,0:T(4,128)S(1)} collective-permute-done((f32[4,4,1024]{2,1,0:T(4,128)S(1)}, f32[4,4,1024]{2,1,0:T(4,128)S(1)}, u32[]{:S(2)}, u32[]{:S(2)}) %collective-permute-start.4) | collective-permute-done | bytes 65568 | tf_op jit(solution)/shard_map/ppermute | solution.py:217
  197.9 0.6 copy.79
  198.5 0.6 copy.78
  199.2 0.6 copy.77
  (53 shorter events, 3.1 us)
Async XLA Ops:
  7.2 52.9 %all-gather.5.cloned.1.call-start = ((), (), s32[]{:S(2)}) async-start(), calls=%async_computation.2 | async-start | bytes 2359296 | tf_op jit(solution)/shard_map/all_gather | solution.py:166
  15.7 169.5 %reduce-scatter.2.cloned.1.call-start = ((), (), s32[]{:S(2)}) async-start(), calls=%async_computation.1 | async-start | bytes 2359296 | tf_op jit(solution)/shard_map/reduce_scatter | solution.py:211
  60.1 2.2 %copy-start.5 = (bf16[4,256,1024]{2,1,0:T(8,128)(2,1)S(1)}, bf16[4,256,1024]{2,1,0:T(8,128)(2,1)}, u32[]{:S(2)}) copy-start(bf16[4,256,1024]{2,1,0:T(8,128)(2,1)} %shard_map.111) | copy-start | bytes 6291460
  63.0 8.1 %copy-start.13 = (s32[1,1,16,16]{3,2,1,0:T(8,128)S(1)}, s32[1,1,16,16]{3,2,1,0:T(8,128)}, u32[]{:S(2)}) copy-start(s32[1,1,16,16]{3,2,1,0:T(8,128)} %param.15) | copy-start | bytes 3076
  63.0 8.2 %copy-start = (bf16[1,2048,1,128]{3,1,2,0:T(8,128)(2,1)S(1)}, bf16[1,2048,1,128]{3,1,2,0:T(8,128)(2,1)}, u32[]{:S(2)}) copy-start(bf16[1,2048,1,128]{3,1,2,0:T(8,128)(2,1)} %param.11) | copy-start | bytes 1572868
  63.1 8.2 %copy-start.1 = (bf16[1,2048,1,128]{3,1,2,0:T(8,128)(2,1)S(1)}, bf16[1,2048,1,128]{3,1,2,0:T(8,128)(2,1)}, u32[]{:S(2)}) copy-start(bf16[1,2048,1,128]{3,1,2,0:T(8,128)(2,1)} %param.12) | copy-start | bytes 1572868
  63.1 8.2 %copy-start.2 = (bf16[1,2048,1,128]{3,1,2,0:T(8,128)(2,1)S(1)}, bf16[1,2048,1,128]{3,1,2,0:T(8,128)(2,1)}, u32[]{:S(2)}) copy-start(bf16[1,2048,1,128]{3,1,2,0:T(8,128)(2,1)} %param.13) | copy-start | bytes 1572868
  63.1 8.2 %copy-start.3 = (bf16[1,256,1024]{2,1,0:T(8,128)(2,1)S(1)}, bf16[1,256,1024]{2,1,0:T(8,128)(2,1)}, u32[]{:S(2)}) copy-start(bf16[1,256,1024]{2,1,0:T(8,128)(2,1)} %param.8) | copy-start | bytes 1572868
  63.1 8.0 %collective-permute-start = (bf16[1024,128]{1,0:T(8,128)(2,1)S(1)}, bf16[1024,128]{1,0:T(8,128)(2,1)S(1)}, u32[]{:S(2)}, u32[]{:S(2)}) collective-permute-start(bf16[1024,128]{1,0:T(8,128)(2,1)S(1)} %convolution_convert_fusion), channel_id=1, source_target_pairs={{0,4},{4,0},{1,5},{5,1},{2,6},{6,2},{3,7},{7,3},{8,12},{12,8},{9,1... | collective-permute-start | bytes 786440 | tf_op jit(solution)/shard_map/ppermute | solution.py:175
  93.5 25.0 %collective-permute-start.1 = (bf16[4,1024,128]{2,1,0:T(8,128)(2,1)S(1)}, bf16[4,1024,128]{2,1,0:T(8,128)(2,1)}, u32[]{:S(2)}, u32[]{:S(2)}) collective-permute-start(bf16[4,1024,128]{2,1,0:T(8,128)(2,1)S(1)} %constant_dynamic-slice_fusion), channel_id=1, source_target_pairs={{0,4},{4,0},{1,5},{5,1},{2,6},{6,2},{3,7},{7,3},{8,12},{12,8},{9,1... | collective-permute-start | bytes 3145736 | tf_op jit(solution)/shard_map/ppermute | solution.py:188
  110.2 3.2 %copy-start.11 = (bf16[2,8,2,4,1024]{4,3,2,1,0:T(4,128)(2,1)S(1)}, bf16[2,8,2,4,1024]{4,3,2,1,0:T(4,128)(2,1)}, u32[]{:S(2)}) copy-start(bf16[2,8,2,4,1024]{4,3,2,1,0:T(4,128)(2,1)} %reshape.105) | copy-start | bytes 786436
  110.2 3.2 %copy-start.14 = (bf16[4,256,1024]{2,1,0:T(8,128)(2,1)S(1)}, bf16[4,256,1024]{2,1,0:T(8,128)(2,1)}, u32[]{:S(2)}) copy-start(bf16[4,256,1024]{2,1,0:T(8,128)(2,1)} %get-tuple-element.13) | copy-start | bytes 6291460
  113.4 1.3 copy-start.12
  128.0 2.3 %copy-start.6 = (f32[1,1,2,8,2,4,1024]{6,3,5,4,2,1,0:T(8,128)S(1)}, f32[1,1,2,8,2,4,1024]{6,3,5,4,2,1,0:T(8,128)}, u32[]{:S(2)}) copy-start(f32[1,1,2,8,2,4,1024]{6,3,5,4,2,1,0:T(8,128)} %convolution_bitcast_fusion.7) | copy-start | bytes 1572868
  128.0 2.3 %copy-start.7 = (f32[1,1,2,8,2,4,1024]{6,3,5,4,2,1,0:T(8,128)S(1)}, f32[1,1,2,8,2,4,1024]{6,3,5,4,2,1,0:T(8,128)}, u32[]{:S(2)}) copy-start(f32[1,1,2,8,2,4,1024]{6,3,5,4,2,1,0:T(8,128)} %convolution_bitcast_fusion.5) | copy-start | bytes 1572868
  128.0 2.3 %copy-start.8 = (f32[1,1,2,8,2,4,1024]{6,3,5,4,2,1,0:T(8,128)S(1)}, f32[1,1,2,8,2,4,1024]{6,3,5,4,2,1,0:T(8,128)}, u32[]{:S(2)}) copy-start(f32[1,1,2,8,2,4,1024]{6,3,5,4,2,1,0:T(8,128)} %convolution_bitcast_fusion.6) | copy-start | bytes 1572868
  128.1 2.3 %copy-start.9 = (f32[1,1,2,8,2,4,1024]{6,3,5,4,2,1,0:T(8,128)S(1)}, f32[1,1,2,8,2,4,1024]{6,3,5,4,2,1,0:T(8,128)}, u32[]{:S(2)}) copy-start(f32[1,1,2,8,2,4,1024]{6,3,5,4,2,1,0:T(8,128)} %convolution_bitcast_fusion.4) | copy-start | bytes 1572868
  128.1 2.3 %copy-start.10 = (f32[1,1,2,8,2,4,1024]{6,3,5,4,2,1,0:T(8,128)S(1)}, f32[1,1,2,8,2,4,1024]{6,3,5,4,2,1,0:T(8,128)}, u32[]{:S(2)}) copy-start(f32[1,1,2,8,2,4,1024]{6,3,5,4,2,1,0:T(8,128)} %convolution_bitcast_fusion.3) | copy-start | bytes 1572868
  131.0 2.6 %copy-start.4 = (f32[2,4,2,8,2,4,1024]{6,3,5,4,2,1,0:T(8,128)}, f32[2,4,2,8,2,4,1024]{6,3,5,4,2,1,0:T(8,128)S(1)}, u32[]{:S(2)}) copy-start(f32[2,4,2,8,2,4,1024]{6,3,5,4,2,1,0:T(8,128)S(1)} %maximum_maximum_fusion) | copy-start | bytes 12582916
  133.6 4.4 %collective-permute-start.2 = (f32[2,4,2,8,4,1024]{5,3,4,2,1,0:T(8,128)}, f32[2,4,2,8,4,1024]{5,3,4,2,1,0:T(8,128)S(1)}, u32[]{:S(2)}, u32[]{:S(2)}) collective-permute-start(f32[2,4,2,8,4,1024]{5,3,4,2,1,0:T(8,128)} %dynamic-slice_bitcast_fusion), channel_id=1, source_target_pairs={{0,8},{8,0},{1,9},{9,1},{2,10},{10,2},{3,11},{11,3},{4,12},{12,4},... | collective-permute-start | bytes 6291464 | tf_op jit(solution)/shard_map/ppermute | solution.py:209
  186.2 5.8 %collective-permute-start.3 = (f32[2,4,4,1024]{3,2,1,0:T(4,128)S(1)}, f32[2,4,4,1024]{3,2,1,0:T(4,128)S(1)}, u32[]{:S(2)}, u32[]{:S(2)}) collective-permute-start(f32[2,4,4,1024]{3,2,1,0:T(4,128)S(1)} %dynamic-slice_bitcast_fusion.5), channel_id=1, source_target_pairs={{0,128},{128,0},{1,129},{129,1},{2,130},{130,2},{3,131},{131,3},{4... | collective-permute-start | bytes 393224 | tf_op jit(solution)/shard_map/ppermute | solution.py:216
  192.0 5.9 %collective-permute-start.4 = (f32[4,4,1024]{2,1,0:T(4,128)S(1)}, f32[4,4,1024]{2,1,0:T(4,128)S(1)}, u32[]{:S(2)}, u32[]{:S(2)}) collective-permute-start(f32[4,4,1024]{2,1,0:T(4,128)S(1)} %slice_bitcast_fusion.4), channel_id=1, source_target_pairs={{0,4},{4,0},{1,5},{5,1},{2,6},{6,2},{3,7},{7,3},{8,12},{12,8},{9,1... | collective-permute-start | bytes 196616 | tf_op jit(solution)/shard_map/ppermute | solution.py:217
Sparse Core Ops, SparseCore 0:
  15.8 44.2 all-gather.4
  143.3 41.8 reduce-scatter.1

commit v10 on v9

--- a/solution.py
+++ b/solution.py
@@ -161,8 +161,7 @@
     swap = [(0, 1), (1, 0)]
     masked = d_output[0] * loss_mask[0][:, None].astype(jnp.bfloat16)
     own_rows, width = out_weight.shape
-    gathered = lax.all_gather(out_weight, "dpc", axis=0)
-    gathered = lax.all_gather(gathered, "dpy", axis=0)
+    gathered = lax.all_gather(out_weight, ("dpy", "dpc"), axis=0).reshape((2, 2) + out_weight.shape)
     gathered = lax.all_gather(gathered, "dpz", axis=0)
     gathered = jnp.transpose(gathered, (1, 0, 2, 3, 4)).reshape(-1, width)
     head_weight = lax.dynamic_slice_in_dim(gathered, head * HD, HD, 0)

time: 208 us -> 206 us (level)
  matrix products: 17.5 us -> 20 us
  local copies, waits for them, and re-layouts: 28.4 us -> 26.1 us
    all_gather x2 -> x1, blocking collectives: 8.44 us -> 7.45 us  [local(): lax.all_gather(out_weight, ('dpy', 'dpc'), axis=0)]
where the time goes in v10:
time: 206 us; the launch traced here: 205 us
  waiting for transfers between devices  72.5 us (35%)
  Pallas kernels  48.5 us (24%)
  local copies, waits for them, and re-layouts  26.1 us (13%)
  matrix products  20 us (10%)
  between operations  14.5 us (7%)
  starting transfers between devices  10.6 us (5%)
  blocking collectives  7.45 us (4%)
  other arithmetic  5.49 us (3%)
    reduce_scatter x1, waiting for transfers between devices, local(): lax.psum_scatter(terms.reshape(nz, -1, 128), 'dpz', scatter_dimension=0,...  41.8 us
    pallas_call x1, Pallas kernels, seq_gather(): pl.pallas_call(functools.partial(gather_kernel, nseq), in_specs=[any_spec...  26.6 us
    pallas_call x1, Pallas kernels, attention_backward(): pl.pallas_call(functools.partial(attention_kernel, nseq), grid=(length //...  21.9 us
    all_gather x1, waiting for transfers between devices, local(): gathered = lax.all_gather(gathered, 'dpz', axis=0)  14.9 us
    another operation x8, local copies, waits for them, and re-layouts  7.47 us
    all_gather x1, blocking collectives, local(): lax.all_gather(out_weight, ('dpy', 'dpc'), axis=0)  7.45 us
    dot_general x2, matrix products, terms_of(): lax.dot_general(parts[0], inputs_half, tn, preferred_element_type=jnp.flo...  6.09 us
    ppermute x1, waiting for transfers between devices, local(): terms = kept + lax.ppermute(sent, 'dpc', swap)  4.37 us
  transfers between devices with their start and end apart: 7, of which 7 were waited for; matrix products, arithmetic and copies ran while one was open for 12% of the time, Pallas kernels for 13%

profile of v10, /device:TPU:2, one launch (start us, length us, event | category | flops | bytes accessed | tf_op | source)
XLA Modules:
  0.0 205.2 jit_solution(10808088358781378763)
XLA Ops:
  7.2 7.5 %all-gather = bf16[128,1024]{1,0:T(8,128)(2,1)} all-gather(bf16[32,1024]{1,0:T(8,128)(2,1)} %param.14), channel_id=2, replica_groups=mesh['dpy'=2,'dpz'=8,'dpc'=2,'sqy'=2,'sqx'=4] {'dpy','dpc'}, dimensions={0}, use_global_device_ids=true | all-gather | bytes 327680 | tf_op jit(solution)/shard_map/all_gather | solution.py:164
  14.8 0.7 convert_reduce_fusion
  15.4 1.9 bitcast_multiply_fusion.a_ref
  17.4 26.6 %shard_map.111 = bf16[4,256,1024]{2,1,0:T(8,128)(2,1)} custom-call(bf16[256,1024]{1,0:T(8,128)(2,1)} %bitcast_multiply_fusion.a_ref), custom_call_target="tpu_custom_call" | custom-call | tf_op jit(solution)/shard_map/pallas_call | solution.py:136
  44.0 14.9 %all-gather.3.cloned.1.call-done = bf16[8,2,2,32,1024]{4,3,2,0,1:T(8,128)(2,1)} async-done(((bf16[1,2,2,32,1024]{4,3,2,0,1:T(8,128)(2,1)}), bf16[8,2,2,32,1024]{4,3,2,0,1:T(8,128)(2,1)}) %all-gather.3.cloned.1.call-update) | async-done | bytes 2097168 | tf_op jit(solution)/shard_map/all_gather | solution.py:165
  58.8 2.3 %convolution_convert_fusion = bf16[1024,128]{1,0:T(8,128)(2,1)S(1)} fusion(bf16[1024,1024]{1,0:T(8,128)(2,1)} %bitcast.115, bf16[1024,1024]{1,0:T(8,128)(2,1)} %bitcast.120, s32[]{:T(128)S(6)} %select_n.30), kind=kOutput, calls=%fused_computation.13 | convolution fusion | flops 268566528 | bytes 2621444 | tf_op jit(solution)/shard_map/dot_general | solution.py:173
  61.2 3.1 %collective-permute-start = (bf16[1024,128]{1,0:T(8,128)(2,1)S(1)}, bf16[1024,128]{1,0:T(8,128)(2,1)S(1)}, u32[]{:S(2)}, u32[]{:S(2)}) collective-permute-start(bf16[1024,128]{1,0:T(8,128)(2,1)S(1)} %convolution_convert_fusion), channel_id=1, source_target_pairs={{0,4},{4,0},{1,5},{5,1},{2,6},{6,2},{3,7},{7,3},{8,12},{12,8},{9,1... | collective-permute-start | bytes 786440 | tf_op jit(solution)/shard_map/ppermute | solution.py:174
  64.4 1.8 fusion.1
  66.2 3.0 %collective-permute-done = bf16[1024,128]{1,0:T(8,128)(2,1)S(1)} collective-permute-done((bf16[1024,128]{1,0:T(8,128)(2,1)S(1)}, bf16[1024,128]{1,0:T(8,128)(2,1)S(1)}, u32[]{:S(2)}, u32[]{:S(2)}) %collective-permute-start) | collective-permute-done | bytes 262176 | tf_op jit(solution)/shard_map/ppermute | solution.py:174
  69.3 21.9 %shard_map.112 = (bf16[2048,128]{1,0:T(8,128)(2,1)S(1)}, bf16[2048,128]{1,0:T(8,128)(2,1)S(1)}, bf16[2048,128]{1,0:T(8,128)(2,1)S(1)}, bf16[2048,128]{1,0:T(8,128)(2,1)S(1)}, bf16[4,256,1024]{2,1,0:T(8,128)(2,1)}) custom-call(bf16[2048,128]{1,0:T(8,128)(2,1)S(1)} %bitcast.111, bf16[2048,128]{1,0:T(8,128)(2,1)S(1)} %bitcast.112, ...), custom_call_target="tpu_custom_call" | custom-call | flops 6442450944 | bytes 4194304 | tf_op jit(solution)/shard_map/pallas_call | solution.py:76
  91.6 3.3 %collective-permute-start.1 = (bf16[4,1024,128]{2,1,0:T(8,128)(2,1)S(1)}, bf16[4,1024,128]{2,1,0:T(8,128)(2,1)}, u32[]{:S(2)}, u32[]{:S(2)}) collective-permute-start(bf16[4,1024,128]{2,1,0:T(8,128)(2,1)S(1)} %constant_dynamic-slice_fusion), channel_id=1, source_target_pairs={{0,4},{4,0},{1,5},{5,1},{2,6},{6,2},{3,7},{7,3},{8,12},{12,8},{9,1... | collective-permute-start | bytes 3145736 | tf_op jit(solution)/shard_map/ppermute | solution.py:187
  94.9 0.9 dynamic-slice_bitcast_fusion.4
  95.8 1.8 copy.36
  97.6 1.7 reshape.102
  99.4 1.8 copy.40
  101.2 1.8 reshape.105
  102.9 1.8 copy.38
  104.7 1.8 reshape.104
  106.5 0.9 copy.42
  107.3 1.1 reshape.106
  108.4 3.2 %convolution_bitcast_fusion.7 = f32[1,1,2,8,2,4,1024]{6,3,5,4,2,1,0:T(8,128)} fusion(bf16[1024,1024,1,1,1]{1,0,4,3,2:T(8,128)(2,1)} %bitcast.123, bf16[2,8,2,4,1024]{4,3,2,1,0:T(4,128)(2,1)} %reshape.102), kind=kOutput, calls=%fused_computation.12 | convolution fusion | flops 268435456 | bytes 2883584 | tf_op jit(solution)/shard_map/dot_general | solution.py:193
  111.6 1.3 convolution_bitcast_fusion.5
  112.9 1.3 convolution_bitcast_fusion.6
  114.3 1.3 convolution_bitcast_fusion.4
  115.6 1.0 collective-permute-done.1
  116.6 1.3 slice_bitcast_fusion.3
  118.1 2.9 %convolution_bitcast_fusion.3 = f32[1,1,2,8,2,4,1024]{6,3,5,4,2,1,0:T(8,128)} fusion(bf16[1024,1024,1,1,1]{1,0,4,3,2:T(8,128)(2,1)} %bitcast.124, bf16[2,8,2,4,1024]{4,3,2,1,0:T(4,128)(2,1)S(1)} %reshape.107), kind=kOutput, calls=%fused_computation.8 | convolution fusion | flops 268435456 | bytes 2883584 | tf_op jit(solution)/shard_map/dot_general | solution.py:193
  121.2 0.8 reshape.110
  122.0 1.5 convolution_bitcast_fusion
  123.8 2.1 %convolution_bitcast_fusion.1 = f32[1,1,2,8,2,4,1024]{6,3,5,4,2,1,0:T(8,128)S(1)} fusion(bf16[1024,1024,1,1,1]{1,0,4,3,2:T(8,128)(2,1)} %bitcast.125, bf16[2,8,2,4,1024]{4,3,2,1,0:T(4,128)(2,1)S(1)} %reshape.109), kind=kOutput, calls=%fused_computation.6 | convolution fusion | flops 268435456 | bytes 2883584 | tf_op jit(solution)/shard_map/dot_general | solution.py:195
  126.2 2.3 %convolution_bitcast_fusion.2 = f32[1,1,2,8,2,4,1024]{6,3,5,4,2,1,0:T(8,128)S(1)} fusion(bf16[1024,1024,1,1,1]{1,0,4,3,2:T(8,128)(2,1)} %bitcast.126, bf16[2,8,2,4,1024]{4,3,2,1,0:T(4,128)(2,1)S(1)} %reshape.108), kind=kOutput, calls=%fused_computation.7 | convolution fusion | flops 268435456 | bytes 2883584 | tf_op jit(solution)/shard_map/dot_general | solution.py:194
  128.5 0.5 maximum_maximum_fusion
  129.1 1.6 dynamic-slice_bitcast_fusion
  130.7 1.0 copy-done.4
  131.7 4.4 %collective-permute-done.2 = f32[2,4,2,8,4,1024]{5,3,4,2,1,0:T(8,128)S(1)} collective-permute-done((f32[2,4,2,8,4,1024]{5,3,4,2,1,0:T(8,128)}, f32[2,4,2,8,4,1024]{5,3,4,2,1,0:T(8,128)S(1)}, u32[]{:S(2)}, u32[]{:S(2)}) %collective-permute-start.2) | collective-permute-done | bytes 2097184 | tf_op jit(solution)/shard_map/ppermute | solution.py:208
  136.1 2.0 fusion
  138.0 1.4 copy.52
  139.4 1.8 reshape.111
  141.3 41.8 %reduce-scatter.2.cloned.1.call-done = f32[1,512,128]{2,1,0:T(8,128)} async-done(((f32[8,512,128]{2,1,0:T(8,128)}), f32[1,512,128]{2,1,0:T(8,128)}) %reduce-scatter.2.cloned.1.call-update) | async-done | bytes 262160 | tf_op jit(solution)/shard_map/reduce_scatter | solution.py:210
  183.1 1.0 reshape.112
  184.2 1.6 collective-permute-start.3
  185.8 4.2 %collective-permute-done.3 = f32[2,4,4,1024]{3,2,1,0:T(4,128)S(1)} collective-permute-done((f32[2,4,4,1024]{3,2,1,0:T(4,128)S(1)}, f32[2,4,4,1024]{3,2,1,0:T(4,128)S(1)}, u32[]{:S(2)}, u32[]{:S(2)}) %collective-permute-start.3) | collective-permute-done | bytes 131104 | tf_op jit(solution)/shard_map/ppermute | solution.py:215
  190.0 2.6 %collective-permute-start.4 = (f32[4,4,1024]{2,1,0:T(4,128)S(1)}, f32[4,4,1024]{2,1,0:T(4,128)S(1)}, u32[]{:S(2)}, u32[]{:S(2)}) collective-permute-start(f32[4,4,1024]{2,1,0:T(4,128)S(1)} %slice_bitcast_fusion.4), channel_id=1, source_target_pairs={{0,4},{4,0},{1,5},{5,1},{2,6},{6,2},{3,7},{7,3},{8,12},{12,8},{9,1... | collective-permute-start | bytes 196616 | tf_op jit(solution)/shard_map/ppermute | solution.py:216
  192.5 3.3 %collective-permute-done.4 = f32[4,4,1024]{2,1,0:T(4,128)S(1)} collective-permute-done((f32[4,4,1024]{2,1,0:T(4,128)S(1)}, f32[4,4,1024]{2,1,0:T(4,128)S(1)}, u32[]{:S(2)}, u32[]{:S(2)}) %collective-permute-start.4) | collective-permute-done | bytes 65568 | tf_op jit(solution)/shard_map/ppermute | solution.py:216
  195.9 0.6 copy.56
  196.5 0.6 copy.55
  197.1 0.6 copy.54
  197.7 0.6 copy.53
  (51 shorter events, 1.7 us)
Async XLA Ops:
  7.2 51.7 %all-gather.3.cloned.1.call-start = ((), (), s32[]{:S(2)}) async-start(), calls=%async_computation.1 | async-start | bytes 2359296 | tf_op jit(solution)/shard_map/all_gather | solution.py:165
  14.7 168.4 %reduce-scatter.2.cloned.1.call-start = ((), (), s32[]{:S(2)}) async-start(), calls=%async_computation.2 | async-start | bytes 2359296 | tf_op jit(solution)/shard_map/reduce_scatter | solution.py:210
  44.0 20.4 %copy-start.5 = (bf16[4,256,1024]{2,1,0:T(8,128)(2,1)S(1)}, bf16[4,256,1024]{2,1,0:T(8,128)(2,1)}, u32[]{:S(2)}) copy-start(bf16[4,256,1024]{2,1,0:T(8,128)(2,1)} %shard_map.111) | copy-start | bytes 6291460
  61.1 8.1 %copy-start.13 = (s32[1,1,16,16]{3,2,1,0:T(8,128)S(1)}, s32[1,1,16,16]{3,2,1,0:T(8,128)}, u32[]{:S(2)}) copy-start(s32[1,1,16,16]{3,2,1,0:T(8,128)} %param.15) | copy-start | bytes 3076
  61.2 8.2 %copy-start = (bf16[1,2048,1,128]{3,1,2,0:T(8,128)(2,1)S(1)}, bf16[1,2048,1,128]{3,1,2,0:T(8,128)(2,1)}, u32[]{:S(2)}) copy-start(bf16[1,2048,1,128]{3,1,2,0:T(8,128)(2,1)} %param.11) | copy-start | bytes 1572868
  61.2 8.2 %copy-start.1 = (bf16[1,2048,1,128]{3,1,2,0:T(8,128)(2,1)S(1)}, bf16[1,2048,1,128]{3,1,2,0:T(8,128)(2,1)}, u32[]{:S(2)}) copy-start(bf16[1,2048,1,128]{3,1,2,0:T(8,128)(2,1)} %param.12) | copy-start | bytes 1572868
  61.2 8.2 %copy-start.2 = (bf16[1,2048,1,128]{3,1,2,0:T(8,128)(2,1)S(1)}, bf16[1,2048,1,128]{3,1,2,0:T(8,128)(2,1)}, u32[]{:S(2)}) copy-start(bf16[1,2048,1,128]{3,1,2,0:T(8,128)(2,1)} %param.13) | copy-start | bytes 1572868
  61.2 8.2 %copy-start.3 = (bf16[1,256,1024]{2,1,0:T(8,128)(2,1)S(1)}, bf16[1,256,1024]{2,1,0:T(8,128)(2,1)}, u32[]{:S(2)}) copy-start(bf16[1,256,1024]{2,1,0:T(8,128)(2,1)} %param.8) | copy-start | bytes 1572868
  61.2 8.0 %collective-permute-start = (bf16[1024,128]{1,0:T(8,128)(2,1)S(1)}, bf16[1024,128]{1,0:T(8,128)(2,1)S(1)}, u32[]{:S(2)}, u32[]{:S(2)}) collective-permute-start(bf16[1024,128]{1,0:T(8,128)(2,1)S(1)} %convolution_convert_fusion), channel_id=1, source_target_pairs={{0,4},{4,0},{1,5},{5,1},{2,6},{6,2},{3,7},{7,3},{8,12},{12,8},{9,1... | collective-permute-start | bytes 786440 | tf_op jit(solution)/shard_map/ppermute | solution.py:174
  91.6 25.0 %collective-permute-start.1 = (bf16[4,1024,128]{2,1,0:T(8,128)(2,1)S(1)}, bf16[4,1024,128]{2,1,0:T(8,128)(2,1)}, u32[]{:S(2)}, u32[]{:S(2)}) collective-permute-start(bf16[4,1024,128]{2,1,0:T(8,128)(2,1)S(1)} %constant_dynamic-slice_fusion), channel_id=1, source_target_pairs={{0,4},{4,0},{1,5},{5,1},{2,6},{6,2},{3,7},{7,3},{8,12},{12,8},{9,1... | collective-permute-start | bytes 3145736 | tf_op jit(solution)/shard_map/ppermute | solution.py:187
  108.4 3.2 %copy-start.11 = (bf16[2,8,2,4,1024]{4,3,2,1,0:T(4,128)(2,1)S(1)}, bf16[2,8,2,4,1024]{4,3,2,1,0:T(4,128)(2,1)}, u32[]{:S(2)}) copy-start(bf16[2,8,2,4,1024]{4,3,2,1,0:T(4,128)(2,1)} %reshape.105) | copy-start | bytes 786436
  108.4 3.2 %copy-start.14 = (bf16[4,256,1024]{2,1,0:T(8,128)(2,1)S(1)}, bf16[4,256,1024]{2,1,0:T(8,128)(2,1)}, u32[]{:S(2)}) copy-start(bf16[4,256,1024]{2,1,0:T(8,128)(2,1)} %get-tuple-element.13) | copy-start | bytes 6291460
  111.6 1.3 copy-start.12
  126.1 2.3 %copy-start.6 = (f32[1,1,2,8,2,4,1024]{6,3,5,4,2,1,0:T(8,128)S(1)}, f32[1,1,2,8,2,4,1024]{6,3,5,4,2,1,0:T(8,128)}, u32[]{:S(2)}) copy-start(f32[1,1,2,8,2,4,1024]{6,3,5,4,2,1,0:T(8,128)} %convolution_bitcast_fusion.7) | copy-start | bytes 1572868
  126.2 2.3 %copy-start.7 = (f32[1,1,2,8,2,4,1024]{6,3,5,4,2,1,0:T(8,128)S(1)}, f32[1,1,2,8,2,4,1024]{6,3,5,4,2,1,0:T(8,128)}, u32[]{:S(2)}) copy-start(f32[1,1,2,8,2,4,1024]{6,3,5,4,2,1,0:T(8,128)} %convolution_bitcast_fusion.5) | copy-start | bytes 1572868
  126.2 2.3 %copy-start.8 = (f32[1,1,2,8,2,4,1024]{6,3,5,4,2,1,0:T(8,128)S(1)}, f32[1,1,2,8,2,4,1024]{6,3,5,4,2,1,0:T(8,128)}, u32[]{:S(2)}) copy-start(f32[1,1,2,8,2,4,1024]{6,3,5,4,2,1,0:T(8,128)} %convolution_bitcast_fusion.6) | copy-start | bytes 1572868
  126.2 2.3 %copy-start.9 = (f32[1,1,2,8,2,4,1024]{6,3,5,4,2,1,0:T(8,128)S(1)}, f32[1,1,2,8,2,4,1024]{6,3,5,4,2,1,0:T(8,128)}, u32[]{:S(2)}) copy-start(f32[1,1,2,8,2,4,1024]{6,3,5,4,2,1,0:T(8,128)} %convolution_bitcast_fusion.4) | copy-start | bytes 1572868
  126.2 2.3 %copy-start.10 = (f32[1,1,2,8,2,4,1024]{6,3,5,4,2,1,0:T(8,128)S(1)}, f32[1,1,2,8,2,4,1024]{6,3,5,4,2,1,0:T(8,128)}, u32[]{:S(2)}) copy-start(f32[1,1,2,8,2,4,1024]{6,3,5,4,2,1,0:T(8,128)} %convolution_bitcast_fusion.3) | copy-start | bytes 1572868
  129.1 2.6 %copy-start.4 = (f32[2,4,2,8,2,4,1024]{6,3,5,4,2,1,0:T(8,128)}, f32[2,4,2,8,2,4,1024]{6,3,5,4,2,1,0:T(8,128)S(1)}, u32[]{:S(2)}) copy-start(f32[2,4,2,8,2,4,1024]{6,3,5,4,2,1,0:T(8,128)S(1)} %maximum_maximum_fusion) | copy-start | bytes 12582916
  131.7 4.4 %collective-permute-start.2 = (f32[2,4,2,8,4,1024]{5,3,4,2,1,0:T(8,128)}, f32[2,4,2,8,4,1024]{5,3,4,2,1,0:T(8,128)S(1)}, u32[]{:S(2)}, u32[]{:S(2)}) collective-permute-start(f32[2,4,2,8,4,1024]{5,3,4,2,1,0:T(8,128)} %dynamic-slice_bitcast_fusion), channel_id=1, source_target_pairs={{0,8},{8,0},{1,9},{9,1},{2,10},{10,2},{3,11},{11,3},{4,12},{12,4},... | collective-permute-start | bytes 6291464 | tf_op jit(solution)/shard_map/ppermute | solution.py:208
  184.2 5.8 %collective-permute-start.3 = (f32[2,4,4,1024]{3,2,1,0:T(4,128)S(1)}, f32[2,4,4,1024]{3,2,1,0:T(4,128)S(1)}, u32[]{:S(2)}, u32[]{:S(2)}) collective-permute-start(f32[2,4,4,1024]{3,2,1,0:T(4,128)S(1)} %dynamic-slice_bitcast_fusion.5), channel_id=1, source_target_pairs={{0,128},{128,0},{1,129},{129,1},{2,130},{130,2},{3,131},{131,3},{4... | collective-permute-start | bytes 393224 | tf_op jit(solution)/shard_map/ppermute | solution.py:215
  190.0 5.9 %collective-permute-start.4 = (f32[4,4,1024]{2,1,0:T(4,128)S(1)}, f32[4,4,1024]{2,1,0:T(4,128)S(1)}, u32[]{:S(2)}, u32[]{:S(2)}) collective-permute-start(f32[4,4,1024]{2,1,0:T(4,128)S(1)} %slice_bitcast_fusion.4), channel_id=1, source_target_pairs={{0,4},{4,0},{1,5},{5,1},{2,6},{6,2},{3,7},{7,3},{8,12},{12,8},{9,1... | collective-permute-start | bytes 196616 | tf_op jit(solution)/shard_map/ppermute | solution.py:216
Sparse Core Ops, SparseCore 0:
  14.8 43.9 all-gather.2
  141.4 41.6 reduce-scatter.1

commit v11 on v10

--- a/solution.py
+++ b/solution.py
@@ -122,29 +122,33 @@
     pl.semaphore_wait(barrier, nseq - 1)
 
 
-def gather_kernel(nseq, a_ref, a_out, send_sem, recv_sem, copy_sem):
+def gather_kernel(nseq, a_ref, b_ref, a_out, b_out, send_sem, recv_sem, copy_sem):
     enter_barrier(nseq)
-    copies = start_gather(nseq, a_ref, a_out, send_sem, recv_sem, copy_sem)
+    copies = start_gather(nseq, a_ref, a_out, send_sem.at[0], recv_sem.at[0], copy_sem.at[0])
+    copies += start_gather(nseq, b_ref, b_out, send_sem.at[1], recv_sem.at[1], copy_sem.at[1])
     for copy in copies:
         copy.start()
     for copy in copies:
         copy.wait()
 
 
-def seq_gather(a, nseq):
+def seq_gather(a, b, nseq):
     any_spec = pl.BlockSpec(memory_space=pl.ANY)
     return pl.pallas_call(
         functools.partial(gather_kernel, nseq),
-        in_specs=[any_spec],
-        out_specs=any_spec,
-        out_shape=jax.ShapeDtypeStruct((nseq,) + a.shape, a.dtype),
+        in_specs=[any_spec, any_spec],
+        out_specs=[any_spec, any_spec],
+        out_shape=[
+            jax.ShapeDtypeStruct((nseq,) + a.shape, a.dtype),
+            jax.ShapeDtypeStruct((nseq,) + b.shape, b.dtype),
+        ],
         scratch_shapes=[
-            pltpu.SemaphoreType.DMA((nseq - 1,)),
-            pltpu.SemaphoreType.DMA((nseq - 1,)),
-            pltpu.SemaphoreType.DMA(()),
+            pltpu.SemaphoreType.DMA((2, nseq - 1)),
+            pltpu.SemaphoreType.DMA((2, nseq - 1)),
+            pltpu.SemaphoreType.DMA((2,)),
         ],
         compiler_params=pltpu.CompilerParams(collective_id=0, has_side_effects=True),
-    )(a)
+    )(a, b)
 
 
 DP = ("dpy", "dpz", "dpc")
@@ -166,7 +170,11 @@
     gathered = jnp.transpose(gathered, (1, 0, 2, 3, 4)).reshape(-1, width)
     head_weight = lax.dynamic_slice_in_dim(gathered, head * HD, HD, 0)
     partner_weight = lax.dynamic_slice_in_dim(gathered, partner_head * HD, HD, 0)
-    masked_half = seq_gather(masked, sizes["sqx"]).reshape(-1, width)
+    slab = inputs.shape[1]
+    lead = slab // 2
+    masked_half, inputs_lead = seq_gather(masked, inputs[0, :lead], sizes["sqx"])
+    masked_half = masked_half.reshape(-1, width)
+    inputs_lead = inputs_lead.reshape(-1, width)
     half_len = masked_half.shape[0]
     nt = (((1,), (1,)), ((), ()))
     d_own = lax.dot_general(masked_half, head_weight, nt, preferred_element_type=jnp.float32).astype(jnp.bfloat16)
@@ -178,21 +186,29 @@
     blocks = block_mask[0, 0]
     live_cols = jnp.repeat(blocks, BLOCK, axis=1)[:, None, :]
     d_query, attended, d_key, d_value, inputs_half = attention_backward(
-        queries[0, :, 0], keys[0, :, 0], values[0, :, 0], d_attn, live_cols, inputs[0], sizes["sqx"]
+        queries[0, :, 0], keys[0, :, 0], values[0, :, 0], d_attn, live_cols, inputs[0, lead:], sizes["sqx"]
     )
-    inputs_half = inputs_half.reshape(-1, width)
+    inputs_tail = inputs_half.reshape(-1, width)
     grads = jnp.stack([d_query, d_key, d_value, attended])
     grads_own = lax.dynamic_slice_in_dim(grads, half * half_len, half_len, 1)
     grads_give = lax.dynamic_slice_in_dim(grads, other * half_len, half_len, 1)
     grads_got = lax.ppermute(grads_give, "sqy", swap)
     tn = (((0,), (0,)), ((), ()))
 
+    def by_inputs(part):
+        rows = part.reshape(sizes["sqx"], slab, HD)
+        lead_rows = rows[:, :lead].reshape(-1, HD)
+        tail_rows = rows[:, lead:].reshape(-1, HD)
+        return lax.dot_general(lead_rows, inputs_lead, tn, preferred_element_type=jnp.float32) + lax.dot_general(
+            tail_rows, inputs_tail, tn, preferred_element_type=jnp.float32
+        )
+
     def terms_of(parts):
         return jnp.stack(
             [
-                lax.dot_general(parts[0], inputs_half, tn, preferred_element_type=jnp.float32),
-                lax.dot_general(parts[1], inputs_half, tn, preferred_element_type=jnp.float32),
-                lax.dot_general(parts[2], inputs_half, tn, preferred_element_type=jnp.float32),
+                by_inputs(parts[0]),
+                by_inputs(parts[1]),
+                by_inputs(parts[2]),
                 lax.dot_general(parts[3], masked_half, tn, preferred_element_type=jnp.float32),
             ],
             axis=0,

time: 206 us -> 225 us (1.092)
  Pallas kernels: 48.5 us -> 60.9 us
  local copies, waits for them, and re-layouts: 26.1 us -> 35.1 us
    all_gather x1, waiting for transfers between devices: 14.9 us -> 1.79 us  [local(): gathered = lax.all_gather(gathered, 'dpz', axis=0)]
    pallas_call x1, Pallas kernels: 26.6 us -> 37.9 us  [seq_gather(): pl.pallas_call(functools.partial(gather_kernel, nseq), in_specs=[any_spec...]
    another operation x8 -> x14, local copies, waits for them, and re-layouts: 7.47 us -> 18.5 us  [the longest x12 16.9 us: terms_of(): jnp.stack([by_inputs(parts[0]), by_inputs(parts[1]), by_inputs(parts[2]),...]
    ppermute x1, waiting for transfers between devices: 0.98 us -> 9.51 us  [local(): grads_got = lax.ppermute(grads_give, 'sqy', swap)]
    dot_general x8 -> x0, local copies, waits for them, and re-layouts: 7.99 us -> none  [the longest x4 4.12 us: terms_of(): lax.dot_general(parts[0], inputs_half, tn, preferred_element_type=jnp.flo...]
    dot_general x6 -> x12, matrix products: 13.2 us -> 8.05 us  [the longest x6 5.27 us: by_inputs(): lax.dot_general(lead_rows, inputs_lead, tn, preferred_element_type=jnp.fl...]
    dot_general x2, matrix products: 2.81 us -> 6 us  [terms_of(): lax.dot_general(parts[3], masked_half, tn, preferred_element_type=jnp.flo...]
    reduce_scatter x1, waiting for transfers between devices: 41.8 us -> 44.9 us  [local(): lax.psum_scatter(terms.reshape(nz, -1, 128), 'dpz', scatter_dimension=0,...]
  transfers between devices with their start and end apart: 7 -> 7, of which waited for: 7 -> 7; matrix products, arithmetic and copies ran while one was open for 12% -> 8% of each run, Pallas kernels for 13% -> 17%
where the time goes in v11:
time: 225 us; the launch traced here: 224 us
  waiting for transfers between devices  71.1 us (32%)
  Pallas kernels  60.9 us (27%)
  local copies, waits for them, and re-layouts  35.1 us (16%)
  matrix products  18.1 us (8%)
  between operations  14.4 us (6%)
  starting transfers between devices  10.4 us (5%)
  blocking collectives  7.45 us (3%)
  other arithmetic  6.46 us (3%)
    reduce_scatter x1, waiting for transfers between devices, local(): lax.psum_scatter(terms.reshape(nz, -1, 128), 'dpz', scatter_dimension=0,...  44.9 us
    pallas_call x1, Pallas kernels, seq_gather(): pl.pallas_call(functools.partial(gather_kernel, nseq), in_specs=[any_spec...  37.9 us
    pallas_call x1, Pallas kernels, attention_backward(): pl.pallas_call(functools.partial(attention_kernel, nseq), grid=(length //...  23 us
    another operation x12, local copies, waits for them, and re-layouts, terms_of(): jnp.stack([by_inputs(parts[0]), by_inputs(parts[1]), by_inputs(parts[2]),...  16.9 us
    ppermute x1, waiting for transfers between devices, local(): grads_got = lax.ppermute(grads_give, 'sqy', swap)  9.51 us
    all_gather x1, blocking collectives, local(): lax.all_gather(out_weight, ('dpy', 'dpc'), axis=0)  7.45 us
    dot_general x2, matrix products, terms_of(): lax.dot_general(parts[3], masked_half, tn, preferred_element_type=jnp.flo...  6 us
    dot_general x6, matrix products, by_inputs(): lax.dot_general(lead_rows, inputs_lead, tn, preferred_element_type=jnp.fl...  5.27 us
  transfers between devices with their start and end apart: 7, of which 7 were waited for; matrix products, arithmetic and copies ran while one was open for 8% of the time, Pallas kernels for 17%

profile of v11, /device:TPU:2, one launch (start us, length us, event | category | flops | bytes accessed | tf_op | source)
XLA Modules:
  0.0 223.9 jit_solution(2761655291979786734)
XLA Ops:
  7.2 7.4 %all-gather = bf16[128,1024]{1,0:T(8,128)(2,1)} all-gather(bf16[32,1024]{1,0:T(8,128)(2,1)} %param.14), channel_id=2, replica_groups=mesh['dpy'=2,'dpz'=8,'dpc'=2,'sqy'=2,'sqx'=4] {'dpy','dpc'}, dimensions={0}, use_global_device_ids=true | all-gather | bytes 327680 | tf_op jit(solution)/shard_map/all_gather | solution.py:168
  15.4 1.8 slice_bitcast_fusion.1
  17.2 1.9 bitcast_multiply_fusion.a_ref
  19.2 37.9 %shard_map.111 = (bf16[4,256,1024]{2,1,0:T(8,128)(2,1)}, bf16[4,128,1024]{2,1,0:T(8,128)(2,1)}) custom-call(bf16[256,1024]{1,0:T(8,128)(2,1)} %bitcast_multiply_fusion.a_ref, bf16[128,1024]{1,0:T(8,128)(2,1)} %get-tuple-element.31.b_ref), custom_call_target="tpu_custom_call" | custom-call | tf_op jit(solution)/shard_map/pallas_call | solution.py:137
  57.0 1.8 all-gather.3.cloned.1.call-done
  58.8 2.3 %convolution_convert_fusion = bf16[1024,128]{1,0:T(8,128)(2,1)S(1)} fusion(bf16[1024,1024]{1,0:T(8,128)(2,1)} %bitcast.124, bf16[1024,1024]{1,0:T(8,128)(2,1)} %bitcast.141, s32[]{:T(128)S(6)} %select_n.30), kind=kOutput, calls=%fused_computation.25 | convolution fusion | flops 268566528 | bytes 2621444 | tf_op jit(solution)/shard_map/dot_general | solution.py:181
  61.2 3.1 %collective-permute-start = (bf16[1024,128]{1,0:T(8,128)(2,1)S(1)}, bf16[1024,128]{1,0:T(8,128)(2,1)S(1)}, u32[]{:S(2)}, u32[]{:S(2)}) collective-permute-start(bf16[1024,128]{1,0:T(8,128)(2,1)S(1)} %convolution_convert_fusion), channel_id=1, source_target_pairs={{0,4},{4,0},{1,5},{5,1},{2,6},{6,2},{3,7},{7,3},{8,12},{12,8},{9,1... | collective-permute-start | bytes 786440 | tf_op jit(solution)/shard_map/ppermute | solution.py:182
  64.4 1.8 fusion.7
  66.1 3.0 %collective-permute-done = bf16[1024,128]{1,0:T(8,128)(2,1)S(1)} collective-permute-done((bf16[1024,128]{1,0:T(8,128)(2,1)S(1)}, bf16[1024,128]{1,0:T(8,128)(2,1)S(1)}, u32[]{:S(2)}, u32[]{:S(2)}) %collective-permute-start) | collective-permute-done | bytes 262176 | tf_op jit(solution)/shard_map/ppermute | solution.py:182
  69.3 23.0 %shard_map.112 = (bf16[2048,128]{1,0:T(8,128)(2,1)S(1)}, bf16[2048,128]{1,0:T(8,128)(2,1)S(1)}, bf16[2048,128]{1,0:T(8,128)(2,1)S(1)}, bf16[2048,128]{1,0:T(8,128)(2,1)S(1)}, bf16[4,128,1024]{2,1,0:T(8,128)(2,1)S(1)}) custom-call(bf16[2048,128]{1,0:T(8,128)(2,1)S(1)} %bitcast.121, bf16[2048,128]{1,0:T(8,128)(2,1)S(1)} %bitcast.122, ...), custom_call_target="tpu_custom_call" | custom-call | flops 6442450944 | bytes 4194304 | tf_op jit(solution)/shard_map/pallas_call | solution.py:76
  92.6 1.0 constant_dynamic-slice_fusion.3
  93.6 0.8 constant_dynamic-slice_fusion.2
  94.6 0.8 reshape.77
  96.5 3.2 %collective-permute-start.1 = (bf16[4,1024,128]{2,1,0:T(8,128)(2,1)}, bf16[4,1024,128]{2,1,0:T(8,128)(2,1)}, u32[]{:S(2)}, u32[]{:S(2)}) collective-permute-start(bf16[4,1024,128]{2,1,0:T(8,128)(2,1)} %constant_dynamic-slice_fusion.3), channel_id=1, source_target_pairs={{0,4},{4,0},{1,5},{5,1},{2,6},{6,2},{3,7},{7,3},{8,12},{12,8},{9,1... | collective-permute-start | bytes 3145736 | tf_op jit(solution)/shard_map/ppermute | solution.py:195
  99.7 1.2 convolution_bitcast_fusion.13
  101.3 1.0 stack.51
  102.2 1.3 copy.59
  103.9 1.1 fusion.2
  105.1 2.0 stack.52
  107.1 2.2 copy.60
  109.3 2.9 %convolution_bitcast_fusion.7 = f32[1,1,2,8,2,4,1024]{6,3,5,4,2,1,0:T(8,128)} fusion(bf16[1024,1024,1,1,1]{1,0,4,3,2:T(8,128)(2,1)} %bitcast.125, bf16[2,8,2,4,1024]{4,3,2,1,0:T(4,128)(2,1)S(1)} %copy-done.13), kind=kOutput, calls=%fused_computation.12 | convolution fusion | flops 268435456 | bytes 2883584 | tf_op jit(solution)/shard_map/dot_general | solution.py:212
  112.2 9.5 %collective-permute-done.1 = bf16[4,1024,128]{2,1,0:T(8,128)(2,1)} collective-permute-done((bf16[4,1024,128]{2,1,0:T(8,128)(2,1)}, bf16[4,1024,128]{2,1,0:T(8,128)(2,1)}, u32[]{:S(2)}, u32[]{:S(2)}) %collective-permute-start.1) | collective-permute-done | bytes 1048608 | tf_op jit(solution)/shard_map/ppermute | solution.py:195
  121.7 2.2 fusion.28
  123.9 1.1 copy.68
  125.0 0.8 reshape.78
  125.8 3.1 %convolution_bitcast_fusion = f32[1,1,2,8,2,4,1024]{6,3,5,4,2,1,0:T(8,128)} fusion(bf16[1024,1024,1,1,1]{1,0,4,3,2:T(8,128)(2,1)} %bitcast.126, bf16[2,8,2,4,1024]{4,3,2,1,0:T(4,128)(2,1)} %reshape.78), kind=kOutput, calls=%fused_computation.5 | convolution fusion | flops 268435456 | bytes 2883584 | tf_op jit(solution)/shard_map/dot_general | solution.py:212
  129.2 1.1 fusion.4
  130.4 2.0 stack.55
  132.3 2.2 copy.70
  135.2 1.1 fusion.5
  136.4 1.1 fusion.6
  137.5 2.1 stack.57
  139.6 1.3 copy.72
  140.9 0.9 stack.56
  141.9 1.3 copy.71
  143.3 1.5 maximum_maximum_fusion
  144.8 1.6 dynamic-slice_bitcast_fusion
  146.4 1.0 copy-done.4
  147.4 4.4 %collective-permute-done.2 = f32[2,4,2,8,4,1024]{5,3,4,2,1,0:T(8,128)S(1)} collective-permute-done((f32[2,4,2,8,4,1024]{5,3,4,2,1,0:T(8,128)}, f32[2,4,2,8,4,1024]{5,3,4,2,1,0:T(8,128)S(1)}, u32[]{:S(2)}, u32[]{:S(2)}) %collective-permute-start.2) | collective-permute-done | bytes 2097184 | tf_op jit(solution)/shard_map/ppermute | solution.py:224
  151.7 2.0 fusion
  153.7 1.4 copy.73
  155.1 1.8 reshape.79
  156.9 44.9 %reduce-scatter.2.cloned.1.call-done = f32[1,512,128]{2,1,0:T(8,128)} async-done(((f32[8,512,128]{2,1,0:T(8,128)}), f32[1,512,128]{2,1,0:T(8,128)}) %reduce-scatter.2.cloned.1.call-update) | async-done | bytes 262160 | tf_op jit(solution)/shard_map/reduce_scatter | solution.py:226
  201.8 1.0 reshape.80
  202.9 1.6 collective-permute-start.3
  204.5 4.1 %collective-permute-done.3 = f32[2,4,4,1024]{3,2,1,0:T(4,128)S(1)} collective-permute-done((f32[2,4,4,1024]{3,2,1,0:T(4,128)S(1)}, f32[2,4,4,1024]{3,2,1,0:T(4,128)S(1)}, u32[]{:S(2)}, u32[]{:S(2)}) %collective-permute-start.3) | collective-permute-done | bytes 131104 | tf_op jit(solution)/shard_map/ppermute | solution.py:231
  208.7 2.5 %collective-permute-start.4 = (f32[4,4,1024]{2,1,0:T(4,128)S(1)}, f32[4,4,1024]{2,1,0:T(4,128)S(1)}, u32[]{:S(2)}, u32[]{:S(2)}) collective-permute-start(f32[4,4,1024]{2,1,0:T(4,128)S(1)} %slice_bitcast_fusion.3), channel_id=1, source_target_pairs={{0,4},{4,0},{1,5},{5,1},{2,6},{6,2},{3,7},{7,3},{8,12},{12,8},{9,1... | collective-permute-start | bytes 196616 | tf_op jit(solution)/shard_map/ppermute | solution.py:232
  211.2 3.4 %collective-permute-done.4 = f32[4,4,1024]{2,1,0:T(4,128)S(1)} collective-permute-done((f32[4,4,1024]{2,1,0:T(4,128)S(1)}, f32[4,4,1024]{2,1,0:T(4,128)S(1)}, u32[]{:S(2)}, u32[]{:S(2)}) %collective-permute-start.4) | collective-permute-done | bytes 65568 | tf_op jit(solution)/shard_map/ppermute | solution.py:232
  (58 shorter events, 6.8 us)
Async XLA Ops:
  7.2 51.7 %all-gather.3.cloned.1.call-start = ((), (), s32[]{:S(2)}) async-start(), calls=%async_computation.1 | async-start | bytes 2359296 | tf_op jit(solution)/shard_map/all_gather | solution.py:169
  14.7 187.1 %reduce-scatter.2.cloned.1.call-start = ((), (), s32[]{:S(2)}) async-start(), calls=%async_computation.2 | async-start | bytes 2359296 | tf_op jit(solution)/shard_map/reduce_scatter | solution.py:226
  57.0 7.3 %copy-start.8 = (bf16[4,256,1024]{2,1,0:T(8,128)(2,1)S(1)}, bf16[4,256,1024]{2,1,0:T(8,128)(2,1)}, u32[]{:S(2)}) copy-start(bf16[4,256,1024]{2,1,0:T(8,128)(2,1)} %get-tuple-element.11) | copy-start | bytes 6291460
  61.1 8.1 %copy-start.14 = (s32[1,1,16,16]{3,2,1,0:T(8,128)S(1)}, s32[1,1,16,16]{3,2,1,0:T(8,128)}, u32[]{:S(2)}) copy-start(s32[1,1,16,16]{3,2,1,0:T(8,128)} %param.15) | copy-start | bytes 3076
  61.2 8.1 %copy-start = (bf16[1,2048,1,128]{3,1,2,0:T(8,128)(2,1)S(1)}, bf16[1,2048,1,128]{3,1,2,0:T(8,128)(2,1)}, u32[]{:S(2)}) copy-start(bf16[1,2048,1,128]{3,1,2,0:T(8,128)(2,1)} %param.11) | copy-start | bytes 1572868
  61.2 8.1 %copy-start.1 = (bf16[1,2048,1,128]{3,1,2,0:T(8,128)(2,1)S(1)}, bf16[1,2048,1,128]{3,1,2,0:T(8,128)(2,1)}, u32[]{:S(2)}) copy-start(bf16[1,2048,1,128]{3,1,2,0:T(8,128)(2,1)} %param.12) | copy-start | bytes 1572868
  61.2 8.1 %copy-start.2 = (bf16[1,2048,1,128]{3,1,2,0:T(8,128)(2,1)S(1)}, bf16[1,2048,1,128]{3,1,2,0:T(8,128)(2,1)}, u32[]{:S(2)}) copy-start(bf16[1,2048,1,128]{3,1,2,0:T(8,128)(2,1)} %param.13) | copy-start | bytes 1572868
  61.2 8.0 %collective-permute-start = (bf16[1024,128]{1,0:T(8,128)(2,1)S(1)}, bf16[1024,128]{1,0:T(8,128)(2,1)S(1)}, u32[]{:S(2)}, u32[]{:S(2)}) collective-permute-start(bf16[1024,128]{1,0:T(8,128)(2,1)S(1)} %convolution_convert_fusion), channel_id=1, source_target_pairs={{0,4},{4,0},{1,5},{5,1},{2,6},{6,2},{3,7},{7,3},{8,12},{12,8},{9,1... | collective-permute-start | bytes 786440 | tf_op jit(solution)/shard_map/ppermute | solution.py:182
  93.6 1.8 copy-start.3
  96.2 4.7 %copy-start.9 = (bf16[1,1024,128]{2,1,0:T(8,128)(2,1)S(1)}, bf16[1,1024,128]{2,1,0:T(8,128)(2,1)}, u32[]{:S(2)}) copy-start(bf16[1,1024,128]{2,1,0:T(8,128)(2,1)} %get-tuple-element.22) | copy-start | bytes 786436
  96.5 25.2 %collective-permute-start.1 = (bf16[4,1024,128]{2,1,0:T(8,128)(2,1)}, bf16[4,1024,128]{2,1,0:T(8,128)(2,1)}, u32[]{:S(2)}, u32[]{:S(2)}) collective-permute-start(bf16[4,1024,128]{2,1,0:T(8,128)(2,1)} %constant_dynamic-slice_fusion.3), channel_id=1, source_target_pairs={{0,4},{4,0},{1,5},{5,1},{2,6},{6,2},{3,7},{7,3},{8,12},{12,8},{9,1... | collective-permute-start | bytes 3145736 | tf_op jit(solution)/shard_map/ppermute | solution.py:195
  105.1 4.2 %copy-start.13 = (bf16[2,8,2,4,1024]{4,3,2,1,0:T(4,128)(2,1)S(1)}, bf16[2,8,2,4,1024]{4,3,2,1,0:T(4,128)(2,1)}, u32[]{:S(2)}) copy-start(bf16[2,8,2,4,1024]{4,3,2,1,0:T(4,128)(2,1)} %reshape.77) | copy-start | bytes 786436
  125.8 3.1 %copy-start.12 = (bf16[1,1024,128]{2,1,0:T(8,128)(2,1)S(1)}, bf16[1,1024,128]{2,1,0:T(8,128)(2,1)}, u32[]{:S(2)}) copy-start(bf16[1,1024,128]{2,1,0:T(8,128)(2,1)} %get-tuple-element.26) | copy-start | bytes 786436
  129.2 5.3 %copy-start.10 = (bf16[1,1024,128]{2,1,0:T(8,128)(2,1)S(1)}, bf16[1,1024,128]{2,1,0:T(8,128)(2,1)}, u32[]{:S(2)}) copy-start(bf16[1,1024,128]{2,1,0:T(8,128)(2,1)} %get-tuple-element.28) | copy-start | bytes 786436
  132.3 2.5 %copy-start.11 = (bf16[1,1024,128]{2,1,0:T(8,128)(2,1)S(1)}, bf16[1,1024,128]{2,1,0:T(8,128)(2,1)}, u32[]{:S(2)}) copy-start(bf16[1,1024,128]{2,1,0:T(8,128)(2,1)} %get-tuple-element.29) | copy-start | bytes 786436
  137.5 3.5 %copy-start.7 = (f32[128,1024]{1,0:T(8,128)S(1)}, f32[128,1024]{1,0:T(8,128)}, u32[]{:S(2)}) copy-start(f32[128,1024]{1,0:T(8,128)} %fusion.5) | copy-start | bytes 1572868
  137.5 5.8 %copy-start.5 = (f32[1,1,2,8,2,4,1024]{6,3,5,4,2,1,0:T(8,128)S(1)}, f32[1,1,2,8,2,4,1024]{6,3,5,4,2,1,0:T(8,128)}, u32[]{:S(2)}) copy-start(f32[1,1,2,8,2,4,1024]{6,3,5,4,2,1,0:T(8,128)} %copy.60) | copy-start | bytes 1572868
  137.5 5.8 %copy-start.6 = (f32[1,1,2,8,2,4,1024]{6,3,5,4,2,1,0:T(8,128)S(1)}, f32[1,1,2,8,2,4,1024]{6,3,5,4,2,1,0:T(8,128)}, u32[]{:S(2)}) copy-start(f32[1,1,2,8,2,4,1024]{6,3,5,4,2,1,0:T(8,128)} %copy.70) | copy-start | bytes 1572868
  144.8 2.6 %copy-start.4 = (f32[2,4,2,8,2,4,1024]{6,3,5,4,2,1,0:T(8,128)}, f32[2,4,2,8,2,4,1024]{6,3,5,4,2,1,0:T(8,128)S(1)}, u32[]{:S(2)}) copy-start(f32[2,4,2,8,2,4,1024]{6,3,5,4,2,1,0:T(8,128)S(1)} %maximum_maximum_fusion) | copy-start | bytes 12582916
  147.4 4.4 %collective-permute-start.2 = (f32[2,4,2,8,4,1024]{5,3,4,2,1,0:T(8,128)}, f32[2,4,2,8,4,1024]{5,3,4,2,1,0:T(8,128)S(1)}, u32[]{:S(2)}, u32[]{:S(2)}) collective-permute-start(f32[2,4,2,8,4,1024]{5,3,4,2,1,0:T(8,128)} %dynamic-slice_bitcast_fusion), channel_id=1, source_target_pairs={{0,8},{8,0},{1,9},{9,1},{2,10},{10,2},{3,11},{11,3},{4,12},{12,4},... | collective-permute-start | bytes 6291464 | tf_op jit(solution)/shard_map/ppermute | solution.py:224
  202.9 5.8 %collective-permute-start.3 = (f32[2,4,4,1024]{3,2,1,0:T(4,128)S(1)}, f32[2,4,4,1024]{3,2,1,0:T(4,128)S(1)}, u32[]{:S(2)}, u32[]{:S(2)}) collective-permute-start(f32[2,4,4,1024]{3,2,1,0:T(4,128)S(1)} %dynamic-slice_bitcast_fusion.2), channel_id=1, source_target_pairs={{0,128},{128,0},{1,129},{129,1},{2,130},{130,2},{3,131},{131,3},{4... | collective-permute-start | bytes 393224 | tf_op jit(solution)/shard_map/ppermute | solution.py:231
  208.7 5.9 %collective-permute-start.4 = (f32[4,4,1024]{2,1,0:T(4,128)S(1)}, f32[4,4,1024]{2,1,0:T(4,128)S(1)}, u32[]{:S(2)}, u32[]{:S(2)}) collective-permute-start(f32[4,4,1024]{2,1,0:T(4,128)S(1)} %slice_bitcast_fusion.3), channel_id=1, source_target_pairs={{0,4},{4,0},{1,5},{5,1},{2,6},{6,2},{3,7},{7,3},{8,12},{12,8},{9,1... | collective-permute-start | bytes 196616 | tf_op jit(solution)/shard_map/ppermute | solution.py:232
Sparse Core Ops, SparseCore 0:
  14.8 43.9 all-gather.2
  157.1 44.6 reduce-scatter.1

commit v12 on v10

--- a/solution.py
+++ b/solution.py
@@ -210,10 +210,15 @@
     terms = lax.psum_scatter(terms.reshape(nz, -1, 128), "dpz", scatter_dimension=0, tiled=True)
     terms = terms.reshape(2, 4, ny, chunk, width)
     row = lax.axis_index("dpy")
-    kept = lax.dynamic_index_in_dim(terms, row, 2, keepdims=False)
-    sent = lax.dynamic_index_in_dim(terms, 1 - row, 2, keepdims=False)
-    terms = kept + lax.ppermute(sent, "dpy", swap)
-    owned = terms[0] + lax.ppermute(terms[1], "sqy", swap)
+    mine = lax.dynamic_index_in_dim(terms, row, 2, keepdims=False)
+    theirs = lax.dynamic_index_in_dim(terms, 1 - row, 2, keepdims=False)
+    cross = [(0, 3), (3, 0), (1, 2), (2, 1)]
+    owned = (
+        mine[0]
+        + lax.ppermute(theirs[0], "dpy", swap)
+        + lax.ppermute(mine[1], "sqy", swap)
+        + lax.ppermute(theirs[1], ("dpy", "sqy"), cross)
+    )
     owned = jnp.transpose(owned, (1, 0, 2))
     return tuple(owned[:, part][:, None, :] for part in range(4))
 

time: 206 us -> 203 us (0.985)
  waiting for transfers between devices: 72.5 us -> 69.4 us
    ppermute x2 -> x3, waiting for transfers between devices: 7.46 us -> 4.35 us  [the longest x1 2.66 us: local(): lax.ppermute(theirs[1], ('dpy', 'sqy'), cross)]
    ppermute x2 -> x3, starting transfers between devices: 4.15 us -> 4.16 us  [the longest x1 3.04 us: local(): lax.ppermute(mine[1], 'sqy', swap)]
  transfers between devices with their start and end apart: 7 -> 8, of which waited for: 7 -> 7; matrix products, arithmetic and copies ran while one was open for 12% -> 12% of each run, Pallas kernels for 13% -> 13%
where the time goes in v12:
time: 203 us; the launch traced here: 202 us
  waiting for transfers between devices  69.4 us (34%)
  Pallas kernels  48.5 us (24%)
  local copies, waits for them, and re-layouts  26.1 us (13%)
  matrix products  20 us (10%)
  between operations  14.5 us (7%)
  starting transfers between devices  10.6 us (5%)
  blocking collectives  7.45 us (4%)
  other arithmetic  5.48 us (3%)
    reduce_scatter x1, waiting for transfers between devices, local(): lax.psum_scatter(terms.reshape(nz, -1, 128), 'dpz', scatter_dimension=0,...  41.8 us
    pallas_call x1, Pallas kernels, seq_gather(): pl.pallas_call(functools.partial(gather_kernel, nseq), in_specs=[any_spec...  26.6 us
    pallas_call x1, Pallas kernels, attention_backward(): pl.pallas_call(functools.partial(attention_kernel, nseq), grid=(length //...  21.9 us
    all_gather x1, waiting for transfers between devices, local(): gathered = lax.all_gather(gathered, 'dpz', axis=0)  14.9 us
    all_gather x1, blocking collectives, local(): lax.all_gather(out_weight, ('dpy', 'dpc'), axis=0)  7.45 us
    another operation x8, local copies, waits for them, and re-layouts  7.44 us
    dot_general x2, matrix products, terms_of(): lax.dot_general(parts[0], inputs_half, tn, preferred_element_type=jnp.flo...  6.1 us
    ppermute x1, waiting for transfers between devices, local(): terms = kept + lax.ppermute(sent, 'dpc', swap)  4.37 us
  transfers between devices with their start and end apart: 8, of which 7 were waited for; matrix products, arithmetic and copies ran while one was open for 12% of the time, Pallas kernels for 13%

profile of v12, /device:TPU:2, one launch (start us, length us, event | category | flops | bytes accessed | tf_op | source)
XLA Modules:
  0.0 202.1 jit_solution(17746858021794572441)
XLA Ops:
  7.2 7.4 %all-gather = bf16[128,1024]{1,0:T(8,128)(2,1)} all-gather(bf16[32,1024]{1,0:T(8,128)(2,1)} %param.14), channel_id=2, replica_groups=mesh['dpy'=2,'dpz'=8,'dpc'=2,'sqy'=2,'sqx'=4] {'dpy','dpc'}, dimensions={0}, use_global_device_ids=true | all-gather | bytes 327680 | tf_op jit(solution)/shard_map/all_gather | solution.py:164
  14.7 0.7 convert_reduce_fusion
  15.4 1.9 bitcast_multiply_fusion.a_ref
  17.4 26.6 %shard_map.111 = bf16[4,256,1024]{2,1,0:T(8,128)(2,1)} custom-call(bf16[256,1024]{1,0:T(8,128)(2,1)} %bitcast_multiply_fusion.a_ref), custom_call_target="tpu_custom_call" | custom-call | tf_op jit(solution)/shard_map/pallas_call | solution.py:136
  44.0 14.9 %all-gather.3.cloned.1.call-done = bf16[8,2,2,32,1024]{4,3,2,0,1:T(8,128)(2,1)} async-done(((bf16[1,2,2,32,1024]{4,3,2,0,1:T(8,128)(2,1)}), bf16[8,2,2,32,1024]{4,3,2,0,1:T(8,128)(2,1)}) %all-gather.3.cloned.1.call-update) | async-done | bytes 2097168 | tf_op jit(solution)/shard_map/all_gather | solution.py:165
  58.8 2.3 %convolution_convert_fusion = bf16[1024,128]{1,0:T(8,128)(2,1)S(1)} fusion(bf16[1024,1024]{1,0:T(8,128)(2,1)} %bitcast.126, bf16[1024,1024]{1,0:T(8,128)(2,1)} %bitcast.131, s32[]{:T(128)S(6)} %select_n.30), kind=kOutput, calls=%fused_computation.13 | convolution fusion | flops 268566528 | bytes 2621444 | tf_op jit(solution)/shard_map/dot_general | solution.py:173
  61.2 3.1 %collective-permute-start = (bf16[1024,128]{1,0:T(8,128)(2,1)S(1)}, bf16[1024,128]{1,0:T(8,128)(2,1)S(1)}, u32[]{:S(2)}, u32[]{:S(2)}) collective-permute-start(bf16[1024,128]{1,0:T(8,128)(2,1)S(1)} %convolution_convert_fusion), channel_id=1, source_target_pairs={{0,4},{4,0},{1,5},{5,1},{2,6},{6,2},{3,7},{7,3},{8,12},{12,8},{9,1... | collective-permute-start | bytes 786440 | tf_op jit(solution)/shard_map/ppermute | solution.py:174
  64.4 1.8 fusion.1
  66.2 3.0 %collective-permute-done = bf16[1024,128]{1,0:T(8,128)(2,1)S(1)} collective-permute-done((bf16[1024,128]{1,0:T(8,128)(2,1)S(1)}, bf16[1024,128]{1,0:T(8,128)(2,1)S(1)}, u32[]{:S(2)}, u32[]{:S(2)}) %collective-permute-start) | collective-permute-done | bytes 262176 | tf_op jit(solution)/shard_map/ppermute | solution.py:174
  69.3 21.9 %shard_map.112 = (bf16[2048,128]{1,0:T(8,128)(2,1)S(1)}, bf16[2048,128]{1,0:T(8,128)(2,1)S(1)}, bf16[2048,128]{1,0:T(8,128)(2,1)S(1)}, bf16[2048,128]{1,0:T(8,128)(2,1)S(1)}, bf16[4,256,1024]{2,1,0:T(8,128)(2,1)}) custom-call(bf16[2048,128]{1,0:T(8,128)(2,1)S(1)} %bitcast.122, bf16[2048,128]{1,0:T(8,128)(2,1)S(1)} %bitcast.123, ...), custom_call_target="tpu_custom_call" | custom-call | flops 6442450944 | bytes 4194304 | tf_op jit(solution)/shard_map/pallas_call | solution.py:76
  91.6 3.3 %collective-permute-start.1 = (bf16[4,1024,128]{2,1,0:T(8,128)(2,1)S(1)}, bf16[4,1024,128]{2,1,0:T(8,128)(2,1)}, u32[]{:S(2)}, u32[]{:S(2)}) collective-permute-start(bf16[4,1024,128]{2,1,0:T(8,128)(2,1)S(1)} %constant_dynamic-slice_fusion), channel_id=1, source_target_pairs={{0,4},{4,0},{1,5},{5,1},{2,6},{6,2},{3,7},{7,3},{8,12},{12,8},{9,1... | collective-permute-start | bytes 3145736 | tf_op jit(solution)/shard_map/ppermute | solution.py:187
  94.9 0.9 dynamic-slice_bitcast_fusion.4
  95.8 1.8 copy.42
  97.6 1.7 reshape.110
  99.4 1.8 copy.46
  101.2 1.8 reshape.113
  102.9 1.8 copy.44
  104.7 1.8 reshape.112
  106.5 0.9 copy.48
  107.3 1.1 reshape.114
  108.4 3.2 %convolution_bitcast_fusion.7 = f32[1,1,2,8,2,4,1024]{6,3,5,4,2,1,0:T(8,128)} fusion(bf16[1024,1024,1,1,1]{1,0,4,3,2:T(8,128)(2,1)} %bitcast.134, bf16[2,8,2,4,1024]{4,3,2,1,0:T(4,128)(2,1)} %reshape.110), kind=kOutput, calls=%fused_computation.12 | convolution fusion | flops 268435456 | bytes 2883584 | tf_op jit(solution)/shard_map/dot_general | solution.py:193
  111.6 1.3 convolution_bitcast_fusion.5
  112.9 1.3 convolution_bitcast_fusion.6
  114.2 1.3 convolution_bitcast_fusion.4
  115.6 1.0 collective-permute-done.1
  116.6 1.3 slice_bitcast_fusion.3
  118.1 2.9 %convolution_bitcast_fusion.3 = f32[1,1,2,8,2,4,1024]{6,3,5,4,2,1,0:T(8,128)} fusion(bf16[1024,1024,1,1,1]{1,0,4,3,2:T(8,128)(2,1)} %bitcast.135, bf16[2,8,2,4,1024]{4,3,2,1,0:T(4,128)(2,1)S(1)} %reshape.115), kind=kOutput, calls=%fused_computation.8 | convolution fusion | flops 268435456 | bytes 2883584 | tf_op jit(solution)/shard_map/dot_general | solution.py:193
  121.2 0.8 reshape.118
  122.0 1.5 convolution_bitcast_fusion
  123.7 2.1 %convolution_bitcast_fusion.1 = f32[1,1,2,8,2,4,1024]{6,3,5,4,2,1,0:T(8,128)S(1)} fusion(bf16[1024,1024,1,1,1]{1,0,4,3,2:T(8,128)(2,1)} %bitcast.136, bf16[2,8,2,4,1024]{4,3,2,1,0:T(4,128)(2,1)S(1)} %reshape.117), kind=kOutput, calls=%fused_computation.6 | convolution fusion | flops 268435456 | bytes 2883584 | tf_op jit(solution)/shard_map/dot_general | solution.py:195
  126.2 2.3 %convolution_bitcast_fusion.2 = f32[1,1,2,8,2,4,1024]{6,3,5,4,2,1,0:T(8,128)S(1)} fusion(bf16[1024,1024,1,1,1]{1,0,4,3,2:T(8,128)(2,1)} %bitcast.137, bf16[2,8,2,4,1024]{4,3,2,1,0:T(4,128)(2,1)S(1)} %reshape.116), kind=kOutput, calls=%fused_computation.7 | convolution fusion | flops 268435456 | bytes 2883584 | tf_op jit(solution)/shard_map/dot_general | solution.py:194
  128.5 0.5 maximum_maximum_fusion
  129.1 1.6 dynamic-slice_bitcast_fusion
  130.7 1.0 copy-done.4
  131.7 4.4 %collective-permute-done.2 = f32[2,4,2,8,4,1024]{5,3,4,2,1,0:T(8,128)S(1)} collective-permute-done((f32[2,4,2,8,4,1024]{5,3,4,2,1,0:T(8,128)}, f32[2,4,2,8,4,1024]{5,3,4,2,1,0:T(8,128)S(1)}, u32[]{:S(2)}, u32[]{:S(2)}) %collective-permute-start.2) | collective-permute-done | bytes 2097184 | tf_op jit(solution)/shard_map/ppermute | solution.py:208
  136.0 2.0 fusion
  138.0 1.4 copy.58
  139.4 1.8 reshape.119
  141.2 41.8 %reduce-scatter.2.cloned.1.call-done = f32[1,512,128]{2,1,0:T(8,128)} async-done(((f32[8,512,128]{2,1,0:T(8,128)}), f32[1,512,128]{2,1,0:T(8,128)}) %reduce-scatter.2.cloned.1.call-update) | async-done | bytes 262160 | tf_op jit(solution)/shard_map/reduce_scatter | solution.py:210
  183.1 1.0 reshape.120
  184.2 3.0 %collective-permute-start.4 = (f32[4,4,1024]{2,1,0:T(4,128)S(1)}, f32[4,4,1024]{2,1,0:T(4,128)S(1)}, u32[]{:S(2)}, u32[]{:S(2)}) collective-permute-start(f32[4,4,1024]{2,1,0:T(4,128)S(1)} %get-tuple-element.30), channel_id=1, source_target_pairs={{0,4},{4,0},{1,5},{5,1},{2,6},{6,2},{3,7},{7,3},{8,12},{12,8},{9,1... | collective-permute-start | bytes 196616 | tf_op jit(solution)/shard_map/ppermute | solution.py:219
  187.2 1.1 collective-permute-start.5
  188.3 1.7 collective-permute-done.4
  190.0 2.7 %collective-permute-done.5 = f32[4,4,1024]{2,1,0:T(4,128)S(1)} collective-permute-done((f32[4,4,1024]{2,1,0:T(4,128)S(1)}, f32[4,4,1024]{2,1,0:T(4,128)S(1)}, u32[]{:S(2)}, u32[]{:S(2)}) %collective-permute-start.5) | collective-permute-done | bytes 65568 | tf_op jit(solution)/shard_map/ppermute | solution.py:220
  192.8 0.6 copy.64
  193.4 0.6 copy.63
  194.0 0.6 copy.62
  194.6 0.6 copy.61
  (53 shorter events, 1.7 us)
Async XLA Ops:
  7.2 51.7 %all-gather.3.cloned.1.call-start = ((), (), s32[]{:S(2)}) async-start(), calls=%async_computation.1 | async-start | bytes 2359296 | tf_op jit(solution)/shard_map/all_gather | solution.py:165
  14.7 168.4 %reduce-scatter.2.cloned.1.call-start = ((), (), s32[]{:S(2)}) async-start(), calls=%async_computation.2 | async-start | bytes 2359296 | tf_op jit(solution)/shard_map/reduce_scatter | solution.py:210
  44.0 20.4 %copy-start.5 = (bf16[4,256,1024]{2,1,0:T(8,128)(2,1)S(1)}, bf16[4,256,1024]{2,1,0:T(8,128)(2,1)}, u32[]{:S(2)}) copy-start(bf16[4,256,1024]{2,1,0:T(8,128)(2,1)} %shard_map.111) | copy-start | bytes 6291460
  61.1 8.1 %copy-start.13 = (s32[1,1,16,16]{3,2,1,0:T(8,128)S(1)}, s32[1,1,16,16]{3,2,1,0:T(8,128)}, u32[]{:S(2)}) copy-start(s32[1,1,16,16]{3,2,1,0:T(8,128)} %param.15) | copy-start | bytes 3076
  61.1 8.2 %copy-start = (bf16[1,2048,1,128]{3,1,2,0:T(8,128)(2,1)S(1)}, bf16[1,2048,1,128]{3,1,2,0:T(8,128)(2,1)}, u32[]{:S(2)}) copy-start(bf16[1,2048,1,128]{3,1,2,0:T(8,128)(2,1)} %param.11) | copy-start | bytes 1572868
  61.2 8.2 %copy-start.1 = (bf16[1,2048,1,128]{3,1,2,0:T(8,128)(2,1)S(1)}, bf16[1,2048,1,128]{3,1,2,0:T(8,128)(2,1)}, u32[]{:S(2)}) copy-start(bf16[1,2048,1,128]{3,1,2,0:T(8,128)(2,1)} %param.12) | copy-start | bytes 1572868
  61.2 8.2 %copy-start.2 = (bf16[1,2048,1,128]{3,1,2,0:T(8,128)(2,1)S(1)}, bf16[1,2048,1,128]{3,1,2,0:T(8,128)(2,1)}, u32[]{:S(2)}) copy-start(bf16[1,2048,1,128]{3,1,2,0:T(8,128)(2,1)} %param.13) | copy-start | bytes 1572868
  61.2 8.2 %copy-start.3 = (bf16[1,256,1024]{2,1,0:T(8,128)(2,1)S(1)}, bf16[1,256,1024]{2,1,0:T(8,128)(2,1)}, u32[]{:S(2)}) copy-start(bf16[1,256,1024]{2,1,0:T(8,128)(2,1)} %param.8) | copy-start | bytes 1572868
  61.2 8.0 %collective-permute-start = (bf16[1024,128]{1,0:T(8,128)(2,1)S(1)}, bf16[1024,128]{1,0:T(8,128)(2,1)S(1)}, u32[]{:S(2)}, u32[]{:S(2)}) collective-permute-start(bf16[1024,128]{1,0:T(8,128)(2,1)S(1)} %convolution_convert_fusion), channel_id=1, source_target_pairs={{0,4},{4,0},{1,5},{5,1},{2,6},{6,2},{3,7},{7,3},{8,12},{12,8},{9,1... | collective-permute-start | bytes 786440 | tf_op jit(solution)/shard_map/ppermute | solution.py:174
  91.6 25.0 %collective-permute-start.1 = (bf16[4,1024,128]{2,1,0:T(8,128)(2,1)S(1)}, bf16[4,1024,128]{2,1,0:T(8,128)(2,1)}, u32[]{:S(2)}, u32[]{:S(2)}) collective-permute-start(bf16[4,1024,128]{2,1,0:T(8,128)(2,1)S(1)} %constant_dynamic-slice_fusion), channel_id=1, source_target_pairs={{0,4},{4,0},{1,5},{5,1},{2,6},{6,2},{3,7},{7,3},{8,12},{12,8},{9,1... | collective-permute-start | bytes 3145736 | tf_op jit(solution)/shard_map/ppermute | solution.py:187
  108.4 3.2 %copy-start.11 = (bf16[2,8,2,4,1024]{4,3,2,1,0:T(4,128)(2,1)S(1)}, bf16[2,8,2,4,1024]{4,3,2,1,0:T(4,128)(2,1)}, u32[]{:S(2)}) copy-start(bf16[2,8,2,4,1024]{4,3,2,1,0:T(4,128)(2,1)} %reshape.113) | copy-start | bytes 786436
  108.4 3.2 %copy-start.14 = (bf16[4,256,1024]{2,1,0:T(8,128)(2,1)S(1)}, bf16[4,256,1024]{2,1,0:T(8,128)(2,1)}, u32[]{:S(2)}) copy-start(bf16[4,256,1024]{2,1,0:T(8,128)(2,1)} %get-tuple-element.13) | copy-start | bytes 6291460
  111.6 1.3 copy-start.12
  126.1 2.3 %copy-start.6 = (f32[1,1,2,8,2,4,1024]{6,3,5,4,2,1,0:T(8,128)S(1)}, f32[1,1,2,8,2,4,1024]{6,3,5,4,2,1,0:T(8,128)}, u32[]{:S(2)}) copy-start(f32[1,1,2,8,2,4,1024]{6,3,5,4,2,1,0:T(8,128)} %convolution_bitcast_fusion.7) | copy-start | bytes 1572868
  126.1 2.3 %copy-start.7 = (f32[1,1,2,8,2,4,1024]{6,3,5,4,2,1,0:T(8,128)S(1)}, f32[1,1,2,8,2,4,1024]{6,3,5,4,2,1,0:T(8,128)}, u32[]{:S(2)}) copy-start(f32[1,1,2,8,2,4,1024]{6,3,5,4,2,1,0:T(8,128)} %convolution_bitcast_fusion.5) | copy-start | bytes 1572868
  126.2 2.3 %copy-start.8 = (f32[1,1,2,8,2,4,1024]{6,3,5,4,2,1,0:T(8,128)S(1)}, f32[1,1,2,8,2,4,1024]{6,3,5,4,2,1,0:T(8,128)}, u32[]{:S(2)}) copy-start(f32[1,1,2,8,2,4,1024]{6,3,5,4,2,1,0:T(8,128)} %convolution_bitcast_fusion.6) | copy-start | bytes 1572868
  126.2 2.3 %copy-start.9 = (f32[1,1,2,8,2,4,1024]{6,3,5,4,2,1,0:T(8,128)S(1)}, f32[1,1,2,8,2,4,1024]{6,3,5,4,2,1,0:T(8,128)}, u32[]{:S(2)}) copy-start(f32[1,1,2,8,2,4,1024]{6,3,5,4,2,1,0:T(8,128)} %convolution_bitcast_fusion.4) | copy-start | bytes 1572868
  126.2 2.3 %copy-start.10 = (f32[1,1,2,8,2,4,1024]{6,3,5,4,2,1,0:T(8,128)S(1)}, f32[1,1,2,8,2,4,1024]{6,3,5,4,2,1,0:T(8,128)}, u32[]{:S(2)}) copy-start(f32[1,1,2,8,2,4,1024]{6,3,5,4,2,1,0:T(8,128)} %convolution_bitcast_fusion.3) | copy-start | bytes 1572868
  129.1 2.6 %copy-start.4 = (f32[2,4,2,8,2,4,1024]{6,3,5,4,2,1,0:T(8,128)}, f32[2,4,2,8,2,4,1024]{6,3,5,4,2,1,0:T(8,128)S(1)}, u32[]{:S(2)}) copy-start(f32[2,4,2,8,2,4,1024]{6,3,5,4,2,1,0:T(8,128)S(1)} %maximum_maximum_fusion) | copy-start | bytes 12582916
  131.7 4.4 %collective-permute-start.2 = (f32[2,4,2,8,4,1024]{5,3,4,2,1,0:T(8,128)}, f32[2,4,2,8,4,1024]{5,3,4,2,1,0:T(8,128)S(1)}, u32[]{:S(2)}, u32[]{:S(2)}) collective-permute-start(f32[2,4,2,8,4,1024]{5,3,4,2,1,0:T(8,128)} %dynamic-slice_bitcast_fusion), channel_id=1, source_target_pairs={{0,8},{8,0},{1,9},{9,1},{2,10},{10,2},{3,11},{11,3},{4,12},{12,4},... | collective-permute-start | bytes 6291464 | tf_op jit(solution)/shard_map/ppermute | solution.py:208
  184.2 5.9 %collective-permute-start.4 = (f32[4,4,1024]{2,1,0:T(4,128)S(1)}, f32[4,4,1024]{2,1,0:T(4,128)S(1)}, u32[]{:S(2)}, u32[]{:S(2)}) collective-permute-start(f32[4,4,1024]{2,1,0:T(4,128)S(1)} %get-tuple-element.30), channel_id=1, source_target_pairs={{0,4},{4,0},{1,5},{5,1},{2,6},{6,2},{3,7},{7,3},{8,12},{12,8},{9,1... | collective-permute-start | bytes 196616 | tf_op jit(solution)/shard_map/ppermute | solution.py:219
  187.2 5.5 %collective-permute-start.5 = (f32[4,4,1024]{2,1,0:T(4,128)S(1)}, f32[4,4,1024]{2,1,0:T(4,128)S(1)}, u32[]{:S(2)}, u32[]{:S(2)}) collective-permute-start(f32[4,4,1024]{2,1,0:T(4,128)S(1)} %get-tuple-element.31), channel_id=1, source_target_pairs={{0,132},{132,0},{4,128},{128,4},{1,133},{133,1},{5,129},{129,5},{2... | collective-permute-start | bytes 196616 | tf_op jit(solution)/shard_map/ppermute | solution.py:220
  188.3 4.4 %collective-permute-start.3 = (f32[4,4,1024]{2,1,0:T(4,128)S(1)}, f32[4,4,1024]{2,1,0:T(4,128)S(1)}, u32[]{:S(2)}, u32[]{:S(2)}) collective-permute-start(f32[4,4,1024]{2,1,0:T(4,128)S(1)} %slice_bitcast_fusion.4), channel_id=1, source_target_pairs={{0,128},{128,0},{1,129},{129,1},{2,130},{130,2},{3,131},{131,3},{4... | collective-permute-start | bytes 196616 | tf_op jit(solution)/shard_map/ppermute | solution.py:218
Sparse Core Ops, SparseCore 0:
  14.8 43.9 all-gather.2
  141.4 41.6 reduce-scatter.1

commit v13 on v11

--- a/solution.py
+++ b/solution.py
@@ -46,7 +46,7 @@
     row_max = jnp.max(scores, axis=1, keepdims=True)
     weights = jnp.exp(scores - row_max)
     row_total = jnp.sum(weights, axis=1, keepdims=True)
-    prob = weights / row_total
+    prob = weights * (1.0 / row_total)
     prob_low = prob.astype(jnp.bfloat16)
     attended = jnp.dot(prob_low, v, preferred_element_type=jnp.float32).astype(jnp.bfloat16)
     row_delta = jnp.sum(g.astype(jnp.float32) * attended.astype(jnp.float32), axis=1, keepdims=True)
@@ -170,11 +170,10 @@
     gathered = jnp.transpose(gathered, (1, 0, 2, 3, 4)).reshape(-1, width)
     head_weight = lax.dynamic_slice_in_dim(gathered, head * HD, HD, 0)
     partner_weight = lax.dynamic_slice_in_dim(gathered, partner_head * HD, HD, 0)
-    slab = inputs.shape[1]
-    lead = slab // 2
-    masked_half, inputs_lead = seq_gather(masked, inputs[0, :lead], sizes["sqx"])
+    split = width // 2
+    masked_half, inputs_lead = seq_gather(masked, inputs[0, :, :split], sizes["sqx"])
     masked_half = masked_half.reshape(-1, width)
-    inputs_lead = inputs_lead.reshape(-1, width)
+    inputs_lead = inputs_lead.reshape(-1, split)
     half_len = masked_half.shape[0]
     nt = (((1,), (1,)), ((), ()))
     d_own = lax.dot_general(masked_half, head_weight, nt, preferred_element_type=jnp.float32).astype(jnp.bfloat16)
@@ -186,51 +185,48 @@
     blocks = block_mask[0, 0]
     live_cols = jnp.repeat(blocks, BLOCK, axis=1)[:, None, :]
     d_query, attended, d_key, d_value, inputs_half = attention_backward(
-        queries[0, :, 0], keys[0, :, 0], values[0, :, 0], d_attn, live_cols, inputs[0, lead:], sizes["sqx"]
-    )
-    inputs_tail = inputs_half.reshape(-1, width)
+        queries[0, :, 0], keys[0, :, 0], values[0, :, 0], d_attn, live_cols, inputs[0, :, split:], sizes["sqx"]
+    )
+    inputs_tail = inputs_half.reshape(-1, split)
+    masked_lead = masked_half[:, :split]
+    masked_tail = masked_half[:, split:]
     grads = jnp.stack([d_query, d_key, d_value, attended])
     grads_own = lax.dynamic_slice_in_dim(grads, half * half_len, half_len, 1)
     grads_give = lax.dynamic_slice_in_dim(grads, other * half_len, half_len, 1)
     grads_got = lax.ppermute(grads_give, "sqy", swap)
     tn = (((0,), (0,)), ((), ()))
 
-    def by_inputs(part):
-        rows = part.reshape(sizes["sqx"], slab, HD)
-        lead_rows = rows[:, :lead].reshape(-1, HD)
-        tail_rows = rows[:, lead:].reshape(-1, HD)
-        return lax.dot_general(lead_rows, inputs_lead, tn, preferred_element_type=jnp.float32) + lax.dot_general(
-            tail_rows, inputs_tail, tn, preferred_element_type=jnp.float32
-        )
-
     def terms_of(parts):
+        sources = ((inputs_lead, inputs_tail),) * 3 + ((masked_lead, masked_tail),)
         return jnp.stack(
             [
-                by_inputs(parts[0]),
-                by_inputs(parts[1]),
-                by_inputs(parts[2]),
-                lax.dot_general(parts[3], masked_half, tn, preferred_element_type=jnp.float32),
-            ],
-            axis=0,
+                jnp.stack([lax.dot_general(part, src, tn, preferred_element_type=jnp.float32) for src in pair])
+                for part, pair in zip(parts, sources)
+            ]
         )
 
     terms = jnp.stack([terms_of(grads_own), terms_of(grads_got)])
     ny, nz, nc = sizes["dpy"], sizes["dpz"], sizes["dpc"]
-    chunk = terms.shape[2] // (ny * nz * nc)
-    terms = terms.reshape(2, 4, ny, nz, nc, chunk, width)
+    chunk = terms.shape[3] // (ny * nz * nc)
+    terms = terms.reshape(2, 4, 2, ny, nz, nc, chunk, split)
     core = lax.axis_index("dpc")
-    kept = lax.dynamic_index_in_dim(terms, core, 4, keepdims=False)
-    sent = lax.dynamic_index_in_dim(terms, 1 - core, 4, keepdims=False)
+    kept = lax.dynamic_index_in_dim(terms, core, 5, keepdims=False)
+    sent = lax.dynamic_index_in_dim(terms, 1 - core, 5, keepdims=False)
     terms = kept + lax.ppermute(sent, "dpc", swap)
-    terms = jnp.transpose(terms, (3, 0, 1, 2, 4, 5))
+    terms = jnp.transpose(terms, (4, 0, 1, 2, 3, 5, 6))
     terms = lax.psum_scatter(terms.reshape(nz, -1, 128), "dpz", scatter_dimension=0, tiled=True)
-    terms = terms.reshape(2, 4, ny, chunk, width)
+    terms = terms.reshape(2, 4, 2, ny, chunk, split)
     row = lax.axis_index("dpy")
-    kept = lax.dynamic_index_in_dim(terms, row, 2, keepdims=False)
-    sent = lax.dynamic_index_in_dim(terms, 1 - row, 2, keepdims=False)
-    terms = kept + lax.ppermute(sent, "dpy", swap)
-    owned = terms[0] + lax.ppermute(terms[1], "sqy", swap)
-    owned = jnp.transpose(owned, (1, 0, 2))
+    mine = lax.dynamic_index_in_dim(terms, row, 3, keepdims=False)
+    theirs = lax.dynamic_index_in_dim(terms, 1 - row, 3, keepdims=False)
+    cross = [(0, 3), (3, 0), (1, 2), (2, 1)]
+    owned = (
+        mine[0]
+        + lax.ppermute(theirs[0], "dpy", swap)
+        + lax.ppermute(mine[1], "sqy", swap)
+        + lax.ppermute(theirs[1], ("dpy", "sqy"), cross)
+    )
+    owned = jnp.transpose(owned, (2, 0, 1, 3)).reshape(chunk, 4, width)
     return tuple(owned[:, part][:, None, :] for part in range(4))
 
 

time: 225 us -> 215 us (0.956)
  local copies, waits for them, and re-layouts: 35.1 us -> 21.1 us
  waiting for transfers between devices: 71.1 us -> 75.3 us
    another operation x14 -> x8, local copies, waits for them, and re-layouts: 18.5 us -> 3.44 us  [the longest x12 16.9 us: terms_of(): jnp.stack([by_inputs(parts[0]), by_inputs(parts[1]), by_inputs(parts[2]),...]
    ppermute x1, waiting for transfers between devices: 9.51 us -> 17 us  [local(): grads_got = lax.ppermute(grads_give, 'sqy', swap)]
    dot_general x2 -> x10, local copies, waits for them, and re-layouts: 1.23 us -> 5.46 us  [terms_of(): lax.dot_general(part, src, tn, preferred_element_type=jnp.float32)]
    ppermute x2 -> x3, waiting for transfers between devices: 7.52 us -> 4.27 us  [the longest x1 2.71 us: local(): lax.ppermute(theirs[1], ('dpy', 'sqy'), cross)]
    slice x2 -> x0, local copies, waits for them, and re-layouts: 2.97 us -> none  [terms_of(): parts[0]]
    dot_general x14 -> x16, matrix products: 14.1 us -> 15.5 us  [terms_of(): lax.dot_general(part, src, tn, preferred_element_type=jnp.float32)]
  transfers between devices with their start and end apart: 7 -> 8, of which waited for: 7 -> 7; matrix products, arithmetic and copies ran while one was open for 8% -> 5% of each run, Pallas kernels for 17% -> 18%
where the time goes in v13:
time: 215 us
  waiting for transfers between devices  75.3 us (35%)
  Pallas kernels  60.8 us (28%)
  local copies, waits for them, and re-layouts  21.1 us (10%)
  matrix products  19.6 us (9%)
  between operations  14.5 us (7%)
  starting transfers between devices  10.4 us (5%)
  blocking collectives  7.46 us (3%)
  other arithmetic  5.47 us (3%)
    reduce_scatter x1, waiting for transfers between devices, local(): lax.psum_scatter(terms.reshape(nz, -1, 128), 'dpz', scatter_dimension=0,...  44.9 us
    pallas_call x1, Pallas kernels, seq_gather(): pl.pallas_call(functools.partial(gather_kernel, nseq), in_specs=[any_spec...  37.9 us
    pallas_call x1, Pallas kernels, attention_backward(): pl.pallas_call(functools.partial(attention_kernel, nseq), grid=(length //...  23 us
    ppermute x1, waiting for transfers between devices, local(): grads_got = lax.ppermute(grads_give, 'sqy', swap)  17 us
    dot_general x16, matrix products, terms_of(): lax.dot_general(part, src, tn, preferred_element_type=jnp.float32)  15.5 us
    all_gather x1, blocking collectives, local(): lax.all_gather(out_weight, ('dpy', 'dpc'), axis=0)  7.46 us
    dot_general x10, local copies, waits for them, and re-layouts, terms_of(): lax.dot_general(part, src, tn, preferred_element_type=jnp.float32)  5.46 us
    ppermute x1, waiting for transfers between devices, local(): terms = kept + lax.ppermute(sent, 'dpc', swap)  4.37 us
  transfers between devices with their start and end apart: 8, of which 7 were waited for; matrix products, arithmetic and copies ran while one was open for 5% of the time, Pallas kernels for 18%

profile of v13, /device:TPU:2, one launch (start us, length us, event | category | flops | bytes accessed | tf_op | source)
XLA Modules:
  0.0 214.6 jit_solution(10011333756740297725)
XLA Ops:
  7.2 7.5 %all-gather = bf16[128,1024]{1,0:T(8,128)(2,1)} all-gather(bf16[32,1024]{1,0:T(8,128)(2,1)} %param.14), channel_id=2, replica_groups=mesh['dpy'=2,'dpz'=8,'dpc'=2,'sqy'=2,'sqx'=4] {'dpy','dpc'}, dimensions={0}, use_global_device_ids=true | all-gather | bytes 327680 | tf_op jit(solution)/shard_map/all_gather | solution.py:168
  14.8 0.7 convert_reduce_fusion
  15.5 1.8 slice_bitcast_fusion.10
  17.2 1.9 bitcast_multiply_fusion.a_ref
  19.2 37.9 %shard_map.111 = (bf16[4,256,1024]{2,1,0:T(8,128)(2,1)}, bf16[4,256,512]{2,1,0:T(8,128)(2,1)}) custom-call(bf16[256,1024]{1,0:T(8,128)(2,1)} %bitcast_multiply_fusion.a_ref, bf16[256,512]{1,0:T(8,128)(2,1)} %get-tuple-element.27.b_ref), custom_call_target="tpu_custom_call" | custom-call | tf_op jit(solution)/shard_map/pallas_call | solution.py:137
  57.0 1.8 all-gather.3.cloned.1.call-done
  58.8 2.3 %convolution_convert_fusion = bf16[1024,128]{1,0:T(8,128)(2,1)S(1)} fusion(bf16[1024,1024]{1,0:T(8,128)(2,1)} %bitcast.173, bf16[1024,1024]{1,0:T(8,128)(2,1)} %bitcast.180, s32[]{:T(128)S(6)} %select_n.30), kind=kOutput, calls=%fused_computation.5 | convolution fusion | flops 268566528 | bytes 2621444 | tf_op jit(solution)/shard_map/dot_general | solution.py:180
  61.2 3.1 %collective-permute-start = (bf16[1024,128]{1,0:T(8,128)(2,1)S(1)}, bf16[1024,128]{1,0:T(8,128)(2,1)S(1)}, u32[]{:S(2)}, u32[]{:S(2)}) collective-permute-start(bf16[1024,128]{1,0:T(8,128)(2,1)S(1)} %convolution_convert_fusion), channel_id=1, source_target_pairs={{0,4},{4,0},{1,5},{5,1},{2,6},{6,2},{3,7},{7,3},{8,12},{12,8},{9,1... | collective-permute-start | bytes 786440 | tf_op jit(solution)/shard_map/ppermute | solution.py:181
  64.4 1.8 fusion.1
  66.2 3.0 %collective-permute-done = bf16[1024,128]{1,0:T(8,128)(2,1)S(1)} collective-permute-done((bf16[1024,128]{1,0:T(8,128)(2,1)S(1)}, bf16[1024,128]{1,0:T(8,128)(2,1)S(1)}, u32[]{:S(2)}, u32[]{:S(2)}) %collective-permute-start) | collective-permute-done | bytes 262176 | tf_op jit(solution)/shard_map/ppermute | solution.py:181
  69.3 23.0 %shard_map.112 = (bf16[2048,128]{1,0:T(8,128)(2,1)S(1)}, bf16[2048,128]{1,0:T(8,128)(2,1)S(1)}, bf16[2048,128]{1,0:T(8,128)(2,1)S(1)}, bf16[2048,128]{1,0:T(8,128)(2,1)S(1)}, bf16[4,256,512]{2,1,0:T(8,128)(2,1)S(1)}) custom-call(bf16[2048,128]{1,0:T(8,128)(2,1)S(1)} %bitcast.164, bf16[2048,128]{1,0:T(8,128)(2,1)S(1)} %bitcast.165, ...), custom_call_target="tpu_custom_call" | custom-call | flops 6442450944 | bytes 4194304 | tf_op jit(solution)/shard_map/pallas_call | solution.py:76
  92.6 1.1 constant_dynamic-slice_fusion
  94.0 0.3 convolution_bitcast_fusion.14
  94.4 0.6 copy-done.3
  94.9 1.0 convolution_bitcast_fusion.15
  95.9 0.8 copy.60
  96.8 1.1 reshape.184
  98.2 0.8 reshape.185
  99.1 2.9 %collective-permute-start.1 = (bf16[4,1024,128]{2,1,0:T(8,128)(2,1)}, bf16[4,1024,128]{2,1,0:T(8,128)(2,1)S(1)}, u32[]{:S(2)}, u32[]{:S(2)}) collective-permute-start(bf16[4,1024,128]{2,1,0:T(8,128)(2,1)} %constant_dynamic-slice_fusion), channel_id=1, source_target_pairs={{0,4},{4,0},{1,5},{5,1},{2,6},{6,2},{3,7},{7,3},{8,12},{12,8},{9,1... | collective-permute-start | bytes 3145736 | tf_op jit(solution)/shard_map/ppermute | solution.py:196
  102.6 1.0 convolution_bitcast_fusion.12
  103.7 1.0 convolution_bitcast_fusion.13
  104.7 1.1 convolution_bitcast_fusion.8
  105.8 1.1 convolution_bitcast_fusion.9
  106.9 17.0 %collective-permute-done.1 = bf16[4,1024,128]{2,1,0:T(8,128)(2,1)S(1)} collective-permute-done((bf16[4,1024,128]{2,1,0:T(8,128)(2,1)}, bf16[4,1024,128]{2,1,0:T(8,128)(2,1)S(1)}, u32[]{:S(2)}, u32[]{:S(2)}) %collective-permute-start.1) | collective-permute-done | bytes 1048608 | tf_op jit(solution)/shard_map/ppermute | solution.py:196
  123.8 0.9 slice_bitcast_fusion.9
  125.0 1.0 convolution_bitcast_fusion.6
  126.0 1.0 convolution_bitcast_fusion.7
  127.4 2.3 %convolution_bitcast_fusion = f32[1,1,1,2,8,2,4,512]{7,4,6,5,3,2,1,0:T(8,128)} fusion(bf16[1024,1024]{1,0:T(8,128)(2,1)} %bitcast.174, bf16[2,8,2,4,1024]{4,3,2,1,0:T(4,128)(2,1)S(1)} %reshape.189), kind=kOutput, calls=%fused_computation.8 | convolution fusion | flops 134217728 | bytes 1572864 | tf_op jit(solution)/shard_map/dot_general | solution.py:203
  129.6 2.3 %convolution_bitcast_fusion.1 = f32[1,1,1,2,8,2,4,512]{7,4,6,5,3,2,1,0:T(8,128)} fusion(bf16[1024,1024]{1,0:T(8,128)(2,1)} %bitcast.175, bf16[2,8,2,4,1024]{4,3,2,1,0:T(4,128)(2,1)S(1)} %reshape.189), kind=kOutput, calls=%fused_computation.9 | convolution fusion | flops 134217728 | bytes 1572864 | tf_op jit(solution)/shard_map/dot_general | solution.py:203
  131.9 1.1 copy.72
  133.1 1.0 convolution_bitcast_fusion.2
  134.1 1.0 convolution_bitcast_fusion.3
  135.2 1.8 copy.69
  137.0 1.1 reshape.187
  139.7 0.5 maximum_maximum_fusion
  140.2 1.7 dynamic-slice_bitcast_fusion
  141.9 0.9 copy-done.4
  142.8 4.4 %collective-permute-done.2 = f32[2,4,2,2,8,4,512]{6,4,5,3,2,1,0:T(8,128)S(1)} collective-permute-done((f32[2,4,2,2,8,4,512]{6,4,5,3,2,1,0:T(8,128)}, f32[2,4,2,2,8,4,512]{6,4,5,3,2,1,0:T(8,128)S(1)}, u32[]{:S(2)}, u32[]{:S(2)}) %collective-permute-start.2) | collective-permute-done | bytes 2097184 | tf_op jit(solution)/shard_map/ppermute | solution.py:215
  147.2 2.1 fusion
  149.2 1.4 copy.78
  150.6 1.8 reshape.190
  152.5 44.9 %reduce-scatter.2.cloned.1.call-done = f32[1,512,128]{2,1,0:T(8,128)} async-done(((f32[8,512,128]{2,1,0:T(8,128)}), f32[1,512,128]{2,1,0:T(8,128)}) %reduce-scatter.2.cloned.1.call-update) | async-done | bytes 262160 | tf_op jit(solution)/shard_map/reduce_scatter | solution.py:217
  197.3 1.0 reshape.191
  198.4 3.1 %collective-permute-start.4 = (f32[4,2,4,512]{3,2,1,0:T(4,128)S(1)}, f32[4,2,4,512]{3,2,1,0:T(4,128)S(1)}, u32[]{:S(2)}, u32[]{:S(2)}) collective-permute-start(f32[4,2,4,512]{3,2,1,0:T(4,128)S(1)} %get-tuple-element.28), channel_id=1, source_target_pairs={{0,4},{4,0},{1,5},{5,1},{2,6},{6,2},{3,7},{7,3},{8,12},{12,8},{9,1... | collective-permute-start | bytes 196616 | tf_op jit(solution)/shard_map/ppermute | solution.py:226
  201.5 1.2 collective-permute-start.5
  202.7 1.5 collective-permute-done.4
  204.3 2.7 %collective-permute-done.5 = f32[4,2,4,512]{3,2,1,0:T(4,128)S(1)} collective-permute-done((f32[4,2,4,512]{3,2,1,0:T(4,128)S(1)}, f32[4,2,4,512]{3,2,1,0:T(4,128)S(1)}, u32[]{:S(2)}, u32[]{:S(2)}) %collective-permute-start.5) | collective-permute-done | bytes 65568 | tf_op jit(solution)/shard_map/ppermute | solution.py:227
  207.1 0.7 fusion.26
  (72 shorter events, 4.4 us)
Async XLA Ops:
  7.2 51.7 %all-gather.3.cloned.1.call-start = ((), (), s32[]{:S(2)}) async-start(), calls=%async_computation.1 | async-start | bytes 2359296 | tf_op jit(solution)/shard_map/all_gather | solution.py:169
  14.7 182.6 %reduce-scatter.2.cloned.1.call-start = ((), (), s32[]{:S(2)}) async-start(), calls=%async_computation.2 | async-start | bytes 2359296 | tf_op jit(solution)/shard_map/reduce_scatter | solution.py:217
  57.0 7.3 %copy-start.5 = (bf16[4,256,1024]{2,1,0:T(8,128)(2,1)S(1)}, bf16[4,256,1024]{2,1,0:T(8,128)(2,1)}, u32[]{:S(2)}) copy-start(bf16[4,256,1024]{2,1,0:T(8,128)(2,1)} %get-tuple-element.11) | copy-start | bytes 6291460
  61.1 8.1 %copy-start.20 = (s32[1,1,16,16]{3,2,1,0:T(8,128)S(1)}, s32[1,1,16,16]{3,2,1,0:T(8,128)}, u32[]{:S(2)}) copy-start(s32[1,1,16,16]{3,2,1,0:T(8,128)} %param.15) | copy-start | bytes 3076
  61.2 8.1 %copy-start = (bf16[1,2048,1,128]{3,1,2,0:T(8,128)(2,1)S(1)}, bf16[1,2048,1,128]{3,1,2,0:T(8,128)(2,1)}, u32[]{:S(2)}) copy-start(bf16[1,2048,1,128]{3,1,2,0:T(8,128)(2,1)} %param.11) | copy-start | bytes 1572868
  61.2 8.1 %copy-start.1 = (bf16[1,2048,1,128]{3,1,2,0:T(8,128)(2,1)S(1)}, bf16[1,2048,1,128]{3,1,2,0:T(8,128)(2,1)}, u32[]{:S(2)}) copy-start(bf16[1,2048,1,128]{3,1,2,0:T(8,128)(2,1)} %param.12) | copy-start | bytes 1572868
  61.2 8.1 %copy-start.2 = (bf16[1,2048,1,128]{3,1,2,0:T(8,128)(2,1)S(1)}, bf16[1,2048,1,128]{3,1,2,0:T(8,128)(2,1)}, u32[]{:S(2)}) copy-start(bf16[1,2048,1,128]{3,1,2,0:T(8,128)(2,1)} %param.13) | copy-start | bytes 1572868
  61.2 8.0 %collective-permute-start = (bf16[1024,128]{1,0:T(8,128)(2,1)S(1)}, bf16[1024,128]{1,0:T(8,128)(2,1)S(1)}, u32[]{:S(2)}, u32[]{:S(2)}) collective-permute-start(bf16[1024,128]{1,0:T(8,128)(2,1)S(1)} %convolution_convert_fusion), channel_id=1, source_target_pairs={{0,4},{4,0},{1,5},{5,1},{2,6},{6,2},{3,7},{7,3},{8,12},{12,8},{9,1... | collective-permute-start | bytes 786440 | tf_op jit(solution)/shard_map/ppermute | solution.py:181
  93.7 1.2 copy-start.3
  99.1 24.8 %collective-permute-start.1 = (bf16[4,1024,128]{2,1,0:T(8,128)(2,1)}, bf16[4,1024,128]{2,1,0:T(8,128)(2,1)S(1)}, u32[]{:S(2)}, u32[]{:S(2)}) collective-permute-start(bf16[4,1024,128]{2,1,0:T(8,128)(2,1)} %constant_dynamic-slice_fusion), channel_id=1, source_target_pairs={{0,4},{4,0},{1,5},{5,1},{2,6},{6,2},{3,7},{7,3},{8,12},{12,8},{9,1... | collective-permute-start | bytes 3145736 | tf_op jit(solution)/shard_map/ppermute | solution.py:196
  102.3 2.4 %copy-start.6 = (bf16[4,256,1024]{2,1,0:T(8,128)(2,1)S(1)}, bf16[4,256,1024]{2,1,0:T(8,128)(2,1)}, u32[]{:S(2)}) copy-start(bf16[4,256,1024]{2,1,0:T(8,128)(2,1)} %get-tuple-element.11) | copy-start | bytes 6291460
  102.3 2.4 %copy-start.19 = (bf16[2,8,2,4,1024]{4,3,2,1,0:T(4,128)(2,1)S(1)}, bf16[2,8,2,4,1024]{4,3,2,1,0:T(4,128)(2,1)}, u32[]{:S(2)}) copy-start(bf16[2,8,2,4,1024]{4,3,2,1,0:T(4,128)(2,1)} %reshape.185) | copy-start | bytes 786436
  125.0 2.1 copy-start.14
  135.2 3.7 %copy-start.7 = (f32[1,1,1,2,8,2,4,512]{7,4,6,5,3,2,1,0:T(8,128)S(1)}, f32[1,1,1,2,8,2,4,512]{7,4,6,5,3,2,1,0:T(8,128)}, u32[]{:S(2)}) copy-start(f32[1,1,1,2,8,2,4,512]{7,4,6,5,3,2,1,0:T(8,128)} %convolution_bitcast_fusion.15) | copy-start | bytes 786436
  138.0 1.0 copy-start.8
  138.1 1.0 copy-start.9
  138.1 1.1 copy-start.10
  138.1 1.2 copy-start.11
  138.1 1.2 copy-start.12
  138.1 1.3 copy-start.13
  138.1 1.4 copy-start.15
  138.1 1.4 copy-start.16
  138.1 1.5 copy-start.17
  138.1 1.6 copy-start.18
  140.2 2.6 %copy-start.4 = (f32[2,4,2,2,8,2,4,512]{7,4,6,5,3,2,1,0:T(8,128)}, f32[2,4,2,2,8,2,4,512]{7,4,6,5,3,2,1,0:T(8,128)S(1)}, u32[]{:S(2)}) copy-start(f32[2,4,2,2,8,2,4,512]{7,4,6,5,3,2,1,0:T(8,128)S(1)} %maximum_maximum_fusion) | copy-start | bytes 12582916
  142.8 4.4 %collective-permute-start.2 = (f32[2,4,2,2,8,4,512]{6,4,5,3,2,1,0:T(8,128)}, f32[2,4,2,2,8,4,512]{6,4,5,3,2,1,0:T(8,128)S(1)}, u32[]{:S(2)}, u32[]{:S(2)}) collective-permute-start(f32[2,4,2,2,8,4,512]{6,4,5,3,2,1,0:T(8,128)} %dynamic-slice_bitcast_fusion), channel_id=1, source_target_pairs={{0,8},{8,0},{1,9},{9,1},{2,10},{10,2},{3,11},{11,3},{4,12},{12,4},... | collective-permute-start | bytes 6291464 | tf_op jit(solution)/shard_map/ppermute | solution.py:215
  198.4 5.9 %collective-permute-start.4 = (f32[4,2,4,512]{3,2,1,0:T(4,128)S(1)}, f32[4,2,4,512]{3,2,1,0:T(4,128)S(1)}, u32[]{:S(2)}, u32[]{:S(2)}) collective-permute-start(f32[4,2,4,512]{3,2,1,0:T(4,128)S(1)} %get-tuple-element.28), channel_id=1, source_target_pairs={{0,4},{4,0},{1,5},{5,1},{2,6},{6,2},{3,7},{7,3},{8,12},{12,8},{9,1... | collective-permute-start | bytes 196616 | tf_op jit(solution)/shard_map/ppermute | solution.py:226
  201.5 5.5 %collective-permute-start.5 = (f32[4,2,4,512]{3,2,1,0:T(4,128)S(1)}, f32[4,2,4,512]{3,2,1,0:T(4,128)S(1)}, u32[]{:S(2)}, u32[]{:S(2)}) collective-permute-start(f32[4,2,4,512]{3,2,1,0:T(4,128)S(1)} %get-tuple-element.29), channel_id=1, source_target_pairs={{0,132},{132,0},{4,128},{128,4},{1,133},{133,1},{5,129},{129,5},{2... | collective-permute-start | bytes 196616 | tf_op jit(solution)/shard_map/ppermute | solution.py:227
  202.7 4.3 %collective-permute-start.3 = (f32[4,2,4,512]{3,2,1,0:T(4,128)S(1)}, f32[4,2,4,512]{3,2,1,0:T(4,128)S(1)}, u32[]{:S(2)}, u32[]{:S(2)}) collective-permute-start(f32[4,2,4,512]{3,2,1,0:T(4,128)S(1)} %slice_bitcast_fusion.12), channel_id=1, source_target_pairs={{0,128},{128,0},{1,129},{129,1},{2,130},{130,2},{3,131},{131,3},{4... | collective-permute-start | bytes 196616 | tf_op jit(solution)/shard_map/ppermute | solution.py:225
Sparse Core Ops, SparseCore 0:
  14.8 43.9 all-gather.2
  152.6 44.6 reduce-scatter.1

commit v14 on v12

--- a/solution.py
+++ b/solution.py
@@ -54,13 +54,13 @@
     d_score = (prob * (d_prob - row_delta)).astype(jnp.bfloat16)
     dq_ref[...] = (jnp.dot(d_score, k, preferred_element_type=jnp.float32) * scale).astype(jnp.bfloat16)
     att_ref[...] = attended
-    dk_acc[...] += lax.dot_general(d_score, q, tn, preferred_element_type=jnp.float32)
-    dv_acc[...] += lax.dot_general(prob_low, g, tn, preferred_element_type=jnp.float32)
+    dk_acc[...] += lax.dot_general(q, d_score, tn, preferred_element_type=jnp.float32)
+    dv_acc[...] += lax.dot_general(g, prob_low, tn, preferred_element_type=jnp.float32)
 
     @pl.when(step == steps - 1)
     def _():
-        dk_ref[...] = (dk_acc[...] * scale).astype(jnp.bfloat16)
-        dv_ref[...] = dv_acc[...].astype(jnp.bfloat16)
+        dk_ref[...] = (dk_acc[...].T * scale).astype(jnp.bfloat16)
+        dv_ref[...] = dv_acc[...].T.astype(jnp.bfloat16)
         for copy in copies:
             copy.wait()
 
@@ -80,8 +80,8 @@
         out_specs=[row_spec, row_spec, full_spec, full_spec, any_spec],
         out_shape=[out, out, out, out, jax.ShapeDtypeStruct((nseq,) + x.shape, x.dtype)],
         scratch_shapes=[
-            pltpu.VMEM((length, HD), jnp.float32),
-            pltpu.VMEM((length, HD), jnp.float32),
+            pltpu.VMEM((HD, length), jnp.float32),
+            pltpu.VMEM((HD, length), jnp.float32),
             pltpu.SemaphoreType.DMA((nseq - 1,)),
             pltpu.SemaphoreType.DMA((nseq - 1,)),
             pltpu.SemaphoreType.DMA(()),

time: 203 us -> 203 us (level)
  no operation moved by 1% of the time
where the time goes in v14:
time: 203 us; the launch traced here: 202 us
  waiting for transfers between devices  70.5 us (35%)
  Pallas kernels  47.4 us (23%)
  local copies, waits for them, and re-layouts  26.1 us (13%)
  matrix products  20 us (10%)
  between operations  14.5 us (7%)
  starting transfers between devices  10.6 us (5%)
  blocking collectives  7.45 us (4%)
  other arithmetic  5.48 us (3%)
    reduce_scatter x1, waiting for transfers between devices, local(): lax.psum_scatter(terms.reshape(nz, -1, 128), 'dpz', scatter_dimension=0,...  41.8 us
    pallas_call x1, Pallas kernels, seq_gather(): pl.pallas_call(functools.partial(gather_kernel, nseq), in_specs=[any_spec...  26.6 us
    pallas_call x1, Pallas kernels, attention_backward(): pl.pallas_call(functools.partial(attention_kernel, nseq), grid=(length //...  20.9 us
    all_gather x1, waiting for transfers between devices, local(): gathered = lax.all_gather(gathered, 'dpz', axis=0)  14.9 us
    all_gather x1, blocking collectives, local(): lax.all_gather(out_weight, ('dpy', 'dpc'), axis=0)  7.45 us
    another operation x8, local copies, waits for them, and re-layouts  7.44 us
    dot_general x2, matrix products, terms_of(): lax.dot_general(parts[0], inputs_half, tn, preferred_element_type=jnp.flo...  6.1 us
    ppermute x1, waiting for transfers between devices, local(): terms = kept + lax.ppermute(sent, 'dpc', swap)  4.37 us
  transfers between devices with their start and end apart: 8, of which 7 were waited for; matrix products, arithmetic and copies ran while one was open for 12% of the time, Pallas kernels for 13%

profile of v14, /device:TPU:2, one launch (start us, length us, event | category | flops | bytes accessed | tf_op | source)
XLA Modules:
  0.0 202.1 jit_solution(1132238332401003047)
XLA Ops:
  7.2 7.4 %all-gather = bf16[128,1024]{1,0:T(8,128)(2,1)} all-gather(bf16[32,1024]{1,0:T(8,128)(2,1)} %param.14), channel_id=2, replica_groups=mesh['dpy'=2,'dpz'=8,'dpc'=2,'sqy'=2,'sqx'=4] {'dpy','dpc'}, dimensions={0}, use_global_device_ids=true | all-gather | bytes 327680 | tf_op jit(solution)/shard_map/all_gather | solution.py:164
  14.7 0.7 convert_reduce_fusion
  15.4 1.9 bitcast_multiply_fusion.a_ref
  17.4 26.6 %shard_map.111 = bf16[4,256,1024]{2,1,0:T(8,128)(2,1)} custom-call(bf16[256,1024]{1,0:T(8,128)(2,1)} %bitcast_multiply_fusion.a_ref), custom_call_target="tpu_custom_call" | custom-call | tf_op jit(solution)/shard_map/pallas_call | solution.py:136
  44.0 14.9 %all-gather.3.cloned.1.call-done = bf16[8,2,2,32,1024]{4,3,2,0,1:T(8,128)(2,1)} async-done(((bf16[1,2,2,32,1024]{4,3,2,0,1:T(8,128)(2,1)}), bf16[8,2,2,32,1024]{4,3,2,0,1:T(8,128)(2,1)}) %all-gather.3.cloned.1.call-update) | async-done | bytes 2097168 | tf_op jit(solution)/shard_map/all_gather | solution.py:165
  58.8 2.3 %convolution_convert_fusion = bf16[1024,128]{1,0:T(8,128)(2,1)S(1)} fusion(bf16[1024,1024]{1,0:T(8,128)(2,1)} %bitcast.126, bf16[1024,1024]{1,0:T(8,128)(2,1)} %bitcast.131, s32[]{:T(128)S(6)} %select_n.30), kind=kOutput, calls=%fused_computation.13 | convolution fusion | flops 268566528 | bytes 2621444 | tf_op jit(solution)/shard_map/dot_general | solution.py:173
  61.2 3.1 %collective-permute-start = (bf16[1024,128]{1,0:T(8,128)(2,1)S(1)}, bf16[1024,128]{1,0:T(8,128)(2,1)S(1)}, u32[]{:S(2)}, u32[]{:S(2)}) collective-permute-start(bf16[1024,128]{1,0:T(8,128)(2,1)S(1)} %convolution_convert_fusion), channel_id=1, source_target_pairs={{0,4},{4,0},{1,5},{5,1},{2,6},{6,2},{3,7},{7,3},{8,12},{12,8},{9,1... | collective-permute-start | bytes 786440 | tf_op jit(solution)/shard_map/ppermute | solution.py:174
  64.4 1.8 fusion.1
  66.2 3.0 %collective-permute-done = bf16[1024,128]{1,0:T(8,128)(2,1)S(1)} collective-permute-done((bf16[1024,128]{1,0:T(8,128)(2,1)S(1)}, bf16[1024,128]{1,0:T(8,128)(2,1)S(1)}, u32[]{:S(2)}, u32[]{:S(2)}) %collective-permute-start) | collective-permute-done | bytes 262176 | tf_op jit(solution)/shard_map/ppermute | solution.py:174
  69.3 20.9 %shard_map.112 = (bf16[2048,128]{1,0:T(8,128)(2,1)S(1)}, bf16[2048,128]{1,0:T(8,128)(2,1)S(1)}, bf16[2048,128]{1,0:T(8,128)(2,1)S(1)}, bf16[2048,128]{1,0:T(8,128)(2,1)S(1)}, bf16[4,256,1024]{2,1,0:T(8,128)(2,1)}) custom-call(bf16[2048,128]{1,0:T(8,128)(2,1)S(1)} %bitcast.122, bf16[2048,128]{1,0:T(8,128)(2,1)S(1)} %bitcast.123, ...), custom_call_target="tpu_custom_call" | custom-call | flops 6442450944 | bytes 4194304 | tf_op jit(solution)/shard_map/pallas_call | solution.py:76
  90.6 3.3 %collective-permute-start.1 = (bf16[4,1024,128]{2,1,0:T(8,128)(2,1)S(1)}, bf16[4,1024,128]{2,1,0:T(8,128)(2,1)}, u32[]{:S(2)}, u32[]{:S(2)}) collective-permute-start(bf16[4,1024,128]{2,1,0:T(8,128)(2,1)S(1)} %constant_dynamic-slice_fusion), channel_id=1, source_target_pairs={{0,4},{4,0},{1,5},{5,1},{2,6},{6,2},{3,7},{7,3},{8,12},{12,8},{9,1... | collective-permute-start | bytes 3145736 | tf_op jit(solution)/shard_map/ppermute | solution.py:187
  93.8 0.9 dynamic-slice_bitcast_fusion.4
  94.8 1.8 copy.42
  96.6 1.7 reshape.110
  98.3 1.8 copy.46
  100.1 1.8 reshape.113
  101.9 1.8 copy.44
  103.7 1.8 reshape.112
  105.4 0.9 copy.48
  106.3 1.1 reshape.114
  107.4 3.2 %convolution_bitcast_fusion.7 = f32[1,1,2,8,2,4,1024]{6,3,5,4,2,1,0:T(8,128)} fusion(bf16[1024,1024,1,1,1]{1,0,4,3,2:T(8,128)(2,1)} %bitcast.134, bf16[2,8,2,4,1024]{4,3,2,1,0:T(4,128)(2,1)} %reshape.110), kind=kOutput, calls=%fused_computation.12 | convolution fusion | flops 268435456 | bytes 2883584 | tf_op jit(solution)/shard_map/dot_general | solution.py:193
  110.5 1.3 convolution_bitcast_fusion.5
  111.8 1.3 convolution_bitcast_fusion.6
  113.2 1.3 convolution_bitcast_fusion.4
  114.5 2.0 %collective-permute-done.1 = bf16[4,1024,128]{2,1,0:T(8,128)(2,1)} collective-permute-done((bf16[4,1024,128]{2,1,0:T(8,128)(2,1)S(1)}, bf16[4,1024,128]{2,1,0:T(8,128)(2,1)}, u32[]{:S(2)}, u32[]{:S(2)}) %collective-permute-start.1) | collective-permute-done | bytes 1048608 | tf_op jit(solution)/shard_map/ppermute | solution.py:187
  116.6 1.3 slice_bitcast_fusion.3
  118.1 2.9 %convolution_bitcast_fusion.3 = f32[1,1,2,8,2,4,1024]{6,3,5,4,2,1,0:T(8,128)} fusion(bf16[1024,1024,1,1,1]{1,0,4,3,2:T(8,128)(2,1)} %bitcast.135, bf16[2,8,2,4,1024]{4,3,2,1,0:T(4,128)(2,1)S(1)} %reshape.115), kind=kOutput, calls=%fused_computation.8 | convolution fusion | flops 268435456 | bytes 2883584 | tf_op jit(solution)/shard_map/dot_general | solution.py:193
  121.2 0.8 reshape.118
  122.0 1.5 convolution_bitcast_fusion
  123.7 2.1 %convolution_bitcast_fusion.1 = f32[1,1,2,8,2,4,1024]{6,3,5,4,2,1,0:T(8,128)S(1)} fusion(bf16[1024,1024,1,1,1]{1,0,4,3,2:T(8,128)(2,1)} %bitcast.136, bf16[2,8,2,4,1024]{4,3,2,1,0:T(4,128)(2,1)S(1)} %reshape.117), kind=kOutput, calls=%fused_computation.6 | convolution fusion | flops 268435456 | bytes 2883584 | tf_op jit(solution)/shard_map/dot_general | solution.py:195
  126.2 2.3 %convolution_bitcast_fusion.2 = f32[1,1,2,8,2,4,1024]{6,3,5,4,2,1,0:T(8,128)S(1)} fusion(bf16[1024,1024,1,1,1]{1,0,4,3,2:T(8,128)(2,1)} %bitcast.137, bf16[2,8,2,4,1024]{4,3,2,1,0:T(4,128)(2,1)S(1)} %reshape.116), kind=kOutput, calls=%fused_computation.7 | convolution fusion | flops 268435456 | bytes 2883584 | tf_op jit(solution)/shard_map/dot_general | solution.py:194
  128.5 0.5 maximum_maximum_fusion
  129.1 1.6 dynamic-slice_bitcast_fusion
  130.7 1.0 copy-done.4
  131.7 4.4 %collective-permute-done.2 = f32[2,4,2,8,4,1024]{5,3,4,2,1,0:T(8,128)S(1)} collective-permute-done((f32[2,4,2,8,4,1024]{5,3,4,2,1,0:T(8,128)}, f32[2,4,2,8,4,1024]{5,3,4,2,1,0:T(8,128)S(1)}, u32[]{:S(2)}, u32[]{:S(2)}) %collective-permute-start.2) | collective-permute-done | bytes 2097184 | tf_op jit(solution)/shard_map/ppermute | solution.py:208
  136.0 2.0 fusion
  138.0 1.4 copy.58
  139.4 1.8 reshape.119
  141.2 41.8 %reduce-scatter.2.cloned.1.call-done = f32[1,512,128]{2,1,0:T(8,128)} async-done(((f32[8,512,128]{2,1,0:T(8,128)}), f32[1,512,128]{2,1,0:T(8,128)}) %reduce-scatter.2.cloned.1.call-update) | async-done | bytes 262160 | tf_op jit(solution)/shard_map/reduce_scatter | solution.py:210
  183.1 1.0 reshape.120
  184.2 3.0 %collective-permute-start.4 = (f32[4,4,1024]{2,1,0:T(4,128)S(1)}, f32[4,4,1024]{2,1,0:T(4,128)S(1)}, u32[]{:S(2)}, u32[]{:S(2)}) collective-permute-start(f32[4,4,1024]{2,1,0:T(4,128)S(1)} %get-tuple-element.30), channel_id=1, source_target_pairs={{0,4},{4,0},{1,5},{5,1},{2,6},{6,2},{3,7},{7,3},{8,12},{12,8},{9,1... | collective-permute-start | bytes 196616 | tf_op jit(solution)/shard_map/ppermute | solution.py:219
  187.2 1.1 collective-permute-start.5
  188.3 1.7 collective-permute-done.4
  190.0 2.7 %collective-permute-done.5 = f32[4,4,1024]{2,1,0:T(4,128)S(1)} collective-permute-done((f32[4,4,1024]{2,1,0:T(4,128)S(1)}, f32[4,4,1024]{2,1,0:T(4,128)S(1)}, u32[]{:S(2)}, u32[]{:S(2)}) %collective-permute-start.5) | collective-permute-done | bytes 65568 | tf_op jit(solution)/shard_map/ppermute | solution.py:220
  192.8 0.6 copy.64
  193.4 0.6 copy.63
  194.0 0.6 copy.62
  194.6 0.6 copy.61
  (53 shorter events, 1.7 us)
Async XLA Ops:
  7.2 51.7 %all-gather.3.cloned.1.call-start = ((), (), s32[]{:S(2)}) async-start(), calls=%async_computation.1 | async-start | bytes 2359296 | tf_op jit(solution)/shard_map/all_gather | solution.py:165
  14.7 168.4 %reduce-scatter.2.cloned.1.call-start = ((), (), s32[]{:S(2)}) async-start(), calls=%async_computation.2 | async-start | bytes 2359296 | tf_op jit(solution)/shard_map/reduce_scatter | solution.py:210
  44.0 20.4 %copy-start.5 = (bf16[4,256,1024]{2,1,0:T(8,128)(2,1)S(1)}, bf16[4,256,1024]{2,1,0:T(8,128)(2,1)}, u32[]{:S(2)}) copy-start(bf16[4,256,1024]{2,1,0:T(8,128)(2,1)} %shard_map.111) | copy-start | bytes 6291460
  61.1 8.1 %copy-start.13 = (s32[1,1,16,16]{3,2,1,0:T(8,128)S(1)}, s32[1,1,16,16]{3,2,1,0:T(8,128)}, u32[]{:S(2)}) copy-start(s32[1,1,16,16]{3,2,1,0:T(8,128)} %param.15) | copy-start | bytes 3076
  61.1 8.2 %copy-start = (bf16[1,2048,1,128]{3,1,2,0:T(8,128)(2,1)S(1)}, bf16[1,2048,1,128]{3,1,2,0:T(8,128)(2,1)}, u32[]{:S(2)}) copy-start(bf16[1,2048,1,128]{3,1,2,0:T(8,128)(2,1)} %param.11) | copy-start | bytes 1572868
  61.2 8.2 %copy-start.1 = (bf16[1,2048,1,128]{3,1,2,0:T(8,128)(2,1)S(1)}, bf16[1,2048,1,128]{3,1,2,0:T(8,128)(2,1)}, u32[]{:S(2)}) copy-start(bf16[1,2048,1,128]{3,1,2,0:T(8,128)(2,1)} %param.12) | copy-start | bytes 1572868
  61.2 8.2 %copy-start.2 = (bf16[1,2048,1,128]{3,1,2,0:T(8,128)(2,1)S(1)}, bf16[1,2048,1,128]{3,1,2,0:T(8,128)(2,1)}, u32[]{:S(2)}) copy-start(bf16[1,2048,1,128]{3,1,2,0:T(8,128)(2,1)} %param.13) | copy-start | bytes 1572868
  61.2 8.2 %copy-start.3 = (bf16[1,256,1024]{2,1,0:T(8,128)(2,1)S(1)}, bf16[1,256,1024]{2,1,0:T(8,128)(2,1)}, u32[]{:S(2)}) copy-start(bf16[1,256,1024]{2,1,0:T(8,128)(2,1)} %param.8) | copy-start | bytes 1572868
  61.2 8.0 %collective-permute-start = (bf16[1024,128]{1,0:T(8,128)(2,1)S(1)}, bf16[1024,128]{1,0:T(8,128)(2,1)S(1)}, u32[]{:S(2)}, u32[]{:S(2)}) collective-permute-start(bf16[1024,128]{1,0:T(8,128)(2,1)S(1)} %convolution_convert_fusion), channel_id=1, source_target_pairs={{0,4},{4,0},{1,5},{5,1},{2,6},{6,2},{3,7},{7,3},{8,12},{12,8},{9,1... | collective-permute-start | bytes 786440 | tf_op jit(solution)/shard_map/ppermute | solution.py:174
  90.6 26.0 %collective-permute-start.1 = (bf16[4,1024,128]{2,1,0:T(8,128)(2,1)S(1)}, bf16[4,1024,128]{2,1,0:T(8,128)(2,1)}, u32[]{:S(2)}, u32[]{:S(2)}) collective-permute-start(bf16[4,1024,128]{2,1,0:T(8,128)(2,1)S(1)} %constant_dynamic-slice_fusion), channel_id=1, source_target_pairs={{0,4},{4,0},{1,5},{5,1},{2,6},{6,2},{3,7},{7,3},{8,12},{12,8},{9,1... | collective-permute-start | bytes 3145736 | tf_op jit(solution)/shard_map/ppermute | solution.py:187
  107.3 3.2 %copy-start.11 = (bf16[2,8,2,4,1024]{4,3,2,1,0:T(4,128)(2,1)S(1)}, bf16[2,8,2,4,1024]{4,3,2,1,0:T(4,128)(2,1)}, u32[]{:S(2)}) copy-start(bf16[2,8,2,4,1024]{4,3,2,1,0:T(4,128)(2,1)} %reshape.113) | copy-start | bytes 786436
  107.3 3.2 %copy-start.14 = (bf16[4,256,1024]{2,1,0:T(8,128)(2,1)S(1)}, bf16[4,256,1024]{2,1,0:T(8,128)(2,1)}, u32[]{:S(2)}) copy-start(bf16[4,256,1024]{2,1,0:T(8,128)(2,1)} %get-tuple-element.13) | copy-start | bytes 6291460
  110.5 1.3 copy-start.12
  126.1 2.3 %copy-start.6 = (f32[1,1,2,8,2,4,1024]{6,3,5,4,2,1,0:T(8,128)S(1)}, f32[1,1,2,8,2,4,1024]{6,3,5,4,2,1,0:T(8,128)}, u32[]{:S(2)}) copy-start(f32[1,1,2,8,2,4,1024]{6,3,5,4,2,1,0:T(8,128)} %convolution_bitcast_fusion.7) | copy-start | bytes 1572868
  126.1 2.3 %copy-start.7 = (f32[1,1,2,8,2,4,1024]{6,3,5,4,2,1,0:T(8,128)S(1)}, f32[1,1,2,8,2,4,1024]{6,3,5,4,2,1,0:T(8,128)}, u32[]{:S(2)}) copy-start(f32[1,1,2,8,2,4,1024]{6,3,5,4,2,1,0:T(8,128)} %convolution_bitcast_fusion.5) | copy-start | bytes 1572868
  126.2 2.3 %copy-start.8 = (f32[1,1,2,8,2,4,1024]{6,3,5,4,2,1,0:T(8,128)S(1)}, f32[1,1,2,8,2,4,1024]{6,3,5,4,2,1,0:T(8,128)}, u32[]{:S(2)}) copy-start(f32[1,1,2,8,2,4,1024]{6,3,5,4,2,1,0:T(8,128)} %convolution_bitcast_fusion.6) | copy-start | bytes 1572868
  126.2 2.3 %copy-start.9 = (f32[1,1,2,8,2,4,1024]{6,3,5,4,2,1,0:T(8,128)S(1)}, f32[1,1,2,8,2,4,1024]{6,3,5,4,2,1,0:T(8,128)}, u32[]{:S(2)}) copy-start(f32[1,1,2,8,2,4,1024]{6,3,5,4,2,1,0:T(8,128)} %convolution_bitcast_fusion.4) | copy-start | bytes 1572868
  126.2 2.3 %copy-start.10 = (f32[1,1,2,8,2,4,1024]{6,3,5,4,2,1,0:T(8,128)S(1)}, f32[1,1,2,8,2,4,1024]{6,3,5,4,2,1,0:T(8,128)}, u32[]{:S(2)}) copy-start(f32[1,1,2,8,2,4,1024]{6,3,5,4,2,1,0:T(8,128)} %convolution_bitcast_fusion.3) | copy-start | bytes 1572868
  129.1 2.6 %copy-start.4 = (f32[2,4,2,8,2,4,1024]{6,3,5,4,2,1,0:T(8,128)}, f32[2,4,2,8,2,4,1024]{6,3,5,4,2,1,0:T(8,128)S(1)}, u32[]{:S(2)}) copy-start(f32[2,4,2,8,2,4,1024]{6,3,5,4,2,1,0:T(8,128)S(1)} %maximum_maximum_fusion) | copy-start | bytes 12582916
  131.7 4.4 %collective-permute-start.2 = (f32[2,4,2,8,4,1024]{5,3,4,2,1,0:T(8,128)}, f32[2,4,2,8,4,1024]{5,3,4,2,1,0:T(8,128)S(1)}, u32[]{:S(2)}, u32[]{:S(2)}) collective-permute-start(f32[2,4,2,8,4,1024]{5,3,4,2,1,0:T(8,128)} %dynamic-slice_bitcast_fusion), channel_id=1, source_target_pairs={{0,8},{8,0},{1,9},{9,1},{2,10},{10,2},{3,11},{11,3},{4,12},{12,4},... | collective-permute-start | bytes 6291464 | tf_op jit(solution)/shard_map/ppermute | solution.py:208
  184.2 5.9 %collective-permute-start.4 = (f32[4,4,1024]{2,1,0:T(4,128)S(1)}, f32[4,4,1024]{2,1,0:T(4,128)S(1)}, u32[]{:S(2)}, u32[]{:S(2)}) collective-permute-start(f32[4,4,1024]{2,1,0:T(4,128)S(1)} %get-tuple-element.30), channel_id=1, source_target_pairs={{0,4},{4,0},{1,5},{5,1},{2,6},{6,2},{3,7},{7,3},{8,12},{12,8},{9,1... | collective-permute-start | bytes 196616 | tf_op jit(solution)/shard_map/ppermute | solution.py:219
  187.2 5.5 %collective-permute-start.5 = (f32[4,4,1024]{2,1,0:T(4,128)S(1)}, f32[4,4,1024]{2,1,0:T(4,128)S(1)}, u32[]{:S(2)}, u32[]{:S(2)}) collective-permute-start(f32[4,4,1024]{2,1,0:T(4,128)S(1)} %get-tuple-element.31), channel_id=1, source_target_pairs={{0,132},{132,0},{4,128},{128,4},{1,133},{133,1},{5,129},{129,5},{2... | collective-permute-start | bytes 196616 | tf_op jit(solution)/shard_map/ppermute | solution.py:220
  188.3 4.4 %collective-permute-start.3 = (f32[4,4,1024]{2,1,0:T(4,128)S(1)}, f32[4,4,1024]{2,1,0:T(4,128)S(1)}, u32[]{:S(2)}, u32[]{:S(2)}) collective-permute-start(f32[4,4,1024]{2,1,0:T(4,128)S(1)} %slice_bitcast_fusion.4), channel_id=1, source_target_pairs={{0,128},{128,0},{1,129},{129,1},{2,130},{130,2},{3,131},{131,3},{4... | collective-permute-start | bytes 196616 | tf_op jit(solution)/shard_map/ppermute | solution.py:218
Sparse Core Ops, SparseCore 0:
  14.8 43.9 all-gather.2
  141.4 41.6 reduce-scatter.1

commit v15 on v14

--- a/solution.py
+++ b/solution.py
@@ -15,14 +15,15 @@
 
 
 def attention_kernel(
-    nseq, q_ref, k_ref, v_ref, g_ref, m_ref, x_ref, dq_ref, att_ref, dk_ref, dv_ref, x_out,
+    nseq, q_ref, k_ref, v_ref, g_ref, m_ref, x_ref, x_buf, dq_ref, att_ref, dk_ref, dv_ref, x_out,
     dk_acc, dv_acc, send_sem, recv_sem, copy_sem,
 ):
     step = pl.program_id(0)
     steps = pl.num_programs(0)
     scale = HD ** (-0.5)
     groups = ROWS // BLOCK
-    copies = start_gather(nseq, x_ref, x_out, send_sem, recv_sem, copy_sem)
+    far = [off for off in range(1, nseq) if min(off, nseq - off) > 1]
+    copies = start_gather(nseq, x_ref, x_out, send_sem, recv_sem, copy_sem, far, local=False)
 
     @pl.when(step == 0)
     def _():
@@ -65,7 +66,7 @@
             copy.wait()
 
 
-def attention_backward(q, k, v, g, live_cols, x, nseq):
+def attention_backward(q, k, v, g, live_cols, x, x_buf, nseq):
     length = q.shape[0]
     row_spec = pl.BlockSpec((ROWS, HD), lambda i: (i, 0))
     full_spec = pl.BlockSpec((length, HD), lambda i: (0, 0))
@@ -76,9 +77,10 @@
     return pl.pallas_call(
         functools.partial(attention_kernel, nseq),
         grid=(length // ROWS,),
-        in_specs=[row_spec, full_spec, full_spec, row_spec, mask_spec, any_spec],
+        in_specs=[row_spec, full_spec, full_spec, row_spec, mask_spec, any_spec, any_spec],
         out_specs=[row_spec, row_spec, full_spec, full_spec, any_spec],
-        out_shape=[out, out, out, out, jax.ShapeDtypeStruct((nseq,) + x.shape, x.dtype)],
+        out_shape=[out, out, out, out, jax.ShapeDtypeStruct(x_buf.shape, x_buf.dtype)],
+        input_output_aliases={6: 4},
         scratch_shapes=[
             pltpu.VMEM((HD, length), jnp.float32),
             pltpu.VMEM((HD, length), jnp.float32),
@@ -92,13 +94,13 @@
         cost_estimate=pl.CostEstimate(
             flops=flops, transcendentals=length * length, bytes_accessed=8 * length * HD * 2
         ),
-    )(q, k, v, g, live_cols, x)
-
-
-def start_gather(nseq, src, dst, send_sem, recv_sem, copy_sem):
+    )(q, k, v, g, live_cols, x, x_buf)
+
+
+def start_gather(nseq, src, dst, send_sem, recv_sem, copy_sem, offsets=None, local=True):
     me = lax.axis_index("sqx")
-    copies = [pltpu.make_async_copy(src, dst.at[me], copy_sem)]
-    for off in range(1, nseq):
+    copies = [pltpu.make_async_copy(src, dst.at[me], copy_sem)] if local else []
+    for off in offsets or range(1, nseq):
         peer = (me + off) % nseq
         copies.append(
             pltpu.make_async_remote_copy(
@@ -122,29 +124,34 @@
     pl.semaphore_wait(barrier, nseq - 1)
 
 
-def gather_kernel(nseq, a_ref, a_out, send_sem, recv_sem, copy_sem):
+def gather_kernel(nseq, a_ref, b_ref, a_out, b_out, send_sem, recv_sem, copy_sem):
     enter_barrier(nseq)
-    copies = start_gather(nseq, a_ref, a_out, send_sem, recv_sem, copy_sem)
+    copies = start_gather(nseq, a_ref, a_out, send_sem.at[0], recv_sem.at[0], copy_sem.at[0])
+    near = [off for off in range(1, nseq) if min(off, nseq - off) == 1]
+    copies += start_gather(nseq, b_ref, b_out, send_sem.at[1], recv_sem.at[1], copy_sem.at[1], near)
     for copy in copies:
         copy.start()
     for copy in copies:
         copy.wait()
 
 
-def seq_gather(a, nseq):
+def seq_gather(a, b, nseq):
     any_spec = pl.BlockSpec(memory_space=pl.ANY)
     return pl.pallas_call(
         functools.partial(gather_kernel, nseq),
-        in_specs=[any_spec],
-        out_specs=any_spec,
-        out_shape=jax.ShapeDtypeStruct((nseq,) + a.shape, a.dtype),
+        in_specs=[any_spec, any_spec],
+        out_specs=[any_spec, any_spec],
+        out_shape=[
+            jax.ShapeDtypeStruct((nseq,) + a.shape, a.dtype),
+            jax.ShapeDtypeStruct((nseq,) + b.shape, b.dtype),
+        ],
         scratch_shapes=[
-            pltpu.SemaphoreType.DMA((nseq - 1,)),
-            pltpu.SemaphoreType.DMA((nseq - 1,)),
-            pltpu.SemaphoreType.DMA(()),
+            pltpu.SemaphoreType.DMA((2, nseq - 1)),
+            pltpu.SemaphoreType.DMA((2, nseq - 1)),
+            pltpu.SemaphoreType.DMA((2,)),
         ],
         compiler_params=pltpu.CompilerParams(collective_id=0, has_side_effects=True),
-    )(a)
+    )(a, b)
 
 
 DP = ("dpy", "dpz", "dpc")
@@ -166,7 +173,8 @@
     gathered = jnp.transpose(gathered, (1, 0, 2, 3, 4)).reshape(-1, width)
     head_weight = lax.dynamic_slice_in_dim(gathered, head * HD, HD, 0)
     partner_weight = lax.dynamic_slice_in_dim(gathered, partner_head * HD, HD, 0)
-    masked_half = seq_gather(masked, sizes["sqx"]).reshape(-1, width)
+    masked_half, inputs_near = seq_gather(masked, inputs[0], sizes["sqx"])
+    masked_half = masked_half.reshape(-1, width)
     half_len = masked_half.shape[0]
     nt = (((1,), (1,)), ((), ()))
     d_own = lax.dot_general(masked_half, head_weight, nt, preferred_element_type=jnp.float32).astype(jnp.bfloat16)
@@ -178,7 +186,7 @@
     blocks = block_mask[0, 0]
     live_cols = jnp.repeat(blocks, BLOCK, axis=1)[:, None, :]
     d_query, attended, d_key, d_value, inputs_half = attention_backward(
-        queries[0, :, 0], keys[0, :, 0], values[0, :, 0], d_attn, live_cols, inputs[0], sizes["sqx"]
+        queries[0, :, 0], keys[0, :, 0], values[0, :, 0], d_attn, live_cols, inputs[0], inputs_near, sizes["sqx"]
     )
     inputs_half = inputs_half.reshape(-1, width)
     grads = jnp.stack([d_query, d_key, d_value, attended])

time: 203 us -> 208 us (1.025)
  Pallas kernels: 47.4 us -> 57.8 us
  waiting for transfers between devices: 70.5 us -> 65.2 us
    pallas_call x1, Pallas kernels: 26.6 us -> 38.7 us  [seq_gather(): pl.pallas_call(functools.partial(gather_kernel, nseq), in_specs=[any_spec...]
    all_gather x1, waiting for transfers between devices: 14.9 us -> 4.53 us  [local(): gathered = lax.all_gather(gathered, 'dpz', axis=0)]
    reduce_scatter x1, waiting for transfers between devices: 41.8 us -> 44.8 us  [local(): lax.psum_scatter(terms.reshape(nz, -1, 128), 'dpz', scatter_dimension=0,...]
  transfers between devices with their start and end apart: 8 -> 8, of which waited for: 7 -> 7; matrix products, arithmetic and copies ran while one was open for 12% -> 12% of each run, Pallas kernels for 13% -> 19%
where the time goes in v15:
time: 208 us; the launch traced here: 207 us
  waiting for transfers between devices  65.2 us (31%)
  Pallas kernels  57.8 us (28%)
  local copies, waits for them, and re-layouts  26.1 us (13%)
  matrix products  20 us (10%)
  between operations  14.5 us (7%)
  starting transfers between devices  10.4 us (5%)
  blocking collectives  7.44 us (4%)
  other arithmetic  5.48 us (3%)
    reduce_scatter x1, waiting for transfers between devices, local(): lax.psum_scatter(terms.reshape(nz, -1, 128), 'dpz', scatter_dimension=0,...  44.8 us
    pallas_call x1, Pallas kernels, seq_gather(): pl.pallas_call(functools.partial(gather_kernel, nseq), in_specs=[any_spec...  38.7 us
    pallas_call x1, Pallas kernels, attention_backward(): pl.pallas_call(functools.partial(attention_kernel, nseq), grid=(length //...  19.1 us
    another operation x8, local copies, waits for them, and re-layouts  7.46 us
    all_gather x1, blocking collectives, local(): lax.all_gather(out_weight, ('dpy', 'dpc'), axis=0)  7.44 us
    dot_general x2, matrix products, terms_of(): lax.dot_general(parts[0], inputs_half, tn, preferred_element_type=jnp.flo...  6.1 us
    ppermute x1, waiting for transfers between devices, local(): d_got = lax.ppermute(d_give, 'sqy', swap)  5.03 us
    all_gather x1, waiting for transfers between devices, local(): gathered = lax.all_gather(gathered, 'dpz', axis=0)  4.53 us
  transfers between devices with their start and end apart: 8, of which 7 were waited for; matrix products, arithmetic and copies ran while one was open for 12% of the time, Pallas kernels for 19%

profile of v15, /device:TPU:2, one launch (start us, length us, event | category | flops | bytes accessed | tf_op | source)
XLA Modules:
  0.0 206.9 jit_solution(14294641668786769389)
XLA Ops:
  7.2 7.4 %all-gather = bf16[128,1024]{1,0:T(8,128)(2,1)} all-gather(bf16[32,1024]{1,0:T(8,128)(2,1)} %param.14), channel_id=2, replica_groups=mesh['dpy'=2,'dpz'=8,'dpc'=2,'sqy'=2,'sqx'=4] {'dpy','dpc'}, dimensions={0}, use_global_device_ids=true | all-gather | bytes 327680 | tf_op jit(solution)/shard_map/all_gather | solution.py:171
  14.7 0.7 convert_reduce_fusion
  15.4 2.0 bitcast_multiply_fusion.a_ref
  17.4 38.7 %shard_map.111 = (bf16[4,256,1024]{2,1,0:T(8,128)(2,1)}, bf16[4,256,1024]{2,1,0:T(8,128)(2,1)}) custom-call(bf16[256,1024]{1,0:T(8,128)(2,1)} %bitcast_multiply_fusion.a_ref, bf16[256,1024]{1,0:T(8,128)(2,1)} %bitcast.117), custom_call_target="tpu_custom_call" | custom-call | tf_op jit(solution)/shard_map/pallas_call | solution.py:140
  56.1 4.5 %all-gather.3.cloned.1.call-done = bf16[8,2,2,32,1024]{4,3,2,0,1:T(8,128)(2,1)} async-done(((bf16[1,2,2,32,1024]{4,3,2,0,1:T(8,128)(2,1)}), bf16[8,2,2,32,1024]{4,3,2,0,1:T(8,128)(2,1)}) %all-gather.3.cloned.1.call-update) | async-done | bytes 2097168 | tf_op jit(solution)/shard_map/all_gather | solution.py:172
  60.6 2.3 %convolution_convert_fusion = bf16[1024,128]{1,0:T(8,128)(2,1)S(1)} fusion(bf16[1024,1024]{1,0:T(8,128)(2,1)} %bitcast.127, bf16[1024,1024]{1,0:T(8,128)(2,1)} %bitcast.132, s32[]{:T(128)S(6)} %select_n.30), kind=kOutput, calls=%fused_computation.13 | convolution fusion | flops 268566528 | bytes 2621444 | tf_op jit(solution)/shard_map/dot_general | solution.py:181
  63.0 3.0 %collective-permute-start = (bf16[1024,128]{1,0:T(8,128)(2,1)S(1)}, bf16[1024,128]{1,0:T(8,128)(2,1)S(1)}, u32[]{:S(2)}, u32[]{:S(2)}) collective-permute-start(bf16[1024,128]{1,0:T(8,128)(2,1)S(1)} %convolution_convert_fusion), channel_id=1, source_target_pairs={{0,4},{4,0},{1,5},{5,1},{2,6},{6,2},{3,7},{7,3},{8,12},{12,8},{9,1... | collective-permute-start | bytes 786440 | tf_op jit(solution)/shard_map/ppermute | solution.py:182
  66.0 1.8 fusion.1
  67.8 5.0 %collective-permute-done = bf16[1024,128]{1,0:T(8,128)(2,1)S(1)} collective-permute-done((bf16[1024,128]{1,0:T(8,128)(2,1)S(1)}, bf16[1024,128]{1,0:T(8,128)(2,1)S(1)}, u32[]{:S(2)}, u32[]{:S(2)}) %collective-permute-start) | collective-permute-done | bytes 262176 | tf_op jit(solution)/shard_map/ppermute | solution.py:182
  73.0 19.1 %shard_map.112 = (bf16[2048,128]{1,0:T(8,128)(2,1)S(1)}, bf16[2048,128]{1,0:T(8,128)(2,1)S(1)}, bf16[2048,128]{1,0:T(8,128)(2,1)S(1)}, bf16[2048,128]{1,0:T(8,128)(2,1)S(1)}, bf16[4,256,1024]{2,1,0:T(8,128)(2,1)}) custom-call(bf16[2048,128]{1,0:T(8,128)(2,1)S(1)} %bitcast.124, bf16[2048,128]{1,0:T(8,128)(2,1)S(1)} %bitcast.125, ...), custom_call_target="tpu_custom_call", output_to_operand_aliasing={{4}: (6, {})} | custom-call | flops 6442450944 | bytes 4194304 | tf_op jit(solution)/shard_map/pallas_call | solution.py:77
  92.5 3.2 %collective-permute-start.1 = (bf16[4,1024,128]{2,1,0:T(8,128)(2,1)S(1)}, bf16[4,1024,128]{2,1,0:T(8,128)(2,1)}, u32[]{:S(2)}, u32[]{:S(2)}) collective-permute-start(bf16[4,1024,128]{2,1,0:T(8,128)(2,1)S(1)} %constant_dynamic-slice_fusion), channel_id=1, source_target_pairs={{0,4},{4,0},{1,5},{5,1},{2,6},{6,2},{3,7},{7,3},{8,12},{12,8},{9,1... | collective-permute-start | bytes 3145736 | tf_op jit(solution)/shard_map/ppermute | solution.py:195
  95.7 0.9 dynamic-slice_bitcast_fusion.4
  96.6 1.8 copy.43
  98.4 1.8 reshape.110
  100.2 1.8 copy.47
  101.9 1.8 reshape.113
  103.7 1.8 copy.45
  105.5 1.8 reshape.112
  107.2 0.8 copy.49
  108.1 1.1 reshape.114
  109.2 3.2 %convolution_bitcast_fusion.7 = f32[1,1,2,8,2,4,1024]{6,3,5,4,2,1,0:T(8,128)} fusion(bf16[1024,1024,1,1,1]{1,0,4,3,2:T(8,128)(2,1)} %bitcast.135, bf16[2,8,2,4,1024]{4,3,2,1,0:T(4,128)(2,1)} %reshape.110), kind=kOutput, calls=%fused_computation.12 | convolution fusion | flops 268435456 | bytes 2883584 | tf_op jit(solution)/shard_map/dot_general | solution.py:201
  112.3 1.3 convolution_bitcast_fusion.5
  113.7 1.3 convolution_bitcast_fusion.6
  115.0 1.3 convolution_bitcast_fusion.4
  116.3 2.1 collective-permute-done.1
  118.4 1.3 slice_bitcast_fusion.3
  119.9 2.9 %convolution_bitcast_fusion.3 = f32[1,1,2,8,2,4,1024]{6,3,5,4,2,1,0:T(8,128)} fusion(bf16[1024,1024,1,1,1]{1,0,4,3,2:T(8,128)(2,1)} %bitcast.136, bf16[2,8,2,4,1024]{4,3,2,1,0:T(4,128)(2,1)S(1)} %reshape.115), kind=kOutput, calls=%fused_computation.8 | convolution fusion | flops 268435456 | bytes 2883584 | tf_op jit(solution)/shard_map/dot_general | solution.py:201
  123.0 0.8 reshape.118
  123.8 1.5 convolution_bitcast_fusion
  125.6 2.1 %convolution_bitcast_fusion.1 = f32[1,1,2,8,2,4,1024]{6,3,5,4,2,1,0:T(8,128)S(1)} fusion(bf16[1024,1024,1,1,1]{1,0,4,3,2:T(8,128)(2,1)} %bitcast.137, bf16[2,8,2,4,1024]{4,3,2,1,0:T(4,128)(2,1)S(1)} %reshape.117), kind=kOutput, calls=%fused_computation.6 | convolution fusion | flops 268435456 | bytes 2883584 | tf_op jit(solution)/shard_map/dot_general | solution.py:203
  128.0 2.3 %convolution_bitcast_fusion.2 = f32[1,1,2,8,2,4,1024]{6,3,5,4,2,1,0:T(8,128)S(1)} fusion(bf16[1024,1024,1,1,1]{1,0,4,3,2:T(8,128)(2,1)} %bitcast.138, bf16[2,8,2,4,1024]{4,3,2,1,0:T(4,128)(2,1)S(1)} %reshape.116), kind=kOutput, calls=%fused_computation.7 | convolution fusion | flops 268435456 | bytes 2883584 | tf_op jit(solution)/shard_map/dot_general | solution.py:202
  130.4 0.5 maximum_maximum_fusion
  130.9 1.6 dynamic-slice_bitcast_fusion
  132.5 1.0 copy-done.4
  133.5 4.4 %collective-permute-done.2 = f32[2,4,2,8,4,1024]{5,3,4,2,1,0:T(8,128)S(1)} collective-permute-done((f32[2,4,2,8,4,1024]{5,3,4,2,1,0:T(8,128)}, f32[2,4,2,8,4,1024]{5,3,4,2,1,0:T(8,128)S(1)}, u32[]{:S(2)}, u32[]{:S(2)}) %collective-permute-start.2) | collective-permute-done | bytes 2097184 | tf_op jit(solution)/shard_map/ppermute | solution.py:216
  137.9 2.0 fusion
  139.8 1.4 copy.59
  141.2 1.8 reshape.119
  143.1 44.8 %reduce-scatter.2.cloned.1.call-done = f32[1,512,128]{2,1,0:T(8,128)} async-done(((f32[8,512,128]{2,1,0:T(8,128)}), f32[1,512,128]{2,1,0:T(8,128)}) %reduce-scatter.2.cloned.1.call-update) | async-done | bytes 262160 | tf_op jit(solution)/shard_map/reduce_scatter | solution.py:218
  187.9 1.0 reshape.120
  189.0 3.1 %collective-permute-start.4 = (f32[4,4,1024]{2,1,0:T(4,128)S(1)}, f32[4,4,1024]{2,1,0:T(4,128)S(1)}, u32[]{:S(2)}, u32[]{:S(2)}) collective-permute-start(f32[4,4,1024]{2,1,0:T(4,128)S(1)} %get-tuple-element.34), channel_id=1, source_target_pairs={{0,4},{4,0},{1,5},{5,1},{2,6},{6,2},{3,7},{7,3},{8,12},{12,8},{9,1... | collective-permute-start | bytes 196616 | tf_op jit(solution)/shard_map/ppermute | solution.py:227
  192.0 1.0 collective-permute-start.5
  193.1 1.7 collective-permute-done.4
  194.8 2.7 %collective-permute-done.5 = f32[4,4,1024]{2,1,0:T(4,128)S(1)} collective-permute-done((f32[4,4,1024]{2,1,0:T(4,128)S(1)}, f32[4,4,1024]{2,1,0:T(4,128)S(1)}, u32[]{:S(2)}, u32[]{:S(2)}) %collective-permute-start.5) | collective-permute-done | bytes 65568 | tf_op jit(solution)/shard_map/ppermute | solution.py:228
  197.6 0.6 copy.65
  198.2 0.6 copy.64
  198.8 0.6 copy.63
  199.4 0.6 copy.62
  (53 shorter events, 1.7 us)
Async XLA Ops:
  7.2 53.4 %all-gather.3.cloned.1.call-start = ((), (), s32[]{:S(2)}) async-start(), calls=%async_computation.1 | async-start | bytes 2359296 | tf_op jit(solution)/shard_map/all_gather | solution.py:172
  14.7 173.2 %reduce-scatter.2.cloned.1.call-start = ((), (), s32[]{:S(2)}) async-start(), calls=%async_computation.2 | async-start | bytes 2359296 | tf_op jit(solution)/shard_map/reduce_scatter | solution.py:218
  56.1 10.0 %copy-start.5 = (bf16[4,256,1024]{2,1,0:T(8,128)(2,1)S(1)}, bf16[4,256,1024]{2,1,0:T(8,128)(2,1)}, u32[]{:S(2)}) copy-start(bf16[4,256,1024]{2,1,0:T(8,128)(2,1)} %get-tuple-element.11) | copy-start | bytes 6291460
  62.9 10.0 %copy-start.13 = (s32[1,1,16,16]{3,2,1,0:T(8,128)S(1)}, s32[1,1,16,16]{3,2,1,0:T(8,128)}, u32[]{:S(2)}) copy-start(s32[1,1,16,16]{3,2,1,0:T(8,128)} %param.15) | copy-start | bytes 3076
  62.9 10.1 %copy-start = (bf16[1,256,1024]{2,1,0:T(8,128)(2,1)S(1)}, bf16[1,256,1024]{2,1,0:T(8,128)(2,1)}, u32[]{:S(2)}) copy-start(bf16[1,256,1024]{2,1,0:T(8,128)(2,1)} %param.8) | copy-start | bytes 1572868
  62.9 10.1 %copy-start.1 = (bf16[1,2048,1,128]{3,1,2,0:T(8,128)(2,1)S(1)}, bf16[1,2048,1,128]{3,1,2,0:T(8,128)(2,1)}, u32[]{:S(2)}) copy-start(bf16[1,2048,1,128]{3,1,2,0:T(8,128)(2,1)} %param.11) | copy-start | bytes 1572868
  63.0 10.1 %copy-start.2 = (bf16[1,2048,1,128]{3,1,2,0:T(8,128)(2,1)S(1)}, bf16[1,2048,1,128]{3,1,2,0:T(8,128)(2,1)}, u32[]{:S(2)}) copy-start(bf16[1,2048,1,128]{3,1,2,0:T(8,128)(2,1)} %param.12) | copy-start | bytes 1572868
  63.0 10.1 %copy-start.3 = (bf16[1,2048,1,128]{3,1,2,0:T(8,128)(2,1)S(1)}, bf16[1,2048,1,128]{3,1,2,0:T(8,128)(2,1)}, u32[]{:S(2)}) copy-start(bf16[1,2048,1,128]{3,1,2,0:T(8,128)(2,1)} %param.13) | copy-start | bytes 1572868
  63.0 9.9 %collective-permute-start = (bf16[1024,128]{1,0:T(8,128)(2,1)S(1)}, bf16[1024,128]{1,0:T(8,128)(2,1)S(1)}, u32[]{:S(2)}, u32[]{:S(2)}) collective-permute-start(bf16[1024,128]{1,0:T(8,128)(2,1)S(1)} %convolution_convert_fusion), channel_id=1, source_target_pairs={{0,4},{4,0},{1,5},{5,1},{2,6},{6,2},{3,7},{7,3},{8,12},{12,8},{9,1... | collective-permute-start | bytes 786440 | tf_op jit(solution)/shard_map/ppermute | solution.py:182
  92.5 25.9 %collective-permute-start.1 = (bf16[4,1024,128]{2,1,0:T(8,128)(2,1)S(1)}, bf16[4,1024,128]{2,1,0:T(8,128)(2,1)}, u32[]{:S(2)}, u32[]{:S(2)}) collective-permute-start(bf16[4,1024,128]{2,1,0:T(8,128)(2,1)S(1)} %constant_dynamic-slice_fusion), channel_id=1, source_target_pairs={{0,4},{4,0},{1,5},{5,1},{2,6},{6,2},{3,7},{7,3},{8,12},{12,8},{9,1... | collective-permute-start | bytes 3145736 | tf_op jit(solution)/shard_map/ppermute | solution.py:195
  109.2 3.2 %copy-start.11 = (bf16[2,8,2,4,1024]{4,3,2,1,0:T(4,128)(2,1)S(1)}, bf16[2,8,2,4,1024]{4,3,2,1,0:T(4,128)(2,1)}, u32[]{:S(2)}) copy-start(bf16[2,8,2,4,1024]{4,3,2,1,0:T(4,128)(2,1)} %reshape.113) | copy-start | bytes 786436
  109.2 3.2 %copy-start.14 = (bf16[4,256,1024]{2,1,0:T(8,128)(2,1)S(1)}, bf16[4,256,1024]{2,1,0:T(8,128)(2,1)}, u32[]{:S(2)}) copy-start(bf16[4,256,1024]{2,1,0:T(8,128)(2,1)} %get-tuple-element.17) | copy-start | bytes 6291460
  112.3 1.3 copy-start.12
  128.0 2.3 %copy-start.6 = (f32[1,1,2,8,2,4,1024]{6,3,5,4,2,1,0:T(8,128)S(1)}, f32[1,1,2,8,2,4,1024]{6,3,5,4,2,1,0:T(8,128)}, u32[]{:S(2)}) copy-start(f32[1,1,2,8,2,4,1024]{6,3,5,4,2,1,0:T(8,128)} %convolution_bitcast_fusion.7) | copy-start | bytes 1572868
  128.0 2.3 %copy-start.7 = (f32[1,1,2,8,2,4,1024]{6,3,5,4,2,1,0:T(8,128)S(1)}, f32[1,1,2,8,2,4,1024]{6,3,5,4,2,1,0:T(8,128)}, u32[]{:S(2)}) copy-start(f32[1,1,2,8,2,4,1024]{6,3,5,4,2,1,0:T(8,128)} %convolution_bitcast_fusion.5) | copy-start | bytes 1572868
  128.0 2.3 %copy-start.8 = (f32[1,1,2,8,2,4,1024]{6,3,5,4,2,1,0:T(8,128)S(1)}, f32[1,1,2,8,2,4,1024]{6,3,5,4,2,1,0:T(8,128)}, u32[]{:S(2)}) copy-start(f32[1,1,2,8,2,4,1024]{6,3,5,4,2,1,0:T(8,128)} %convolution_bitcast_fusion.6) | copy-start | bytes 1572868
  128.0 2.3 %copy-start.9 = (f32[1,1,2,8,2,4,1024]{6,3,5,4,2,1,0:T(8,128)S(1)}, f32[1,1,2,8,2,4,1024]{6,3,5,4,2,1,0:T(8,128)}, u32[]{:S(2)}) copy-start(f32[1,1,2,8,2,4,1024]{6,3,5,4,2,1,0:T(8,128)} %convolution_bitcast_fusion.4) | copy-start | bytes 1572868
  128.0 2.3 %copy-start.10 = (f32[1,1,2,8,2,4,1024]{6,3,5,4,2,1,0:T(8,128)S(1)}, f32[1,1,2,8,2,4,1024]{6,3,5,4,2,1,0:T(8,128)}, u32[]{:S(2)}) copy-start(f32[1,1,2,8,2,4,1024]{6,3,5,4,2,1,0:T(8,128)} %convolution_bitcast_fusion.3) | copy-start | bytes 1572868
  130.9 2.6 %copy-start.4 = (f32[2,4,2,8,2,4,1024]{6,3,5,4,2,1,0:T(8,128)}, f32[2,4,2,8,2,4,1024]{6,3,5,4,2,1,0:T(8,128)S(1)}, u32[]{:S(2)}) copy-start(f32[2,4,2,8,2,4,1024]{6,3,5,4,2,1,0:T(8,128)S(1)} %maximum_maximum_fusion) | copy-start | bytes 12582916
  133.5 4.4 %collective-permute-start.2 = (f32[2,4,2,8,4,1024]{5,3,4,2,1,0:T(8,128)}, f32[2,4,2,8,4,1024]{5,3,4,2,1,0:T(8,128)S(1)}, u32[]{:S(2)}, u32[]{:S(2)}) collective-permute-start(f32[2,4,2,8,4,1024]{5,3,4,2,1,0:T(8,128)} %dynamic-slice_bitcast_fusion), channel_id=1, source_target_pairs={{0,8},{8,0},{1,9},{9,1},{2,10},{10,2},{3,11},{11,3},{4,12},{12,4},... | collective-permute-start | bytes 6291464 | tf_op jit(solution)/shard_map/ppermute | solution.py:216
  189.0 5.9 %collective-permute-start.4 = (f32[4,4,1024]{2,1,0:T(4,128)S(1)}, f32[4,4,1024]{2,1,0:T(4,128)S(1)}, u32[]{:S(2)}, u32[]{:S(2)}) collective-permute-start(f32[4,4,1024]{2,1,0:T(4,128)S(1)} %get-tuple-element.34), channel_id=1, source_target_pairs={{0,4},{4,0},{1,5},{5,1},{2,6},{6,2},{3,7},{7,3},{8,12},{12,8},{9,1... | collective-permute-start | bytes 196616 | tf_op jit(solution)/shard_map/ppermute | solution.py:227
  192.0 5.5 %collective-permute-start.5 = (f32[4,4,1024]{2,1,0:T(4,128)S(1)}, f32[4,4,1024]{2,1,0:T(4,128)S(1)}, u32[]{:S(2)}, u32[]{:S(2)}) collective-permute-start(f32[4,4,1024]{2,1,0:T(4,128)S(1)} %get-tuple-element.35), channel_id=1, source_target_pairs={{0,132},{132,0},{4,128},{128,4},{1,133},{133,1},{5,129},{129,5},{2... | collective-permute-start | bytes 196616 | tf_op jit(solution)/shard_map/ppermute | solution.py:228
  193.1 4.4 %collective-permute-start.3 = (f32[4,4,1024]{2,1,0:T(4,128)S(1)}, f32[4,4,1024]{2,1,0:T(4,128)S(1)}, u32[]{:S(2)}, u32[]{:S(2)}) collective-permute-start(f32[4,4,1024]{2,1,0:T(4,128)S(1)} %slice_bitcast_fusion.4), channel_id=1, source_target_pairs={{0,128},{128,0},{1,129},{129,1},{2,130},{130,2},{3,131},{131,3},{4... | collective-permute-start | bytes 196616 | tf_op jit(solution)/shard_map/ppermute | solution.py:226
Sparse Core Ops, SparseCore 0:
  14.8 45.7 all-gather.2
  143.2 44.6 reduce-scatter.1

commit v16 on v14

--- a/solution.py
+++ b/solution.py
@@ -22,7 +22,7 @@
     steps = pl.num_programs(0)
     scale = HD ** (-0.5)
     groups = ROWS // BLOCK
-    copies = start_gather(nseq, x_ref, x_out, send_sem, recv_sem, copy_sem)
+    copies = start_gather(nseq, x_ref, x_out, send_sem, recv_sem, copy_sem, local=False)
 
     @pl.when(step == 0)
     def _():
@@ -95,9 +95,9 @@
     )(q, k, v, g, live_cols, x)
 
 
-def start_gather(nseq, src, dst, send_sem, recv_sem, copy_sem):
+def start_gather(nseq, src, dst, send_sem, recv_sem, copy_sem, local=True):
     me = lax.axis_index("sqx")
-    copies = [pltpu.make_async_copy(src, dst.at[me], copy_sem)]
+    copies = [pltpu.make_async_copy(src, dst.at[me], copy_sem)] if local else []
     for off in range(1, nseq):
         peer = (me + off) % nseq
         copies.append(
@@ -180,7 +180,7 @@
     d_query, attended, d_key, d_value, inputs_half = attention_backward(
         queries[0, :, 0], keys[0, :, 0], values[0, :, 0], d_attn, live_cols, inputs[0], sizes["sqx"]
     )
-    inputs_half = inputs_half.reshape(-1, width)
+    inputs_half = lax.dynamic_update_index_in_dim(inputs_half, inputs[0], col, 0).reshape(-1, width)
     grads = jnp.stack([d_query, d_key, d_value, attended])
     grads_own = lax.dynamic_slice_in_dim(grads, half * half_len, half_len, 1)
     grads_give = lax.dynamic_slice_in_dim(grads, other * half_len, half_len, 1)

time: 203 us -> 202 us (level)
  waiting for transfers between devices: 70.5 us -> 75.2 us
  matrix products: 20 us -> 16 us
    ppermute x1, waiting for transfers between devices: 2.04 us -> 6.72 us  [local(): grads_got = lax.ppermute(grads_give, 'sqy', swap)]
    dot_general x2, matrix products: 6.1 us -> 1.89 us  [terms_of(): lax.dot_general(parts[0], inputs_half, tn, preferred_element_type=jnp.flo...]
    unnamed x34 -> x38, local copies, waits for them, and re-layouts: 3.54 us -> 4.9 us
  transfers between devices with their start and end apart: 8 -> 8, of which waited for: 7 -> 7; matrix products, arithmetic and copies ran while one was open for 12% -> 10% of each run, Pallas kernels for 13% -> 13%
where the time goes in v16:
time: 202 us; the launch traced here: 201 us
  waiting for transfers between devices  75.2 us (37%)
  Pallas kernels  47.4 us (23%)
  local copies, waits for them, and re-layouts  24.7 us (12%)
  matrix products  16 us (8%)
  between operations  14.4 us (7%)
  starting transfers between devices  10.3 us (5%)
  blocking collectives  7.45 us (4%)
  other arithmetic  5.45 us (3%)
    reduce_scatter x1, waiting for transfers between devices, local(): lax.psum_scatter(terms.reshape(nz, -1, 128), 'dpz', scatter_dimension=0,...  41.8 us
    pallas_call x1, Pallas kernels, seq_gather(): pl.pallas_call(functools.partial(gather_kernel, nseq), in_specs=[any_spec...  26.6 us
    pallas_call x1, Pallas kernels, attention_backward(): pl.pallas_call(functools.partial(attention_kernel, nseq), grid=(length //...  20.9 us
    all_gather x1, waiting for transfers between devices, local(): gathered = lax.all_gather(gathered, 'dpz', axis=0)  14.8 us
    all_gather x1, blocking collectives, local(): lax.all_gather(out_weight, ('dpy', 'dpc'), axis=0)  7.45 us
    ppermute x1, waiting for transfers between devices, local(): grads_got = lax.ppermute(grads_give, 'sqy', swap)  6.72 us
    another operation x8, local copies, waits for them, and re-layouts  6.27 us
    dot_general x2, matrix products, terms_of(): lax.dot_general(parts[2], inputs_half, tn, preferred_element_type=jnp.flo...  5.36 us
  transfers between devices with their start and end apart: 8, of which 7 were waited for; matrix products, arithmetic and copies ran while one was open for 10% of the time, Pallas kernels for 13%

profile of v16, /device:TPU:2, one launch (start us, length us, event | category | flops | bytes accessed | tf_op | source)
XLA Modules:
  0.0 201.0 jit_solution(4901621504665694704)
XLA Ops:
  7.2 7.5 %all-gather = bf16[128,1024]{1,0:T(8,128)(2,1)} all-gather(bf16[32,1024]{1,0:T(8,128)(2,1)} %param.14), channel_id=2, replica_groups=mesh['dpy'=2,'dpz'=8,'dpc'=2,'sqy'=2,'sqx'=4] {'dpy','dpc'}, dimensions={0}, use_global_device_ids=true | all-gather | bytes 327680 | tf_op jit(solution)/shard_map/all_gather | solution.py:164
  14.8 0.7 convert_reduce_fusion
  15.5 2.0 bitcast_multiply_fusion.a_ref
  17.4 26.6 %shard_map.111 = bf16[4,256,1024]{2,1,0:T(8,128)(2,1)} custom-call(bf16[256,1024]{1,0:T(8,128)(2,1)} %bitcast_multiply_fusion.a_ref), custom_call_target="tpu_custom_call" | custom-call | tf_op jit(solution)/shard_map/pallas_call | solution.py:136
  44.0 14.8 %all-gather.3.cloned.1.call-done = bf16[8,2,2,32,1024]{4,3,2,0,1:T(8,128)(2,1)} async-done(((bf16[1,2,2,32,1024]{4,3,2,0,1:T(8,128)(2,1)}), bf16[8,2,2,32,1024]{4,3,2,0,1:T(8,128)(2,1)}) %all-gather.3.cloned.1.call-update) | async-done | bytes 2097168 | tf_op jit(solution)/shard_map/all_gather | solution.py:165
  58.8 2.3 %convolution_convert_fusion = bf16[1024,128]{1,0:T(8,128)(2,1)S(1)} fusion(bf16[1024,1024]{1,0:T(8,128)(2,1)} %bitcast.126, bf16[1024,1024]{1,0:T(8,128)(2,1)} %bitcast.131, s32[]{:T(128)S(6)} %select_n.34), kind=kOutput, calls=%fused_computation.13 | convolution fusion | flops 268566528 | bytes 2621444 | tf_op jit(solution)/shard_map/dot_general | solution.py:173
  61.2 3.1 %collective-permute-start = (bf16[1024,128]{1,0:T(8,128)(2,1)S(1)}, bf16[1024,128]{1,0:T(8,128)(2,1)S(1)}, u32[]{:S(2)}, u32[]{:S(2)}) collective-permute-start(bf16[1024,128]{1,0:T(8,128)(2,1)S(1)} %convolution_convert_fusion), channel_id=1, source_target_pairs={{0,4},{4,0},{1,5},{5,1},{2,6},{6,2},{3,7},{7,3},{8,12},{12,8},{9,1... | collective-permute-start | bytes 786440 | tf_op jit(solution)/shard_map/ppermute | solution.py:174
  64.4 1.8 fusion.1
  66.2 3.0 %collective-permute-done = bf16[1024,128]{1,0:T(8,128)(2,1)S(1)} collective-permute-done((bf16[1024,128]{1,0:T(8,128)(2,1)S(1)}, bf16[1024,128]{1,0:T(8,128)(2,1)S(1)}, u32[]{:S(2)}, u32[]{:S(2)}) %collective-permute-start) | collective-permute-done | bytes 262176 | tf_op jit(solution)/shard_map/ppermute | solution.py:174
  69.4 20.9 %shard_map.112 = (bf16[2048,128]{1,0:T(8,128)(2,1)S(1)}, bf16[2048,128]{1,0:T(8,128)(2,1)S(1)}, bf16[2048,128]{1,0:T(8,128)(2,1)S(1)}, bf16[2048,128]{1,0:T(8,128)(2,1)S(1)}, bf16[4,256,1024]{2,1,0:T(8,128)(2,1)}) custom-call(bf16[2048,128]{1,0:T(8,128)(2,1)S(1)} %bitcast.123, bf16[2048,128]{1,0:T(8,128)(2,1)S(1)} %bitcast.124, ...), custom_call_target="tpu_custom_call" | custom-call | flops 6442450944 | bytes 4194304 | tf_op jit(solution)/shard_map/pallas_call | solution.py:76
  90.5 1.1 constant_dynamic-slice_fusion
  91.6 3.0 %collective-permute-start.1 = (bf16[4,1024,128]{2,1,0:T(8,128)(2,1)}, bf16[4,1024,128]{2,1,0:T(8,128)(2,1)}, u32[]{:S(2)}, u32[]{:S(2)}) collective-permute-start(bf16[4,1024,128]{2,1,0:T(8,128)(2,1)} %constant_dynamic-slice_fusion), channel_id=1, source_target_pairs={{0,4},{4,0},{1,5},{5,1},{2,6},{6,2},{3,7},{7,3},{8,12},{12,8},{9,1... | collective-permute-start | bytes 3145736 | tf_op jit(solution)/shard_map/ppermute | solution.py:187
  94.6 0.8 dynamic-slice_bitcast_fusion.4
  95.4 1.8 copy.42
  97.2 1.8 reshape.110
  98.9 0.9 copy.46
  99.8 1.8 reshape.113
  101.7 0.8 reshape.112
  102.8 0.9 constant_dynamic-update-slice_fusion
  103.6 3.1 %convolution_bitcast_fusion.5 = f32[1,1,2,8,2,4,1024]{6,3,5,4,2,1,0:T(8,128)} fusion(bf16[1024,1024,1,1,1]{1,0,4,3,2:T(8,128)(2,1)} %bitcast.134, bf16[2,8,2,4,1024]{4,3,2,1,0:T(4,128)(2,1)S(1)} %copy-done.12), kind=kOutput, calls=%fused_computation.10 | convolution fusion | flops 268435456 | bytes 2883584 | tf_op jit(solution)/shard_map/dot_general | solution.py:195
  106.7 1.3 convolution_bitcast_fusion.6
  108.1 1.4 convolution_bitcast_fusion.7
  109.4 1.4 convolution_bitcast_fusion.4
  110.8 6.7 %collective-permute-done.1 = bf16[4,1024,128]{2,1,0:T(8,128)(2,1)} collective-permute-done((bf16[4,1024,128]{2,1,0:T(8,128)(2,1)}, bf16[4,1024,128]{2,1,0:T(8,128)(2,1)}, u32[]{:S(2)}, u32[]{:S(2)}) %collective-permute-start.1) | collective-permute-done | bytes 1048608 | tf_op jit(solution)/shard_map/ppermute | solution.py:187
  117.5 1.3 slice_bitcast_fusion.3
  118.9 0.8 reshape.115
  119.9 0.8 reshape.118
  120.7 1.5 convolution_bitcast_fusion
  122.7 2.3 %convolution_bitcast_fusion.1 = f32[1,1,2,8,2,4,1024]{6,3,5,4,2,1,0:T(8,128)S(1)} fusion(bf16[1024,1024,1,1,1]{1,0,4,3,2:T(8,128)(2,1)} %bitcast.135, bf16[2,8,2,4,1024]{4,3,2,1,0:T(4,128)(2,1)S(1)} %reshape.117), kind=kOutput, calls=%fused_computation.6 | convolution fusion | flops 268435456 | bytes 2883584 | tf_op jit(solution)/shard_map/dot_general | solution.py:195
  125.0 0.5 convolution_bitcast_fusion.2
  126.0 0.5 convolution_bitcast_fusion.3
  127.5 0.5 maximum_maximum_fusion
  128.0 1.6 dynamic-slice_bitcast_fusion
  129.6 1.0 copy-done.4
  130.6 4.4 %collective-permute-done.2 = f32[2,4,2,8,4,1024]{5,3,4,2,1,0:T(8,128)S(1)} collective-permute-done((f32[2,4,2,8,4,1024]{5,3,4,2,1,0:T(8,128)}, f32[2,4,2,8,4,1024]{5,3,4,2,1,0:T(8,128)S(1)}, u32[]{:S(2)}, u32[]{:S(2)}) %collective-permute-start.2) | collective-permute-done | bytes 2097184 | tf_op jit(solution)/shard_map/ppermute | solution.py:208
  134.9 2.0 fusion
  136.9 1.4 copy.58
  138.3 1.8 reshape.119
  140.1 41.8 %reduce-scatter.2.cloned.1.call-done = f32[1,512,128]{2,1,0:T(8,128)} async-done(((f32[8,512,128]{2,1,0:T(8,128)}), f32[1,512,128]{2,1,0:T(8,128)}) %reduce-scatter.2.cloned.1.call-update) | async-done | bytes 262160 | tf_op jit(solution)/shard_map/reduce_scatter | solution.py:210
  182.0 1.0 reshape.120
  183.0 3.1 %collective-permute-start.4 = (f32[4,4,1024]{2,1,0:T(4,128)S(1)}, f32[4,4,1024]{2,1,0:T(4,128)S(1)}, u32[]{:S(2)}, u32[]{:S(2)}) collective-permute-start(f32[4,4,1024]{2,1,0:T(4,128)S(1)} %get-tuple-element.30), channel_id=1, source_target_pairs={{0,4},{4,0},{1,5},{5,1},{2,6},{6,2},{3,7},{7,3},{8,12},{12,8},{9,1... | collective-permute-start | bytes 196616 | tf_op jit(solution)/shard_map/ppermute | solution.py:219
  186.1 1.0 collective-permute-start.5
  187.2 1.7 collective-permute-done.4
  188.9 2.7 %collective-permute-done.5 = f32[4,4,1024]{2,1,0:T(4,128)S(1)} collective-permute-done((f32[4,4,1024]{2,1,0:T(4,128)S(1)}, f32[4,4,1024]{2,1,0:T(4,128)S(1)}, u32[]{:S(2)}, u32[]{:S(2)}) %collective-permute-start.5) | collective-permute-done | bytes 65568 | tf_op jit(solution)/shard_map/ppermute | solution.py:220
  191.7 0.6 copy.64
  192.3 0.6 copy.63
  192.9 0.6 copy.62
  193.6 0.6 copy.61
  (58 shorter events, 3.3 us)
Async XLA Ops:
  7.2 51.7 %all-gather.3.cloned.1.call-start = ((), (), s32[]{:S(2)}) async-start(), calls=%async_computation.1 | async-start | bytes 2359296 | tf_op jit(solution)/shard_map/all_gather | solution.py:165
  14.7 167.3 %reduce-scatter.2.cloned.1.call-start = ((), (), s32[]{:S(2)}) async-start(), calls=%async_computation.2 | async-start | bytes 2359296 | tf_op jit(solution)/shard_map/reduce_scatter | solution.py:210
  44.0 20.4 %copy-start.5 = (bf16[4,256,1024]{2,1,0:T(8,128)(2,1)S(1)}, bf16[4,256,1024]{2,1,0:T(8,128)(2,1)}, u32[]{:S(2)}) copy-start(bf16[4,256,1024]{2,1,0:T(8,128)(2,1)} %shard_map.111) | copy-start | bytes 6291460
  61.1 8.1 %copy-start.14 = (s32[1,1,16,16]{3,2,1,0:T(8,128)S(1)}, s32[1,1,16,16]{3,2,1,0:T(8,128)}, u32[]{:S(2)}) copy-start(s32[1,1,16,16]{3,2,1,0:T(8,128)} %param.15) | copy-start | bytes 3076
  61.2 8.2 %copy-start = (bf16[1,256,1024]{2,1,0:T(8,128)(2,1)S(1)}, bf16[1,256,1024]{2,1,0:T(8,128)(2,1)}, u32[]{:S(2)}) copy-start(bf16[1,256,1024]{2,1,0:T(8,128)(2,1)} %param.8) | copy-start | bytes 1572868
  61.2 8.2 %copy-start.1 = (bf16[1,2048,1,128]{3,1,2,0:T(8,128)(2,1)S(1)}, bf16[1,2048,1,128]{3,1,2,0:T(8,128)(2,1)}, u32[]{:S(2)}) copy-start(bf16[1,2048,1,128]{3,1,2,0:T(8,128)(2,1)} %param.11) | copy-start | bytes 1572868
  61.2 8.2 %copy-start.2 = (bf16[1,2048,1,128]{3,1,2,0:T(8,128)(2,1)S(1)}, bf16[1,2048,1,128]{3,1,2,0:T(8,128)(2,1)}, u32[]{:S(2)}) copy-start(bf16[1,2048,1,128]{3,1,2,0:T(8,128)(2,1)} %param.12) | copy-start | bytes 1572868
  61.2 8.2 %copy-start.3 = (bf16[1,2048,1,128]{3,1,2,0:T(8,128)(2,1)S(1)}, bf16[1,2048,1,128]{3,1,2,0:T(8,128)(2,1)}, u32[]{:S(2)}) copy-start(bf16[1,2048,1,128]{3,1,2,0:T(8,128)(2,1)} %param.13) | copy-start | bytes 1572868
  61.2 8.0 %collective-permute-start = (bf16[1024,128]{1,0:T(8,128)(2,1)S(1)}, bf16[1024,128]{1,0:T(8,128)(2,1)S(1)}, u32[]{:S(2)}, u32[]{:S(2)}) collective-permute-start(bf16[1024,128]{1,0:T(8,128)(2,1)S(1)} %convolution_convert_fusion), channel_id=1, source_target_pairs={{0,4},{4,0},{1,5},{5,1},{2,6},{6,2},{3,7},{7,3},{8,12},{12,8},{9,1... | collective-permute-start | bytes 786440 | tf_op jit(solution)/shard_map/ppermute | solution.py:174
  91.6 26.0 %collective-permute-start.1 = (bf16[4,1024,128]{2,1,0:T(8,128)(2,1)}, bf16[4,1024,128]{2,1,0:T(8,128)(2,1)}, u32[]{:S(2)}, u32[]{:S(2)}) collective-permute-start(bf16[4,1024,128]{2,1,0:T(8,128)(2,1)} %constant_dynamic-slice_fusion), channel_id=1, source_target_pairs={{0,4},{4,0},{1,5},{5,1},{2,6},{6,2},{3,7},{7,3},{8,12},{12,8},{9,1... | collective-permute-start | bytes 3145736 | tf_op jit(solution)/shard_map/ppermute | solution.py:187
  102.5 1.1 copy-start.12
  103.6 3.1 %copy-start.13 = (bf16[2,8,2,4,1024]{4,3,2,1,0:T(4,128)(2,1)S(1)}, bf16[2,8,2,4,1024]{4,3,2,1,0:T(4,128)(2,1)}, u32[]{:S(2)}) copy-start(bf16[2,8,2,4,1024]{4,3,2,1,0:T(4,128)(2,1)} %reshape.112) | copy-start | bytes 786436
  103.6 3.1 %copy-start.15 = (bf16[4,256,1024]{2,1,0:T(8,128)(2,1)S(1)}, bf16[4,256,1024]{2,1,0:T(8,128)(2,1)}, u32[]{:S(2)}) copy-start(bf16[4,256,1024]{2,1,0:T(8,128)(2,1)} %constant_dynamic-update-slice_fusion) | copy-start | bytes 6291460
  106.7 1.3 copy-start.10
  122.7 2.3 %copy-start.16 = (bf16[4,256,1024]{2,1,0:T(8,128)(2,1)S(1)}, bf16[4,256,1024]{2,1,0:T(8,128)(2,1)}, u32[]{:S(2)}) copy-start(bf16[4,256,1024]{2,1,0:T(8,128)(2,1)} %constant_dynamic-update-slice_fusion) | copy-start | bytes 6291460
  125.0 1.0 copy-start.11
  126.0 1.0 copy-start.6
  126.0 1.2 copy-start.7
  126.0 1.4 copy-start.8
  126.0 1.5 copy-start.9
  128.0 2.6 %copy-start.4 = (f32[2,4,2,8,2,4,1024]{6,3,5,4,2,1,0:T(8,128)}, f32[2,4,2,8,2,4,1024]{6,3,5,4,2,1,0:T(8,128)S(1)}, u32[]{:S(2)}) copy-start(f32[2,4,2,8,2,4,1024]{6,3,5,4,2,1,0:T(8,128)S(1)} %maximum_maximum_fusion) | copy-start | bytes 12582916
  130.6 4.4 %collective-permute-start.2 = (f32[2,4,2,8,4,1024]{5,3,4,2,1,0:T(8,128)}, f32[2,4,2,8,4,1024]{5,3,4,2,1,0:T(8,128)S(1)}, u32[]{:S(2)}, u32[]{:S(2)}) collective-permute-start(f32[2,4,2,8,4,1024]{5,3,4,2,1,0:T(8,128)} %dynamic-slice_bitcast_fusion), channel_id=1, source_target_pairs={{0,8},{8,0},{1,9},{9,1},{2,10},{10,2},{3,11},{11,3},{4,12},{12,4},... | collective-permute-start | bytes 6291464 | tf_op jit(solution)/shard_map/ppermute | solution.py:208
  183.0 5.9 %collective-permute-start.4 = (f32[4,4,1024]{2,1,0:T(4,128)S(1)}, f32[4,4,1024]{2,1,0:T(4,128)S(1)}, u32[]{:S(2)}, u32[]{:S(2)}) collective-permute-start(f32[4,4,1024]{2,1,0:T(4,128)S(1)} %get-tuple-element.30), channel_id=1, source_target_pairs={{0,4},{4,0},{1,5},{5,1},{2,6},{6,2},{3,7},{7,3},{8,12},{12,8},{9,1... | collective-permute-start | bytes 196616 | tf_op jit(solution)/shard_map/ppermute | solution.py:219
  186.1 5.5 %collective-permute-start.5 = (f32[4,4,1024]{2,1,0:T(4,128)S(1)}, f32[4,4,1024]{2,1,0:T(4,128)S(1)}, u32[]{:S(2)}, u32[]{:S(2)}) collective-permute-start(f32[4,4,1024]{2,1,0:T(4,128)S(1)} %get-tuple-element.31), channel_id=1, source_target_pairs={{0,132},{132,0},{4,128},{128,4},{1,133},{133,1},{5,129},{129,5},{2... | collective-permute-start | bytes 196616 | tf_op jit(solution)/shard_map/ppermute | solution.py:220
  187.2 4.5 %collective-permute-start.3 = (f32[4,4,1024]{2,1,0:T(4,128)S(1)}, f32[4,4,1024]{2,1,0:T(4,128)S(1)}, u32[]{:S(2)}, u32[]{:S(2)}) collective-permute-start(f32[4,4,1024]{2,1,0:T(4,128)S(1)} %slice_bitcast_fusion.4), channel_id=1, source_target_pairs={{0,128},{128,0},{1,129},{129,1},{2,130},{130,2},{3,131},{131,3},{4... | collective-permute-start | bytes 196616 | tf_op jit(solution)/shard_map/ppermute | solution.py:218
Sparse Core Ops, SparseCore 0:
  14.8 43.9 all-gather.2
  140.3 41.6 reduce-scatter.1

commit v17 on v14

--- a/solution.py
+++ b/solution.py
@@ -169,9 +169,10 @@
     masked_half = seq_gather(masked, sizes["sqx"]).reshape(-1, width)
     half_len = masked_half.shape[0]
     nt = (((1,), (1,)), ((), ()))
-    d_own = lax.dot_general(masked_half, head_weight, nt, preferred_element_type=jnp.float32).astype(jnp.bfloat16)
     d_give = lax.dot_general(masked_half, partner_weight, nt, preferred_element_type=jnp.float32).astype(jnp.bfloat16)
     d_got = lax.ppermute(d_give, "sqy", swap)
+    d_give, masked_half, head_weight = lax.optimization_barrier((d_give, masked_half, head_weight))
+    d_own = lax.dot_general(masked_half, head_weight, nt, preferred_element_type=jnp.float32).astype(jnp.bfloat16)
     d_attn = jnp.zeros((2 * half_len, HD), jnp.bfloat16)
     d_attn = lax.dynamic_update_slice_in_dim(d_attn, d_own, half * half_len, 0)
     d_attn = lax.dynamic_update_slice_in_dim(d_attn, d_got, other * half_len, 0)

time: 203 us -> 204 us (level)
  no operation moved by 1% of the time
where the time goes in v17:
time: 204 us; the launch traced here: 203 us
  waiting for transfers between devices  71.4 us (35%)
  Pallas kernels  47.4 us (23%)
  local copies, waits for them, and re-layouts  27.1 us (13%)
  matrix products  19.1 us (9%)
  between operations  14.5 us (7%)
  starting transfers between devices  10.7 us (5%)
  blocking collectives  7.45 us (4%)
  other arithmetic  5.48 us (3%)
    reduce_scatter x1, waiting for transfers between devices, local(): lax.psum_scatter(terms.reshape(nz, -1, 128), 'dpz', scatter_dimension=0,...  41.8 us
    pallas_call x1, Pallas kernels, seq_gather(): pl.pallas_call(functools.partial(gather_kernel, nseq), in_specs=[any_spec...  26.6 us
    pallas_call x1, Pallas kernels, attention_backward(): pl.pallas_call(functools.partial(attention_kernel, nseq), grid=(length //...  20.9 us
    all_gather x1, waiting for transfers between devices, local(): gathered = lax.all_gather(gathered, 'dpz', axis=0)  14.9 us
    all_gather x1, blocking collectives, local(): lax.all_gather(out_weight, ('dpy', 'dpc'), axis=0)  7.45 us
    another operation x8, local copies, waits for them, and re-layouts  7.44 us
    dot_general x2, matrix products, terms_of(): lax.dot_general(parts[0], inputs_half, tn, preferred_element_type=jnp.flo...  6.1 us
    ppermute x1, waiting for transfers between devices, local(): terms = kept + lax.ppermute(sent, 'dpc', swap)  4.37 us
  transfers between devices with their start and end apart: 8, of which 7 were waited for; matrix products, arithmetic and copies ran while one was open for 12% of the time, Pallas kernels for 13%

profile of v17, /device:TPU:2, one launch (start us, length us, event | category | flops | bytes accessed | tf_op | source)
XLA Modules:
  0.0 203.1 jit_solution(1349948755828747083)
XLA Ops:
  7.2 7.4 %all-gather = bf16[128,1024]{1,0:T(8,128)(2,1)} all-gather(bf16[32,1024]{1,0:T(8,128)(2,1)} %param.14), channel_id=2, replica_groups=mesh['dpy'=2,'dpz'=8,'dpc'=2,'sqy'=2,'sqx'=4] {'dpy','dpc'}, dimensions={0}, use_global_device_ids=true | all-gather | bytes 327680 | tf_op jit(solution)/shard_map/all_gather | solution.py:164
  14.7 0.7 convert_reduce_fusion
  15.4 1.9 bitcast_multiply_fusion.a_ref
  17.4 26.6 %shard_map.111 = bf16[4,256,1024]{2,1,0:T(8,128)(2,1)} custom-call(bf16[256,1024]{1,0:T(8,128)(2,1)} %bitcast_multiply_fusion.a_ref), custom_call_target="tpu_custom_call" | custom-call | tf_op jit(solution)/shard_map/pallas_call | solution.py:136
  44.0 14.9 %all-gather.3.cloned.1.call-done = bf16[8,2,2,32,1024]{4,3,2,0,1:T(8,128)(2,1)} async-done(((bf16[1,2,2,32,1024]{4,3,2,0,1:T(8,128)(2,1)}), bf16[8,2,2,32,1024]{4,3,2,0,1:T(8,128)(2,1)}) %all-gather.3.cloned.1.call-update) | async-done | bytes 2097168 | tf_op jit(solution)/shard_map/all_gather | solution.py:165
  58.8 1.0 constant_dynamic-slice_fusion.1
  59.8 2.3 %convolution_convert_fusion.1 = bf16[1024,128]{1,0:T(8,128)(2,1)S(1)} fusion(bf16[1024,1024]{1,0:T(8,128)(2,1)} %bitcast.132, bf16[1024,1024]{1,0:T(8,128)(2,1)} %bitcast.138, s32[]{:T(128)S(6)} %select_n.28), kind=kOutput, calls=%fused_computation.19 | convolution fusion | flops 268566528 | bytes 2621444 | tf_op jit(solution)/shard_map/dot_general | solution.py:172
  62.2 3.1 %collective-permute-start = (bf16[1024,128]{1,0:T(8,128)(2,1)S(1)}, bf16[1024,128]{1,0:T(8,128)(2,1)S(1)}, u32[]{:S(2)}, u32[]{:S(2)}) collective-permute-start(bf16[1024,128]{1,0:T(8,128)(2,1)S(1)} %convolution_convert_fusion.1), channel_id=1, source_target_pairs={{0,4},{4,0},{1,5},{5,1},{2,6},{6,2},{3,7},{7,3},{8,12},{12,8},{9,1... | collective-permute-start | bytes 786440 | tf_op jit(solution)/shard_map/ppermute | solution.py:173
  65.4 0.8 fusion.11
  66.2 4.0 %collective-permute-done = bf16[1024,128]{1,0:T(8,128)(2,1)S(1)} collective-permute-done((bf16[1024,128]{1,0:T(8,128)(2,1)S(1)}, bf16[1024,128]{1,0:T(8,128)(2,1)S(1)}, u32[]{:S(2)}, u32[]{:S(2)}) %collective-permute-start) | collective-permute-done | bytes 262176 | tf_op jit(solution)/shard_map/ppermute | solution.py:173
  70.3 20.9 %shard_map.112 = (bf16[2048,128]{1,0:T(8,128)(2,1)S(1)}, bf16[2048,128]{1,0:T(8,128)(2,1)S(1)}, bf16[2048,128]{1,0:T(8,128)(2,1)S(1)}, bf16[2048,128]{1,0:T(8,128)(2,1)S(1)}, bf16[4,256,1024]{2,1,0:T(8,128)(2,1)}) custom-call(bf16[2048,128]{1,0:T(8,128)(2,1)S(1)} %bitcast.128, bf16[2048,128]{1,0:T(8,128)(2,1)S(1)} %bitcast.129, ...), custom_call_target="tpu_custom_call" | custom-call | flops 6442450944 | bytes 4194304 | tf_op jit(solution)/shard_map/pallas_call | solution.py:76
  91.5 3.3 %collective-permute-start.1 = (bf16[4,1024,128]{2,1,0:T(8,128)(2,1)S(1)}, bf16[4,1024,128]{2,1,0:T(8,128)(2,1)}, u32[]{:S(2)}, u32[]{:S(2)}) collective-permute-start(bf16[4,1024,128]{2,1,0:T(8,128)(2,1)S(1)} %constant_dynamic-slice_fusion), channel_id=1, source_target_pairs={{0,4},{4,0},{1,5},{5,1},{2,6},{6,2},{3,7},{7,3},{8,12},{12,8},{9,1... | collective-permute-start | bytes 3145736 | tf_op jit(solution)/shard_map/ppermute | solution.py:188
  94.8 0.9 dynamic-slice_bitcast_fusion.4
  95.8 1.8 copy.42
  97.5 1.7 reshape.110
  99.3 1.8 copy.46
  101.1 1.8 reshape.113
  102.8 1.8 copy.44
  104.6 1.8 reshape.112
  106.4 0.9 copy.48
  107.3 1.1 reshape.114
  108.3 3.2 %convolution_bitcast_fusion.5 = f32[1,1,2,8,2,4,1024]{6,3,5,4,2,1,0:T(8,128)} fusion(bf16[1024,1024,1,1,1]{1,0,4,3,2:T(8,128)(2,1)} %bitcast.140, bf16[2,8,2,4,1024]{4,3,2,1,0:T(4,128)(2,1)} %reshape.110), kind=kOutput, calls=%fused_computation.16 | convolution fusion | flops 268435456 | bytes 2883584 | tf_op jit(solution)/shard_map/dot_general | solution.py:194
  111.5 1.3 convolution_bitcast_fusion.3
  112.8 1.3 convolution_bitcast_fusion.4
  114.2 1.3 fusion.5
  115.5 2.0 %collective-permute-done.1 = bf16[4,1024,128]{2,1,0:T(8,128)(2,1)} collective-permute-done((bf16[4,1024,128]{2,1,0:T(8,128)(2,1)S(1)}, bf16[4,1024,128]{2,1,0:T(8,128)(2,1)}, u32[]{:S(2)}, u32[]{:S(2)}) %collective-permute-start.1) | collective-permute-done | bytes 1048608 | tf_op jit(solution)/shard_map/ppermute | solution.py:188
  117.5 1.3 slice_bitcast_fusion.3
  119.1 2.9 %convolution_bitcast_fusion.2 = f32[1,1,2,8,2,4,1024]{6,3,5,4,2,1,0:T(8,128)} fusion(bf16[1024,1024,1,1,1]{1,0,4,3,2:T(8,128)(2,1)} %bitcast.141, bf16[2,8,2,4,1024]{4,3,2,1,0:T(4,128)(2,1)S(1)} %reshape.115), kind=kOutput, calls=%fused_computation.13 | convolution fusion | flops 268435456 | bytes 2883584 | tf_op jit(solution)/shard_map/dot_general | solution.py:194
  122.2 0.8 reshape.118
  123.0 1.5 fusion.8
  124.7 2.1 %convolution_bitcast_fusion = f32[1,1,2,8,2,4,1024]{6,3,5,4,2,1,0:T(8,128)S(1)} fusion(bf16[1024,1024,1,1,1]{1,0,4,3,2:T(8,128)(2,1)} %bitcast.142, bf16[2,8,2,4,1024]{4,3,2,1,0:T(4,128)(2,1)S(1)} %reshape.117), kind=kOutput, calls=%fused_computation.11 | convolution fusion | flops 268435456 | bytes 2883584 | tf_op jit(solution)/shard_map/dot_general | solution.py:196
  127.2 2.3 %convolution_bitcast_fusion.1 = f32[1,1,2,8,2,4,1024]{6,3,5,4,2,1,0:T(8,128)S(1)} fusion(bf16[1024,1024,1,1,1]{1,0,4,3,2:T(8,128)(2,1)} %bitcast.143, bf16[2,8,2,4,1024]{4,3,2,1,0:T(4,128)(2,1)S(1)} %reshape.116), kind=kOutput, calls=%fused_computation.12 | convolution fusion | flops 268435456 | bytes 2883584 | tf_op jit(solution)/shard_map/dot_general | solution.py:195
  130.1 1.6 dynamic-slice_bitcast_fusion
  131.7 1.0 copy-done.4
  132.6 4.4 %collective-permute-done.2 = f32[2,4,2,8,4,1024]{5,3,4,2,1,0:T(8,128)S(1)} collective-permute-done((f32[2,4,2,8,4,1024]{5,3,4,2,1,0:T(8,128)}, f32[2,4,2,8,4,1024]{5,3,4,2,1,0:T(8,128)S(1)}, u32[]{:S(2)}, u32[]{:S(2)}) %collective-permute-start.2) | collective-permute-done | bytes 2097184 | tf_op jit(solution)/shard_map/ppermute | solution.py:209
  137.0 2.0 fusion
  139.0 1.4 copy.58
  140.4 1.8 reshape.119
  142.2 41.8 %reduce-scatter.2.cloned.1.call-done = f32[1,512,128]{2,1,0:T(8,128)} async-done(((f32[8,512,128]{2,1,0:T(8,128)}), f32[1,512,128]{2,1,0:T(8,128)}) %reduce-scatter.2.cloned.1.call-update) | async-done | bytes 262160 | tf_op jit(solution)/shard_map/reduce_scatter | solution.py:211
  184.0 1.0 reshape.120
  185.1 3.2 %collective-permute-start.4 = (f32[4,4,1024]{2,1,0:T(4,128)S(1)}, f32[4,4,1024]{2,1,0:T(4,128)S(1)}, u32[]{:S(2)}, u32[]{:S(2)}) collective-permute-start(f32[4,4,1024]{2,1,0:T(4,128)S(1)} %get-tuple-element.34), channel_id=1, source_target_pairs={{0,4},{4,0},{1,5},{5,1},{2,6},{6,2},{3,7},{7,3},{8,12},{12,8},{9,1... | collective-permute-start | bytes 196616 | tf_op jit(solution)/shard_map/ppermute | solution.py:220
  188.3 1.1 collective-permute-start.5
  189.3 1.6 collective-permute-done.4
  191.0 2.8 %collective-permute-done.5 = f32[4,4,1024]{2,1,0:T(4,128)S(1)} collective-permute-done((f32[4,4,1024]{2,1,0:T(4,128)S(1)}, f32[4,4,1024]{2,1,0:T(4,128)S(1)}, u32[]{:S(2)}, u32[]{:S(2)}) %collective-permute-start.5) | collective-permute-done | bytes 65568 | tf_op jit(solution)/shard_map/ppermute | solution.py:221
  193.8 0.6 copy.64
  194.4 0.6 copy.63
  195.0 0.6 copy.62
  195.7 0.6 copy.61
  (54 shorter events, 2.3 us)
Async XLA Ops:
  7.2 51.7 %all-gather.3.cloned.1.call-start = ((), (), s32[]{:S(2)}) async-start(), calls=%async_computation.1 | async-start | bytes 2359296 | tf_op jit(solution)/shard_map/all_gather | solution.py:165
  14.7 169.3 %reduce-scatter.2.cloned.1.call-start = ((), (), s32[]{:S(2)}) async-start(), calls=%async_computation.2 | async-start | bytes 2359296 | tf_op jit(solution)/shard_map/reduce_scatter | solution.py:211
  44.0 21.4 %copy-start.5 = (bf16[4,256,1024]{2,1,0:T(8,128)(2,1)S(1)}, bf16[4,256,1024]{2,1,0:T(8,128)(2,1)}, u32[]{:S(2)}) copy-start(bf16[4,256,1024]{2,1,0:T(8,128)(2,1)} %shard_map.111) | copy-start | bytes 6291460
  62.1 8.1 %copy-start.13 = (s32[1,1,16,16]{3,2,1,0:T(8,128)S(1)}, s32[1,1,16,16]{3,2,1,0:T(8,128)}, u32[]{:S(2)}) copy-start(s32[1,1,16,16]{3,2,1,0:T(8,128)} %param.15) | copy-start | bytes 3076
  62.1 8.2 %copy-start = (bf16[1,2048,1,128]{3,1,2,0:T(8,128)(2,1)S(1)}, bf16[1,2048,1,128]{3,1,2,0:T(8,128)(2,1)}, u32[]{:S(2)}) copy-start(bf16[1,2048,1,128]{3,1,2,0:T(8,128)(2,1)} %param.11) | copy-start | bytes 1572868
  62.1 8.2 %copy-start.1 = (bf16[1,2048,1,128]{3,1,2,0:T(8,128)(2,1)S(1)}, bf16[1,2048,1,128]{3,1,2,0:T(8,128)(2,1)}, u32[]{:S(2)}) copy-start(bf16[1,2048,1,128]{3,1,2,0:T(8,128)(2,1)} %param.12) | copy-start | bytes 1572868
  62.1 8.2 %copy-start.2 = (bf16[1,2048,1,128]{3,1,2,0:T(8,128)(2,1)S(1)}, bf16[1,2048,1,128]{3,1,2,0:T(8,128)(2,1)}, u32[]{:S(2)}) copy-start(bf16[1,2048,1,128]{3,1,2,0:T(8,128)(2,1)} %param.13) | copy-start | bytes 1572868
  62.2 8.2 %copy-start.3 = (bf16[1,256,1024]{2,1,0:T(8,128)(2,1)S(1)}, bf16[1,256,1024]{2,1,0:T(8,128)(2,1)}, u32[]{:S(2)}) copy-start(bf16[1,256,1024]{2,1,0:T(8,128)(2,1)} %param.8) | copy-start | bytes 1572868
  62.2 8.0 %collective-permute-start = (bf16[1024,128]{1,0:T(8,128)(2,1)S(1)}, bf16[1024,128]{1,0:T(8,128)(2,1)S(1)}, u32[]{:S(2)}, u32[]{:S(2)}) collective-permute-start(bf16[1024,128]{1,0:T(8,128)(2,1)S(1)} %convolution_convert_fusion.1), channel_id=1, source_target_pairs={{0,4},{4,0},{1,5},{5,1},{2,6},{6,2},{3,7},{7,3},{8,12},{12,8},{9,1... | collective-permute-start | bytes 786440 | tf_op jit(solution)/shard_map/ppermute | solution.py:173
  91.5 26.0 %collective-permute-start.1 = (bf16[4,1024,128]{2,1,0:T(8,128)(2,1)S(1)}, bf16[4,1024,128]{2,1,0:T(8,128)(2,1)}, u32[]{:S(2)}, u32[]{:S(2)}) collective-permute-start(bf16[4,1024,128]{2,1,0:T(8,128)(2,1)S(1)} %constant_dynamic-slice_fusion), channel_id=1, source_target_pairs={{0,4},{4,0},{1,5},{5,1},{2,6},{6,2},{3,7},{7,3},{8,12},{12,8},{9,1... | collective-permute-start | bytes 3145736 | tf_op jit(solution)/shard_map/ppermute | solution.py:188
  108.3 3.2 %copy-start.11 = (bf16[2,8,2,4,1024]{4,3,2,1,0:T(4,128)(2,1)S(1)}, bf16[2,8,2,4,1024]{4,3,2,1,0:T(4,128)(2,1)}, u32[]{:S(2)}) copy-start(bf16[2,8,2,4,1024]{4,3,2,1,0:T(4,128)(2,1)} %reshape.113) | copy-start | bytes 786436
  108.3 3.2 %copy-start.14 = (bf16[4,256,1024]{2,1,0:T(8,128)(2,1)S(1)}, bf16[4,256,1024]{2,1,0:T(8,128)(2,1)}, u32[]{:S(2)}) copy-start(bf16[4,256,1024]{2,1,0:T(8,128)(2,1)} %get-tuple-element.17) | copy-start | bytes 6291460
  111.5 1.3 copy-start.12
  127.1 2.3 %copy-start.6 = (f32[1,1,2,8,2,4,1024]{6,3,5,4,2,1,0:T(8,128)S(1)}, f32[1,1,2,8,2,4,1024]{6,3,5,4,2,1,0:T(8,128)}, u32[]{:S(2)}) copy-start(f32[1,1,2,8,2,4,1024]{6,3,5,4,2,1,0:T(8,128)} %convolution_bitcast_fusion.5) | copy-start | bytes 1572868
  127.1 2.3 %copy-start.7 = (f32[1,1,2,8,2,4,1024]{6,3,5,4,2,1,0:T(8,128)S(1)}, f32[1,1,2,8,2,4,1024]{6,3,5,4,2,1,0:T(8,128)}, u32[]{:S(2)}) copy-start(f32[1,1,2,8,2,4,1024]{6,3,5,4,2,1,0:T(8,128)} %convolution_bitcast_fusion.3) | copy-start | bytes 1572868
  127.1 2.3 %copy-start.8 = (f32[1,1,2,8,2,4,1024]{6,3,5,4,2,1,0:T(8,128)S(1)}, f32[1,1,2,8,2,4,1024]{6,3,5,4,2,1,0:T(8,128)}, u32[]{:S(2)}) copy-start(f32[1,1,2,8,2,4,1024]{6,3,5,4,2,1,0:T(8,128)} %convolution_bitcast_fusion.4) | copy-start | bytes 1572868
  127.1 2.3 %copy-start.9 = (f32[1,1,2,8,2,4,1024]{6,3,5,4,2,1,0:T(8,128)S(1)}, f32[1,1,2,8,2,4,1024]{6,3,5,4,2,1,0:T(8,128)}, u32[]{:S(2)}) copy-start(f32[1,1,2,8,2,4,1024]{6,3,5,4,2,1,0:T(8,128)} %fusion.5) | copy-start | bytes 1572868
  127.2 2.3 %copy-start.10 = (f32[1,1,2,8,2,4,1024]{6,3,5,4,2,1,0:T(8,128)S(1)}, f32[1,1,2,8,2,4,1024]{6,3,5,4,2,1,0:T(8,128)}, u32[]{:S(2)}) copy-start(f32[1,1,2,8,2,4,1024]{6,3,5,4,2,1,0:T(8,128)} %convolution_bitcast_fusion.2) | copy-start | bytes 1572868
  130.0 2.6 %copy-start.4 = (f32[2,4,2,8,2,4,1024]{6,3,5,4,2,1,0:T(8,128)}, f32[2,4,2,8,2,4,1024]{6,3,5,4,2,1,0:T(8,128)S(1)}, u32[]{:S(2)}) copy-start(f32[2,4,2,8,2,4,1024]{6,3,5,4,2,1,0:T(8,128)S(1)} %maximum_maximum_fusion) | copy-start | bytes 12582916
  132.6 4.4 %collective-permute-start.2 = (f32[2,4,2,8,4,1024]{5,3,4,2,1,0:T(8,128)}, f32[2,4,2,8,4,1024]{5,3,4,2,1,0:T(8,128)S(1)}, u32[]{:S(2)}, u32[]{:S(2)}) collective-permute-start(f32[2,4,2,8,4,1024]{5,3,4,2,1,0:T(8,128)} %dynamic-slice_bitcast_fusion), channel_id=1, source_target_pairs={{0,8},{8,0},{1,9},{9,1},{2,10},{10,2},{3,11},{11,3},{4,12},{12,4},... | collective-permute-start | bytes 6291464 | tf_op jit(solution)/shard_map/ppermute | solution.py:209
  185.1 5.9 %collective-permute-start.4 = (f32[4,4,1024]{2,1,0:T(4,128)S(1)}, f32[4,4,1024]{2,1,0:T(4,128)S(1)}, u32[]{:S(2)}, u32[]{:S(2)}) collective-permute-start(f32[4,4,1024]{2,1,0:T(4,128)S(1)} %get-tuple-element.34), channel_id=1, source_target_pairs={{0,4},{4,0},{1,5},{5,1},{2,6},{6,2},{3,7},{7,3},{8,12},{12,8},{9,1... | collective-permute-start | bytes 196616 | tf_op jit(solution)/shard_map/ppermute | solution.py:220
  188.3 5.5 %collective-permute-start.5 = (f32[4,4,1024]{2,1,0:T(4,128)S(1)}, f32[4,4,1024]{2,1,0:T(4,128)S(1)}, u32[]{:S(2)}, u32[]{:S(2)}) collective-permute-start(f32[4,4,1024]{2,1,0:T(4,128)S(1)} %get-tuple-element.35), channel_id=1, source_target_pairs={{0,132},{132,0},{4,128},{128,4},{1,133},{133,1},{5,129},{129,5},{2... | collective-permute-start | bytes 196616 | tf_op jit(solution)/shard_map/ppermute | solution.py:221
  189.3 4.4 %collective-permute-start.3 = (f32[4,4,1024]{2,1,0:T(4,128)S(1)}, f32[4,4,1024]{2,1,0:T(4,128)S(1)}, u32[]{:S(2)}, u32[]{:S(2)}) collective-permute-start(f32[4,4,1024]{2,1,0:T(4,128)S(1)} %slice_bitcast_fusion.4), channel_id=1, source_target_pairs={{0,128},{128,0},{1,129},{129,1},{2,130},{130,2},{3,131},{131,3},{4... | collective-permute-start | bytes 196616 | tf_op jit(solution)/shard_map/ppermute | solution.py:219
Sparse Core Ops, SparseCore 0:
  14.8 43.9 all-gather.2
  142.3 41.6 reduce-scatter.1

commit v18 on v14

--- a/solution.py
+++ b/solution.py
@@ -9,7 +9,7 @@
 
 HD = 128
 BLOCK = 128
-ROWS = 256
+ROWS = 512
 
 masked_score = -1e30
 

time: 203 us -> 203 us (level)
  no operation moved by 1% of the time
where the time goes in v18:
time: 203 us; the launch traced here: 202 us
  waiting for transfers between devices  70.5 us (35%)
  Pallas kernels  47.4 us (23%)
  local copies, waits for them, and re-layouts  26.1 us (13%)
  matrix products  20 us (10%)
  between operations  14.5 us (7%)
  starting transfers between devices  10.6 us (5%)
  blocking collectives  7.45 us (4%)
  other arithmetic  5.48 us (3%)
    reduce_scatter x1, waiting for transfers between devices, local(): lax.psum_scatter(terms.reshape(nz, -1, 128), 'dpz', scatter_dimension=0,...  41.8 us
    pallas_call x1, Pallas kernels, seq_gather(): pl.pallas_call(functools.partial(gather_kernel, nseq), in_specs=[any_spec...  26.6 us
    pallas_call x1, Pallas kernels, attention_backward(): pl.pallas_call(functools.partial(attention_kernel, nseq), grid=(length //...  20.9 us
    all_gather x1, waiting for transfers between devices, local(): gathered = lax.all_gather(gathered, 'dpz', axis=0)  14.9 us
    all_gather x1, blocking collectives, local(): lax.all_gather(out_weight, ('dpy', 'dpc'), axis=0)  7.45 us
    another operation x8, local copies, waits for them, and re-layouts  7.44 us
    dot_general x2, matrix products, terms_of(): lax.dot_general(parts[0], inputs_half, tn, preferred_element_type=jnp.flo...  6.1 us
    ppermute x1, waiting for transfers between devices, local(): terms = kept + lax.ppermute(sent, 'dpc', swap)  4.37 us
  transfers between devices with their start and end apart: 8, of which 7 were waited for; matrix products, arithmetic and copies ran while one was open for 12% of the time, Pallas kernels for 13%

profile of v18, /device:TPU:2, one launch (start us, length us, event | category | flops | bytes accessed | tf_op | source)
XLA Modules:
  0.0 202.1 jit_solution(14124102247986335747)
XLA Ops:
  7.2 7.4 %all-gather = bf16[128,1024]{1,0:T(8,128)(2,1)} all-gather(bf16[32,1024]{1,0:T(8,128)(2,1)} %param.14), channel_id=2, replica_groups=mesh['dpy'=2,'dpz'=8,'dpc'=2,'sqy'=2,'sqx'=4] {'dpy','dpc'}, dimensions={0}, use_global_device_ids=true | all-gather | bytes 327680 | tf_op jit(solution)/shard_map/all_gather | solution.py:164
  14.7 0.7 convert_reduce_fusion
  15.4 1.9 bitcast_multiply_fusion.a_ref
  17.4 26.6 %shard_map.111 = bf16[4,256,1024]{2,1,0:T(8,128)(2,1)} custom-call(bf16[256,1024]{1,0:T(8,128)(2,1)} %bitcast_multiply_fusion.a_ref), custom_call_target="tpu_custom_call" | custom-call | tf_op jit(solution)/shard_map/pallas_call | solution.py:136
  44.0 14.9 %all-gather.3.cloned.1.call-done = bf16[8,2,2,32,1024]{4,3,2,0,1:T(8,128)(2,1)} async-done(((bf16[1,2,2,32,1024]{4,3,2,0,1:T(8,128)(2,1)}), bf16[8,2,2,32,1024]{4,3,2,0,1:T(8,128)(2,1)}) %all-gather.3.cloned.1.call-update) | async-done | bytes 2097168 | tf_op jit(solution)/shard_map/all_gather | solution.py:165
  58.8 2.3 %convolution_convert_fusion = bf16[1024,128]{1,0:T(8,128)(2,1)S(1)} fusion(bf16[1024,1024]{1,0:T(8,128)(2,1)} %bitcast.126, bf16[1024,1024]{1,0:T(8,128)(2,1)} %bitcast.131, s32[]{:T(128)S(6)} %select_n.30), kind=kOutput, calls=%fused_computation.13 | convolution fusion | flops 268566528 | bytes 2621444 | tf_op jit(solution)/shard_map/dot_general | solution.py:173
  61.2 3.1 %collective-permute-start = (bf16[1024,128]{1,0:T(8,128)(2,1)S(1)}, bf16[1024,128]{1,0:T(8,128)(2,1)S(1)}, u32[]{:S(2)}, u32[]{:S(2)}) collective-permute-start(bf16[1024,128]{1,0:T(8,128)(2,1)S(1)} %convolution_convert_fusion), channel_id=1, source_target_pairs={{0,4},{4,0},{1,5},{5,1},{2,6},{6,2},{3,7},{7,3},{8,12},{12,8},{9,1... | collective-permute-start | bytes 786440 | tf_op jit(solution)/shard_map/ppermute | solution.py:174
  64.4 1.8 fusion.1
  66.2 3.0 %collective-permute-done = bf16[1024,128]{1,0:T(8,128)(2,1)S(1)} collective-permute-done((bf16[1024,128]{1,0:T(8,128)(2,1)S(1)}, bf16[1024,128]{1,0:T(8,128)(2,1)S(1)}, u32[]{:S(2)}, u32[]{:S(2)}) %collective-permute-start) | collective-permute-done | bytes 262176 | tf_op jit(solution)/shard_map/ppermute | solution.py:174
  69.3 20.9 %shard_map.112 = (bf16[2048,128]{1,0:T(8,128)(2,1)S(1)}, bf16[2048,128]{1,0:T(8,128)(2,1)S(1)}, bf16[2048,128]{1,0:T(8,128)(2,1)S(1)}, bf16[2048,128]{1,0:T(8,128)(2,1)S(1)}, bf16[4,256,1024]{2,1,0:T(8,128)(2,1)}) custom-call(bf16[2048,128]{1,0:T(8,128)(2,1)S(1)} %bitcast.122, bf16[2048,128]{1,0:T(8,128)(2,1)S(1)} %bitcast.123, ...), custom_call_target="tpu_custom_call" | custom-call | flops 6442450944 | bytes 4194304 | tf_op jit(solution)/shard_map/pallas_call | solution.py:76
  90.6 3.3 %collective-permute-start.1 = (bf16[4,1024,128]{2,1,0:T(8,128)(2,1)S(1)}, bf16[4,1024,128]{2,1,0:T(8,128)(2,1)}, u32[]{:S(2)}, u32[]{:S(2)}) collective-permute-start(bf16[4,1024,128]{2,1,0:T(8,128)(2,1)S(1)} %constant_dynamic-slice_fusion), channel_id=1, source_target_pairs={{0,4},{4,0},{1,5},{5,1},{2,6},{6,2},{3,7},{7,3},{8,12},{12,8},{9,1... | collective-permute-start | bytes 3145736 | tf_op jit(solution)/shard_map/ppermute | solution.py:187
  93.8 0.9 dynamic-slice_bitcast_fusion.4
  94.8 1.8 copy.42
  96.6 1.7 reshape.110
  98.3 1.8 copy.46
  100.1 1.8 reshape.113
  101.9 1.8 copy.44
  103.7 1.8 reshape.112
  105.4 0.9 copy.48
  106.3 1.1 reshape.114
  107.4 3.2 %convolution_bitcast_fusion.7 = f32[1,1,2,8,2,4,1024]{6,3,5,4,2,1,0:T(8,128)} fusion(bf16[1024,1024,1,1,1]{1,0,4,3,2:T(8,128)(2,1)} %bitcast.134, bf16[2,8,2,4,1024]{4,3,2,1,0:T(4,128)(2,1)} %reshape.110), kind=kOutput, calls=%fused_computation.12 | convolution fusion | flops 268435456 | bytes 2883584 | tf_op jit(solution)/shard_map/dot_general | solution.py:193
  110.5 1.3 convolution_bitcast_fusion.5
  111.8 1.3 convolution_bitcast_fusion.6
  113.2 1.3 convolution_bitcast_fusion.4
  114.5 2.0 %collective-permute-done.1 = bf16[4,1024,128]{2,1,0:T(8,128)(2,1)} collective-permute-done((bf16[4,1024,128]{2,1,0:T(8,128)(2,1)S(1)}, bf16[4,1024,128]{2,1,0:T(8,128)(2,1)}, u32[]{:S(2)}, u32[]{:S(2)}) %collective-permute-start.1) | collective-permute-done | bytes 1048608 | tf_op jit(solution)/shard_map/ppermute | solution.py:187
  116.6 1.3 slice_bitcast_fusion.3
  118.1 2.9 %convolution_bitcast_fusion.3 = f32[1,1,2,8,2,4,1024]{6,3,5,4,2,1,0:T(8,128)} fusion(bf16[1024,1024,1,1,1]{1,0,4,3,2:T(8,128)(2,1)} %bitcast.135, bf16[2,8,2,4,1024]{4,3,2,1,0:T(4,128)(2,1)S(1)} %reshape.115), kind=kOutput, calls=%fused_computation.8 | convolution fusion | flops 268435456 | bytes 2883584 | tf_op jit(solution)/shard_map/dot_general | solution.py:193
  121.2 0.8 reshape.118
  122.0 1.5 convolution_bitcast_fusion
  123.7 2.1 %convolution_bitcast_fusion.1 = f32[1,1,2,8,2,4,1024]{6,3,5,4,2,1,0:T(8,128)S(1)} fusion(bf16[1024,1024,1,1,1]{1,0,4,3,2:T(8,128)(2,1)} %bitcast.136, bf16[2,8,2,4,1024]{4,3,2,1,0:T(4,128)(2,1)S(1)} %reshape.117), kind=kOutput, calls=%fused_computation.6 | convolution fusion | flops 268435456 | bytes 2883584 | tf_op jit(solution)/shard_map/dot_general | solution.py:195
  126.2 2.3 %convolution_bitcast_fusion.2 = f32[1,1,2,8,2,4,1024]{6,3,5,4,2,1,0:T(8,128)S(1)} fusion(bf16[1024,1024,1,1,1]{1,0,4,3,2:T(8,128)(2,1)} %bitcast.137, bf16[2,8,2,4,1024]{4,3,2,1,0:T(4,128)(2,1)S(1)} %reshape.116), kind=kOutput, calls=%fused_computation.7 | convolution fusion | flops 268435456 | bytes 2883584 | tf_op jit(solution)/shard_map/dot_general | solution.py:194
  128.5 0.5 maximum_maximum_fusion
  129.1 1.6 dynamic-slice_bitcast_fusion
  130.7 1.0 copy-done.4
  131.7 4.4 %collective-permute-done.2 = f32[2,4,2,8,4,1024]{5,3,4,2,1,0:T(8,128)S(1)} collective-permute-done((f32[2,4,2,8,4,1024]{5,3,4,2,1,0:T(8,128)}, f32[2,4,2,8,4,1024]{5,3,4,2,1,0:T(8,128)S(1)}, u32[]{:S(2)}, u32[]{:S(2)}) %collective-permute-start.2) | collective-permute-done | bytes 2097184 | tf_op jit(solution)/shard_map/ppermute | solution.py:208
  136.0 2.0 fusion
  138.0 1.4 copy.58
  139.4 1.8 reshape.119
  141.2 41.8 %reduce-scatter.2.cloned.1.call-done = f32[1,512,128]{2,1,0:T(8,128)} async-done(((f32[8,512,128]{2,1,0:T(8,128)}), f32[1,512,128]{2,1,0:T(8,128)}) %reduce-scatter.2.cloned.1.call-update) | async-done | bytes 262160 | tf_op jit(solution)/shard_map/reduce_scatter | solution.py:210
  183.1 1.0 reshape.120
  184.2 3.0 %collective-permute-start.4 = (f32[4,4,1024]{2,1,0:T(4,128)S(1)}, f32[4,4,1024]{2,1,0:T(4,128)S(1)}, u32[]{:S(2)}, u32[]{:S(2)}) collective-permute-start(f32[4,4,1024]{2,1,0:T(4,128)S(1)} %get-tuple-element.30), channel_id=1, source_target_pairs={{0,4},{4,0},{1,5},{5,1},{2,6},{6,2},{3,7},{7,3},{8,12},{12,8},{9,1... | collective-permute-start | bytes 196616 | tf_op jit(solution)/shard_map/ppermute | solution.py:219
  187.2 1.1 collective-permute-start.5
  188.3 1.7 collective-permute-done.4
  190.0 2.7 %collective-permute-done.5 = f32[4,4,1024]{2,1,0:T(4,128)S(1)} collective-permute-done((f32[4,4,1024]{2,1,0:T(4,128)S(1)}, f32[4,4,1024]{2,1,0:T(4,128)S(1)}, u32[]{:S(2)}, u32[]{:S(2)}) %collective-permute-start.5) | collective-permute-done | bytes 65568 | tf_op jit(solution)/shard_map/ppermute | solution.py:220
  192.8 0.6 copy.64
  193.4 0.6 copy.63
  194.0 0.6 copy.62
  194.6 0.6 copy.61
  (53 shorter events, 1.7 us)
Async XLA Ops:
  7.2 51.7 %all-gather.3.cloned.1.call-start = ((), (), s32[]{:S(2)}) async-start(), calls=%async_computation.1 | async-start | bytes 2359296 | tf_op jit(solution)/shard_map/all_gather | solution.py:165
  14.7 168.4 %reduce-scatter.2.cloned.1.call-start = ((), (), s32[]{:S(2)}) async-start(), calls=%async_computation.2 | async-start | bytes 2359296 | tf_op jit(solution)/shard_map/reduce_scatter | solution.py:210
  44.0 20.4 %copy-start.5 = (bf16[4,256,1024]{2,1,0:T(8,128)(2,1)S(1)}, bf16[4,256,1024]{2,1,0:T(8,128)(2,1)}, u32[]{:S(2)}) copy-start(bf16[4,256,1024]{2,1,0:T(8,128)(2,1)} %shard_map.111) | copy-start | bytes 6291460
  61.1 8.1 %copy-start.13 = (s32[1,1,16,16]{3,2,1,0:T(8,128)S(1)}, s32[1,1,16,16]{3,2,1,0:T(8,128)}, u32[]{:S(2)}) copy-start(s32[1,1,16,16]{3,2,1,0:T(8,128)} %param.15) | copy-start | bytes 3076
  61.1 8.2 %copy-start = (bf16[1,2048,1,128]{3,1,2,0:T(8,128)(2,1)S(1)}, bf16[1,2048,1,128]{3,1,2,0:T(8,128)(2,1)}, u32[]{:S(2)}) copy-start(bf16[1,2048,1,128]{3,1,2,0:T(8,128)(2,1)} %param.11) | copy-start | bytes 1572868
  61.2 8.2 %copy-start.1 = (bf16[1,2048,1,128]{3,1,2,0:T(8,128)(2,1)S(1)}, bf16[1,2048,1,128]{3,1,2,0:T(8,128)(2,1)}, u32[]{:S(2)}) copy-start(bf16[1,2048,1,128]{3,1,2,0:T(8,128)(2,1)} %param.12) | copy-start | bytes 1572868
  61.2 8.2 %copy-start.2 = (bf16[1,2048,1,128]{3,1,2,0:T(8,128)(2,1)S(1)}, bf16[1,2048,1,128]{3,1,2,0:T(8,128)(2,1)}, u32[]{:S(2)}) copy-start(bf16[1,2048,1,128]{3,1,2,0:T(8,128)(2,1)} %param.13) | copy-start | bytes 1572868
  61.2 8.2 %copy-start.3 = (bf16[1,256,1024]{2,1,0:T(8,128)(2,1)S(1)}, bf16[1,256,1024]{2,1,0:T(8,128)(2,1)}, u32[]{:S(2)}) copy-start(bf16[1,256,1024]{2,1,0:T(8,128)(2,1)} %param.8) | copy-start | bytes 1572868
  61.2 8.0 %collective-permute-start = (bf16[1024,128]{1,0:T(8,128)(2,1)S(1)}, bf16[1024,128]{1,0:T(8,128)(2,1)S(1)}, u32[]{:S(2)}, u32[]{:S(2)}) collective-permute-start(bf16[1024,128]{1,0:T(8,128)(2,1)S(1)} %convolution_convert_fusion), channel_id=1, source_target_pairs={{0,4},{4,0},{1,5},{5,1},{2,6},{6,2},{3,7},{7,3},{8,12},{12,8},{9,1... | collective-permute-start | bytes 786440 | tf_op jit(solution)/shard_map/ppermute | solution.py:174
  90.6 26.0 %collective-permute-start.1 = (bf16[4,1024,128]{2,1,0:T(8,128)(2,1)S(1)}, bf16[4,1024,128]{2,1,0:T(8,128)(2,1)}, u32[]{:S(2)}, u32[]{:S(2)}) collective-permute-start(bf16[4,1024,128]{2,1,0:T(8,128)(2,1)S(1)} %constant_dynamic-slice_fusion), channel_id=1, source_target_pairs={{0,4},{4,0},{1,5},{5,1},{2,6},{6,2},{3,7},{7,3},{8,12},{12,8},{9,1... | collective-permute-start | bytes 3145736 | tf_op jit(solution)/shard_map/ppermute | solution.py:187
  107.3 3.2 %copy-start.11 = (bf16[2,8,2,4,1024]{4,3,2,1,0:T(4,128)(2,1)S(1)}, bf16[2,8,2,4,1024]{4,3,2,1,0:T(4,128)(2,1)}, u32[]{:S(2)}) copy-start(bf16[2,8,2,4,1024]{4,3,2,1,0:T(4,128)(2,1)} %reshape.113) | copy-start | bytes 786436
  107.3 3.2 %copy-start.14 = (bf16[4,256,1024]{2,1,0:T(8,128)(2,1)S(1)}, bf16[4,256,1024]{2,1,0:T(8,128)(2,1)}, u32[]{:S(2)}) copy-start(bf16[4,256,1024]{2,1,0:T(8,128)(2,1)} %get-tuple-element.13) | copy-start | bytes 6291460
  110.5 1.3 copy-start.12
  126.1 2.3 %copy-start.6 = (f32[1,1,2,8,2,4,1024]{6,3,5,4,2,1,0:T(8,128)S(1)}, f32[1,1,2,8,2,4,1024]{6,3,5,4,2,1,0:T(8,128)}, u32[]{:S(2)}) copy-start(f32[1,1,2,8,2,4,1024]{6,3,5,4,2,1,0:T(8,128)} %convolution_bitcast_fusion.7) | copy-start | bytes 1572868
  126.1 2.3 %copy-start.7 = (f32[1,1,2,8,2,4,1024]{6,3,5,4,2,1,0:T(8,128)S(1)}, f32[1,1,2,8,2,4,1024]{6,3,5,4,2,1,0:T(8,128)}, u32[]{:S(2)}) copy-start(f32[1,1,2,8,2,4,1024]{6,3,5,4,2,1,0:T(8,128)} %convolution_bitcast_fusion.5) | copy-start | bytes 1572868
  126.2 2.3 %copy-start.8 = (f32[1,1,2,8,2,4,1024]{6,3,5,4,2,1,0:T(8,128)S(1)}, f32[1,1,2,8,2,4,1024]{6,3,5,4,2,1,0:T(8,128)}, u32[]{:S(2)}) copy-start(f32[1,1,2,8,2,4,1024]{6,3,5,4,2,1,0:T(8,128)} %convolution_bitcast_fusion.6) | copy-start | bytes 1572868
  126.2 2.3 %copy-start.9 = (f32[1,1,2,8,2,4,1024]{6,3,5,4,2,1,0:T(8,128)S(1)}, f32[1,1,2,8,2,4,1024]{6,3,5,4,2,1,0:T(8,128)}, u32[]{:S(2)}) copy-start(f32[1,1,2,8,2,4,1024]{6,3,5,4,2,1,0:T(8,128)} %convolution_bitcast_fusion.4) | copy-start | bytes 1572868
  126.2 2.3 %copy-start.10 = (f32[1,1,2,8,2,4,1024]{6,3,5,4,2,1,0:T(8,128)S(1)}, f32[1,1,2,8,2,4,1024]{6,3,5,4,2,1,0:T(8,128)}, u32[]{:S(2)}) copy-start(f32[1,1,2,8,2,4,1024]{6,3,5,4,2,1,0:T(8,128)} %convolution_bitcast_fusion.3) | copy-start | bytes 1572868
  129.1 2.6 %copy-start.4 = (f32[2,4,2,8,2,4,1024]{6,3,5,4,2,1,0:T(8,128)}, f32[2,4,2,8,2,4,1024]{6,3,5,4,2,1,0:T(8,128)S(1)}, u32[]{:S(2)}) copy-start(f32[2,4,2,8,2,4,1024]{6,3,5,4,2,1,0:T(8,128)S(1)} %maximum_maximum_fusion) | copy-start | bytes 12582916
  131.7 4.4 %collective-permute-start.2 = (f32[2,4,2,8,4,1024]{5,3,4,2,1,0:T(8,128)}, f32[2,4,2,8,4,1024]{5,3,4,2,1,0:T(8,128)S(1)}, u32[]{:S(2)}, u32[]{:S(2)}) collective-permute-start(f32[2,4,2,8,4,1024]{5,3,4,2,1,0:T(8,128)} %dynamic-slice_bitcast_fusion), channel_id=1, source_target_pairs={{0,8},{8,0},{1,9},{9,1},{2,10},{10,2},{3,11},{11,3},{4,12},{12,4},... | collective-permute-start | bytes 6291464 | tf_op jit(solution)/shard_map/ppermute | solution.py:208
  184.2 5.9 %collective-permute-start.4 = (f32[4,4,1024]{2,1,0:T(4,128)S(1)}, f32[4,4,1024]{2,1,0:T(4,128)S(1)}, u32[]{:S(2)}, u32[]{:S(2)}) collective-permute-start(f32[4,4,1024]{2,1,0:T(4,128)S(1)} %get-tuple-element.30), channel_id=1, source_target_pairs={{0,4},{4,0},{1,5},{5,1},{2,6},{6,2},{3,7},{7,3},{8,12},{12,8},{9,1... | collective-permute-start | bytes 196616 | tf_op jit(solution)/shard_map/ppermute | solution.py:219
  187.2 5.5 %collective-permute-start.5 = (f32[4,4,1024]{2,1,0:T(4,128)S(1)}, f32[4,4,1024]{2,1,0:T(4,128)S(1)}, u32[]{:S(2)}, u32[]{:S(2)}) collective-permute-start(f32[4,4,1024]{2,1,0:T(4,128)S(1)} %get-tuple-element.31), channel_id=1, source_target_pairs={{0,132},{132,0},{4,128},{128,4},{1,133},{133,1},{5,129},{129,5},{2... | collective-permute-start | bytes 196616 | tf_op jit(solution)/shard_map/ppermute | solution.py:220
  188.3 4.4 %collective-permute-start.3 = (f32[4,4,1024]{2,1,0:T(4,128)S(1)}, f32[4,4,1024]{2,1,0:T(4,128)S(1)}, u32[]{:S(2)}, u32[]{:S(2)}) collective-permute-start(f32[4,4,1024]{2,1,0:T(4,128)S(1)} %slice_bitcast_fusion.4), channel_id=1, source_target_pairs={{0,128},{128,0},{1,129},{129,1},{2,130},{130,2},{3,131},{131,3},{4... | collective-permute-start | bytes 196616 | tf_op jit(solution)/shard_map/ppermute | solution.py:218
Sparse Core Ops, SparseCore 0:
  14.8 43.9 all-gather.2
  141.4 41.6 reduce-scatter.1
